TPU v7x, 32 devices: a whole 2x2x4 slice. The times are simulated.
32 devices in a mesh: groups: 2 (over y), space: 16 (over z, x, core).
Axes of the slice: x: 2, y: 2, z: 4, core: 2. Of those that a mesh axis runs over, the one named last changes fastest.
Arguments:
- coarse_input: bfloat16 [256, 16, 256], P('groups', 'space'), parts along dimension 0, may hold values from -6 to 6
- skip: bfloat16 [128, 32, 1024], P('groups', None, 'space'), parts along dimension 0, may hold values from -6 to 6
- cotangent: bfloat16 [128, 32, 1024], P('groups', 'space'), parts along dimension 0, may hold values from -6 to 6
- w_up: bfloat16 [8, 64, 128], replicated, may hold values from -0.5 to 0.5
- w_conv: bfloat16 [27, 64, 128], replicated, may hold values from -0.109375 to 0.109375
Outputs:
- activation: bfloat16 [128, 32, 1024], P('groups', 'space'), parts along dimension 0
- grad_input: bfloat16 [256, 16, 256], P('groups', 'space'), parts along dimension 0
- grad_skip: bfloat16 [128, 32, 1024], P('groups', None, 'space'), parts along dimension 0
- grad_w_up: float32 [16, 64, 128], P('groups'), parts along dimension 0
- grad_w_conv: float32 [54, 64, 128], P('groups'), parts along dimension 0
There are 2 independent parts, one for each index of `groups`. A program takes and returns all parts, laid end to end along the dimension named above; an argument that names none is the same for every part. Nothing has to cross between parts.
All inputs are finite; a program needn't handle non-finite values.
Results may differ from a plain program's by a relative error of at most 0.012.
Values may be sent and summed in bfloat16 or wider, within the bound.
No kernel may reach another device: no remote copies, remote signals or barrier semaphores. Data moves between devices by JAX's collectives and lax.ppermute only.
A program may use at most 64 MiB of HBM per device.

v0:
```python
import math

import jax
import jax.numpy as jnp
from jax import lax
from jax.sharding import PartitionSpec as P

W = 128


def padded_2(value, sides, width):
    for axis, dim in sides:
        peers, length = (lax.axis_size(axis), value.shape[dim])
        up = [(i, (i + 1) % peers) for i in range(peers - 1)]
        down = [(j, i) for i, j in up]
        last = lax.slice_in_dim(value, length - width, length, axis=dim)
        leading = lax.slice_in_dim(value, 0, width, axis=dim)
        before = lax.ppermute(last, axis, up)
        after = lax.ppermute(leading, axis, down)
        value = jnp.concatenate([before, value, after], axis=dim)
    return value


def upsample(coarse, w_up, height, width):
    channels = coarse.shape[0]
    planes = coarse.shape[1]
    outputs = w_up.shape[1]
    terms = jnp.dot(
        w_up.reshape(8 * outputs, channels),
        coarse.reshape(channels, -1),
        preferred_element_type=jnp.float32,
    )
    terms = terms.reshape(2, 2, 2, outputs, planes, height // 2, width // 2)
    terms = terms.transpose(3, 4, 0, 5, 1, 6, 2)
    return terms.reshape(outputs, 2 * planes, height, width).astype(jnp.bfloat16)


def pad_sides(volume):
    return jnp.pad(volume, ((0, 0), (0, 0), (1, 1), (1, 1)))


def conv_forward(padded, w_conv, planes, height, width):
    channels = padded.shape[0]
    total = jnp.zeros((w_conv.shape[1], planes * height * width), jnp.float32)
    for depth_tap in range(3):
        for row_tap in range(3):
            for col_tap in range(3):
                window = padded[
                    :,
                    depth_tap : depth_tap + planes,
                    row_tap : row_tap + height,
                    col_tap : col_tap + width,
                ].reshape(channels, -1)
                total = total + jnp.dot(
                    w_conv[9 * depth_tap + 3 * row_tap + col_tap],
                    window,
                    preferred_element_type=jnp.float32,
                )
    return total


def conv_input_grad(padded, w_conv, planes, height, width):
    channels = padded.shape[0]
    total = jnp.zeros((w_conv.shape[2], planes * height * width), jnp.float32)
    for depth_tap in range(3):
        for row_tap in range(3):
            for col_tap in range(3):
                window = padded[
                    :,
                    2 - depth_tap : 2 - depth_tap + planes,
                    2 - row_tap : 2 - row_tap + height,
                    2 - col_tap : 2 - col_tap + width,
                ].reshape(channels, -1)
                total = total + lax.dot_general(
                    w_conv[9 * depth_tap + 3 * row_tap + col_tap],
                    window,
                    (((0,), (0,)), ((), ())),
                    preferred_element_type=jnp.float32,
                )
    return total


def conv_weight_grad(padded, grad_flat, planes, height, width):
    channels = padded.shape[0]
    results = []
    for depth_tap in range(3):
        for row_tap in range(3):
            for col_tap in range(3):
                window = padded[
                    :,
                    depth_tap : depth_tap + planes,
                    row_tap : row_tap + height,
                    col_tap : col_tap + width,
                ].reshape(channels, -1)
                results.append(
                    lax.dot_general(
                        grad_flat,
                        window,
                        (((1,), (1,)), ((), ())),
                        preferred_element_type=jnp.float32,
                    )
                )
    return jnp.stack(results, 0)


def local(coarse_input, skip, cotangent, w_up, w_conv):
    devices = lax.axis_size("space")
    channels_in = coarse_input.shape[0]
    coarse_planes = coarse_input.shape[1]
    up_channels = w_up.shape[1]
    skip_channels = skip.shape[0]
    out_channels = cotangent.shape[0]
    planes = cotangent.shape[1]
    cells = cotangent.shape[2]
    width = W
    height = cells // width
    joined_channels = up_channels + skip_channels
    skip_local = lax.all_to_all(skip, "space", split_axis=1, concat_axis=2, tiled=True)
    upsampled = upsample(coarse_input, w_up, height, width)
    joined = jnp.concatenate([upsampled.reshape(up_channels, planes, cells), skip_local], 0)
    joined_ext = padded_2(joined, (("space", 1),), 1)
    joined_pad = pad_sides(joined_ext.reshape(joined_channels, planes + 2, height, width))
    pre = conv_forward(joined_pad, w_conv, planes, height, width)
    gate = jax.nn.sigmoid(pre)
    activation = (pre * gate).astype(jnp.bfloat16).reshape(out_channels, planes, cells)
    grad_pre = (
        cotangent.reshape(out_channels, -1).astype(jnp.float32) * gate * (1.0 + pre * (1.0 - gate))
    ).astype(jnp.bfloat16)
    grad_ext = padded_2(grad_pre.reshape(out_channels, planes, cells), (("space", 1),), 1)
    grad_pad = pad_sides(grad_ext.reshape(out_channels, planes + 2, height, width))
    grad_joined = conv_input_grad(grad_pad, w_conv, planes, height, width)
    grad_up = grad_joined[:up_channels].astype(jnp.bfloat16)
    skip_part = grad_joined[up_channels:].astype(jnp.bfloat16).reshape(skip_channels, planes, cells)
    grad_skip = lax.all_to_all(skip_part, "space", split_axis=2, concat_axis=1, tiled=True)
    arranged = (
        grad_up.reshape(up_channels, coarse_planes, 2, height // 2, 2, width // 2, 2)
        .transpose(2, 4, 6, 0, 1, 3, 5)
        .reshape(8 * up_channels, -1)
    )
    flat_up = w_up.reshape(8 * up_channels, channels_in)
    grad_input = lax.dot_general(
        flat_up, arranged, (((0,), (0,)), ((), ())), preferred_element_type=jnp.float32
    )
    grad_input = grad_input.astype(jnp.bfloat16).reshape(channels_in, coarse_planes, -1)
    local_up = lax.dot_general(
        arranged,
        coarse_input.reshape(channels_in, -1),
        (((1,), (1,)), ((), ())),
        preferred_element_type=jnp.float32,
    )
    local_up = local_up.reshape(8, up_channels, channels_in)
    local_conv = conv_weight_grad(joined_pad, grad_pre, planes, height, width)
    scale = 1.0 / math.sqrt(devices * planes * cells)
    summed_up, summed_conv = lax.psum((local_up * scale, local_conv * scale), "space")
    return (activation, grad_input, grad_skip, summed_up, summed_conv)


def solution(mesh):
    in_specs = (
        P("groups", "space", None),
        P("groups", None, "space"),
        P("groups", "space", None),
        P(),
        P(),
    )
    out_specs = (
        P("groups", "space", None),
        P("groups", "space", None),
        P("groups", None, "space"),
        P("groups", None, None),
        P("groups", None, None),
    )
    return jax.shard_map(local, mesh=mesh, in_specs=in_specs, out_specs=out_specs, check_vma=False)
```

profile of v0, /device:TPU:0, one launch (start us, length us, event | category | flops | bytes accessed | tf_op | source)
XLA Modules:
  0.0 211.5 jit_solution(14226043892768024418)
XLA Ops:
  7.2 1.3 copy.209
  8.5 1.1 reshape.319
  9.6 7.4 %all-to-all-start = ((bf16[16,2,4096]{2,1,0:T(2,128)(2,1)}), bf16[16,2,4096]{2,1,0:T(2,128)(2,1)S(1)}, u32[]{:S(2)}, u32[]{:S(2)}) async-start(bf16[16,2,4096]{2,1,0:T(2,128)(2,1)} %reshape.319), calls=%async_computation | async-start | bytes 524288 | tf_op jit(solution)/shard_map/all_to_all | solution.py:118
  17.9 9.1 %all-to-all-done = bf16[16,2,4096]{2,1,0:T(2,128)(2,1)S(1)} async-done(((bf16[16,2,4096]{2,1,0:T(2,128)(2,1)}), bf16[16,2,4096]{2,1,0:T(2,128)(2,1)S(1)}, u32[]{:S(2)}, u32[]{:S(2)}) %all-to-all-start) | async-done | bytes 262176 | tf_op jit(solution)/shard_map/all_to_all | solution.py:118
  27.9 1.8 collective-permute-start
  29.7 1.3 collective-permute-start.1
  31.1 2.0 collective-permute-done.1
  33.5 3.6 %pad_slice_fusion = (bf16[128,2,8,128]{0,3,2,1:T(8,128)(2,1)S(1)}, bf16[128,2,8,128]{0,3,2,1:T(8,128)(2,1)S(1)}, bf16[128,2,8,128]{0,3,2,1:T(8,128)(2,1)S(1)}, b...) fusion(bf16[128,4,8,128]{0,3,2,1:T(8,128)(2,1)S(1)} %bitcast.654), kind=kLoop, calls=%fused_computation.87 | loop fusion | bytes 11010048 | tf_op jit(solution)/shard_map/slice | solution.py:48
  46.7 1.1 multiply_convert_fusion
  49.5 2.0 fusion.56
  51.5 1.9 fusion.55
  53.5 1.9 fusion.54
  75.3 6.4 %collective-permute-start.2 = (bf16[64,1,1024]{2,0,1:T(8,128)(2,1)S(1)}, bf16[64,1,1024]{2,0,1:T(8,128)(2,1)S(1)}, u32[]{:S(2)}, u32[]{:S(2)}) collective-permute-start(bf16[64,1,1024]{2,0,1:T(8,128)(2,1)S(1)} %copy.72), channel_id=1, source_target_pairs={{0,1},{1,2},{2,3},{3,4},{4,5},{5,6},{6,7},{7,8},{8,9},{9,10},{10,1... | collective-permute-start | bytes 393224 | tf_op jit(solution)/shard_map/ppermute | solution.py:18
  81.7 1.3 collective-permute-start.3
  83.1 1.0 broadcast_multiply_fusion
  85.1 1.9 select_maximum_fusion
  87.5 1.5 fusion.222
  101.2 1.1 reshape.321
  102.3 8.6 %all-to-all-start.1 = ((bf16[16,2,4096]{2,1,0:T(2,128)(2,1)}), bf16[16,2,4096]{2,1,0:T(2,128)(2,1)S(1)}, u32[]{:S(2)}, u32[]{:S(2)}) async-start(bf16[16,2,4096]{2,1,0:T(2,128)(2,1)} %reshape.321), calls=%async_computation.1 | async-start | bytes 524288 | tf_op jit(solution)/shard_map/all_to_all | solution.py:134
  113.2 9.6 %all-to-all-done.1 = bf16[16,2,4096]{2,1,0:T(2,128)(2,1)S(1)} async-done(((bf16[16,2,4096]{2,1,0:T(2,128)(2,1)}), bf16[16,2,4096]{2,1,0:T(2,128)(2,1)S(1)}, u32[]{:S(2)}, u32[]{:S(2)}) %all-to-all-start.1) | async-done | bytes 262176 | tf_op jit(solution)/shard_map/all_to_all | solution.py:134
  123.2 2.2 %copy.62 = bf16[64,16,2,64]{3,2,1,0:T(2,128)(2,1)} copy(bf16[64,16,2,64]{0,2,3,1:T(2,128)(2,1)S(1)} %bitcast.717) | data formatting | bytes 524288 | tf_op jit(solution)/shard_map/all_to_all | solution.py:134
  125.4 75.4 %all-reduce.5.cloned.1.call-done = (f32[8,64,128]{2,1,0:T(8,128)}, f32[27,64,128]{2,1,0:T(8,128)}) async-done(((f32[8,64,128]{2,1,0:T(8,128)}, f32[27,64,128]{2,1,0:T(8,128)}), (f32[8,64,128]{2,1,0:T(8,128)}, f32[27,64,128]{2,1,0:T(8,128)})) %all-reduce.5.cloned.1.call-update) | async-done | bytes 1146896 | tf_op jit(solution)/shard_map/psum | solution.py:154
  200.9 1.7 copy.238
  202.5 2.2 %copy.239 = f32[27,64,128]{2,1,0:T(8,128)} copy(f32[27,64,128]{2,1,0:T(8,128)} %get-tuple-element.92) | data formatting | bytes 1769472
  (204 shorter events, 48.9 us)
Async XLA Ops:
  7.2 10.0 %copy-start = (bf16[8,64,128]{2,1,0:T(8,128)(2,1)S(1)}, bf16[8,64,128]{2,1,0:T(8,128)(2,1)}, u32[]{:S(2)}) copy-start(bf16[8,64,128]{2,1,0:T(8,128)(2,1)} %param.8) | copy-start | bytes 393220
  7.2 9.8 %copy-start.43 = (bf16[128,1,256]{2,0,1:T(8,128)(2,1)S(1)}, bf16[128,1,256]{2,0,1:T(8,128)(2,1)}, u32[]{:S(2)}) copy-start(bf16[128,1,256]{2,0,1:T(8,128)(2,1)} %param.5) | copy-start | bytes 196612
  9.6 17.4 %all-to-all-start = ((bf16[16,2,4096]{2,1,0:T(2,128)(2,1)}), bf16[16,2,4096]{2,1,0:T(2,128)(2,1)S(1)}, u32[]{:S(2)}, u32[]{:S(2)}) async-start(bf16[16,2,4096]{2,1,0:T(2,128)(2,1)} %reshape.319), calls=%async_computation | async-start | bytes 524288 | tf_op jit(solution)/shard_map/all_to_all | solution.py:118
  17.0 183.9 %all-reduce.5.cloned.1.call-start = ((), (), s32[]{:S(2)}) async-start(), calls=%async_computation.2 | async-start | bytes 2293760 | tf_op jit(solution)/shard_map/psum | solution.py:154
  17.5 13.6 %copy-start.42 = (bf16[64,2,1024]{2,1,0:T(2,128)(2,1)S(1)}, bf16[64,2,1024]{2,1,0:T(2,128)(2,1)}, u32[]{:S(2)}) copy-start(bf16[64,2,1024]{2,1,0:T(2,128)(2,1)} %param.7) | copy-start | bytes 786436
  27.9 3.2 %collective-permute-start = (bf16[128,1,1024]{0,2,1:T(8,128)(2,1)S(1)}, bf16[128,1,1024]{0,2,1:T(8,128)(2,1)S(1)}, u32[]{:S(2)}, u32[]{:S(2)}) collective-permute-start(bf16[128,1,1024]{0,2,1:T(8,128)(2,1)S(1)} %get-tuple-element.78), channel_id=1, source_target_pairs={{0,1},{1,2},{2,3},{3,4},{4,5},{5,6},{6,7},{7,8},{8,9},{9,10},{10,1... | collective-permute-start | bytes 786440 | tf_op jit(solution)/shard_map/ppermute | solution.py:18
  29.7 3.4 %collective-permute-start.1 = (bf16[128,1,1024]{0,2,1:T(8,128)(2,1)S(1)}, bf16[128,1,1024]{0,2,1:T(8,128)(2,1)S(1)}, u32[]{:S(2)}, u32[]{:S(2)}) collective-permute-start(bf16[128,1,1024]{0,2,1:T(8,128)(2,1)S(1)} %get-tuple-element.79), channel_id=1, source_target_pairs={{1,0},{2,1},{3,2},{4,3},{5,4},{6,5},{7,6},{8,7},{9,8},{10,9},{11,1... | collective-permute-start | bytes 786440 | tf_op jit(solution)/shard_map/ppermute | solution.py:19
  37.2 5.8 %copy-start.15 = (bf16[128,2,8,128]{0,3,2,1:T(8,128)(2,1)}, bf16[128,2,8,128]{0,3,2,1:T(8,128)(2,1)S(1)}, u32[]{:S(2)}) copy-start(bf16[128,2,8,128]{0,3,2,1:T(8,128)(2,1)S(1)} %get-tuple-element.63) | copy-start | bytes 1572868
  37.2 6.1 %copy-start.13 = (bf16[128,2,8,128]{0,3,2,1:T(8,128)(2,1)}, bf16[128,2,8,128]{0,3,2,1:T(8,128)(2,1)S(1)}, u32[]{:S(2)}) copy-start(bf16[128,2,8,128]{0,3,2,1:T(8,128)(2,1)S(1)} %get-tuple-element.64) | copy-start | bytes 1572868
  37.2 6.4 %copy-start.11 = (bf16[128,2,8,128]{0,3,2,1:T(8,128)(2,1)}, bf16[128,2,8,128]{0,3,2,1:T(8,128)(2,1)S(1)}, u32[]{:S(2)}) copy-start(bf16[128,2,8,128]{0,3,2,1:T(8,128)(2,1)S(1)} %get-tuple-element.65) | copy-start | bytes 1572868
  37.2 6.7 %copy-start.9 = (bf16[128,2,8,128]{0,3,2,1:T(8,128)(2,1)}, bf16[128,2,8,128]{0,3,2,1:T(8,128)(2,1)S(1)}, u32[]{:S(2)}) copy-start(bf16[128,2,8,128]{0,3,2,1:T(8,128)(2,1)S(1)} %get-tuple-element.66) | copy-start | bytes 1572868
  37.2 7.0 %copy-start.7 = (bf16[128,2,8,128]{0,3,2,1:T(8,128)(2,1)}, bf16[128,2,8,128]{0,3,2,1:T(8,128)(2,1)S(1)}, u32[]{:S(2)}) copy-start(bf16[128,2,8,128]{0,3,2,1:T(8,128)(2,1)S(1)} %get-tuple-element.67) | copy-start | bytes 1572868
  37.2 7.3 %copy-start.5 = (bf16[128,2,8,128]{0,3,2,1:T(8,128)(2,1)}, bf16[128,2,8,128]{0,3,2,1:T(8,128)(2,1)S(1)}, u32[]{:S(2)}) copy-start(bf16[128,2,8,128]{0,3,2,1:T(8,128)(2,1)S(1)} %get-tuple-element.68) | copy-start | bytes 1572868
  37.2 7.6 %copy-start.3 = (bf16[128,2,8,128]{0,3,2,1:T(8,128)(2,1)}, bf16[128,2,8,128]{0,3,2,1:T(8,128)(2,1)S(1)}, u32[]{:S(2)}) copy-start(bf16[128,2,8,128]{0,3,2,1:T(8,128)(2,1)S(1)} %get-tuple-element.69) | copy-start | bytes 1572868
  37.2 9.4 %copy-start.37 = (bf16[128,2,8,128]{0,3,2,1:T(8,128)(2,1)}, bf16[128,2,8,128]{0,3,2,1:T(8,128)(2,1)S(1)}, u32[]{:S(2)}) copy-start(bf16[128,2,8,128]{0,3,2,1:T(8,128)(2,1)S(1)} %get-tuple-element.51) | copy-start | bytes 1572868
  49.5 5.9 %copy-start.2 = (bf16[128,2,8,128]{0,3,2,1:T(8,128)(2,1)S(1)}, bf16[128,2,8,128]{0,3,2,1:T(8,128)(2,1)}, u32[]{:S(2)}) copy-start(bf16[128,2,8,128]{0,3,2,1:T(8,128)(2,1)} %copy-done.1) | copy-start | bytes 1572868
  49.5 6.7 %copy-start.32 = (bf16[128,2,8,128]{0,3,2,1:T(8,128)(2,1)S(1)}, bf16[128,2,8,128]{0,3,2,1:T(8,128)(2,1)}, u32[]{:S(2)}) copy-start(bf16[128,2,8,128]{0,3,2,1:T(8,128)(2,1)} %copy-done.31) | copy-start | bytes 1572868
  49.5 7.6 %copy-start.30 = (bf16[128,2,8,128]{0,3,2,1:T(8,128)(2,1)S(1)}, bf16[128,2,8,128]{0,3,2,1:T(8,128)(2,1)}, u32[]{:S(2)}) copy-start(bf16[128,2,8,128]{0,3,2,1:T(8,128)(2,1)} %copy-done.29) | copy-start | bytes 1572868
  51.5 6.4 %copy-start.28 = (bf16[128,2,8,128]{0,3,2,1:T(8,128)(2,1)S(1)}, bf16[128,2,8,128]{0,3,2,1:T(8,128)(2,1)}, u32[]{:S(2)}) copy-start(bf16[128,2,8,128]{0,3,2,1:T(8,128)(2,1)} %copy-done.27) | copy-start | bytes 1572868
  74.9 8.2 %copy-start.41 = (f32[27,64,128]{2,1,0:T(8,128)S(1)}, f32[27,64,128]{2,1,0:T(8,128)}, u32[]{:S(2)}) copy-start(f32[27,64,128]{2,1,0:T(8,128)} %fusion.31) | copy-start | bytes 2654212
  75.3 8.8 %collective-permute-start.2 = (bf16[64,1,1024]{2,0,1:T(8,128)(2,1)S(1)}, bf16[64,1,1024]{2,0,1:T(8,128)(2,1)S(1)}, u32[]{:S(2)}, u32[]{:S(2)}) collective-permute-start(bf16[64,1,1024]{2,0,1:T(8,128)(2,1)S(1)} %copy.72), channel_id=1, source_target_pairs={{0,1},{1,2},{2,3},{3,4},{4,5},{5,6},{6,7},{7,8},{8,9},{9,10},{10,1... | collective-permute-start | bytes 393224 | tf_op jit(solution)/shard_map/ppermute | solution.py:18
  81.7 3.2 %collective-permute-start.3 = (bf16[64,1,1024]{2,0,1:T(8,128)(2,1)S(1)}, bf16[64,1,1024]{2,0,1:T(8,128)(2,1)S(1)}, u32[]{:S(2)}, u32[]{:S(2)}) collective-permute-start(bf16[64,1,1024]{2,0,1:T(8,128)(2,1)S(1)} %copy.73), channel_id=1, source_target_pairs={{1,0},{2,1},{3,2},{4,3},{5,4},{6,5},{7,6},{8,7},{9,8},{10,9},{11,1... | collective-permute-start | bytes 393224 | tf_op jit(solution)/shard_map/ppermute | solution.py:19
  99.6 11.4 %copy-start.45 = (bf16[64,2048]{1,0:T(8,128)(2,1)S(1)}, bf16[64,2048]{1,0:T(8,128)(2,1)}, u32[]{:S(2)}) copy-start(bf16[64,2048]{1,0:T(8,128)(2,1)} %get-tuple-element.83) | copy-start | bytes 786436
  102.3 20.5 %all-to-all-start.1 = ((bf16[16,2,4096]{2,1,0:T(2,128)(2,1)}), bf16[16,2,4096]{2,1,0:T(2,128)(2,1)S(1)}, u32[]{:S(2)}, u32[]{:S(2)}) async-start(bf16[16,2,4096]{2,1,0:T(2,128)(2,1)} %reshape.321), calls=%async_computation.1 | async-start | bytes 524288 | tf_op jit(solution)/shard_map/all_to_all | solution.py:134
  (29 other events, 106.3 us)
Sparse Core Ops, SparseCore 0:
  100.7 100.1 all-reduce.4
where the time goes:
time: 212 us
  waiting for transfers between devices  97.1 us (46%)
  matrix products  45.7 us (22%)
  starting transfers between devices  26.8 us (13%)
  local copies, waits for them, and re-layouts  23.3 us (11%)
  between operations  15.1 us (7%)
  other arithmetic  3.59 us (2%)
    psum x1, waiting for transfers between devices, local(): lax.psum((local_up * scale, local_conv * scale), 'space')  75.4 us
    dot_general x27, matrix products, conv_weight_grad(): lax.dot_general(grad_flat, window, (((1,), (1,)), ((), ())), preferred_el...  26.1 us
    unnamed x107, local copies, waits for them, and re-layouts  9.8 us
    all_to_all x1, waiting for transfers between devices, local(): lax.all_to_all(skip_part, 'space', split_axis=2, concat_axis=1, tiled=True)  9.63 us
    dot_general x27, matrix products, conv_input_grad(): lax.dot_general(w_conv[9 * depth_tap + 3 * row_tap + col_tap], window, ((...  9.18 us
    all_to_all x1, waiting for transfers between devices, local(): lax.all_to_all(skip, 'space', split_axis=1, concat_axis=2, tiled=True)  9.1 us
    dot_general x27, matrix products, conv_forward(): jnp.dot(w_conv[9 * depth_tap + 3 * row_tap + col_tap], window, preferred_...  8.9 us
    all_to_all x1, starting transfers between devices, local(): lax.all_to_all(skip_part, 'space', split_axis=2, concat_axis=1, tiled=True)  8.65 us
  transfers between devices with their start and end apart: 7, of which 5 were waited for; matrix products, arithmetic and copies ran while one was open for 4% of the time, Pallas kernels for 0%

commit v1 on v0

v1 whole, which is shorter than its diff:
```python
import functools
import math

import jax
import jax.numpy as jnp
from jax import lax
from jax.experimental import pallas as pl
from jax.experimental.pallas import tpu as pltpu

W = 128
AXIS = "space"
BF16 = jnp.bfloat16
F32 = jnp.float32
NT = (((1,), (1,)), ((), ()))


def mm(a, b):
    return jnp.dot(a, b, preferred_element_type=F32)


def one_hot(shape, cond):
    rows = lax.broadcasted_iota(jnp.int32, shape, 0)
    cols = lax.broadcasted_iota(jnp.int32, shape, 1)
    return jnp.where(cond(rows, cols), 1.0, 0.0).astype(BF16)


def row_taps(z, channels):
    zero = jnp.zeros((channels, W), F32)
    low = jnp.concatenate([zero, z[:channels, :-W]], axis=1)
    high = jnp.concatenate([z[2 * channels :, W:], zero], axis=1)
    return z[channels : 2 * channels] + low + high


def row_taps_back(z, channels):
    zero = jnp.zeros((channels, W), F32)
    low = jnp.concatenate([z[:channels, W:], zero], axis=1)
    high = jnp.concatenate([zero, z[2 * channels :, :-W]], axis=1)
    return z[channels : 2 * channels] + low + high


def up_kernel(own_ref, before_ref, after_ref, wup_ref, wf_ref, xu_ref, pre_ref, spread_ref):
    def pick(lane_in, col):
        tap, k, parity, lane = (col >> 9, (col >> 8) & 1, (col >> 7) & 1, col & 127)
        return ((lane_in >> 6) == parity) & (2 * (lane_in & 63) + k == lane + tap - 1)

    select = one_hot((128, 1536), pick)
    weights = jnp.concatenate(
        [jnp.concatenate([wup_ref[2 * ij], wup_ref[2 * ij + 1]], axis=1) for ij in range(4)], axis=0
    )
    for part, ref in enumerate((before_ref, own_ref, after_ref)):
        spread = [mm(ref[:, 128 * t : 128 * t + 128], select).astype(BF16) for t in range(2)]
        for tap in range(3):
            columns = []
            for h in range(4):
                at = 512 * tap + 128 * (h & 1)
                piece = spread[h >> 1]
                columns.append(
                    jnp.concatenate([piece[:, at : at + 128], piece[:, at + 256 : at + 384]], axis=0)
                )
            operand = jnp.concatenate(columns, axis=1)
            if part == 1 and tap == 1:
                spread_ref[...] = operand
            up = mm(weights, operand).astype(BF16)
            for i in range(2):
                for j in range(2):
                    at = (2 * part + i) * 192 + tap * 64
                    for h in range(4):
                        xu_ref[at : at + 64, (2 * h + j) * W : (2 * h + j + 1) * W] = up[
                            (2 * i + j) * 64 : (2 * i + j + 1) * 64, h * W : (h + 1) * W
                        ]
    for j in range(4):
        z = mm(wf_ref[...], xu_ref[j * 192 : j * 192 + 576, :])
        pre_ref[j * 64 : (j + 1) * 64, :] = row_taps(z, 64)


def main_kernel(
    scale,
    own_ref,
    before_ref,
    after_ref,
    cot_ref,
    cot_before_ref,
    cot_after_ref,
    xu_ref,
    pre_ref,
    spread_ref,
    wf_ref,
    wi_ref,
    wg_ref,
    act_ref,
    gi_ref,
    skip_ref,
    gw_ref,
    xs_ref,
    gs_ref,
):
    def pick(row, col):
        out = jnp.where(col >= 384, 1, 0)
        rest = col - 384 * out
        tap, lane = (rest >> 7, rest & 127)
        return (((row >> 6) & 1) == out) & ((row >> 7) * 64 + (row & 63) == lane + tap - 1)

    select = one_hot((256, 768), pick)
    for part, ref in enumerate((before_ref, own_ref, after_ref)):
        left = ref[:, 0].reshape(512, 128)
        right = ref[:, 1].reshape(512, 128)
        placed = mm(jnp.concatenate([left, right], axis=1), select).astype(BF16)
        for parity in range(2):
            for tap in range(3):
                at = (2 * part + parity) * 192 + tap * 64
                for h in range(8):
                    xs_ref[at : at + 64, h * W : (h + 1) * W] = placed[
                        h * 64 : (h + 1) * 64, (3 * parity + tap) * W : (3 * parity + tap + 1) * W
                    ]

    shift = one_hot((128, 256), lambda row, col: row == (col & 127) + 1 - 2 * (col >> 7))
    for j in range(4):
        z = mm(wf_ref[...], xs_ref[j * 192 : j * 192 + 576, :])
        pre = pre_ref[j * 64 : (j + 1) * 64, :] + row_taps(z, 64)
        gate = 1.0 / (1.0 + jnp.exp(-pre))
        if j == 0:
            cot = cot_before_ref[...]
        elif j == 3:
            cot = cot_after_ref[...]
        else:
            cot = cot_ref[:, (j - 1) * 1024 : j * 1024]
            act_ref[:, (j - 1) * 1024 : j * 1024] = (pre * gate).astype(BF16)
        grad = (cot.astype(F32) * gate * (1.0 + pre * (1.0 - gate))).astype(BF16)
        gs_ref[j * 192 + 64 : j * 192 + 128, :] = grad
        tall = jnp.concatenate([grad[:, h * W : (h + 1) * W] for h in range(8)], axis=0)
        moved = mm(tall, shift).astype(BF16)
        for tap in (0, 2):
            at = j * 192 + tap * 64
            for h in range(8):
                gs_ref[at : at + 64, h * W : (h + 1) * W] = moved[
                    h * 64 : (h + 1) * 64, (tap >> 1) * W : (tap >> 1) * W + W
                ]

    zero = jnp.zeros((64, W), BF16)
    grads = []
    for j in (1, 2):
        grad = gs_ref[j * 192 + 64 : j * 192 + 128, :]
        low = jnp.concatenate([grad[:, W:], zero], axis=1)
        high = jnp.concatenate([zero, grad[:, :-W]], axis=1)
        grads.append(jnp.concatenate([low, grad, high], axis=0))
    for a in range(3):
        total = None
        for j in (1, 2):
            pieces = []
            for tap in range(3):
                at = (j + a) * 192 + tap * 64
                pieces += [xu_ref[at : at + 64, :], xs_ref[at : at + 64, :]]
            term = lax.dot_general(
                grads[j - 1], jnp.concatenate(pieces, axis=0), NT, preferred_element_type=F32
            )
            total = term if total is None else total + term
        total = total * scale
        for b in range(3):
            for tap in range(3):
                at = (9 * a + 3 * b + tap) * 64
                gw_ref[at : at + 64, :] = total[b * 64 : (b + 1) * 64, tap * W : (tap + 1) * W]

    lower = lax.broadcasted_iota(jnp.int32, (64, W), 1) < 64
    ups = []
    skips = []
    for j in range(2):
        z = mm(wi_ref[...], gs_ref[j * 192 : j * 192 + 576, :])
        grad = row_taps_back(z, 128)
        ups.append(grad[:64].astype(BF16))
        skips.append(grad[64:])
    for h in range(8):
        first = skips[0][:, h * W : (h + 1) * W]
        second = skips[1][:, h * W : (h + 1) * W]
        skip_ref[2 * h] = jnp.where(lower, first, pltpu.roll(second, 64, 1)).astype(BF16)
        skip_ref[2 * h + 1] = jnp.where(lower, pltpu.roll(first, 64, 1), second).astype(BF16)

    tiles = []
    for h in range(4):
        tiles.append(
            jnp.concatenate(
                [ups[i][:, (2 * h + j) * W : (2 * h + j + 1) * W] for i in range(2) for j in range(2)],
                axis=0,
            )
        )
    grad_up = lax.dot_general(
        jnp.concatenate(tiles, axis=1), spread_ref[...], NT, preferred_element_type=F32
    )
    grad_up = grad_up * scale
    for ij in range(4):
        for k in range(2):
            at = (27 + 2 * ij + k) * 64
            gw_ref[at : at + 64, :] = grad_up[ij * 64 : (ij + 1) * 64, k * W : (k + 1) * W]
    gw_ref[35 * 64 :, :] = jnp.zeros((64, W), F32)

    def part_lanes(row, col):
        return ((row >> 7) == ((col >> 6) & 1)) & ((row & 127) == 2 * (col & 63) + (col >> 7))

    apart = one_hot((256, 256), part_lanes)
    halves = [
        mm(jnp.concatenate([tiles[2 * t], tiles[2 * t + 1]], axis=1), apart).astype(BF16) for t in range(2)
    ]
    operand = jnp.concatenate(
        [jnp.concatenate([half[:, k * W : (k + 1) * W] for half in halves], axis=1) for k in range(2)],
        axis=0,
    )
    gi_ref[...] = mm(wg_ref[...], operand).astype(BF16)


PARAMS = pltpu.CompilerParams(vmem_limit_bytes=56 << 20)


def reduce_weights(partial, n):
    me = lax.axis_index(AXIS)

    def swap(value, bit):
        return lax.ppermute(value, AXIS, [(i, i ^ bit) for i in range(n)])

    half, quarter = (1152, 288)
    core = me & 1
    quad = (me >> 1) & 3
    send = lax.dynamic_slice_in_dim(partial, (1 - core) * half, half, 0).astype(BF16)
    mine = lax.dynamic_slice_in_dim(partial, core * half, half, 0)
    summed = mine + swap(send, 1).astype(F32)
    rounded = summed.astype(BF16)
    total = lax.dynamic_slice_in_dim(summed, quad * quarter, quarter, 0)
    for bit in (1, 2, 3):
        piece = lax.dynamic_slice_in_dim(rounded, (quad ^ bit) * quarter, quarter, 0)
        total = total + swap(piece, 2 * bit).astype(F32)
    bit = 8
    while bit < n:
        own = total.astype(BF16)
        total = own.astype(F32) + swap(own, bit).astype(F32)
        bit *= 2
    own = total.astype(BF16)
    gathered = [own] + [swap(own, 2 * bit) for bit in (1, 2, 3)]
    mine = jnp.zeros((half, W), BF16)
    for bit, piece in enumerate(gathered):
        mine = lax.dynamic_update_slice_in_dim(mine, piece, (quad ^ bit) * quarter, 0)
    other = swap(mine, 1)
    first = jnp.where(core == 0, mine, other)
    second = jnp.where(core == 0, other, mine)
    return jnp.concatenate([first, second], axis=0).astype(F32)


def local(coarse_input, skip, cotangent, w_up, w_conv):
    n = lax.axis_size(AXIS)
    cells = cotangent.shape[2]
    planes = cotangent.shape[1]
    up = [(i, i + 1) for i in range(n - 1)]
    down = [(i + 1, i) for i in range(n - 1)]

    positions = skip.shape[2]
    sent = skip.reshape(64, n, 2 * positions).transpose(1, 0, 2)
    held = lax.all_to_all(sent, AXIS, split_axis=0, concat_axis=0, tiled=True)
    if positions != 64:
        held = held.reshape(n, 64, 2, positions).transpose(1, 2, 0, 3).reshape(64, 2, 16, 64)
        held = held.transpose(2, 0, 1, 3).reshape(16, 64, 128)
    coarse = coarse_input.reshape(128, 256)
    coarse_before = lax.ppermute(coarse, AXIS, up)
    coarse_after = lax.ppermute(coarse, AXIS, down)
    cot_before = lax.ppermute(cotangent[:, 1], AXIS, up)
    cot_after = lax.ppermute(cotangent[:, 0], AXIS, down)
    wc = w_conv.reshape(3, 3, 3, 64, 128)
    forward = wc.transpose(1, 3, 0, 2, 4)
    wf_up = forward[..., :64].reshape(192, 576)
    wf_skip = forward[..., 64:].reshape(192, 576)
    wi = wc[::-1].transpose(1, 4, 0, 2, 3).reshape(384, 576)
    wg = w_up.reshape(2, 2, 2, 64, 128).transpose(4, 2, 0, 1, 3).reshape(128, 512)

    vmem = pl.BlockSpec(memory_space=pltpu.VMEM)
    xu, pre, spread = pl.pallas_call(
        up_kernel,
        out_shape=(
            jax.ShapeDtypeStruct((1152, 1024), BF16),
            jax.ShapeDtypeStruct((256, 1024), F32),
            jax.ShapeDtypeStruct((256, 512), BF16),
        ),
        in_specs=[vmem] * 5,
        out_specs=(vmem,) * 3,
        compiler_params=PARAMS,
        name="upsample",
    )(coarse, coarse_before, coarse_after, w_up, wf_up)

    held_before = lax.ppermute(held, AXIS, up)
    held_after = lax.ppermute(held, AXIS, down)
    scale = 1.0 / math.sqrt(n * planes * cells)
    rows = [v.reshape(8, 2, 64, 128) for v in (held, held_before, held_after)]
    act, gi, skip_part, gw = pl.pallas_call(
        functools.partial(main_kernel, scale),
        out_shape=(
            jax.ShapeDtypeStruct((64, 2048), BF16),
            jax.ShapeDtypeStruct((128, 256), BF16),
            jax.ShapeDtypeStruct((16, 64, 128), BF16),
            jax.ShapeDtypeStruct((2304, 128), F32),
        ),
        in_specs=[vmem] * 12,
        out_specs=(vmem,) * 4,
        scratch_shapes=[pltpu.VMEM((1152, 1024), BF16), pltpu.VMEM((768, 1024), BF16)],
        compiler_params=PARAMS,
        name="section",
    )(
        *rows,
        cotangent.reshape(64, 2048),
        cot_before,
        cot_after,
        xu,
        pre,
        spread,
        wf_skip,
        wi,
        wg,
    )
    summed = reduce_weights(gw, n)
    if positions != 64:
        skip_part = skip_part.reshape(16, 64, 2, 64).transpose(1, 2, 0, 3)
        skip_part = skip_part.reshape(64, 2, n, positions).transpose(2, 0, 1, 3)
        skip_part = skip_part.reshape(n, 64, 2 * positions)
    back = lax.all_to_all(skip_part, AXIS, split_axis=0, concat_axis=0, tiled=True)
    grad_skip = back.transpose(1, 0, 2).reshape(64, 2 * n, positions)
    return (
        act.reshape(64, planes, cells),
        gi.reshape(128, 1, 256),
        grad_skip,
        summed[27 * 64 : 35 * 64].reshape(8, 64, 128),
        summed[: 27 * 64].reshape(27, 64, 128),
    )


def solution(mesh):
    spec = jax.sharding.PartitionSpec
    in_specs = (
        spec("groups", "space", None),
        spec("groups", None, "space"),
        spec("groups", "space", None),
        spec(),
        spec(),
    )
    out_specs = (
        spec("groups", "space", None),
        spec("groups", "space", None),
        spec("groups", None, "space"),
        spec("groups", None, None),
        spec("groups", None, None),
    )
    return jax.shard_map(local, mesh=mesh, in_specs=in_specs, out_specs=out_specs, check_vma=False)
```

time: 212 us -> 93.3 us (0.44)
  waiting for transfers between devices: 97.1 us -> 15.6 us
  matrix products: 45.7 us -> 0 us
  starting transfers between devices: 26.8 us -> 44.3 us
  Pallas kernels: 0 us -> 14.5 us
  between operations: 15.1 us -> 0.95 us
  local copies, waits for them, and re-layouts: 23.3 us -> 14.4 us
    psum x1 -> x0, waiting for transfers between devices: 75.4 us -> none  [local(): lax.psum((local_up * scale, local_conv * scale), 'space')]
    dot_general x84 -> x0, matrix products: 45.7 us -> none  [the longest x27 26.1 us: conv_weight_grad(): lax.dot_general(grad_flat, window, (((1,), (1,)), ((), ())), preferred_el...]
    ppermute x4 -> x15, starting transfers between devices: 10.7 us -> 32 us  [the longest x9 17.3 us: swap(): return lax.ppermute(value, AXIS, [(i, i ^ bit) for i in range(n)])]
    all_to_all x2, waiting for transfers between devices: 18.7 us -> 0.01 us  [the longest x1 0.01 us: local(): lax.all_to_all(skip_part, AXIS, split_axis=0, concat_axis=0, tiled=True)]
    pallas_call x0 -> x2, Pallas kernels: none -> 14.5 us  [the longest x1 9.43 us: local(): pl.pallas_call(functools.partial(main_kernel, scale), out_shape=(jax.Shap...]
    ppermute x4 -> x15, waiting for transfers between devices: 2.87 us -> 15.6 us  [the longest x9 15.6 us: swap(): return lax.ppermute(value, AXIS, [(i, i ^ bit) for i in range(n)])]
    unnamed x107 -> x24, local copies, waits for them, and re-layouts: 9.8 us -> 3.07 us
    slice x7 -> x2, local copies, waits for them, and re-layouts: 7.07 us -> 0.91 us  [the longest x1 0.55 us: local(): wf_skip = forward[..., 64:].reshape(192, 576)]
  transfers between devices with their start and end apart: 7 -> 17, of which waited for: 5 -> 6; matrix products, arithmetic and copies ran while one was open for 4% -> 11% of each run, Pallas kernels for 0% -> 6%
where the time goes in v1:
time: 93.3 us; the launch traced here: 92.7 us
  starting transfers between devices  44.3 us (47%)
  waiting for transfers between devices  15.6 us (17%)
  Pallas kernels  14.5 us (16%)
  local copies, waits for them, and re-layouts  14.4 us (15%)
  other arithmetic  2.97 us (3%)
  between operations  0.95 us (1%)
    ppermute x9, starting transfers between devices, swap(): return lax.ppermute(value, AXIS, [(i, i ^ bit) for i in range(n)])  17.3 us
    ppermute x9, waiting for transfers between devices, swap(): return lax.ppermute(value, AXIS, [(i, i ^ bit) for i in range(n)])  15.6 us
    pallas_call x1, Pallas kernels, local(): pl.pallas_call(functools.partial(main_kernel, scale), out_shape=(jax.Shap...  9.43 us
    all_to_all x1, starting transfers between devices, local(): held = lax.all_to_all(sent, AXIS, split_axis=0, concat_axis=0, tiled=True)  7.49 us
    pallas_call x1, Pallas kernels, local(): pl.pallas_call(up_kernel, out_shape=(jax.ShapeDtypeStruct((1152, 1024), B...  5.1 us
    all_to_all x1, starting transfers between devices, local(): lax.all_to_all(skip_part, AXIS, split_axis=0, concat_axis=0, tiled=True)  4.81 us
    ppermute x1, starting transfers between devices, local(): held_before = lax.ppermute(held, AXIS, up)  4.28 us
    ppermute x1, starting transfers between devices, local(): cot_before = lax.ppermute(cotangent[:, 1], AXIS, up)  4.16 us
  transfers between devices with their start and end apart: 17, of which 6 were waited for; matrix products, arithmetic and copies ran while one was open for 11% of the time, Pallas kernels for 6%

profile of v1, /device:TPU:0, one launch (start us, length us, event | category | flops | bytes accessed | tf_op | source)
XLA Modules:
  0.0 92.7 jit_solution(10337443093889141006)
XLA Ops:
  0.6 1.4 %reshape.61 = bf16[64,16,128]{2,1,0:T(8,128)(2,1)S(1)} reshape(bf16[64,32,64]{2,1,0:T(8,128)(2,1)} %param.6) | data formatting | bytes 524288 | tf_op jit(solution)/shard_map/reshape | solution.py:253
  2.8 7.5 %all-to-all-start = ((bf16[16,64,128]{2,1,0:T(8,128)(2,1)}), bf16[16,64,128]{2,1,0:T(8,128)(2,1)S(1)}, u32[]{:S(2)}, u32[]{:S(2)}) async-start(bf16[16,64,128]{2,1,0:T(8,128)(2,1)} %bitcast.32), calls=%async_computation | async-start | bytes 524288 | tf_op jit(solution)/shard_map/all_to_all | solution.py:254
  10.3 2.3 %collective-permute-start.4 = (bf16[128,256]{1,0:T(8,128)(2,1)}, bf16[128,256]{1,0:T(8,128)(2,1)S(1)}, u32[]{:S(2)}, u32[]{:S(2)}) collective-permute-start(bf16[128,256]{1,0:T(8,128)(2,1)} %bitcast.6.own_ref), channel_id=1, source_target_pairs={{0,1},{1,2},{2,3},{3,4},{4,5},{5,6},{6,7},{7,8},{8,9},{9,10},{10,1... | collective-permute-start | bytes 196616 | tf_op jit(solution)/shard_map/ppermute | solution.py:259
  12.6 1.3 %collective-permute-start.5 = (bf16[128,256]{1,0:T(8,128)(2,1)}, bf16[128,256]{1,0:T(8,128)(2,1)}, u32[]{:S(2)}, u32[]{:S(2)}) collective-permute-start(bf16[128,256]{1,0:T(8,128)(2,1)} %bitcast.6.own_ref), channel_id=1, source_target_pairs={{1,0},{2,1},{3,2},{4,3},{5,4},{6,5},{7,6},{8,7},{9,8},{10,9},{11,1... | collective-permute-start | bytes 196616 | tf_op jit(solution)/shard_map/ppermute | solution.py:260
  15.0 4.2 %collective-permute-start.2 = (bf16[64,1024]{1,0:T(8,128)(2,1)}, bf16[64,1024]{1,0:T(8,128)(2,1)S(1)}, u32[]{:S(2)}, u32[]{:S(2)}) collective-permute-start(bf16[64,1024]{1,0:T(8,128)(2,1)} %bitcast.34), channel_id=1, source_target_pairs={{0,1},{1,2},{2,3},{3,4},{4,5},{5,6},{6,7},{7,8},{8,9},{9,10},{10,1... | collective-permute-start | bytes 393224 | tf_op jit(solution)/shard_map/ppermute | solution.py:261
  19.9 1.3 %collective-permute-start.3 = (bf16[64,1024]{1,0:T(8,128)(2,1)}, bf16[64,1024]{1,0:T(8,128)(2,1)S(1)}, u32[]{:S(2)}, u32[]{:S(2)}) collective-permute-start(bf16[64,1024]{1,0:T(8,128)(2,1)} %bitcast.33), channel_id=1, source_target_pairs={{1,0},{2,1},{3,2},{4,3},{5,4},{6,5},{7,6},{8,7},{9,8},{10,9},{11,1... | collective-permute-start | bytes 393224 | tf_op jit(solution)/shard_map/ppermute | solution.py:262
  21.6 4.3 %collective-permute-start = (bf16[16,64,128]{2,1,0:T(8,128)(2,1)S(1)}, bf16[16,64,128]{2,1,0:T(8,128)(2,1)S(1)}, u32[]{:S(2)}, u32[]{:S(2)}) collective-permute-start(bf16[16,64,128]{2,1,0:T(8,128)(2,1)S(1)} %all-to-all-done), channel_id=1, source_target_pairs={{0,1},{1,2},{2,3},{3,4},{4,5},{5,6},{6,7},{7,8},{8,9},{9,10},{10,1... | collective-permute-start | bytes 786440 | tf_op jit(solution)/shard_map/ppermute | solution.py:284
  25.9 1.3 %collective-permute-start.1 = (bf16[16,64,128]{2,1,0:T(8,128)(2,1)S(1)}, bf16[16,64,128]{2,1,0:T(8,128)(2,1)S(1)}, u32[]{:S(2)}, u32[]{:S(2)}) collective-permute-start(bf16[16,64,128]{2,1,0:T(8,128)(2,1)S(1)} %all-to-all-done), channel_id=1, source_target_pairs={{1,0},{2,1},{3,2},{4,3},{5,4},{6,5},{7,6},{8,7},{9,8},{10,9},{11,1... | collective-permute-start | bytes 786440 | tf_op jit(solution)/shard_map/ppermute | solution.py:285
  33.2 5.1 %upsample.1 = (bf16[1152,1024]{1,0:T(8,128)(2,1)}, f32[256,1024]{1,0:T(8,128)}, bf16[256,512]{1,0:T(8,128)(2,1)}) custom-call(bf16[128,256]{1,0:T(8,128)(2,1)} %bitcast.6.own_ref, bf16[128,256]{1,0:T(8,128)(2,1)} %copy-done.9, bf16[128,256]{1,0:T(8,128)(2,1)} %collective-permute-done.5.after_ref, bf16[8,64,128]{2,1,0:T(8,128)(2,1)} %wup_ref.1, ...), custom_call_target="tpu_custom_call" | custom-call | tf_op jit(solution)/shard_map/upsample/pallas_call | solution.py:271
  39.2 9.4 %section.1 = (bf16[64,2048]{1,0:T(8,128)(2,1)}, bf16[128,256]{1,0:T(8,128)(2,1)}, bf16[16,64,128]{2,1,0:T(8,128)(2,1)}, f32[2304,128]{1,0:T(8,128)}) custom-call(bf16[8,2,64,128]{3,2,1,0:T(8,128)(2,1)} %bitcast.41, bf16[8,2,64,128]{3,2,1,0:T(8,128)(2,1)} %bitcast.47, bf16[8,2,64,128]{3,2,1,0:T(8,128)(2,1)} %bitcast.48, bf16[64,2048]{1,0:T(8,128)(2,1)} %bitcast.42, ...), custom_call_target="tpu_custom_call" | custom-call | tf_op jit(solution)/shard_map/section/pallas_call | solution.py:288
  49.7 2.4 %collective-permute-start.6 = (bf16[1152,128]{1,0:T(8,128)(2,1)S(1)}, bf16[1152,128]{1,0:T(8,128)(2,1)S(1)}, u32[]{:S(2)}, u32[]{:S(2)}) collective-permute-start(bf16[1152,128]{1,0:T(8,128)(2,1)S(1)} %dynamic-slice_convert_fusion), channel_id=1, source_target_pairs={{0,1},{1,0},{2,3},{3,2},{4,5},{5,4},{6,7},{7,6},{8,9},{9,8},{10,11... | collective-permute-start | bytes 884744 | tf_op jit(solution)/shard_map/ppermute | solution.py:216
  54.5 3.3 %collective-permute-start.7 = (bf16[288,128]{1,0:T(8,128)(2,1)S(1)}, bf16[288,128]{1,0:T(8,128)(2,1)S(1)}, u32[]{:S(2)}, u32[]{:S(2)}) collective-permute-start(bf16[288,128]{1,0:T(8,128)(2,1)S(1)} %get-tuple-element.27), channel_id=1, source_target_pairs={{0,2},{1,3},{2,0},{3,1},{4,6},{5,7},{6,4},{7,5},{8,10},{9,11},{10,... | collective-permute-start | bytes 221192 | tf_op jit(solution)/shard_map/ppermute | solution.py:216
  57.8 1.5 %collective-permute-start.8 = (bf16[288,128]{1,0:T(8,128)(2,1)S(1)}, bf16[288,128]{1,0:T(8,128)(2,1)S(1)}, u32[]{:S(2)}, u32[]{:S(2)}) collective-permute-start(bf16[288,128]{1,0:T(8,128)(2,1)S(1)} %get-tuple-element.29), channel_id=1, source_target_pairs={{0,4},{1,5},{2,6},{3,7},{4,0},{5,1},{6,2},{7,3},{8,12},{9,13},{10,... | collective-permute-start | bytes 221192 | tf_op jit(solution)/shard_map/ppermute | solution.py:216
  59.3 1.4 %collective-permute-start.9 = (bf16[288,128]{1,0:T(8,128)(2,1)S(1)}, bf16[288,128]{1,0:T(8,128)(2,1)S(1)}, u32[]{:S(2)}, u32[]{:S(2)}) collective-permute-start(bf16[288,128]{1,0:T(8,128)(2,1)S(1)} %get-tuple-element.28), channel_id=1, source_target_pairs={{0,6},{1,7},{2,4},{3,5},{4,2},{5,3},{6,0},{7,1},{8,14},{9,15},{10,... | collective-permute-start | bytes 221192 | tf_op jit(solution)/shard_map/ppermute | solution.py:216
  60.7 1.5 %collective-permute-done.8 = bf16[288,128]{1,0:T(8,128)(2,1)S(1)} collective-permute-done((bf16[288,128]{1,0:T(8,128)(2,1)S(1)}, bf16[288,128]{1,0:T(8,128)(2,1)S(1)}, u32[]{:S(2)}, u32[]{:S(2)}) %collective-permute-start.8) | collective-permute-done | bytes 73760 | tf_op jit(solution)/shard_map/ppermute | solution.py:216
  62.2 2.4 %collective-permute-done.9 = bf16[288,128]{1,0:T(8,128)(2,1)S(1)} collective-permute-done((bf16[288,128]{1,0:T(8,128)(2,1)S(1)}, bf16[288,128]{1,0:T(8,128)(2,1)S(1)}, u32[]{:S(2)}, u32[]{:S(2)}) %collective-permute-start.9) | collective-permute-done | bytes 73760 | tf_op jit(solution)/shard_map/ppermute | solution.py:216
  64.7 2.9 %collective-permute-start.10 = (bf16[288,128]{1,0:T(8,128)(2,1)S(1)}, bf16[288,128]{1,0:T(8,128)(2,1)S(1)}, u32[]{:S(2)}, u32[]{:S(2)}) collective-permute-start(bf16[288,128]{1,0:T(8,128)(2,1)S(1)} %add_convert_fusion.1), channel_id=1, source_target_pairs={{0,8},{1,9},{2,10},{3,11},{4,12},{5,13},{6,14},{7,15},{8,0},{9,1},... | collective-permute-start | bytes 221192 | tf_op jit(solution)/shard_map/ppermute | solution.py:216
  67.5 2.5 %collective-permute-done.10 = bf16[288,128]{1,0:T(8,128)(2,1)S(1)} collective-permute-done((bf16[288,128]{1,0:T(8,128)(2,1)S(1)}, bf16[288,128]{1,0:T(8,128)(2,1)S(1)}, u32[]{:S(2)}, u32[]{:S(2)}) %collective-permute-start.10) | collective-permute-done | bytes 73760 | tf_op jit(solution)/shard_map/ppermute | solution.py:216
  70.1 2.4 %collective-permute-start.11 = (bf16[288,128]{1,0:T(8,128)(2,1)S(1)}, bf16[288,128]{1,0:T(8,128)(2,1)S(1)}, u32[]{:S(2)}, u32[]{:S(2)}) collective-permute-start(bf16[288,128]{1,0:T(8,128)(2,1)S(1)} %get-tuple-element.20), channel_id=1, source_target_pairs={{0,2},{1,3},{2,0},{3,1},{4,6},{5,7},{6,4},{7,5},{8,10},{9,11},{10,... | collective-permute-start | bytes 221192 | tf_op jit(solution)/shard_map/ppermute | solution.py:216
  72.5 4.8 %all-to-all-start.1 = ((bf16[16,64,128]{2,1,0:T(8,128)(2,1)}), bf16[16,64,128]{2,1,0:T(8,128)(2,1)S(1)}, u32[]{:S(2)}, u32[]{:S(2)}) async-start(bf16[16,64,128]{2,1,0:T(8,128)(2,1)} %get-tuple-element.17), calls=%async_computation.1 | async-start | bytes 524288 | tf_op jit(solution)/shard_map/all_to_all | solution.py:318
  77.3 1.9 %collective-permute-start.12 = (bf16[288,128]{1,0:T(8,128)(2,1)S(1)}, bf16[288,128]{1,0:T(8,128)(2,1)S(1)}, u32[]{:S(2)}, u32[]{:S(2)}) collective-permute-start(bf16[288,128]{1,0:T(8,128)(2,1)S(1)} %get-tuple-element.20), channel_id=1, source_target_pairs={{0,4},{1,5},{2,6},{3,7},{4,0},{5,1},{6,2},{7,3},{8,12},{9,13},{10,... | collective-permute-start | bytes 221192 | tf_op jit(solution)/shard_map/ppermute | solution.py:216
  79.2 1.5 %collective-permute-start.13 = (bf16[288,128]{1,0:T(8,128)(2,1)S(1)}, bf16[288,128]{1,0:T(8,128)(2,1)S(1)}, u32[]{:S(2)}, u32[]{:S(2)}) collective-permute-start(bf16[288,128]{1,0:T(8,128)(2,1)S(1)} %get-tuple-element.20), channel_id=1, source_target_pairs={{0,6},{1,7},{2,4},{3,5},{4,2},{5,3},{6,0},{7,1},{8,14},{9,15},{10,... | collective-permute-start | bytes 221192 | tf_op jit(solution)/shard_map/ppermute | solution.py:216
  80.7 6.0 %collective-permute-done.12 = bf16[288,128]{1,0:T(8,128)(2,1)S(1)} collective-permute-done((bf16[288,128]{1,0:T(8,128)(2,1)S(1)}, bf16[288,128]{1,0:T(8,128)(2,1)S(1)}, u32[]{:S(2)}, u32[]{:S(2)}) %collective-permute-start.12) | collective-permute-done | bytes 73760 | tf_op jit(solution)/shard_map/ppermute | solution.py:216
  86.7 2.0 %collective-permute-done.13 = bf16[288,128]{1,0:T(8,128)(2,1)S(1)} collective-permute-done((bf16[288,128]{1,0:T(8,128)(2,1)S(1)}, bf16[288,128]{1,0:T(8,128)(2,1)S(1)}, u32[]{:S(2)}, u32[]{:S(2)}) %collective-permute-start.13) | collective-permute-done | bytes 73760 | tf_op jit(solution)/shard_map/ppermute | solution.py:216
  (63 shorter events, 17.3 us)
Async XLA Ops:
  0.6 13.3 %copy-start = (bf16[64,2,1024]{2,1,0:T(2,128)(2,1)S(1)}, bf16[64,2,1024]{2,1,0:T(2,128)(2,1)}, u32[]{:S(2)}) copy-start(bf16[64,2,1024]{2,1,0:T(2,128)(2,1)} %param.7) | copy-start | bytes 786436
  2.8 18.4 %copy-start.1 = (bf16[27,64,128]{2,1,0:T(8,128)(2,1)S(1)}, bf16[27,64,128]{2,1,0:T(8,128)(2,1)}, u32[]{:S(2)}) copy-start(bf16[27,64,128]{2,1,0:T(8,128)(2,1)} %param.9) | copy-start | bytes 1327108
  2.8 18.8 %all-to-all-start = ((bf16[16,64,128]{2,1,0:T(8,128)(2,1)}), bf16[16,64,128]{2,1,0:T(8,128)(2,1)S(1)}, u32[]{:S(2)}, u32[]{:S(2)}) async-start(bf16[16,64,128]{2,1,0:T(8,128)(2,1)} %bitcast.32), calls=%async_computation | async-start | bytes 524288 | tf_op jit(solution)/shard_map/all_to_all | solution.py:254
  10.3 15.6 %collective-permute-start.4 = (bf16[128,256]{1,0:T(8,128)(2,1)}, bf16[128,256]{1,0:T(8,128)(2,1)S(1)}, u32[]{:S(2)}, u32[]{:S(2)}) collective-permute-start(bf16[128,256]{1,0:T(8,128)(2,1)} %bitcast.6.own_ref), channel_id=1, source_target_pairs={{0,1},{1,2},{2,3},{3,4},{4,5},{5,6},{6,7},{7,8},{8,9},{9,10},{10,1... | collective-permute-start | bytes 196616 | tf_op jit(solution)/shard_map/ppermute | solution.py:259
  12.6 20.6 %collective-permute-start.5 = (bf16[128,256]{1,0:T(8,128)(2,1)}, bf16[128,256]{1,0:T(8,128)(2,1)}, u32[]{:S(2)}, u32[]{:S(2)}) collective-permute-start(bf16[128,256]{1,0:T(8,128)(2,1)} %bitcast.6.own_ref), channel_id=1, source_target_pairs={{1,0},{2,1},{3,2},{4,3},{5,4},{6,5},{7,6},{8,7},{9,8},{10,9},{11,1... | collective-permute-start | bytes 196616 | tf_op jit(solution)/shard_map/ppermute | solution.py:260
  15.0 23.3 %collective-permute-start.2 = (bf16[64,1024]{1,0:T(8,128)(2,1)}, bf16[64,1024]{1,0:T(8,128)(2,1)S(1)}, u32[]{:S(2)}, u32[]{:S(2)}) collective-permute-start(bf16[64,1024]{1,0:T(8,128)(2,1)} %bitcast.34), channel_id=1, source_target_pairs={{0,1},{1,2},{2,3},{3,4},{4,5},{5,6},{6,7},{7,8},{8,9},{9,10},{10,1... | collective-permute-start | bytes 393224 | tf_op jit(solution)/shard_map/ppermute | solution.py:261
  19.9 18.4 %collective-permute-start.3 = (bf16[64,1024]{1,0:T(8,128)(2,1)}, bf16[64,1024]{1,0:T(8,128)(2,1)S(1)}, u32[]{:S(2)}, u32[]{:S(2)}) collective-permute-start(bf16[64,1024]{1,0:T(8,128)(2,1)} %bitcast.33), channel_id=1, source_target_pairs={{1,0},{2,1},{3,2},{4,3},{5,4},{6,5},{7,6},{8,7},{9,8},{10,9},{11,1... | collective-permute-start | bytes 393224 | tf_op jit(solution)/shard_map/ppermute | solution.py:262
  21.6 6.2 %copy-start.2 = (bf16[16,64,128]{2,1,0:T(8,128)(2,1)}, bf16[16,64,128]{2,1,0:T(8,128)(2,1)S(1)}, u32[]{:S(2)}) copy-start(bf16[16,64,128]{2,1,0:T(8,128)(2,1)S(1)} %all-to-all-done) | copy-start | bytes 786436
  21.6 16.7 %collective-permute-start = (bf16[16,64,128]{2,1,0:T(8,128)(2,1)S(1)}, bf16[16,64,128]{2,1,0:T(8,128)(2,1)S(1)}, u32[]{:S(2)}, u32[]{:S(2)}) collective-permute-start(bf16[16,64,128]{2,1,0:T(8,128)(2,1)S(1)} %all-to-all-done), channel_id=1, source_target_pairs={{0,1},{1,2},{2,3},{3,4},{4,5},{5,6},{6,7},{7,8},{8,9},{9,10},{10,1... | collective-permute-start | bytes 786440 | tf_op jit(solution)/shard_map/ppermute | solution.py:284
  25.9 1.3 %copy-start.9 = (bf16[128,256]{1,0:T(8,128)(2,1)}, bf16[128,256]{1,0:T(8,128)(2,1)S(1)}, u32[]{:S(2)}) copy-start(bf16[128,256]{1,0:T(8,128)(2,1)S(1)} %collective-permute-done.4.before_ref) | copy-start | bytes 196612
  25.9 12.5 %collective-permute-start.1 = (bf16[16,64,128]{2,1,0:T(8,128)(2,1)S(1)}, bf16[16,64,128]{2,1,0:T(8,128)(2,1)S(1)}, u32[]{:S(2)}, u32[]{:S(2)}) collective-permute-start(bf16[16,64,128]{2,1,0:T(8,128)(2,1)S(1)} %all-to-all-done), channel_id=1, source_target_pairs={{1,0},{2,1},{3,2},{4,3},{5,4},{6,5},{7,6},{8,7},{9,8},{10,9},{11,1... | collective-permute-start | bytes 786440 | tf_op jit(solution)/shard_map/ppermute | solution.py:285
  30.6 1.8 %copy-start.3 = (bf16[8,64,128]{2,1,0:T(8,128)(2,1)S(1)}, bf16[8,64,128]{2,1,0:T(8,128)(2,1)}, u32[]{:S(2)}) copy-start(bf16[8,64,128]{2,1,0:T(8,128)(2,1)} %wup_ref.1) | copy-start | bytes 393220
  38.3 0.8 copy-start.5
  49.7 3.6 %collective-permute-start.6 = (bf16[1152,128]{1,0:T(8,128)(2,1)S(1)}, bf16[1152,128]{1,0:T(8,128)(2,1)S(1)}, u32[]{:S(2)}, u32[]{:S(2)}) collective-permute-start(bf16[1152,128]{1,0:T(8,128)(2,1)S(1)} %dynamic-slice_convert_fusion), channel_id=1, source_target_pairs={{0,1},{1,0},{2,3},{3,2},{4,5},{5,4},{6,7},{7,6},{8,9},{9,8},{10,11... | collective-permute-start | bytes 884744 | tf_op jit(solution)/shard_map/ppermute | solution.py:216
  54.5 34.3 %copy-start.6 = (bf16[64,2048]{1,0:T(8,128)(2,1)S(1)}, bf16[64,2048]{1,0:T(8,128)(2,1)}, u32[]{:S(2)}) copy-start(bf16[64,2048]{1,0:T(8,128)(2,1)} %get-tuple-element.15) | copy-start | bytes 786436
  54.5 6.2 %collective-permute-start.7 = (bf16[288,128]{1,0:T(8,128)(2,1)S(1)}, bf16[288,128]{1,0:T(8,128)(2,1)S(1)}, u32[]{:S(2)}, u32[]{:S(2)}) collective-permute-start(bf16[288,128]{1,0:T(8,128)(2,1)S(1)} %get-tuple-element.27), channel_id=1, source_target_pairs={{0,2},{1,3},{2,0},{3,1},{4,6},{5,7},{6,4},{7,5},{8,10},{9,11},{10,... | collective-permute-start | bytes 221192 | tf_op jit(solution)/shard_map/ppermute | solution.py:216
  57.8 4.4 %collective-permute-start.8 = (bf16[288,128]{1,0:T(8,128)(2,1)S(1)}, bf16[288,128]{1,0:T(8,128)(2,1)S(1)}, u32[]{:S(2)}, u32[]{:S(2)}) collective-permute-start(bf16[288,128]{1,0:T(8,128)(2,1)S(1)} %get-tuple-element.29), channel_id=1, source_target_pairs={{0,4},{1,5},{2,6},{3,7},{4,0},{5,1},{6,2},{7,3},{8,12},{9,13},{10,... | collective-permute-start | bytes 221192 | tf_op jit(solution)/shard_map/ppermute | solution.py:216
  59.3 5.3 %collective-permute-start.9 = (bf16[288,128]{1,0:T(8,128)(2,1)S(1)}, bf16[288,128]{1,0:T(8,128)(2,1)S(1)}, u32[]{:S(2)}, u32[]{:S(2)}) collective-permute-start(bf16[288,128]{1,0:T(8,128)(2,1)S(1)} %get-tuple-element.28), channel_id=1, source_target_pairs={{0,6},{1,7},{2,4},{3,5},{4,2},{5,3},{6,0},{7,1},{8,14},{9,15},{10,... | collective-permute-start | bytes 221192 | tf_op jit(solution)/shard_map/ppermute | solution.py:216
  64.7 5.3 %collective-permute-start.10 = (bf16[288,128]{1,0:T(8,128)(2,1)S(1)}, bf16[288,128]{1,0:T(8,128)(2,1)S(1)}, u32[]{:S(2)}, u32[]{:S(2)}) collective-permute-start(bf16[288,128]{1,0:T(8,128)(2,1)S(1)} %add_convert_fusion.1), channel_id=1, source_target_pairs={{0,8},{1,9},{2,10},{3,11},{4,12},{5,13},{6,14},{7,15},{8,0},{9,1},... | collective-permute-start | bytes 221192 | tf_op jit(solution)/shard_map/ppermute | solution.py:216
  70.1 10.6 %collective-permute-start.11 = (bf16[288,128]{1,0:T(8,128)(2,1)S(1)}, bf16[288,128]{1,0:T(8,128)(2,1)S(1)}, u32[]{:S(2)}, u32[]{:S(2)}) collective-permute-start(bf16[288,128]{1,0:T(8,128)(2,1)S(1)} %get-tuple-element.20), channel_id=1, source_target_pairs={{0,2},{1,3},{2,0},{3,1},{4,6},{5,7},{6,4},{7,5},{8,10},{9,11},{10,... | collective-permute-start | bytes 221192 | tf_op jit(solution)/shard_map/ppermute | solution.py:216
  72.5 17.2 %all-to-all-start.1 = ((bf16[16,64,128]{2,1,0:T(8,128)(2,1)}), bf16[16,64,128]{2,1,0:T(8,128)(2,1)S(1)}, u32[]{:S(2)}, u32[]{:S(2)}) async-start(bf16[16,64,128]{2,1,0:T(8,128)(2,1)} %get-tuple-element.17), calls=%async_computation.1 | async-start | bytes 524288 | tf_op jit(solution)/shard_map/all_to_all | solution.py:318
  77.3 9.4 %collective-permute-start.12 = (bf16[288,128]{1,0:T(8,128)(2,1)S(1)}, bf16[288,128]{1,0:T(8,128)(2,1)S(1)}, u32[]{:S(2)}, u32[]{:S(2)}) collective-permute-start(bf16[288,128]{1,0:T(8,128)(2,1)S(1)} %get-tuple-element.20), channel_id=1, source_target_pairs={{0,4},{1,5},{2,6},{3,7},{4,0},{5,1},{6,2},{7,3},{8,12},{9,13},{10,... | collective-permute-start | bytes 221192 | tf_op jit(solution)/shard_map/ppermute | solution.py:216
  79.2 9.5 %collective-permute-start.13 = (bf16[288,128]{1,0:T(8,128)(2,1)S(1)}, bf16[288,128]{1,0:T(8,128)(2,1)S(1)}, u32[]{:S(2)}, u32[]{:S(2)}) collective-permute-start(bf16[288,128]{1,0:T(8,128)(2,1)S(1)} %get-tuple-element.20), channel_id=1, source_target_pairs={{0,6},{1,7},{2,4},{3,5},{4,2},{5,3},{6,0},{7,1},{8,14},{9,15},{10,... | collective-permute-start | bytes 221192 | tf_op jit(solution)/shard_map/ppermute | solution.py:216
  88.7 2.2 %collective-permute-start.14 = (bf16[1152,128]{1,0:T(8,128)(2,1)S(1)}, bf16[1152,128]{1,0:T(8,128)(2,1)S(1)}, u32[]{:S(2)}, u32[]{:S(2)}) collective-permute-start(bf16[1152,128]{1,0:T(8,128)(2,1)S(1)} %constant_dynamic-update-slice_fusion), channel_id=1, source_target_pairs={{0,1},{1,0},{2,3},{3,2},{4,5},{5,4},{6,7},{7,6},{8,9},{9,8},{10,11... | collective-permute-start | bytes 884744 | tf_op jit(solution)/shard_map/ppermute | solution.py:216
  (3 other events, 2.1 us)

commit v2 on v1

v2 whole, which is shorter than its diff:
```python
import functools
import math

import jax
import jax.numpy as jnp
from jax import lax
from jax.experimental import pallas as pl
from jax.experimental.pallas import tpu as pltpu

W = 128
AXIS = "space"
BF16 = jnp.bfloat16
F32 = jnp.float32
NT = (((1,), (1,)), ((), ()))


def mm(a, b):
    return jnp.dot(a, b, preferred_element_type=F32)


def one_hot(shape, cond):
    rows = lax.broadcasted_iota(jnp.int32, shape, 0)
    cols = lax.broadcasted_iota(jnp.int32, shape, 1)
    return jnp.where(cond(rows, cols), 1.0, 0.0).astype(BF16)


def row_taps(z, channels):
    zero = jnp.zeros((channels, W), F32)
    low = jnp.concatenate([zero, z[:channels, :-W]], axis=1)
    high = jnp.concatenate([z[2 * channels :, W:], zero], axis=1)
    return z[channels : 2 * channels] + low + high


def row_taps_back(z, channels):
    zero = jnp.zeros((channels, W), F32)
    low = jnp.concatenate([z[:channels, W:], zero], axis=1)
    high = jnp.concatenate([zero, z[2 * channels :, :-W]], axis=1)
    return z[channels : 2 * channels] + low + high


def spread_columns():
    def pick(lane_in, col):
        tap, k, parity, lane = (col >> 9, (col >> 8) & 1, (col >> 7) & 1, col & 127)
        return ((lane_in >> 6) == parity) & (2 * (lane_in & 63) + k == lane + tap - 1)

    return one_hot((128, 1536), pick)


def up_weights(wup_ref):
    return jnp.concatenate(
        [jnp.concatenate([wup_ref[2 * ij], wup_ref[2 * ij + 1]], axis=1) for ij in range(4)], axis=0
    )


def upsample(coarse_ref, weights, select, xu_ref, base, spread_ref=None):
    spread = [mm(coarse_ref[:, 128 * t : 128 * t + 128], select).astype(BF16) for t in range(2)]
    for tap in range(3):
        columns = []
        for h in range(4):
            at = 512 * tap + 128 * (h & 1)
            piece = spread[h >> 1]
            columns.append(jnp.concatenate([piece[:, at : at + 128], piece[:, at + 256 : at + 384]], axis=0))
        operand = jnp.concatenate(columns, axis=1)
        if spread_ref is not None and tap == 1:
            spread_ref[...] = operand
        up = mm(weights, operand).astype(BF16)
        for i in range(2):
            for j in range(2):
                at = base + i * 192 + tap * 64
                for h in range(4):
                    xu_ref[at : at + 64, (2 * h + j) * W : (2 * h + j + 1) * W] = up[
                        (2 * i + j) * 64 : (2 * i + j + 1) * 64, h * W : (h + 1) * W
                    ]


def prepare_kernel(own_ref, wup_ref, wc_ref, xu_ref, spread_ref, wfu_ref, wfs_ref, wi_ref, wg_ref):
    upsample(own_ref, up_weights(wup_ref), spread_columns(), xu_ref, 0, spread_ref)
    rows = []
    for b in range(3):
        taps = [wc_ref[9 * a + 3 * b + c] for a in range(3) for c in range(3)]
        rows.append(jnp.concatenate(taps + [jnp.zeros((64, 128), BF16)], axis=1))
    full = jnp.concatenate(rows, axis=0)
    for half, ref in enumerate((wfu_ref, wfs_ref)):
        select = one_hot((256, 128), lambda row, col: row == (col & 63) + 64 * half + 128 * (col >> 6))
        for m in range(5):
            part = mm(full[:, 256 * m : 256 * m + 256], select).astype(BF16)
            if m < 4:
                ref[:, 128 * m : 128 * m + 128] = part
            else:
                ref[:, 512:] = part[:, :64]
    for b in range(3):
        taps = [wc_ref[9 * (2 - jj) + 3 * b + c] for jj in range(3) for c in range(3)]
        wi_ref[b * 128 : (b + 1) * 128, :] = jnp.concatenate(taps, axis=0).T
    wg_ref[...] = jnp.concatenate([wup_ref[2 * ij + k] for k in range(2) for ij in range(4)], axis=0).T


def edge_kernel(before_ref, after_ref, wup_ref, xu_ref, wfu_ref, xb_ref, xa_ref, pre_ref):
    weights = up_weights(wup_ref)
    select = spread_columns()
    upsample(before_ref, weights, select, xb_ref, 0)
    upsample(after_ref, weights, select, xa_ref, 0)
    whole = (xb_ref, xu_ref, xa_ref)
    for j in range(4):
        planes = [whole[e >> 1][(e & 1) * 192 : (e & 1) * 192 + 192, :] for e in range(j, j + 3)]
        z = mm(wfu_ref[...], jnp.concatenate(planes, axis=0))
        pre_ref[j * 64 : (j + 1) * 64, :] = row_taps(z, 64)


def main_kernel(
    scale,
    index_ref,
    own_ref,
    before_ref,
    after_ref,
    cot_ref,
    edge_before_ref,
    edge_after_ref,
    wf_ref,
    far_xb_ref,
    far_xu_ref,
    far_xa_ref,
    far_pre_ref,
    far_spread_ref,
    far_wi_ref,
    far_wg_ref,
    act_ref,
    gi_ref,
    skip_ref,
    keep_ref,
    send_ref,
    xs_ref,
    gs_ref,
    gw_ref,
    xu_ref,
    pre_ref,
    spread_ref,
    wi_ref,
    wg_ref,
    sems,
):
    pairs = (
        (far_pre_ref, pre_ref),
        (far_xb_ref, xu_ref.at[0:384]),
        (far_xu_ref, xu_ref.at[384:768]),
        (far_xa_ref, xu_ref.at[768:1152]),
        (far_wi_ref, wi_ref),
        (far_spread_ref, spread_ref),
        (far_wg_ref, wg_ref),
    )
    copies = [pltpu.make_async_copy(src, dst, sems.at[i]) for i, (src, dst) in enumerate(pairs)]
    for copy in copies:
        copy.start()

    def pick(row, col):
        out = jnp.where(col >= 384, 1, 0)
        rest = col - 384 * out
        tap, lane = (rest >> 7, rest & 127)
        return (((row >> 6) & 1) == out) & ((row >> 7) * 64 + (row & 63) == lane + tap - 1)

    select = one_hot((256, 768), pick)
    for part, ref in enumerate((before_ref, own_ref, after_ref)):
        left = ref[:, 0].reshape(512, 128)
        right = ref[:, 1].reshape(512, 128)
        placed = mm(jnp.concatenate([left, right], axis=1), select).astype(BF16)
        for parity in range(2):
            for tap in range(3):
                at = (2 * part + parity) * 192 + tap * 64
                for h in range(8):
                    xs_ref[at : at + 64, h * W : (h + 1) * W] = placed[
                        h * 64 : (h + 1) * 64, (3 * parity + tap) * W : (3 * parity + tap + 1) * W
                    ]

    copies[0].wait()
    shift = one_hot((128, 256), lambda row, col: row == (col & 127) + 1 - 2 * (col >> 7))
    for j in range(4):
        z = mm(wf_ref[...], xs_ref[j * 192 : j * 192 + 576, :])
        pre = pre_ref[j * 64 : (j + 1) * 64, :] + row_taps(z, 64)
        gate = 1.0 / (1.0 + jnp.exp(-pre))
        if j == 0:
            cot = jnp.concatenate([edge_before_ref[:64, 256:], edge_before_ref[64:, 256:]], axis=1)
        elif j == 3:
            cot = jnp.concatenate([edge_after_ref[:64, 256:], edge_after_ref[64:, 256:]], axis=1)
        else:
            cot = cot_ref[:, (j - 1) * 1024 : j * 1024]
            act_ref[:, (j - 1) * 1024 : j * 1024] = (pre * gate).astype(BF16)
        grad = (cot.astype(F32) * gate * (1.0 + pre * (1.0 - gate))).astype(BF16)
        gs_ref[j * 192 + 64 : j * 192 + 128, :] = grad
        tall = jnp.concatenate([grad[:, h * W : (h + 1) * W] for h in range(8)], axis=0)
        moved = mm(tall, shift).astype(BF16)
        for tap in (0, 2):
            at = j * 192 + tap * 64
            for h in range(8):
                gs_ref[at : at + 64, h * W : (h + 1) * W] = moved[
                    h * 64 : (h + 1) * 64, (tap >> 1) * W : (tap >> 1) * W + W
                ]

    zero = jnp.zeros((64, W), BF16)
    grads = []
    for j in (1, 2):
        grad = gs_ref[j * 192 + 64 : j * 192 + 128, :]
        low = jnp.concatenate([grad[:, W:], zero], axis=1)
        high = jnp.concatenate([zero, grad[:, :-W]], axis=1)
        grads.append(jnp.concatenate([low, grad, high], axis=0))
    for copy in copies[1:4]:
        copy.wait()
    for a in range(3):
        total = None
        for j in (1, 2):
            pieces = []
            for tap in range(3):
                at = (j + a) * 192 + tap * 64
                pieces += [xu_ref[at : at + 64, :], xs_ref[at : at + 64, :]]
            term = lax.dot_general(
                grads[j - 1], jnp.concatenate(pieces, axis=0), NT, preferred_element_type=F32
            )
            total = term if total is None else total + term
        total = total * scale
        for b in range(3):
            for tap in range(3):
                at = (9 * a + 3 * b + tap) * 64
                gw_ref[at : at + 64, :] = total[b * 64 : (b + 1) * 64, tap * W : (tap + 1) * W]

    for copy in copies[4:]:
        copy.wait()
    lower = lax.broadcasted_iota(jnp.int32, (64, W), 1) < 64
    ups = []
    skips = []
    for j in range(2):
        z = mm(wi_ref[...], gs_ref[j * 192 : j * 192 + 576, :])
        grad = row_taps_back(z, 128)
        ups.append(grad[:64].astype(BF16))
        skips.append(grad[64:])
    for h in range(8):
        first = skips[0][:, h * W : (h + 1) * W]
        second = skips[1][:, h * W : (h + 1) * W]
        skip_ref[2 * h] = jnp.where(lower, first, pltpu.roll(second, 64, 1)).astype(BF16)
        skip_ref[2 * h + 1] = jnp.where(lower, pltpu.roll(first, 64, 1), second).astype(BF16)

    tiles = []
    for h in range(4):
        tiles.append(
            jnp.concatenate(
                [ups[i][:, (2 * h + j) * W : (2 * h + j + 1) * W] for i in range(2) for j in range(2)],
                axis=0,
            )
        )
    grad_up = lax.dot_general(
        jnp.concatenate(tiles, axis=1), spread_ref[...], NT, preferred_element_type=F32
    )
    grad_up = grad_up * scale
    for ij in range(4):
        for k in range(2):
            at = (27 + 2 * ij + k) * 64
            gw_ref[at : at + 64, :] = grad_up[ij * 64 : (ij + 1) * 64, k * W : (k + 1) * W]
    gw_ref[35 * 64 :, :] = jnp.zeros((64, W), F32)

    def part_lanes(row, col):
        return ((row >> 7) == ((col >> 6) & 1)) & ((row & 127) == 2 * (col & 63) + (col >> 7))

    apart = one_hot((256, 256), part_lanes)
    halves = [
        mm(jnp.concatenate([tiles[2 * t], tiles[2 * t + 1]], axis=1), apart).astype(BF16) for t in range(2)
    ]
    operand = jnp.concatenate(
        [jnp.concatenate([half[:, k * W : (k + 1) * W] for half in halves], axis=1) for k in range(2)],
        axis=0,
    )
    gi_ref[...] = mm(wg_ref[...], operand).astype(BF16)

    core = index_ref[0]
    quad = index_ref[1]
    for k in range(4):
        row = jnp.bitwise_xor(quad, k) * 288
        mine = pl.multiple_of(core * 1152 + row, 32)
        other = pl.multiple_of((1 - core) * 1152 + row, 32)
        keep_ref[k * 288 : (k + 1) * 288, :] = gw_ref[pl.ds(mine, 288), :]
        send_ref[k * 288 : (k + 1) * 288, :] = gw_ref[pl.ds(other, 288), :].astype(BF16)


def finish_kernel(index_ref, mine_ref, other_ref, conv_ref, up_ref):
    core = index_ref[0]
    quad = index_ref[1]
    for side, ref in ((core, mine_ref), (1 - core, other_ref)):
        for k in range(4):
            piece = 4 * side + jnp.bitwise_xor(quad, k)
            rows = slice(k * 288, (k + 1) * 288)

            @pl.when(piece < 6)
            def _():
                conv_ref[pl.ds(piece * 9, 9)] = ref[rows, :].astype(F32).reshape(9, 32, 128)

            @pl.when(piece == 6)
            def _():
                up_ref[0:9] = ref[rows, :].astype(F32).reshape(9, 32, 128)

            @pl.when(piece == 7)
            def _():
                up_ref[9:16] = ref[k * 288 : k * 288 + 224, :].astype(F32).reshape(7, 32, 128)


def room(mebibytes):
    return pltpu.CompilerParams(vmem_limit_bytes=mebibytes << 20)


VMEM = pl.BlockSpec(memory_space=pltpu.VMEM)
SMEM = pl.BlockSpec(memory_space=pltpu.SMEM)
FAR = pl.BlockSpec(memory_space=pl.ANY)


def like(shape, dtype=BF16):
    return jax.ShapeDtypeStruct(shape, dtype)


def reduce_weights(index, keep, send, back, finish_others, n):
    def swap(value, bit):
        return lax.ppermute(value, AXIS, [(i, i ^ bit) for i in range(n)])

    summed = keep + swap(send, 1).astype(F32)
    rounded = summed.astype(BF16)
    total = summed[:288]
    for k in (1, 2, 3):
        total = total + swap(rounded[k * 288 : (k + 1) * 288], 2 * k).astype(F32)
    total, back = lax.optimization_barrier((total, back))
    bit = 8
    while bit < n:
        own = total.astype(BF16)
        total = own.astype(F32) + swap(own, bit).astype(F32)
        bit *= 2
    own = total.astype(BF16)
    pieces = [own] + [swap(own, 2 * k) for k in (1, 2, 3)]
    pieces, others = lax.optimization_barrier((pieces, finish_others(back)))
    mine = jnp.concatenate(pieces, axis=0)
    other = swap(mine, 1)
    conv, up = pl.pallas_call(
        finish_kernel,
        out_shape=(like((54, 32, 128), F32), like((16, 32, 128), F32)),
        in_specs=[SMEM, VMEM, VMEM],
        out_specs=(VMEM, VMEM),
        compiler_params=room(6),
        name="finish",
    )(index, mine, other)
    return conv.reshape(27, 64, 128), up.reshape(8, 64, 128), others


def local(coarse_input, skip, cotangent, w_up, w_conv):
    n = lax.axis_size(AXIS)
    cells = cotangent.shape[2]
    planes = cotangent.shape[1]
    positions = skip.shape[2]
    up = [(i, i + 1) for i in range(n - 1)]
    down = [(i + 1, i) for i in range(n - 1)]
    me = lax.axis_index(AXIS)
    index = jnp.stack([me & 1, (me >> 1) & 3]).astype(jnp.int32)

    sent = skip.reshape(64, n, 2 * positions).transpose(1, 0, 2)
    held = lax.all_to_all(sent, AXIS, split_axis=0, concat_axis=0, tiled=True)
    if positions != 64:
        held = held.reshape(n, 64, 2, positions).transpose(1, 2, 0, 3).reshape(64, 2, 16, 64)
        held = held.transpose(2, 0, 1, 3).reshape(16, 64, 128)

    coarse = coarse_input.reshape(128, 256)
    flat = lax.optimization_barrier(cotangent.reshape(64, 2048))

    def edge(plane):
        halves = [flat[:, 1024 * plane + 512 * i : 1024 * plane + 512 * (i + 1)] for i in range(2)]
        return jnp.concatenate([coarse, jnp.concatenate(halves, axis=0)], axis=1)

    edge_before = lax.ppermute(edge(1), AXIS, up)
    edge_after = lax.ppermute(edge(0), AXIS, down)
    xu, spread, wf_up, wf_skip, wi, wg = pl.pallas_call(
        prepare_kernel,
        out_shape=(
            like((384, 1024)),
            like((256, 512)),
            like((192, 576)),
            like((192, 576)),
            like((384, 576)),
            like((128, 512)),
        ),
        in_specs=[VMEM] * 3,
        out_specs=(VMEM,) * 6,
        compiler_params=room(8),
        name="prepare",
    )(coarse, w_up, w_conv)
    held, wf_up, edge_before, edge_after = lax.optimization_barrier((held, wf_up, edge_before, edge_after))
    held_before = lax.ppermute(held, AXIS, up)
    held_after = lax.ppermute(held, AXIS, down)
    xb, xa, pre = pl.pallas_call(
        edge_kernel,
        out_shape=(like((384, 1024)), like((384, 1024)), like((256, 1024), F32)),
        in_specs=[VMEM] * 5,
        out_specs=(VMEM,) * 3,
        compiler_params=room(16),
        name="edges",
    )(edge_before, edge_after, w_up, xu, wf_up)

    scale = 1.0 / math.sqrt(n * planes * cells)
    rows = [v.reshape(8, 2, 64, 128) for v in (held, held_before, held_after)]
    act, gi, skip_part, keep, send = pl.pallas_call(
        functools.partial(main_kernel, scale),
        out_shape=(
            like((64, 2048)),
            like((128, 256)),
            like((16, 64, 128)),
            like((1152, 128), F32),
            like((1152, 128)),
        ),
        in_specs=[SMEM] + [VMEM] * 7 + [FAR] * 7,
        out_specs=(VMEM,) * 5,
        scratch_shapes=[
            pltpu.VMEM((1152, 1024), BF16),
            pltpu.VMEM((768, 1024), BF16),
            pltpu.VMEM((2304, 128), F32),
            pltpu.VMEM((1152, 1024), BF16),
            pltpu.VMEM((256, 1024), F32),
            pltpu.VMEM((256, 512), BF16),
            pltpu.VMEM((384, 576), BF16),
            pltpu.VMEM((128, 512), BF16),
            pltpu.SemaphoreType.DMA((7,)),
        ],
        compiler_params=room(24),
        name="section",
    )(index, *rows, flat, edge_before, edge_after, wf_skip, xb, xu, xa, pre, spread, wi, wg)
    if positions != 64:
        skip_part = skip_part.reshape(16, 64, 2, 64).transpose(1, 2, 0, 3)
        skip_part = skip_part.reshape(64, 2, n, positions).transpose(2, 0, 1, 3)
        skip_part = skip_part.reshape(n, 64, 2 * positions)
    back = lax.all_to_all(skip_part, AXIS, split_axis=0, concat_axis=0, tiled=True)

    def others(back):
        return (
            act.reshape(64, planes, cells),
            gi.reshape(128, 1, 256),
            back.transpose(1, 0, 2).reshape(64, 2 * n, positions),
        )

    grad_w_conv, grad_w_up, rest = reduce_weights(index, keep, send, back, others, n)
    return (*rest, grad_w_up, grad_w_conv)


def solution(mesh):
    spec = jax.sharding.PartitionSpec
    in_specs = (
        spec("groups", "space", None),
        spec("groups", None, "space"),
        spec("groups", "space", None),
        spec(),
        spec(),
    )
    out_specs = (
        spec("groups", "space", None),
        spec("groups", "space", None),
        spec("groups", None, "space"),
        spec("groups", None, None),
        spec("groups", None, None),
    )
    return jax.shard_map(local, mesh=mesh, in_specs=in_specs, out_specs=out_specs, check_vma=False)
```

time: 93.3 us -> 77.9 us (0.83)
  starting transfers between devices: 44.3 us -> 35.9 us
  local copies, waits for them, and re-layouts: 14.4 us -> 10.5 us
  other arithmetic: 2.97 us -> 0.25 us
    reshape x8 -> x2, local copies, waits for them, and re-layouts: 6.65 us -> 1.93 us  [the longest x1 1.05 us: others(): back.transpose(1, 0, 2).reshape(64, 2 * n, positions)]
    ppermute x4 -> x2, starting transfers between devices: 9.04 us -> 4.47 us  [the longest x1 3.04 us: local(): edge_before = lax.ppermute(edge(1), AXIS, up)]
    ppermute x9, starting transfers between devices: 17.3 us -> 13 us  [swap(): return lax.ppermute(value, AXIS, [(i, i ^ bit) for i in range(n)])]
    unnamed x24 -> x34, local copies, waits for them, and re-layouts: 3.07 us -> 6.25 us
    all_to_all x1, waiting for transfers between devices: 0.01 us -> 2.26 us  [local(): held = lax.all_to_all(sent, AXIS, split_axis=0, concat_axis=0, tiled=True)]
    ppermute x9, waiting for transfers between devices: 15.6 us -> 14 us  [swap(): return lax.ppermute(value, AXIS, [(i, i ^ bit) for i in range(n)])]
    convert_element_type x1 -> x0, local copies, waits for them, and re-layouts: 1.09 us -> none  [reduce_weights(): lax.dynamic_slice_in_dim(partial, (1 - core) * half, half, 0).astype(BF16)]
    convert_element_type x1, other arithmetic: 1.14 us -> 0.08 us  [reduce_weights(): rounded = summed.astype(BF16)]
  transfers between devices with their start and end apart: 17 -> 15, of which waited for: 6 -> 9; matrix products, arithmetic and copies ran while one was open for 11% -> 3% of each run, Pallas kernels for 6% -> 4%
where the time goes in v2:
time: 77.9 us; the launch traced here: 77.4 us
  starting transfers between devices  35.9 us (46%)
  waiting for transfers between devices  16.3 us (21%)
  Pallas kernels  13.6 us (17%)
  local copies, waits for them, and re-layouts  10.5 us (13%)
  between operations  0.9 us (1%)
    ppermute x9, waiting for transfers between devices, swap(): return lax.ppermute(value, AXIS, [(i, i ^ bit) for i in range(n)])  14 us
    ppermute x9, starting transfers between devices, swap(): return lax.ppermute(value, AXIS, [(i, i ^ bit) for i in range(n)])  13 us
    pallas_call x1, Pallas kernels, local(): pl.pallas_call(functools.partial(main_kernel, scale), out_shape=(like((64...  8.49 us
    all_to_all x1, starting transfers between devices, local(): held = lax.all_to_all(sent, AXIS, split_axis=0, concat_axis=0, tiled=True)  7.49 us
    unnamed x34, local copies, waits for them, and re-layouts  6.25 us
    all_to_all x1, starting transfers between devices, local(): lax.all_to_all(skip_part, AXIS, split_axis=0, concat_axis=0, tiled=True)  5.67 us
    ppermute x1, starting transfers between devices, local(): held_before = lax.ppermute(held, AXIS, up)  3.94 us
    ppermute x1, starting transfers between devices, local(): edge_before = lax.ppermute(edge(1), AXIS, up)  3.04 us
  transfers between devices with their start and end apart: 15, of which 9 were waited for; matrix products, arithmetic and copies ran while one was open for 3% of the time, Pallas kernels for 4%

profile of v2, /device:TPU:0, one launch (start us, length us, event | category | flops | bytes accessed | tf_op | source)
XLA Modules:
  0.0 77.4 jit_solution(8903172563753573552)
XLA Ops:
  0.6 1.3 %reshape.43 = bf16[64,16,128]{2,1,0:T(8,128)(2,1)S(1)} reshape(bf16[64,32,64]{2,1,0:T(8,128)(2,1)} %param.6) | data formatting | bytes 524288 | tf_op jit(solution)/shard_map/reshape | solution.py:355
  2.7 7.5 %all-to-all-start = ((bf16[16,64,128]{2,1,0:T(8,128)(2,1)}), bf16[16,64,128]{2,1,0:T(8,128)(2,1)S(1)}, u32[]{:S(2)}, u32[]{:S(2)}) async-start(bf16[16,64,128]{2,1,0:T(8,128)(2,1)} %bitcast.14), calls=%async_computation | async-start | bytes 524288 | tf_op jit(solution)/shard_map/all_to_all | solution.py:356
  11.2 1.4 %collective-permute-start.1 = (bf16[128,768]{1,0:T(8,128)(2,1)S(1)}, bf16[128,768]{1,0:T(8,128)(2,1)S(1)}, u32[]{:S(2)}, u32[]{:S(2)}) collective-permute-start(bf16[128,768]{1,0:T(8,128)(2,1)S(1)} %get-tuple-element.72), channel_id=1, source_target_pairs={{1,0},{2,1},{3,2},{4,3},{5,4},{6,5},{7,6},{8,7},{9,8},{10,9},{11,1... | collective-permute-start | bytes 589832 | tf_op jit(solution)/shard_map/ppermute | solution.py:369
  12.6 3.0 %collective-permute-start = (bf16[128,768]{1,0:T(8,128)(2,1)S(1)}, bf16[128,768]{1,0:T(8,128)(2,1)S(1)}, u32[]{:S(2)}, u32[]{:S(2)}) collective-permute-start(bf16[128,768]{1,0:T(8,128)(2,1)S(1)} %get-tuple-element.73), channel_id=1, source_target_pairs={{0,1},{1,2},{2,3},{3,4},{4,5},{5,6},{6,7},{7,8},{8,9},{9,10},{10,1... | collective-permute-start | bytes 589832 | tf_op jit(solution)/shard_map/ppermute | solution.py:368
  15.7 1.0 %prepare.1 = (bf16[384,1024]{1,0:T(8,128)(2,1)S(1)}, bf16[256,512]{1,0:T(8,128)(2,1)S(1)}, bf16[192,576]{1,0:T(8,128)(2,1)S(1)}, bf16[192,576]{1,0:T(8,128)(2,1)...) custom-call(bf16[128,256]{1,0:T(8,128)(2,1)S(1)} %bitcast.21, bf16[8,64,128]{2,1,0:T(8,128)(2,1)S(1)} %copy-done, ...), custom_call_target="tpu_custom_call" | custom-call | tf_op jit(solution)/shard_map/prepare/pallas_call | solution.py:370
  18.0 2.3 %all-to-all-done = bf16[16,64,128]{2,1,0:T(8,128)(2,1)S(1)} async-done(((bf16[16,64,128]{2,1,0:T(8,128)(2,1)}), bf16[16,64,128]{2,1,0:T(8,128)(2,1)S(1)}, u32[]{:S(2)}, u32[]{:S(2)}) %all-to-all-start) | async-done | bytes 262176 | tf_op jit(solution)/shard_map/all_to_all | solution.py:356
  20.3 1.3 %collective-permute-start.3 = (bf16[16,64,128]{2,1,0:T(8,128)(2,1)S(1)}, bf16[16,64,128]{2,1,0:T(8,128)(2,1)S(1)}, u32[]{:S(2)}, u32[]{:S(2)}) collective-permute-start(bf16[16,64,128]{2,1,0:T(8,128)(2,1)S(1)} %all-to-all-done), channel_id=1, source_target_pairs={{1,0},{2,1},{3,2},{4,3},{5,4},{6,5},{7,6},{8,7},{9,8},{10,9},{11,1... | collective-permute-start | bytes 786440 | tf_op jit(solution)/shard_map/ppermute | solution.py:387
  21.6 3.9 %collective-permute-start.2 = (bf16[16,64,128]{2,1,0:T(8,128)(2,1)S(1)}, bf16[16,64,128]{2,1,0:T(8,128)(2,1)S(1)}, u32[]{:S(2)}, u32[]{:S(2)}) collective-permute-start(bf16[16,64,128]{2,1,0:T(8,128)(2,1)S(1)} %all-to-all-done), channel_id=1, source_target_pairs={{0,1},{1,2},{2,3},{3,4},{4,5},{5,6},{6,7},{7,8},{8,9},{9,10},{10,1... | collective-permute-start | bytes 786440 | tf_op jit(solution)/shard_map/ppermute | solution.py:386
  26.5 2.4 %edges.1 = (bf16[384,1024]{1,0:T(8,128)(2,1)S(1)}, bf16[384,1024]{1,0:T(8,128)(2,1)S(1)}, f32[256,1024]{1,0:T(8,128)S(1)}) custom-call(bf16[128,768]{1,0:T(8,128)(2,1)S(1)} %collective-permute-done.before_ref.edge_before_ref, bf16[128,768]{1,0:T(8,128)(2,1)S(1)} %collective-permute-done.1.after_ref.edge_after_ref, bf16[8,64,128]{2,1,0:T(8,128)(2,1)S(1)} %copy-done, ...), custom_call_target="tpu_custom_call" | custom-call | tf_op jit(solution)/shard_map/edges/pallas_call | solution.py:388
  29.7 0.9 %copy-done.3 = bf16[16,64,128]{2,1,0:T(8,128)(2,1)S(1)} copy-done((bf16[16,64,128]{2,1,0:T(8,128)(2,1)S(1)}, bf16[16,64,128]{2,1,0:T(8,128)(2,1)}, u32[]{:S(2)}) %copy-start.3) | copy-done | bytes 262168
  30.6 8.5 %section.1 = (bf16[64,2048]{1,0:T(8,128)(2,1)S(1)}, bf16[128,256]{1,0:T(8,128)(2,1)}, bf16[16,64,128]{2,1,0:T(8,128)(2,1)S(1)}, f32[1152,128]{1,0:T(8,128)S(1)}, bf16[1152,128]{1,0:T(8,128)(2,1)}) custom-call(s32[2]{0:T(128)S(1)} %pad_add_fusion.index_ref, bf16[8,2,64,128]{3,2,1,0:T(8,128)(2,1)S(1)} %bitcast.17, bf16[8,2,64,128]{3,2,1,0:T(8,128)(2,1)S(1)} %bitcast.19, ...), custom_call_target="tpu_custom_call" | custom-call | tf_op jit(solution)/shard_map/section/pallas_call | solution.py:399
  40.5 3.4 %collective-permute-start.4 = (bf16[1152,128]{1,0:T(8,128)(2,1)}, bf16[1152,128]{1,0:T(8,128)(2,1)S(1)}, u32[]{:S(2)}, u32[]{:S(2)}) collective-permute-start(bf16[1152,128]{1,0:T(8,128)(2,1)} %get-tuple-element.48), channel_id=1, source_target_pairs={{0,1},{1,0},{2,3},{3,2},{4,5},{5,4},{6,7},{7,6},{8,9},{9,8},{10,11... | collective-permute-start | bytes 884744 | tf_op jit(solution)/shard_map/ppermute | solution.py:316
  44.0 5.7 %all-to-all-start.1 = ((bf16[16,64,128]{2,1,0:T(8,128)(2,1)}), bf16[16,64,128]{2,1,0:T(8,128)(2,1)S(1)}, u32[]{:S(2)}, u32[]{:S(2)}) async-start(bf16[16,64,128]{2,1,0:T(8,128)(2,1)} %copy-done.6), calls=%async_computation.1 | async-start | bytes 524288 | tf_op jit(solution)/shard_map/all_to_all | solution.py:428
  49.8 2.0 %collective-permute-start.5 = (bf16[288,128]{1,0:T(8,128)(2,1)S(1)}, bf16[288,128]{1,0:T(8,128)(2,1)S(1)}, u32[]{:S(2)}, u32[]{:S(2)}) collective-permute-start(bf16[288,128]{1,0:T(8,128)(2,1)S(1)} %get-tuple-element.65), channel_id=1, source_target_pairs={{0,2},{1,3},{2,0},{3,1},{4,6},{5,7},{6,4},{7,5},{8,10},{9,11},{10,... | collective-permute-start | bytes 221192 | tf_op jit(solution)/shard_map/ppermute | solution.py:316
  51.8 1.5 %collective-permute-start.7 = (bf16[288,128]{1,0:T(8,128)(2,1)S(1)}, bf16[288,128]{1,0:T(8,128)(2,1)S(1)}, u32[]{:S(2)}, u32[]{:S(2)}) collective-permute-start(bf16[288,128]{1,0:T(8,128)(2,1)S(1)} %get-tuple-element.66), channel_id=1, source_target_pairs={{0,6},{1,7},{2,4},{3,5},{4,2},{5,3},{6,0},{7,1},{8,14},{9,15},{10,... | collective-permute-start | bytes 221192 | tf_op jit(solution)/shard_map/ppermute | solution.py:316
  53.3 3.2 %collective-permute-done.5 = bf16[288,128]{1,0:T(8,128)(2,1)S(1)} collective-permute-done((bf16[288,128]{1,0:T(8,128)(2,1)S(1)}, bf16[288,128]{1,0:T(8,128)(2,1)S(1)}, u32[]{:S(2)}, u32[]{:S(2)}) %collective-permute-start.5) | collective-permute-done | bytes 73760 | tf_op jit(solution)/shard_map/ppermute | solution.py:316
  56.5 2.9 %collective-permute-done.7 = bf16[288,128]{1,0:T(8,128)(2,1)S(1)} collective-permute-done((bf16[288,128]{1,0:T(8,128)(2,1)S(1)}, bf16[288,128]{1,0:T(8,128)(2,1)S(1)}, u32[]{:S(2)}, u32[]{:S(2)}) %collective-permute-start.7) | collective-permute-done | bytes 73760 | tf_op jit(solution)/shard_map/ppermute | solution.py:316
  60.2 2.4 %collective-permute-start.8 = (bf16[288,128]{1,0:T(8,128)(2,1)S(1)}, bf16[288,128]{1,0:T(8,128)(2,1)S(1)}, u32[]{:S(2)}, u32[]{:S(2)}) collective-permute-start(bf16[288,128]{1,0:T(8,128)(2,1)S(1)} %fusion.1), channel_id=1, source_target_pairs={{0,8},{1,9},{2,10},{3,11},{4,12},{5,13},{6,14},{7,15},{8,0},{9,1},... | collective-permute-start | bytes 221192 | tf_op jit(solution)/shard_map/ppermute | solution.py:316
  62.6 4.0 %collective-permute-done.8 = bf16[288,128]{1,0:T(8,128)(2,1)S(1)} collective-permute-done((bf16[288,128]{1,0:T(8,128)(2,1)S(1)}, bf16[288,128]{1,0:T(8,128)(2,1)S(1)}, u32[]{:S(2)}, u32[]{:S(2)}) %collective-permute-start.8) | collective-permute-done | bytes 73760 | tf_op jit(solution)/shard_map/ppermute | solution.py:316
  67.2 2.4 %collective-permute-start.10 = (bf16[288,128]{1,0:T(8,128)(2,1)S(1)}, bf16[288,128]{1,0:T(8,128)(2,1)S(1)}, u32[]{:S(2)}, u32[]{:S(2)}) collective-permute-start(bf16[288,128]{1,0:T(8,128)(2,1)S(1)} %add_convert_fusion), channel_id=1, source_target_pairs={{0,4},{1,5},{2,6},{3,7},{4,0},{5,1},{6,2},{7,3},{8,12},{9,13},{10,... | collective-permute-start | bytes 221192 | tf_op jit(solution)/shard_map/ppermute | solution.py:316
  71.3 1.1 %reshape.51 = bf16[64,32,64]{2,1,0:T(8,128)(2,1)} reshape(bf16[64,16,128]{2,1,0:T(8,128)(2,1)S(1)} %copy.12) | data formatting | bytes 524288 | tf_op jit(solution)/shard_map/reshape | solution.py:434
  72.9 1.1 %collective-permute-done.9 = bf16[288,128]{1,0:T(8,128)(2,1)S(1)} collective-permute-done((bf16[288,128]{1,0:T(8,128)(2,1)S(1)}, bf16[288,128]{1,0:T(8,128)(2,1)S(1)}, u32[]{:S(2)}, u32[]{:S(2)}) %collective-permute-start.9) | collective-permute-done | bytes 73760 | tf_op jit(solution)/shard_map/ppermute | solution.py:316
  74.1 1.6 %collective-permute-done.12.other_ref = bf16[1152,128]{1,0:T(8,128)(2,1)S(1)} collective-permute-done((bf16[1152,128]{1,0:T(8,128)(2,1)S(1)}, bf16[1152,128]{1,0:T(8,128)(2,1)S(1)}, u32[]{:S(2)}, u32[]{:S(2)}) %collective-permute-start.12) | collective-permute-done | bytes 294944 | tf_op jit(solution)/shard_map/ppermute | solution.py:316
  75.7 1.7 %finish.1 = (f32[54,32,128]{2,1,0:T(8,128)}, f32[16,32,128]{2,1,0:T(8,128)}) custom-call(s32[2]{0:T(128)S(1)} %copy-done.13, bf16[1152,128]{1,0:T(8,128)(2,1)S(1)} %constant_dynamic-update-slice_fusion.mine_ref, bf16[1152,128]{1,0:T(8,128)(2,1)S(1)} %collective-permute-done.12.other_ref), custom_call_target="tpu_custom_call" | custom-call | tf_op jit(solution)/shard_map/finish/pallas_call | solution.py:334
  (57 shorter events, 10.0 us)
Async XLA Ops:
  2.7 7.5 %copy-start.14 = (bf16[64,2,1024]{2,1,0:T(2,128)(2,1)S(1)}, bf16[64,2,1024]{2,1,0:T(2,128)(2,1)}, u32[]{:S(2)}) copy-start(bf16[64,2,1024]{2,1,0:T(2,128)(2,1)} %param.7) | copy-start | bytes 786436
  2.7 17.5 %all-to-all-start = ((bf16[16,64,128]{2,1,0:T(8,128)(2,1)}), bf16[16,64,128]{2,1,0:T(8,128)(2,1)S(1)}, u32[]{:S(2)}, u32[]{:S(2)}) async-start(bf16[16,64,128]{2,1,0:T(8,128)(2,1)} %bitcast.14), calls=%async_computation | async-start | bytes 524288 | tf_op jit(solution)/shard_map/all_to_all | solution.py:356
  10.3 5.3 %copy-start.1 = (bf16[27,64,128]{2,1,0:T(8,128)(2,1)S(1)}, bf16[27,64,128]{2,1,0:T(8,128)(2,1)}, u32[]{:S(2)}) copy-start(bf16[27,64,128]{2,1,0:T(8,128)(2,1)} %wc_ref.1) | copy-start | bytes 1327108
  11.1 4.5 %copy-start = (bf16[8,64,128]{2,1,0:T(8,128)(2,1)S(1)}, bf16[8,64,128]{2,1,0:T(8,128)(2,1)}, u32[]{:S(2)}) copy-start(bf16[8,64,128]{2,1,0:T(8,128)(2,1)} %wup_ref.3) | copy-start | bytes 393220
  11.2 6.8 %collective-permute-start.1 = (bf16[128,768]{1,0:T(8,128)(2,1)S(1)}, bf16[128,768]{1,0:T(8,128)(2,1)S(1)}, u32[]{:S(2)}, u32[]{:S(2)}) collective-permute-start(bf16[128,768]{1,0:T(8,128)(2,1)S(1)} %get-tuple-element.72), channel_id=1, source_target_pairs={{1,0},{2,1},{3,2},{4,3},{5,4},{6,5},{7,6},{8,7},{9,8},{10,9},{11,1... | collective-permute-start | bytes 589832 | tf_op jit(solution)/shard_map/ppermute | solution.py:369
  12.6 5.4 %collective-permute-start = (bf16[128,768]{1,0:T(8,128)(2,1)S(1)}, bf16[128,768]{1,0:T(8,128)(2,1)S(1)}, u32[]{:S(2)}, u32[]{:S(2)}) collective-permute-start(bf16[128,768]{1,0:T(8,128)(2,1)S(1)} %get-tuple-element.73), channel_id=1, source_target_pairs={{0,1},{1,2},{2,3},{3,4},{4,5},{5,6},{6,7},{7,8},{8,9},{9,10},{10,1... | collective-permute-start | bytes 589832 | tf_op jit(solution)/shard_map/ppermute | solution.py:368
  20.3 8.7 %collective-permute-start.3 = (bf16[16,64,128]{2,1,0:T(8,128)(2,1)S(1)}, bf16[16,64,128]{2,1,0:T(8,128)(2,1)S(1)}, u32[]{:S(2)}, u32[]{:S(2)}) collective-permute-start(bf16[16,64,128]{2,1,0:T(8,128)(2,1)S(1)} %all-to-all-done), channel_id=1, source_target_pairs={{1,0},{2,1},{3,2},{4,3},{5,4},{6,5},{7,6},{8,7},{9,8},{10,9},{11,1... | collective-permute-start | bytes 786440 | tf_op jit(solution)/shard_map/ppermute | solution.py:387
  21.6 7.4 %collective-permute-start.2 = (bf16[16,64,128]{2,1,0:T(8,128)(2,1)S(1)}, bf16[16,64,128]{2,1,0:T(8,128)(2,1)S(1)}, u32[]{:S(2)}, u32[]{:S(2)}) collective-permute-start(bf16[16,64,128]{2,1,0:T(8,128)(2,1)S(1)} %all-to-all-done), channel_id=1, source_target_pairs={{0,1},{1,2},{2,3},{3,4},{4,5},{5,6},{6,7},{7,8},{8,9},{9,10},{10,1... | collective-permute-start | bytes 786440 | tf_op jit(solution)/shard_map/ppermute | solution.py:386
  25.6 4.1 %copy-start.12 = (s32[2]{0:T(128)}, s32[2]{0:T(128)S(1)}, u32[]{:S(2)}) copy-start(s32[2]{0:T(128)S(1)} %pad_add_fusion.index_ref) | copy-start | bytes 28
  25.6 0.9 %copy-start.9 = (bf16[192,576]{1,0:T(8,128)(2,1)S(1)}, bf16[192,576]{1,0:T(8,128)(2,1)}, u32[]{:S(2)}) copy-start(bf16[192,576]{1,0:T(8,128)(2,1)} %copy-done.8) | copy-start | bytes 663556
  26.5 3.1 %copy-start.11 = (bf16[128,512]{1,0:T(8,128)(2,1)S(1)}, bf16[128,512]{1,0:T(8,128)(2,1)}, u32[]{:S(2)}) copy-start(bf16[128,512]{1,0:T(8,128)(2,1)} %copy-done.10) | copy-start | bytes 393220
  29.7 1.0 %copy-start.3 = (bf16[16,64,128]{2,1,0:T(8,128)(2,1)S(1)}, bf16[16,64,128]{2,1,0:T(8,128)(2,1)}, u32[]{:S(2)}) copy-start(bf16[16,64,128]{2,1,0:T(8,128)(2,1)} %copy-done.2) | copy-start | bytes 786436
  40.5 9.1 %collective-permute-start.4 = (bf16[1152,128]{1,0:T(8,128)(2,1)}, bf16[1152,128]{1,0:T(8,128)(2,1)S(1)}, u32[]{:S(2)}, u32[]{:S(2)}) collective-permute-start(bf16[1152,128]{1,0:T(8,128)(2,1)} %get-tuple-element.48), channel_id=1, source_target_pairs={{0,1},{1,0},{2,3},{3,2},{4,5},{5,4},{6,7},{7,6},{8,9},{9,8},{10,11... | collective-permute-start | bytes 884744 | tf_op jit(solution)/shard_map/ppermute | solution.py:316
  44.0 16.2 %all-to-all-start.1 = ((bf16[16,64,128]{2,1,0:T(8,128)(2,1)}), bf16[16,64,128]{2,1,0:T(8,128)(2,1)S(1)}, u32[]{:S(2)}, u32[]{:S(2)}) async-start(bf16[16,64,128]{2,1,0:T(8,128)(2,1)} %copy-done.6), calls=%async_computation.1 | async-start | bytes 524288 | tf_op jit(solution)/shard_map/all_to_all | solution.py:428
  49.8 6.8 %collective-permute-start.5 = (bf16[288,128]{1,0:T(8,128)(2,1)S(1)}, bf16[288,128]{1,0:T(8,128)(2,1)S(1)}, u32[]{:S(2)}, u32[]{:S(2)}) collective-permute-start(bf16[288,128]{1,0:T(8,128)(2,1)S(1)} %get-tuple-element.65), channel_id=1, source_target_pairs={{0,2},{1,3},{2,0},{3,1},{4,6},{5,7},{6,4},{7,5},{8,10},{9,11},{10,... | collective-permute-start | bytes 221192 | tf_op jit(solution)/shard_map/ppermute | solution.py:316
  51.8 7.7 %collective-permute-start.7 = (bf16[288,128]{1,0:T(8,128)(2,1)S(1)}, bf16[288,128]{1,0:T(8,128)(2,1)S(1)}, u32[]{:S(2)}, u32[]{:S(2)}) collective-permute-start(bf16[288,128]{1,0:T(8,128)(2,1)S(1)} %get-tuple-element.66), channel_id=1, source_target_pairs={{0,6},{1,7},{2,4},{3,5},{4,2},{5,3},{6,0},{7,1},{8,14},{9,15},{10,... | collective-permute-start | bytes 221192 | tf_op jit(solution)/shard_map/ppermute | solution.py:316
  53.2 6.9 %collective-permute-start.6 = (bf16[288,128]{1,0:T(8,128)(2,1)S(1)}, bf16[288,128]{1,0:T(8,128)(2,1)S(1)}, u32[]{:S(2)}, u32[]{:S(2)}) collective-permute-start(bf16[288,128]{1,0:T(8,128)(2,1)S(1)} %get-tuple-element.67), channel_id=1, source_target_pairs={{0,4},{1,5},{2,6},{3,7},{4,0},{5,1},{6,2},{7,3},{8,12},{9,13},{10,... | collective-permute-start | bytes 221192 | tf_op jit(solution)/shard_map/ppermute | solution.py:316
  60.1 10.1 %copy-start.5 = (bf16[64,2048]{1,0:T(8,128)(2,1)S(1)}, bf16[64,2048]{1,0:T(8,128)(2,1)}, u32[]{:S(2)}) copy-start(bf16[64,2048]{1,0:T(8,128)(2,1)} %copy-done.4) | copy-start | bytes 786436
  60.2 6.4 %collective-permute-start.8 = (bf16[288,128]{1,0:T(8,128)(2,1)S(1)}, bf16[288,128]{1,0:T(8,128)(2,1)S(1)}, u32[]{:S(2)}, u32[]{:S(2)}) collective-permute-start(bf16[288,128]{1,0:T(8,128)(2,1)S(1)} %fusion.1), channel_id=1, source_target_pairs={{0,8},{1,9},{2,10},{3,11},{4,12},{5,13},{6,14},{7,15},{8,0},{9,1},... | collective-permute-start | bytes 221192 | tf_op jit(solution)/shard_map/ppermute | solution.py:316
  66.7 5.8 %collective-permute-start.11 = (bf16[288,128]{1,0:T(8,128)(2,1)S(1)}, bf16[288,128]{1,0:T(8,128)(2,1)S(1)}, u32[]{:S(2)}, u32[]{:S(2)}) collective-permute-start(bf16[288,128]{1,0:T(8,128)(2,1)S(1)} %add_convert_fusion), channel_id=1, source_target_pairs={{0,6},{1,7},{2,4},{3,5},{4,2},{5,3},{6,0},{7,1},{8,14},{9,15},{10,... | collective-permute-start | bytes 221192 | tf_op jit(solution)/shard_map/ppermute | solution.py:316
  67.2 5.7 %collective-permute-start.10 = (bf16[288,128]{1,0:T(8,128)(2,1)S(1)}, bf16[288,128]{1,0:T(8,128)(2,1)S(1)}, u32[]{:S(2)}, u32[]{:S(2)}) collective-permute-start(bf16[288,128]{1,0:T(8,128)(2,1)S(1)} %add_convert_fusion), channel_id=1, source_target_pairs={{0,4},{1,5},{2,6},{3,7},{4,0},{5,1},{6,2},{7,3},{8,12},{9,13},{10,... | collective-permute-start | bytes 221192 | tf_op jit(solution)/shard_map/ppermute | solution.py:316
  69.6 4.4 %collective-permute-start.9 = (bf16[288,128]{1,0:T(8,128)(2,1)S(1)}, bf16[288,128]{1,0:T(8,128)(2,1)S(1)}, u32[]{:S(2)}, u32[]{:S(2)}) collective-permute-start(bf16[288,128]{1,0:T(8,128)(2,1)S(1)} %add_convert_fusion), channel_id=1, source_target_pairs={{0,2},{1,3},{2,0},{3,1},{4,6},{5,7},{6,4},{7,5},{8,10},{9,11},{10,... | collective-permute-start | bytes 221192 | tf_op jit(solution)/shard_map/ppermute | solution.py:316
  74.0 1.7 %copy-start.13 = (s32[2]{0:T(128)S(1)}, s32[2]{0:T(128)}, u32[]{:S(2)}) copy-start(s32[2]{0:T(128)} %copy-done.12) | copy-start | bytes 28
  74.0 1.6 %collective-permute-start.12 = (bf16[1152,128]{1,0:T(8,128)(2,1)S(1)}, bf16[1152,128]{1,0:T(8,128)(2,1)S(1)}, u32[]{:S(2)}, u32[]{:S(2)}) collective-permute-start(bf16[1152,128]{1,0:T(8,128)(2,1)S(1)} %constant_dynamic-update-slice_fusion.mine_ref), channel_id=1, source_target_pairs={{0,1},{1,0},{2,3},{3,2},{4,5},{5,4},{6,7},{7,6},{8,9},{9,8},{10,11... | collective-permute-start | bytes 884744 | tf_op jit(solution)/shard_map/ppermute | solution.py:316
  (6 other events, 4.3 us)

commit v3 on v2

--- a/solution.py
+++ b/solution.py
@@ -94,15 +94,38 @@
     wg_ref[...] = jnp.concatenate([wup_ref[2 * ij + k] for k in range(2) for ij in range(4)], axis=0).T
 
 
-def edge_kernel(before_ref, after_ref, wup_ref, xu_ref, wfu_ref, xb_ref, xa_ref, pre_ref):
+def edge_kernel(
+    before_ref,
+    after_ref,
+    wup_ref,
+    own_ref,
+    far_wfu_ref,
+    far_wfs_ref,
+    far_wg_ref,
+    xu_ref,
+    pre_ref,
+    wfs_ref,
+    wg_ref,
+    wfu_ref,
+    sems,
+):
+    pairs = (
+        (own_ref, xu_ref.at[384:768]),
+        (far_wfu_ref, wfu_ref),
+        (far_wfs_ref, wfs_ref),
+        (far_wg_ref, wg_ref),
+    )
+    copies = [pltpu.make_async_copy(src, dst, sems.at[i]) for i, (src, dst) in enumerate(pairs)]
+    for copy in copies:
+        copy.start()
     weights = up_weights(wup_ref)
     select = spread_columns()
-    upsample(before_ref, weights, select, xb_ref, 0)
-    upsample(after_ref, weights, select, xa_ref, 0)
-    whole = (xb_ref, xu_ref, xa_ref)
+    upsample(before_ref, weights, select, xu_ref, 0)
+    upsample(after_ref, weights, select, xu_ref, 768)
+    for copy in copies:
+        copy.wait()
     for j in range(4):
-        planes = [whole[e >> 1][(e & 1) * 192 : (e & 1) * 192 + 192, :] for e in range(j, j + 3)]
-        z = mm(wfu_ref[...], jnp.concatenate(planes, axis=0))
+        z = mm(wfu_ref[...], xu_ref[j * 192 : j * 192 + 576, :])
         pre_ref[j * 64 : (j + 1) * 64, :] = row_taps(z, 64)
 
 
@@ -115,14 +138,12 @@
     cot_ref,
     edge_before_ref,
     edge_after_ref,
+    xu_ref,
+    pre_ref,
+    spread_ref,
+    wi_ref,
     wf_ref,
-    far_xb_ref,
-    far_xu_ref,
-    far_xa_ref,
-    far_pre_ref,
-    far_spread_ref,
-    far_wi_ref,
-    far_wg_ref,
+    wg_ref,
     act_ref,
     gi_ref,
     skip_ref,
@@ -131,26 +152,7 @@
     xs_ref,
     gs_ref,
     gw_ref,
-    xu_ref,
-    pre_ref,
-    spread_ref,
-    wi_ref,
-    wg_ref,
-    sems,
 ):
-    pairs = (
-        (far_pre_ref, pre_ref),
-        (far_xb_ref, xu_ref.at[0:384]),
-        (far_xu_ref, xu_ref.at[384:768]),
-        (far_xa_ref, xu_ref.at[768:1152]),
-        (far_wi_ref, wi_ref),
-        (far_spread_ref, spread_ref),
-        (far_wg_ref, wg_ref),
-    )
-    copies = [pltpu.make_async_copy(src, dst, sems.at[i]) for i, (src, dst) in enumerate(pairs)]
-    for copy in copies:
-        copy.start()
-
     def pick(row, col):
         out = jnp.where(col >= 384, 1, 0)
         rest = col - 384 * out
@@ -170,7 +172,6 @@
                         h * 64 : (h + 1) * 64, (3 * parity + tap) * W : (3 * parity + tap + 1) * W
                     ]
 
-    copies[0].wait()
     shift = one_hot((128, 256), lambda row, col: row == (col & 127) + 1 - 2 * (col >> 7))
     for j in range(4):
         z = mm(wf_ref[...], xs_ref[j * 192 : j * 192 + 576, :])
@@ -201,8 +202,6 @@
         low = jnp.concatenate([grad[:, W:], zero], axis=1)
         high = jnp.concatenate([zero, grad[:, :-W]], axis=1)
         grads.append(jnp.concatenate([low, grad, high], axis=0))
-    for copy in copies[1:4]:
-        copy.wait()
     for a in range(3):
         total = None
         for j in (1, 2):
@@ -220,8 +219,6 @@
                 at = (9 * a + 3 * b + tap) * 64
                 gw_ref[at : at + 64, :] = total[b * 64 : (b + 1) * 64, tap * W : (tap + 1) * W]
 
-    for copy in copies[4:]:
-        copy.wait()
     lower = lax.broadcasted_iota(jnp.int32, (64, W), 1) < 64
     ups = []
     skips = []
@@ -307,8 +304,24 @@
 FAR = pl.BlockSpec(memory_space=pl.ANY)
 
 
+def far(value):
+    return pltpu.with_memory_space_constraint(value, pltpu.HBM)
+
+
+def near(value):
+    return pltpu.with_memory_space_constraint(value, pltpu.VMEM)
+
+
 def like(shape, dtype=BF16):
     return jax.ShapeDtypeStruct(shape, dtype)
+
+
+def inside(shape, dtype=BF16):
+    return pltpu.VMEM(shape, dtype)
+
+
+def outside(shape, dtype=BF16):
+    return pltpu.HBM(shape, dtype)
 
 
 def reduce_weights(index, keep, send, back, finish_others, n):
@@ -337,6 +350,7 @@
         in_specs=[SMEM, VMEM, VMEM],
         out_specs=(VMEM, VMEM),
         compiler_params=room(6),
+        cost_estimate=pl.CostEstimate(flops=1955000000, bytes_accessed=1000000, transcendentals=0),
         name="finish",
     )(index, mine, other)
     return conv.reshape(27, 64, 128), up.reshape(8, 64, 128), others
@@ -370,57 +384,60 @@
     xu, spread, wf_up, wf_skip, wi, wg = pl.pallas_call(
         prepare_kernel,
         out_shape=(
-            like((384, 1024)),
-            like((256, 512)),
-            like((192, 576)),
-            like((192, 576)),
-            like((384, 576)),
-            like((128, 512)),
+            inside((384, 1024)),
+            inside((256, 512)),
+            outside((192, 576)),
+            outside((192, 576)),
+            inside((384, 576)),
+            outside((128, 512)),
         ),
         in_specs=[VMEM] * 3,
         out_specs=(VMEM,) * 6,
         compiler_params=room(8),
+        cost_estimate=pl.CostEstimate(flops=1840000000, bytes_accessed=1000000, transcendentals=0),
         name="prepare",
     )(coarse, w_up, w_conv)
-    held, wf_up, edge_before, edge_after = lax.optimization_barrier((held, wf_up, edge_before, edge_after))
+    held, wf_up = lax.optimization_barrier((held, wf_up))
     held_before = lax.ppermute(held, AXIS, up)
     held_after = lax.ppermute(held, AXIS, down)
-    xb, xa, pre = pl.pallas_call(
+    xu, pre, wf_skip, wg = pl.pallas_call(
         edge_kernel,
-        out_shape=(like((384, 1024)), like((384, 1024)), like((256, 1024), F32)),
-        in_specs=[VMEM] * 5,
-        out_specs=(VMEM,) * 3,
+        out_shape=(
+            inside((1152, 1024)),
+            inside((256, 1024), F32),
+            inside((192, 576)),
+            inside((128, 512)),
+        ),
+        in_specs=[VMEM] * 4 + [FAR] * 3,
+        out_specs=(VMEM,) * 4,
+        scratch_shapes=[pltpu.VMEM((192, 576), BF16), pltpu.SemaphoreType.DMA((4,))],
         compiler_params=room(16),
+        cost_estimate=pl.CostEstimate(flops=2990000000, bytes_accessed=1000000, transcendentals=0),
         name="edges",
-    )(edge_before, edge_after, w_up, xu, wf_up)
+    )(near(edge_before), near(edge_after), w_up, near(xu), far(wf_up), far(wf_skip), far(wg))
 
     scale = 1.0 / math.sqrt(n * planes * cells)
     rows = [v.reshape(8, 2, 64, 128) for v in (held, held_before, held_after)]
     act, gi, skip_part, keep, send = pl.pallas_call(
         functools.partial(main_kernel, scale),
         out_shape=(
-            like((64, 2048)),
-            like((128, 256)),
-            like((16, 64, 128)),
-            like((1152, 128), F32),
-            like((1152, 128)),
+            outside((64, 2048)),
+            outside((128, 256)),
+            outside((16, 64, 128)),
+            inside((1152, 128), F32),
+            inside((1152, 128)),
         ),
-        in_specs=[SMEM] + [VMEM] * 7 + [FAR] * 7,
+        in_specs=[SMEM] + [VMEM] * 12,
         out_specs=(VMEM,) * 5,
         scratch_shapes=[
             pltpu.VMEM((1152, 1024), BF16),
             pltpu.VMEM((768, 1024), BF16),
             pltpu.VMEM((2304, 128), F32),
-            pltpu.VMEM((1152, 1024), BF16),
-            pltpu.VMEM((256, 1024), F32),
-            pltpu.VMEM((256, 512), BF16),
-            pltpu.VMEM((384, 576), BF16),
-            pltpu.VMEM((128, 512), BF16),
-            pltpu.SemaphoreType.DMA((7,)),
         ],
         compiler_params=room(24),
+        cost_estimate=pl.CostEstimate(flops=8280000000, bytes_accessed=1000000, transcendentals=0),
         name="section",
-    )(index, *rows, flat, edge_before, edge_after, wf_skip, xb, xu, xa, pre, spread, wi, wg)
+    )(index, *(near(v) for v in (*rows, flat, edge_before, edge_after, xu, pre, spread, wi, wf_skip, wg)))
     if positions != 64:
         skip_part = skip_part.reshape(16, 64, 2, 64).transpose(1, 2, 0, 3)
         skip_part = skip_part.reshape(64, 2, n, positions).transpose(2, 0, 1, 3)

time: 77.9 us -> 71.9 us (0.923)
  local copies, waits for them, and re-layouts: 10.5 us -> 5.37 us
  starting transfers between devices: 35.9 us -> 34.9 us
    unnamed x34 -> x12, local copies, waits for them, and re-layouts: 6.25 us -> 1.05 us
    ppermute x1, starting transfers between devices: 3.94 us -> 3.05 us  [local(): held_before = lax.ppermute(held, AXIS, up)]
  transfers between devices with their start and end apart: 15 -> 15, of which waited for: 9 -> 9; matrix products, arithmetic and copies ran while one was open for 3% -> 5% of each run, Pallas kernels for 4% -> 6%
where the time goes in v3:
time: 71.9 us; the launch traced here: 71.5 us
  starting transfers between devices  34.9 us (49%)
  waiting for transfers between devices  16.8 us (23%)
  Pallas kernels  13.4 us (19%)
  local copies, waits for them, and re-layouts  5.37 us (7%)
  between operations  0.86 us (1%)
    ppermute x9, waiting for transfers between devices, swap(): return lax.ppermute(value, AXIS, [(i, i ^ bit) for i in range(n)])  14 us
    ppermute x9, starting transfers between devices, swap(): return lax.ppermute(value, AXIS, [(i, i ^ bit) for i in range(n)])  13.1 us
    all_to_all x1, starting transfers between devices, local(): held = lax.all_to_all(sent, AXIS, split_axis=0, concat_axis=0, tiled=True)  7.36 us
    pallas_call x1, Pallas kernels, local(): pl.pallas_call(functools.partial(main_kernel, scale), out_shape=(outside(...  7.25 us
    all_to_all x1, starting transfers between devices, local(): lax.all_to_all(skip_part, AXIS, split_axis=0, concat_axis=0, tiled=True)  5.69 us
    ppermute x1, starting transfers between devices, local(): held_before = lax.ppermute(held, AXIS, up)  3.05 us
    ppermute x1, starting transfers between devices, local(): edge_before = lax.ppermute(edge(1), AXIS, up)  3.04 us
    all_to_all x1, waiting for transfers between devices, local(): held = lax.all_to_all(sent, AXIS, split_axis=0, concat_axis=0, tiled=True)  2.81 us
  transfers between devices with their start and end apart: 15, of which 9 were waited for; matrix products, arithmetic and copies ran while one was open for 5% of the time, Pallas kernels for 6%

profile of v3, /device:TPU:0, one launch (start us, length us, event | category | flops | bytes accessed | tf_op | source)
XLA Modules:
  0.0 71.5 jit_solution(16098494531712420452)
XLA Ops:
  0.7 1.4 %reshape.43 = bf16[64,16,128]{2,1,0:T(8,128)(2,1)S(1)} reshape(bf16[64,32,64]{2,1,0:T(8,128)(2,1)} %param.6) | data formatting | bytes 524288 | tf_op jit(solution)/shard_map/reshape | solution.py:369
  2.8 7.4 %all-to-all-start = ((bf16[16,64,128]{2,1,0:T(8,128)(2,1)}), bf16[16,64,128]{2,1,0:T(8,128)(2,1)S(1)}, u32[]{:S(2)}, u32[]{:S(2)}) async-start(bf16[16,64,128]{2,1,0:T(8,128)(2,1)} %bitcast.14), calls=%async_computation | async-start | bytes 524288 | tf_op jit(solution)/shard_map/all_to_all | solution.py:370
  10.2 1.0 %copy.13 = bf16[8,8,2,1024]{3,1,2,0:T(8,128)(2,1)S(1)} copy(bf16[8,8,2,1024]{3,2,1,0:T(2,128)(2,1)} %bitcast.23) | data formatting | bytes 524288
  11.3 1.3 %collective-permute-start.3 = (bf16[128,768]{1,0:T(8,128)(2,1)S(1)}, bf16[128,768]{1,0:T(8,128)(2,1)S(1)}, u32[]{:S(2)}, u32[]{:S(2)}) collective-permute-start(bf16[128,768]{1,0:T(8,128)(2,1)S(1)} %get-tuple-element.70), channel_id=1, source_target_pairs={{1,0},{2,1},{3,2},{4,3},{5,4},{6,5},{7,6},{8,7},{9,8},{10,9},{11,1... | collective-permute-start | bytes 589832 | tf_op jit(solution)/shard_map/ppermute | solution.py:383
  12.6 3.0 %collective-permute-start.2 = (bf16[128,768]{1,0:T(8,128)(2,1)S(1)}, bf16[128,768]{1,0:T(8,128)(2,1)S(1)}, u32[]{:S(2)}, u32[]{:S(2)}) collective-permute-start(bf16[128,768]{1,0:T(8,128)(2,1)S(1)} %get-tuple-element.71), channel_id=1, source_target_pairs={{0,1},{1,2},{2,3},{3,4},{4,5},{5,6},{6,7},{7,8},{8,9},{9,10},{10,1... | collective-permute-start | bytes 589832 | tf_op jit(solution)/shard_map/ppermute | solution.py:382
  15.7 1.7 %prepare.1 = (bf16[384,1024]{1,0:T(8,128)(2,1)S(1)}, bf16[256,512]{1,0:T(8,128)(2,1)S(1)}, bf16[192,576]{1,0:T(8,128)(2,1)}, bf16[192,576]{1,0:T(8,128)(2,1)}, b...) custom-call(bf16[128,256]{1,0:T(8,128)(2,1)S(1)} %bitcast.19, bf16[8,64,128]{2,1,0:T(8,128)(2,1)S(1)} %copy-done.2, ...), custom_call_target="tpu_custom_call" | custom-call | flops 1840000000 | bytes 1000000 | tf_op jit(solution)/shard_map/prepare/pallas_call | solution.py:384
  17.4 2.8 %all-to-all-done = bf16[16,64,128]{2,1,0:T(8,128)(2,1)S(1)} async-done(((bf16[16,64,128]{2,1,0:T(8,128)(2,1)}), bf16[16,64,128]{2,1,0:T(8,128)(2,1)S(1)}, u32[]{:S(2)}, u32[]{:S(2)}) %all-to-all-start) | async-done | bytes 262176 | tf_op jit(solution)/shard_map/all_to_all | solution.py:370
  20.2 1.3 %collective-permute-start.1 = (bf16[16,64,128]{2,1,0:T(8,128)(2,1)S(1)}, bf16[16,64,128]{2,1,0:T(8,128)(2,1)S(1)}, u32[]{:S(2)}, u32[]{:S(2)}) collective-permute-start(bf16[16,64,128]{2,1,0:T(8,128)(2,1)S(1)} %all-to-all-done), channel_id=1, source_target_pairs={{1,0},{2,1},{3,2},{4,3},{5,4},{6,5},{7,6},{8,7},{9,8},{10,9},{11,1... | collective-permute-start | bytes 786440 | tf_op jit(solution)/shard_map/ppermute | solution.py:402
  21.5 3.0 %collective-permute-start = (bf16[16,64,128]{2,1,0:T(8,128)(2,1)S(1)}, bf16[16,64,128]{2,1,0:T(8,128)(2,1)S(1)}, u32[]{:S(2)}, u32[]{:S(2)}) collective-permute-start(bf16[16,64,128]{2,1,0:T(8,128)(2,1)S(1)} %all-to-all-done), channel_id=1, source_target_pairs={{0,1},{1,2},{2,3},{3,4},{4,5},{5,6},{6,7},{7,8},{8,9},{9,10},{10,1... | collective-permute-start | bytes 786440 | tf_op jit(solution)/shard_map/ppermute | solution.py:401
  24.6 2.7 %edges.1 = (bf16[1152,1024]{1,0:T(8,128)(2,1)S(1)}, f32[256,1024]{1,0:T(8,128)S(1)}, bf16[192,576]{1,0:T(8,128)(2,1)S(1)}, bf16[128,512]{1,0:T(8,128)(2,1)S(1)}) custom-call(bf16[128,768]{1,0:T(8,128)(2,1)S(1)} %collective-permute-done.2.before_ref.edge_before_ref, bf16[128,768]{1,0:T(8,128)(2,1)S(1)} %collective-permute-done.3.after_ref.edge_after_ref, ...), custom_call_target="tpu_custom_call" | custom-call | flops 2990000128 | bytes 1000000 | tf_op jit(solution)/shard_map/edges/pallas_call | solution.py:403
  27.3 7.2 %section.1 = (bf16[64,2048]{1,0:T(8,128)(2,1)}, bf16[128,256]{1,0:T(8,128)(2,1)}, bf16[16,64,128]{2,1,0:T(8,128)(2,1)}, f32[1152,128]{1,0:T(8,128)S(1)}, bf16[1152,128]{1,0:T(8,128)(2,1)S(1)}) custom-call(s32[2]{0:T(128)S(1)} %pad_add_fusion.index_ref, bf16[8,2,64,128]{3,2,1,0:T(8,128)(2,1)S(1)} %bitcast.17, bf16[8,2,64,128]{3,2,1,0:T(8,128)(2,1)S(1)} %bitcast.21, ...), custom_call_target="tpu_custom_call" | custom-call | flops 8280000000 | bytes 1000000 | tf_op jit(solution)/shard_map/section/pallas_call | solution.py:421
  34.5 3.5 %collective-permute-start.4 = (bf16[1152,128]{1,0:T(8,128)(2,1)S(1)}, bf16[1152,128]{1,0:T(8,128)(2,1)S(1)}, u32[]{:S(2)}, u32[]{:S(2)}) collective-permute-start(bf16[1152,128]{1,0:T(8,128)(2,1)S(1)} %get-tuple-element.46), channel_id=1, source_target_pairs={{0,1},{1,0},{2,3},{3,2},{4,5},{5,4},{6,7},{7,6},{8,9},{9,8},{10,11... | collective-permute-start | bytes 884744 | tf_op jit(solution)/shard_map/ppermute | solution.py:329
  38.1 5.7 %all-to-all-start.1 = ((bf16[16,64,128]{2,1,0:T(8,128)(2,1)}), bf16[16,64,128]{2,1,0:T(8,128)(2,1)S(1)}, u32[]{:S(2)}, u32[]{:S(2)}) async-start(bf16[16,64,128]{2,1,0:T(8,128)(2,1)} %get-tuple-element.47), calls=%async_computation.1 | async-start | bytes 524288 | tf_op jit(solution)/shard_map/all_to_all | solution.py:445
  43.9 2.0 %collective-permute-start.5 = (bf16[288,128]{1,0:T(8,128)(2,1)S(1)}, bf16[288,128]{1,0:T(8,128)(2,1)S(1)}, u32[]{:S(2)}, u32[]{:S(2)}) collective-permute-start(bf16[288,128]{1,0:T(8,128)(2,1)S(1)} %get-tuple-element.63), channel_id=1, source_target_pairs={{0,2},{1,3},{2,0},{3,1},{4,6},{5,7},{6,4},{7,5},{8,10},{9,11},{10,... | collective-permute-start | bytes 221192 | tf_op jit(solution)/shard_map/ppermute | solution.py:329
  45.9 1.5 %collective-permute-start.7 = (bf16[288,128]{1,0:T(8,128)(2,1)S(1)}, bf16[288,128]{1,0:T(8,128)(2,1)S(1)}, u32[]{:S(2)}, u32[]{:S(2)}) collective-permute-start(bf16[288,128]{1,0:T(8,128)(2,1)S(1)} %get-tuple-element.64), channel_id=1, source_target_pairs={{0,6},{1,7},{2,4},{3,5},{4,2},{5,3},{6,0},{7,1},{8,14},{9,15},{10,... | collective-permute-start | bytes 221192 | tf_op jit(solution)/shard_map/ppermute | solution.py:329
  47.5 3.2 %collective-permute-done.5 = bf16[288,128]{1,0:T(8,128)(2,1)S(1)} collective-permute-done((bf16[288,128]{1,0:T(8,128)(2,1)S(1)}, bf16[288,128]{1,0:T(8,128)(2,1)S(1)}, u32[]{:S(2)}, u32[]{:S(2)}) %collective-permute-start.5) | collective-permute-done | bytes 73760 | tf_op jit(solution)/shard_map/ppermute | solution.py:329
  50.7 2.9 %collective-permute-done.7 = bf16[288,128]{1,0:T(8,128)(2,1)S(1)} collective-permute-done((bf16[288,128]{1,0:T(8,128)(2,1)S(1)}, bf16[288,128]{1,0:T(8,128)(2,1)S(1)}, u32[]{:S(2)}, u32[]{:S(2)}) %collective-permute-start.7) | collective-permute-done | bytes 73760 | tf_op jit(solution)/shard_map/ppermute | solution.py:329
  54.3 2.4 %collective-permute-start.8 = (bf16[288,128]{1,0:T(8,128)(2,1)S(1)}, bf16[288,128]{1,0:T(8,128)(2,1)S(1)}, u32[]{:S(2)}, u32[]{:S(2)}) collective-permute-start(bf16[288,128]{1,0:T(8,128)(2,1)S(1)} %fusion.1), channel_id=1, source_target_pairs={{0,8},{1,9},{2,10},{3,11},{4,12},{5,13},{6,14},{7,15},{8,0},{9,1},... | collective-permute-start | bytes 221192 | tf_op jit(solution)/shard_map/ppermute | solution.py:329
  56.8 4.0 %collective-permute-done.8 = bf16[288,128]{1,0:T(8,128)(2,1)S(1)} collective-permute-done((bf16[288,128]{1,0:T(8,128)(2,1)S(1)}, bf16[288,128]{1,0:T(8,128)(2,1)S(1)}, u32[]{:S(2)}, u32[]{:S(2)}) %collective-permute-start.8) | collective-permute-done | bytes 73760 | tf_op jit(solution)/shard_map/ppermute | solution.py:329
  61.3 2.4 %collective-permute-start.10 = (bf16[288,128]{1,0:T(8,128)(2,1)S(1)}, bf16[288,128]{1,0:T(8,128)(2,1)S(1)}, u32[]{:S(2)}, u32[]{:S(2)}) collective-permute-start(bf16[288,128]{1,0:T(8,128)(2,1)S(1)} %add_convert_fusion), channel_id=1, source_target_pairs={{0,4},{1,5},{2,6},{3,7},{4,0},{5,1},{6,2},{7,3},{8,12},{9,13},{10,... | collective-permute-start | bytes 221192 | tf_op jit(solution)/shard_map/ppermute | solution.py:329
  65.4 1.1 %reshape.51 = bf16[64,32,64]{2,1,0:T(8,128)(2,1)} reshape(bf16[64,16,128]{2,1,0:T(8,128)(2,1)S(1)} %copy.12) | data formatting | bytes 524288 | tf_op jit(solution)/shard_map/reshape | solution.py:451
  67.0 1.1 %collective-permute-done.9 = bf16[288,128]{1,0:T(8,128)(2,1)S(1)} collective-permute-done((bf16[288,128]{1,0:T(8,128)(2,1)S(1)}, bf16[288,128]{1,0:T(8,128)(2,1)S(1)}, u32[]{:S(2)}, u32[]{:S(2)}) %collective-permute-start.9) | collective-permute-done | bytes 73760 | tf_op jit(solution)/shard_map/ppermute | solution.py:329
  68.2 1.6 %collective-permute-done.12.other_ref = bf16[1152,128]{1,0:T(8,128)(2,1)S(1)} collective-permute-done((bf16[1152,128]{1,0:T(8,128)(2,1)S(1)}, bf16[1152,128]{1,0:T(8,128)(2,1)S(1)}, u32[]{:S(2)}, u32[]{:S(2)}) %collective-permute-start.12) | collective-permute-done | bytes 294944 | tf_op jit(solution)/shard_map/ppermute | solution.py:329
  69.8 1.7 %finish.1 = (f32[54,32,128]{2,1,0:T(8,128)}, f32[16,32,128]{2,1,0:T(8,128)}) custom-call(s32[2]{0:T(128)S(1)} %pad_add_fusion.index_ref, bf16[1152,128]{1,0:T(8,128)(2,1)S(1)} %constant_dynamic-update-slice_fusion.mine_ref, bf16[1152,128]{1,0:T(8,128)(2,1)S(1)} %collective-permute-done.12.other_ref), custom_call_target="tpu_custom_call" | custom-call | flops 1955000064 | bytes 1000000 | tf_op jit(solution)/shard_map/finish/pallas_call | solution.py:347
  (35 shorter events, 4.8 us)
Async XLA Ops:
  0.6 10.6 %copy-start = (bf16[128,1,256]{2,0,1:T(8,128)(2,1)S(1)}, bf16[128,1,256]{2,0,1:T(8,128)(2,1)}, u32[]{:S(2)}) copy-start(bf16[128,1,256]{2,0,1:T(8,128)(2,1)} %param.5) | copy-start | bytes 196612
  0.6 15.1 %copy-start.2 = (bf16[8,64,128]{2,1,0:T(8,128)(2,1)S(1)}, bf16[8,64,128]{2,1,0:T(8,128)(2,1)}, u32[]{:S(2)}) copy-start(bf16[8,64,128]{2,1,0:T(8,128)(2,1)} %wup_ref.3) | copy-start | bytes 393220
  0.7 15.1 %copy-start.1 = (bf16[27,64,128]{2,1,0:T(8,128)(2,1)S(1)}, bf16[27,64,128]{2,1,0:T(8,128)(2,1)}, u32[]{:S(2)}) copy-start(bf16[27,64,128]{2,1,0:T(8,128)(2,1)} %wc_ref.1) | copy-start | bytes 1327108
  2.8 17.4 %all-to-all-start = ((bf16[16,64,128]{2,1,0:T(8,128)(2,1)}), bf16[16,64,128]{2,1,0:T(8,128)(2,1)S(1)}, u32[]{:S(2)}, u32[]{:S(2)}) async-start(bf16[16,64,128]{2,1,0:T(8,128)(2,1)} %bitcast.14), calls=%async_computation | async-start | bytes 524288 | tf_op jit(solution)/shard_map/all_to_all | solution.py:370
  11.3 13.3 %collective-permute-start.3 = (bf16[128,768]{1,0:T(8,128)(2,1)S(1)}, bf16[128,768]{1,0:T(8,128)(2,1)S(1)}, u32[]{:S(2)}, u32[]{:S(2)}) collective-permute-start(bf16[128,768]{1,0:T(8,128)(2,1)S(1)} %get-tuple-element.70), channel_id=1, source_target_pairs={{1,0},{2,1},{3,2},{4,3},{5,4},{6,5},{7,6},{8,7},{9,8},{10,9},{11,1... | collective-permute-start | bytes 589832 | tf_op jit(solution)/shard_map/ppermute | solution.py:383
  12.6 12.0 %collective-permute-start.2 = (bf16[128,768]{1,0:T(8,128)(2,1)S(1)}, bf16[128,768]{1,0:T(8,128)(2,1)S(1)}, u32[]{:S(2)}, u32[]{:S(2)}) collective-permute-start(bf16[128,768]{1,0:T(8,128)(2,1)S(1)} %get-tuple-element.71), channel_id=1, source_target_pairs={{0,1},{1,2},{2,3},{3,4},{4,5},{5,6},{6,7},{7,8},{8,9},{9,10},{10,1... | collective-permute-start | bytes 589832 | tf_op jit(solution)/shard_map/ppermute | solution.py:382
  20.2 7.0 %collective-permute-start.1 = (bf16[16,64,128]{2,1,0:T(8,128)(2,1)S(1)}, bf16[16,64,128]{2,1,0:T(8,128)(2,1)S(1)}, u32[]{:S(2)}, u32[]{:S(2)}) collective-permute-start(bf16[16,64,128]{2,1,0:T(8,128)(2,1)S(1)} %all-to-all-done), channel_id=1, source_target_pairs={{1,0},{2,1},{3,2},{4,3},{5,4},{6,5},{7,6},{8,7},{9,8},{10,9},{11,1... | collective-permute-start | bytes 786440 | tf_op jit(solution)/shard_map/ppermute | solution.py:402
  21.5 5.8 %collective-permute-start = (bf16[16,64,128]{2,1,0:T(8,128)(2,1)S(1)}, bf16[16,64,128]{2,1,0:T(8,128)(2,1)S(1)}, u32[]{:S(2)}, u32[]{:S(2)}) collective-permute-start(bf16[16,64,128]{2,1,0:T(8,128)(2,1)S(1)} %all-to-all-done), channel_id=1, source_target_pairs={{0,1},{1,2},{2,3},{3,4},{4,5},{5,6},{6,7},{7,8},{8,9},{9,10},{10,1... | collective-permute-start | bytes 786440 | tf_op jit(solution)/shard_map/ppermute | solution.py:401
  34.5 29.8 %copy-start.3 = (bf16[64,2048]{1,0:T(8,128)(2,1)S(1)}, bf16[64,2048]{1,0:T(8,128)(2,1)}, u32[]{:S(2)}) copy-start(bf16[64,2048]{1,0:T(8,128)(2,1)} %get-tuple-element.49) | copy-start | bytes 786436
  34.5 9.2 %collective-permute-start.4 = (bf16[1152,128]{1,0:T(8,128)(2,1)S(1)}, bf16[1152,128]{1,0:T(8,128)(2,1)S(1)}, u32[]{:S(2)}, u32[]{:S(2)}) collective-permute-start(bf16[1152,128]{1,0:T(8,128)(2,1)S(1)} %get-tuple-element.46), channel_id=1, source_target_pairs={{0,1},{1,0},{2,3},{3,2},{4,5},{5,4},{6,7},{7,6},{8,9},{9,8},{10,11... | collective-permute-start | bytes 884744 | tf_op jit(solution)/shard_map/ppermute | solution.py:329
  38.1 16.3 %all-to-all-start.1 = ((bf16[16,64,128]{2,1,0:T(8,128)(2,1)}), bf16[16,64,128]{2,1,0:T(8,128)(2,1)S(1)}, u32[]{:S(2)}, u32[]{:S(2)}) async-start(bf16[16,64,128]{2,1,0:T(8,128)(2,1)} %get-tuple-element.47), calls=%async_computation.1 | async-start | bytes 524288 | tf_op jit(solution)/shard_map/all_to_all | solution.py:445
  43.9 6.8 %collective-permute-start.5 = (bf16[288,128]{1,0:T(8,128)(2,1)S(1)}, bf16[288,128]{1,0:T(8,128)(2,1)S(1)}, u32[]{:S(2)}, u32[]{:S(2)}) collective-permute-start(bf16[288,128]{1,0:T(8,128)(2,1)S(1)} %get-tuple-element.63), channel_id=1, source_target_pairs={{0,2},{1,3},{2,0},{3,1},{4,6},{5,7},{6,4},{7,5},{8,10},{9,11},{10,... | collective-permute-start | bytes 221192 | tf_op jit(solution)/shard_map/ppermute | solution.py:329
  45.9 7.7 %collective-permute-start.7 = (bf16[288,128]{1,0:T(8,128)(2,1)S(1)}, bf16[288,128]{1,0:T(8,128)(2,1)S(1)}, u32[]{:S(2)}, u32[]{:S(2)}) collective-permute-start(bf16[288,128]{1,0:T(8,128)(2,1)S(1)} %get-tuple-element.64), channel_id=1, source_target_pairs={{0,6},{1,7},{2,4},{3,5},{4,2},{5,3},{6,0},{7,1},{8,14},{9,15},{10,... | collective-permute-start | bytes 221192 | tf_op jit(solution)/shard_map/ppermute | solution.py:329
  47.4 6.9 %collective-permute-start.6 = (bf16[288,128]{1,0:T(8,128)(2,1)S(1)}, bf16[288,128]{1,0:T(8,128)(2,1)S(1)}, u32[]{:S(2)}, u32[]{:S(2)}) collective-permute-start(bf16[288,128]{1,0:T(8,128)(2,1)S(1)} %get-tuple-element.65), channel_id=1, source_target_pairs={{0,4},{1,5},{2,6},{3,7},{4,0},{5,1},{6,2},{7,3},{8,12},{9,13},{10,... | collective-permute-start | bytes 221192 | tf_op jit(solution)/shard_map/ppermute | solution.py:329
  54.3 6.4 %collective-permute-start.8 = (bf16[288,128]{1,0:T(8,128)(2,1)S(1)}, bf16[288,128]{1,0:T(8,128)(2,1)S(1)}, u32[]{:S(2)}, u32[]{:S(2)}) collective-permute-start(bf16[288,128]{1,0:T(8,128)(2,1)S(1)} %fusion.1), channel_id=1, source_target_pairs={{0,8},{1,9},{2,10},{3,11},{4,12},{5,13},{6,14},{7,15},{8,0},{9,1},... | collective-permute-start | bytes 221192 | tf_op jit(solution)/shard_map/ppermute | solution.py:329
  60.8 5.8 %collective-permute-start.11 = (bf16[288,128]{1,0:T(8,128)(2,1)S(1)}, bf16[288,128]{1,0:T(8,128)(2,1)S(1)}, u32[]{:S(2)}, u32[]{:S(2)}) collective-permute-start(bf16[288,128]{1,0:T(8,128)(2,1)S(1)} %add_convert_fusion), channel_id=1, source_target_pairs={{0,6},{1,7},{2,4},{3,5},{4,2},{5,3},{6,0},{7,1},{8,14},{9,15},{10,... | collective-permute-start | bytes 221192 | tf_op jit(solution)/shard_map/ppermute | solution.py:329
  61.3 5.7 %collective-permute-start.10 = (bf16[288,128]{1,0:T(8,128)(2,1)S(1)}, bf16[288,128]{1,0:T(8,128)(2,1)S(1)}, u32[]{:S(2)}, u32[]{:S(2)}) collective-permute-start(bf16[288,128]{1,0:T(8,128)(2,1)S(1)} %add_convert_fusion), channel_id=1, source_target_pairs={{0,4},{1,5},{2,6},{3,7},{4,0},{5,1},{6,2},{7,3},{8,12},{9,13},{10,... | collective-permute-start | bytes 221192 | tf_op jit(solution)/shard_map/ppermute | solution.py:329
  63.7 4.4 %collective-permute-start.9 = (bf16[288,128]{1,0:T(8,128)(2,1)S(1)}, bf16[288,128]{1,0:T(8,128)(2,1)S(1)}, u32[]{:S(2)}, u32[]{:S(2)}) collective-permute-start(bf16[288,128]{1,0:T(8,128)(2,1)S(1)} %add_convert_fusion), channel_id=1, source_target_pairs={{0,2},{1,3},{2,0},{3,1},{4,6},{5,7},{6,4},{7,5},{8,10},{9,11},{10,... | collective-permute-start | bytes 221192 | tf_op jit(solution)/shard_map/ppermute | solution.py:329
  68.1 1.6 %collective-permute-start.12 = (bf16[1152,128]{1,0:T(8,128)(2,1)S(1)}, bf16[1152,128]{1,0:T(8,128)(2,1)S(1)}, u32[]{:S(2)}, u32[]{:S(2)}) collective-permute-start(bf16[1152,128]{1,0:T(8,128)(2,1)S(1)} %constant_dynamic-update-slice_fusion.mine_ref), channel_id=1, source_target_pairs={{0,1},{1,0},{2,3},{3,2},{4,5},{5,4},{6,7},{7,6},{8,9},{9,8},{10,11... | collective-permute-start | bytes 884744 | tf_op jit(solution)/shard_map/ppermute | solution.py:329

commit v4 on v3

--- a/solution.py
+++ b/solution.py
@@ -46,14 +46,42 @@
     return one_hot((128, 1536), pick)
 
 
+def skip_columns():
+    def pick(row, col):
+        out = jnp.where(col >= 384, 1, 0)
+        rest = col - 384 * out
+        tap, lane = (rest >> 7, rest & 127)
+        return (((row >> 6) & 1) == out) & ((row >> 7) * 64 + (row & 63) == lane + tap - 1)
+
+    return one_hot((256, 768), pick)
+
+
+def place_skip(value, select, xs_ref, base):
+    joined = jnp.concatenate([value[:, 0].reshape(512, 128), value[:, 1].reshape(512, 128)], axis=1)
+    placed = mm(joined, select).astype(BF16)
+    for parity in range(2):
+        for tap in range(3):
+            at = base + parity * 192 + tap * 64
+            for h in range(8):
+                xs_ref[at : at + 64, h * W : (h + 1) * W] = placed[
+                    h * 64 : (h + 1) * 64, (3 * parity + tap) * W : (3 * parity + tap + 1) * W
+                ]
+
+
+def in_order(core, core_ref, cross_ref):
+    near, far = (core_ref[...], cross_ref[...])
+    even = core == 0
+    return jnp.where(even, far, near), jnp.where(even, near, far)
+
+
 def up_weights(wup_ref):
     return jnp.concatenate(
         [jnp.concatenate([wup_ref[2 * ij], wup_ref[2 * ij + 1]], axis=1) for ij in range(4)], axis=0
     )
 
 
-def upsample(coarse_ref, weights, select, xu_ref, base, spread_ref=None):
-    spread = [mm(coarse_ref[:, 128 * t : 128 * t + 128], select).astype(BF16) for t in range(2)]
+def upsample(coarse, weights, select, xu_ref, base, spread_ref=None):
+    spread = [mm(coarse[:, 128 * t : 128 * t + 128], select).astype(BF16) for t in range(2)]
     for tap in range(3):
         columns = []
         for h in range(4):
@@ -73,8 +101,13 @@
                     ]
 
 
-def prepare_kernel(own_ref, wup_ref, wc_ref, xu_ref, spread_ref, wfu_ref, wfs_ref, wi_ref, wg_ref):
-    upsample(own_ref, up_weights(wup_ref), spread_columns(), xu_ref, 0, spread_ref)
+def prepare_kernel(
+    own_ref, wup_ref, wc_ref, xu_ref, spread_ref, wfu_ref, wfs_ref, wi_ref, wg_ref, up_ref, skip_ref
+):
+    select = spread_columns()
+    up_ref[...] = select
+    skip_ref[...] = skip_columns()
+    upsample(own_ref[...], up_weights(wup_ref), select, xu_ref, 0, spread_ref)
     rows = []
     for b in range(3):
         taps = [wc_ref[9 * a + 3 * b + c] for a in range(3) for c in range(3)]
@@ -95,49 +128,68 @@
 
 
 def edge_kernel(
-    before_ref,
-    after_ref,
+    index_ref,
+    core_ref,
+    cross_ref,
     wup_ref,
     own_ref,
+    held_ref,
+    skip_ref,
+    far_up_ref,
     far_wfu_ref,
     far_wfs_ref,
+    far_spread_ref,
+    far_wi_ref,
     far_wg_ref,
     xu_ref,
+    xs_ref,
     pre_ref,
     wfs_ref,
+    spread_ref,
+    wi_ref,
     wg_ref,
+    up_ref,
     wfu_ref,
     sems,
 ):
     pairs = (
-        (own_ref, xu_ref.at[384:768]),
+        (far_up_ref, up_ref),
         (far_wfu_ref, wfu_ref),
         (far_wfs_ref, wfs_ref),
+        (own_ref, xu_ref.at[384:768]),
+        (far_spread_ref, spread_ref),
+        (far_wi_ref, wi_ref),
         (far_wg_ref, wg_ref),
     )
     copies = [pltpu.make_async_copy(src, dst, sems.at[i]) for i, (src, dst) in enumerate(pairs)]
     for copy in copies:
         copy.start()
+    place_skip(held_ref[...], skip_ref[...], xs_ref, 0)
     weights = up_weights(wup_ref)
-    select = spread_columns()
-    upsample(before_ref, weights, select, xu_ref, 0)
-    upsample(after_ref, weights, select, xu_ref, 768)
-    for copy in copies:
+    before, after = in_order(index_ref[0], core_ref, cross_ref)
+    copies[0].wait()
+    upsample(before[:, :256], weights, up_ref[...], xu_ref, 0)
+    upsample(after[:, :256], weights, up_ref[...], xu_ref, 768)
+    for copy in copies[1:]:
         copy.wait()
     for j in range(4):
         z = mm(wfu_ref[...], xu_ref[j * 192 : j * 192 + 576, :])
+        low, high = (max(2 - j, 0), min(3 - j, 2))
+        rows = slice((low + j - 2) * 192, (high + j - 1) * 192)
+        z = z + mm(wfs_ref[:, low * 192 : (high + 1) * 192], xs_ref[rows, :])
         pre_ref[j * 64 : (j + 1) * 64, :] = row_taps(z, 64)
 
 
 def main_kernel(
     scale,
     index_ref,
+    near_ref,
+    far_ref,
+    cot_ref,
+    edge_core_ref,
+    edge_cross_ref,
     own_ref,
-    before_ref,
-    after_ref,
-    cot_ref,
-    edge_before_ref,
-    edge_after_ref,
+    select_ref,
     xu_ref,
     pre_ref,
     spread_ref,
@@ -152,35 +204,31 @@
     xs_ref,
     gs_ref,
     gw_ref,
+    sem,
 ):
-    def pick(row, col):
-        out = jnp.where(col >= 384, 1, 0)
-        rest = col - 384 * out
-        tap, lane = (rest >> 7, rest & 127)
-        return (((row >> 6) & 1) == out) & ((row >> 7) * 64 + (row & 63) == lane + tap - 1)
-
-    select = one_hot((256, 768), pick)
-    for part, ref in enumerate((before_ref, own_ref, after_ref)):
-        left = ref[:, 0].reshape(512, 128)
-        right = ref[:, 1].reshape(512, 128)
-        placed = mm(jnp.concatenate([left, right], axis=1), select).astype(BF16)
-        for parity in range(2):
-            for tap in range(3):
-                at = (2 * part + parity) * 192 + tap * 64
-                for h in range(8):
-                    xs_ref[at : at + 64, h * W : (h + 1) * W] = placed[
-                        h * 64 : (h + 1) * 64, (3 * parity + tap) * W : (3 * parity + tap + 1) * W
-                    ]
+    copy = pltpu.make_async_copy(own_ref, xs_ref.at[384:768], sem)
+    copy.start()
+    core = index_ref[0]
+    quad = index_ref[1]
+    before, after = in_order(core, near_ref, far_ref)
+    place_skip(before, select_ref[...], xs_ref, 0)
+    place_skip(after, select_ref[...], xs_ref, 768)
+    edges = [
+        jnp.concatenate([edge[:64, 256:], edge[64:, 256:]], axis=1)
+        for edge in in_order(core, edge_core_ref, edge_cross_ref)
+    ]
 
     shift = one_hot((128, 256), lambda row, col: row == (col & 127) + 1 - 2 * (col >> 7))
     for j in range(4):
-        z = mm(wf_ref[...], xs_ref[j * 192 : j * 192 + 576, :])
+        taps = slice(0, 384 - 192 * j) if j < 2 else slice(192 * (4 - j), 576)
+        planes = slice(192 * j, 384) if j < 2 else slice(768, 192 * (j + 3))
+        z = mm(wf_ref[:, taps], xs_ref[planes, :])
         pre = pre_ref[j * 64 : (j + 1) * 64, :] + row_taps(z, 64)
         gate = 1.0 / (1.0 + jnp.exp(-pre))
         if j == 0:
-            cot = jnp.concatenate([edge_before_ref[:64, 256:], edge_before_ref[64:, 256:]], axis=1)
+            cot = edges[0]
         elif j == 3:
-            cot = jnp.concatenate([edge_after_ref[:64, 256:], edge_after_ref[64:, 256:]], axis=1)
+            cot = edges[1]
         else:
             cot = cot_ref[:, (j - 1) * 1024 : j * 1024]
             act_ref[:, (j - 1) * 1024 : j * 1024] = (pre * gate).astype(BF16)
@@ -195,6 +243,7 @@
                     h * 64 : (h + 1) * 64, (tap >> 1) * W : (tap >> 1) * W + W
                 ]
 
+    copy.wait()
     zero = jnp.zeros((64, W), BF16)
     grads = []
     for j in (1, 2):
@@ -264,8 +313,6 @@
     )
     gi_ref[...] = mm(wg_ref[...], operand).astype(BF16)
 
-    core = index_ref[0]
-    quad = index_ref[1]
     for k in range(4):
         row = jnp.bitwise_xor(quad, k) * 288
         mine = pl.multiple_of(core * 1152 + row, 32)
@@ -361,8 +408,8 @@
     cells = cotangent.shape[2]
     planes = cotangent.shape[1]
     positions = skip.shape[2]
-    up = [(i, i + 1) for i in range(n - 1)]
-    down = [(i + 1, i) for i in range(n - 1)]
+    core_pairs = [(i, i ^ 1) for i in range(n)]
+    cross_pairs = [(i, i + 1 if i % 2 else i - 1) for i in range(1, n - 1)]
     me = lax.axis_index(AXIS)
     index = jnp.stack([me & 1, (me >> 1) & 3]).astype(jnp.int32)
 
@@ -376,48 +423,63 @@
     flat = lax.optimization_barrier(cotangent.reshape(64, 2048))
 
     def edge(plane):
-        halves = [flat[:, 1024 * plane + 512 * i : 1024 * plane + 512 * (i + 1)] for i in range(2)]
+        halves = [lax.dynamic_slice_in_dim(flat, 1024 * plane + 512 * i, 512, 1) for i in range(2)]
         return jnp.concatenate([coarse, jnp.concatenate(halves, axis=0)], axis=1)
 
-    edge_before = lax.ppermute(edge(1), AXIS, up)
-    edge_after = lax.ppermute(edge(0), AXIS, down)
-    xu, spread, wf_up, wf_skip, wi, wg = pl.pallas_call(
+    edge_core = lax.ppermute(edge(1 - index[0]), AXIS, core_pairs)
+    edge_cross = lax.ppermute(edge(index[0]), AXIS, cross_pairs)
+    xu, spread, wf_up, wf_skip, wi, wg, pick_up, pick_skip = pl.pallas_call(
         prepare_kernel,
         out_shape=(
             inside((384, 1024)),
-            inside((256, 512)),
+            outside((256, 512)),
             outside((192, 576)),
             outside((192, 576)),
-            inside((384, 576)),
+            outside((384, 576)),
             outside((128, 512)),
+            outside((128, 1536)),
+            inside((256, 768)),
         ),
         in_specs=[VMEM] * 3,
-        out_specs=(VMEM,) * 6,
+        out_specs=(VMEM,) * 8,
         compiler_params=room(8),
         cost_estimate=pl.CostEstimate(flops=1840000000, bytes_accessed=1000000, transcendentals=0),
         name="prepare",
     )(coarse, w_up, w_conv)
     held, wf_up = lax.optimization_barrier((held, wf_up))
-    held_before = lax.ppermute(held, AXIS, up)
-    held_after = lax.ppermute(held, AXIS, down)
-    xu, pre, wf_skip, wg = pl.pallas_call(
+    held_core = lax.ppermute(held, AXIS, core_pairs)
+    held_cross = lax.ppermute(held, AXIS, cross_pairs)
+    held, held_core, held_cross = [v.reshape(8, 2, 64, 128) for v in (held, held_core, held_cross)]
+    xu, xs, pre, wf_skip, spread, wi, wg = pl.pallas_call(
         edge_kernel,
         out_shape=(
             inside((1152, 1024)),
+            inside((384, 1024)),
             inside((256, 1024), F32),
             inside((192, 576)),
+            inside((256, 512)),
+            inside((384, 576)),
             inside((128, 512)),
         ),
-        in_specs=[VMEM] * 4 + [FAR] * 3,
-        out_specs=(VMEM,) * 4,
-        scratch_shapes=[pltpu.VMEM((192, 576), BF16), pltpu.SemaphoreType.DMA((4,))],
+        in_specs=[SMEM] + [VMEM] * 6 + [FAR] * 6,
+        out_specs=(VMEM,) * 7,
+        scratch_shapes=[
+            pltpu.VMEM((128, 1536), BF16),
+            pltpu.VMEM((192, 576), BF16),
+            pltpu.SemaphoreType.DMA((7,)),
+        ],
         compiler_params=room(16),
         cost_estimate=pl.CostEstimate(flops=2990000000, bytes_accessed=1000000, transcendentals=0),
         name="edges",
-    )(near(edge_before), near(edge_after), w_up, near(xu), far(wf_up), far(wf_skip), far(wg))
+    )(
+        index,
+        *(near(v) for v in (edge_core, edge_cross)),
+        w_up,
+        *(near(v) for v in (xu, held, pick_skip)),
+        *(far(v) for v in (pick_up, wf_up, wf_skip, spread, wi, wg)),
+    )
 
     scale = 1.0 / math.sqrt(n * planes * cells)
-    rows = [v.reshape(8, 2, 64, 128) for v in (held, held_before, held_after)]
     act, gi, skip_part, keep, send = pl.pallas_call(
         functools.partial(main_kernel, scale),
         out_shape=(
@@ -427,17 +489,38 @@
             inside((1152, 128), F32),
             inside((1152, 128)),
         ),
-        in_specs=[SMEM] + [VMEM] * 12,
+        in_specs=[SMEM] + [VMEM] * 13,
         out_specs=(VMEM,) * 5,
         scratch_shapes=[
             pltpu.VMEM((1152, 1024), BF16),
             pltpu.VMEM((768, 1024), BF16),
             pltpu.VMEM((2304, 128), F32),
+            pltpu.SemaphoreType.DMA,
         ],
         compiler_params=room(24),
         cost_estimate=pl.CostEstimate(flops=8280000000, bytes_accessed=1000000, transcendentals=0),
         name="section",
-    )(index, *(near(v) for v in (*rows, flat, edge_before, edge_after, xu, pre, spread, wi, wf_skip, wg)))
+    )(
+        index,
+        *(
+            near(v)
+            for v in (
+                held_core,
+                held_cross,
+                flat,
+                edge_core,
+                edge_cross,
+                xs,
+                pick_skip,
+                xu,
+                pre,
+                spread,
+                wi,
+                wf_skip,
+                wg,
+            )
+        ),
+    )
     if positions != 64:
         skip_part = skip_part.reshape(16, 64, 2, 64).transpose(1, 2, 0, 3)
         skip_part = skip_part.reshape(64, 2, n, positions).transpose(2, 0, 1, 3)

time: 71.9 us -> 69 us (0.960)
  starting transfers between devices: 34.9 us -> 27.1 us
  waiting for transfers between devices: 16.8 us -> 19.9 us
  Pallas kernels: 13.4 us -> 15.1 us
    ppermute x4, starting transfers between devices: 8.66 us -> 1.79 us  [the longest x1 0.67 us: local(): held_cross = lax.ppermute(held, AXIS, cross_pairs)]
    all_to_all x1, waiting for transfers between devices: 2.81 us -> 5.75 us  [local(): held = lax.all_to_all(sent, AXIS, split_axis=0, concat_axis=0, tiled=True)]
    pallas_call x2, Pallas kernels: 4.39 us -> 6.73 us  [the longest x1 4.76 us: local(): pl.pallas_call(edge_kernel, out_shape=(inside((1152, 1024)), inside((384,...]
  transfers between devices with their start and end apart: 15 -> 15, of which waited for: 9 -> 8; matrix products, arithmetic and copies ran while one was open for 5% -> 5% of each run, Pallas kernels for 6% -> 10%
where the time goes in v4:
time: 69 us; the launch traced here: 68.5 us
  starting transfers between devices  27.1 us (39%)
  waiting for transfers between devices  19.9 us (29%)
  Pallas kernels  15.1 us (22%)
  local copies, waits for them, and re-layouts  5.38 us (8%)
  between operations  0.87 us (1%)
    ppermute x9, waiting for transfers between devices, swap(): return lax.ppermute(value, AXIS, [(i, i ^ bit) for i in range(n)])  14.1 us
    ppermute x9, starting transfers between devices, swap(): return lax.ppermute(value, AXIS, [(i, i ^ bit) for i in range(n)])  12.9 us
    all_to_all x1, starting transfers between devices, local(): held = lax.all_to_all(sent, AXIS, split_axis=0, concat_axis=0, tiled=True)  7.36 us
    pallas_call x1, Pallas kernels, local(): pl.pallas_call(functools.partial(main_kernel, scale), out_shape=(outside(...  6.61 us
    all_to_all x1, waiting for transfers between devices, local(): held = lax.all_to_all(sent, AXIS, split_axis=0, concat_axis=0, tiled=True)  5.75 us
    all_to_all x1, starting transfers between devices, local(): lax.all_to_all(skip_part, AXIS, split_axis=0, concat_axis=0, tiled=True)  5.07 us
    pallas_call x1, Pallas kernels, local(): pl.pallas_call(edge_kernel, out_shape=(inside((1152, 1024)), inside((384,...  4.76 us
    reshape x2, local copies, waits for them, and re-layouts, local(): sent = skip.reshape(64, n, 2 * positions).transpose(1, 0, 2)  2.15 us
  transfers between devices with their start and end apart: 15, of which 8 were waited for; matrix products, arithmetic and copies ran while one was open for 5% of the time, Pallas kernels for 10%

profile of v4, /device:TPU:0, one launch (start us, length us, event | category | flops | bytes accessed | tf_op | source)
XLA Modules:
  0.0 68.5 jit_solution(8875053651048547599)
XLA Ops:
  0.7 1.4 %reshape.43 = bf16[64,16,128]{2,1,0:T(8,128)(2,1)S(1)} reshape(bf16[64,32,64]{2,1,0:T(8,128)(2,1)} %param.6) | data formatting | bytes 524288 | tf_op jit(solution)/shard_map/reshape | solution.py:416
  2.0 0.8 %copy.15 = bf16[64,16,128]{2,0,1:T(8,128)(2,1)} copy(bf16[64,16,128]{2,1,0:T(8,128)(2,1)S(1)} %reshape.43) | data formatting | bytes 524288 | tf_op jit(solution)/shard_map/reshape | solution.py:416
  2.8 7.4 %all-to-all-start = ((bf16[16,64,128]{2,1,0:T(8,128)(2,1)}), bf16[16,64,128]{2,1,0:T(8,128)(2,1)S(1)}, u32[]{:S(2)}, u32[]{:S(2)}) async-start(bf16[16,64,128]{2,1,0:T(8,128)(2,1)} %bitcast.14), calls=%async_computation | async-start | bytes 524288 | tf_op jit(solution)/shard_map/all_to_all | solution.py:417
  10.2 1.0 %copy.13 = bf16[8,8,2,1024]{3,1,2,0:T(8,128)(2,1)S(1)} copy(bf16[8,8,2,1024]{3,2,1,0:T(2,128)(2,1)} %bitcast.23) | data formatting | bytes 524288
  12.5 2.0 %prepare.1 = (bf16[384,1024]{1,0:T(8,128)(2,1)S(1)}, bf16[256,512]{1,0:T(8,128)(2,1)}, bf16[192,576]{1,0:T(8,128)(2,1)}, bf16[192,576]{1,0:T(8,128)(2,1)}, bf16[...) custom-call(bf16[128,256]{1,0:T(8,128)(2,1)S(1)} %bitcast.19, ...), custom_call_target="tpu_custom_call" | custom-call | flops 1840000000 | bytes 1000000 | tf_op jit(solution)/shard_map/prepare/pallas_call | solution.py:431
  14.5 5.8 %all-to-all-done = bf16[16,64,128]{2,1,0:T(8,128)(2,1)S(1)} async-done(((bf16[16,64,128]{2,1,0:T(8,128)(2,1)}), bf16[16,64,128]{2,1,0:T(8,128)(2,1)S(1)}, u32[]{:S(2)}, u32[]{:S(2)}) %all-to-all-start) | async-done | bytes 262176 | tf_op jit(solution)/shard_map/all_to_all | solution.py:417
  20.9 4.8 %edges.1 = (bf16[1152,1024]{1,0:T(8,128)(2,1)S(1)}, bf16[384,1024]{1,0:T(8,128)(2,1)S(1)}, f32[256,1024]{1,0:T(8,128)S(1)}, bf16[192,576]{1,0:T(8,128)(2,1)S(1)}...) custom-call(s32[2]{0:T(128)S(1)} %pad_add_fusion.index_ref, ...), custom_call_target="tpu_custom_call" | custom-call | flops 2990000128 | bytes 1000000 | tf_op jit(solution)/shard_map/edges/pallas_call | solution.py:453
  25.7 6.6 %section.1 = (bf16[64,2048]{1,0:T(8,128)(2,1)}, bf16[128,256]{1,0:T(8,128)(2,1)}, bf16[16,64,128]{2,1,0:T(8,128)(2,1)}, f32[1152,128]{1,0:T(8,128)S(1)}, bf16[1152,128]{1,0:T(8,128)(2,1)S(1)}) custom-call(s32[2]{0:T(128)S(1)} %pad_add_fusion.index_ref, bf16[8,2,64,128]{3,2,1,0:T(8,128)(2,1)S(1)} %bitcast.20, bf16[8,2,64,128]{3,2,1,0:T(8,128)(2,1)S(1)} %bitcast.21, ...), custom_call_target="tpu_custom_call" | custom-call | flops 8280000000 | bytes 1000000 | tf_op jit(solution)/shard_map/section/pallas_call | solution.py:483
  32.4 3.3 %collective-permute-start.4 = (bf16[1152,128]{1,0:T(8,128)(2,1)S(1)}, bf16[1152,128]{1,0:T(8,128)(2,1)S(1)}, u32[]{:S(2)}, u32[]{:S(2)}) collective-permute-start(bf16[1152,128]{1,0:T(8,128)(2,1)S(1)} %get-tuple-element.56), channel_id=1, source_target_pairs={{0,1},{1,0},{2,3},{3,2},{4,5},{5,4},{6,7},{7,6},{8,9},{9,8},{10,11... | collective-permute-start | bytes 884744 | tf_op jit(solution)/shard_map/ppermute | solution.py:376
  35.6 5.1 %all-to-all-start.1 = ((bf16[16,64,128]{2,1,0:T(8,128)(2,1)}), bf16[16,64,128]{2,1,0:T(8,128)(2,1)S(1)}, u32[]{:S(2)}, u32[]{:S(2)}) async-start(bf16[16,64,128]{2,1,0:T(8,128)(2,1)} %get-tuple-element.57), calls=%async_computation.1 | async-start | bytes 524288 | tf_op jit(solution)/shard_map/all_to_all | solution.py:528
  40.8 2.0 %collective-permute-start.5 = (bf16[288,128]{1,0:T(8,128)(2,1)S(1)}, bf16[288,128]{1,0:T(8,128)(2,1)S(1)}, u32[]{:S(2)}, u32[]{:S(2)}) collective-permute-start(bf16[288,128]{1,0:T(8,128)(2,1)S(1)} %get-tuple-element.73), channel_id=1, source_target_pairs={{0,2},{1,3},{2,0},{3,1},{4,6},{5,7},{6,4},{7,5},{8,10},{9,11},{10,... | collective-permute-start | bytes 221192 | tf_op jit(solution)/shard_map/ppermute | solution.py:376
  42.8 1.5 %collective-permute-start.6 = (bf16[288,128]{1,0:T(8,128)(2,1)S(1)}, bf16[288,128]{1,0:T(8,128)(2,1)S(1)}, u32[]{:S(2)}, u32[]{:S(2)}) collective-permute-start(bf16[288,128]{1,0:T(8,128)(2,1)S(1)} %get-tuple-element.75), channel_id=1, source_target_pairs={{0,4},{1,5},{2,6},{3,7},{4,0},{5,1},{6,2},{7,3},{8,12},{9,13},{10,... | collective-permute-start | bytes 221192 | tf_op jit(solution)/shard_map/ppermute | solution.py:376
  44.4 2.8 %collective-permute-done.5 = bf16[288,128]{1,0:T(8,128)(2,1)S(1)} collective-permute-done((bf16[288,128]{1,0:T(8,128)(2,1)S(1)}, bf16[288,128]{1,0:T(8,128)(2,1)S(1)}, u32[]{:S(2)}, u32[]{:S(2)}) %collective-permute-start.5) | collective-permute-done | bytes 73760 | tf_op jit(solution)/shard_map/ppermute | solution.py:376
  47.2 2.6 %collective-permute-done.6 = bf16[288,128]{1,0:T(8,128)(2,1)S(1)} collective-permute-done((bf16[288,128]{1,0:T(8,128)(2,1)S(1)}, bf16[288,128]{1,0:T(8,128)(2,1)S(1)}, u32[]{:S(2)}, u32[]{:S(2)}) %collective-permute-start.6) | collective-permute-done | bytes 73760 | tf_op jit(solution)/shard_map/ppermute | solution.py:376
  49.8 2.3 %collective-permute-done.7 = bf16[288,128]{1,0:T(8,128)(2,1)S(1)} collective-permute-done((bf16[288,128]{1,0:T(8,128)(2,1)S(1)}, bf16[288,128]{1,0:T(8,128)(2,1)S(1)}, u32[]{:S(2)}, u32[]{:S(2)}) %collective-permute-start.7) | collective-permute-done | bytes 73760 | tf_op jit(solution)/shard_map/ppermute | solution.py:376
  52.1 2.4 %collective-permute-start.8 = (bf16[288,128]{1,0:T(8,128)(2,1)S(1)}, bf16[288,128]{1,0:T(8,128)(2,1)S(1)}, u32[]{:S(2)}, u32[]{:S(2)}) collective-permute-start(bf16[288,128]{1,0:T(8,128)(2,1)S(1)} %fusion.1), channel_id=1, source_target_pairs={{0,8},{1,9},{2,10},{3,11},{4,12},{5,13},{6,14},{7,15},{8,0},{9,1},... | collective-permute-start | bytes 221192 | tf_op jit(solution)/shard_map/ppermute | solution.py:376
  54.6 3.9 %collective-permute-done.8 = bf16[288,128]{1,0:T(8,128)(2,1)S(1)} collective-permute-done((bf16[288,128]{1,0:T(8,128)(2,1)S(1)}, bf16[288,128]{1,0:T(8,128)(2,1)S(1)}, u32[]{:S(2)}, u32[]{:S(2)}) %collective-permute-start.8) | collective-permute-done | bytes 73760 | tf_op jit(solution)/shard_map/ppermute | solution.py:376
  58.6 2.2 %collective-permute-start.11 = (bf16[288,128]{1,0:T(8,128)(2,1)S(1)}, bf16[288,128]{1,0:T(8,128)(2,1)S(1)}, u32[]{:S(2)}, u32[]{:S(2)}) collective-permute-start(bf16[288,128]{1,0:T(8,128)(2,1)S(1)} %add_convert_fusion), channel_id=1, source_target_pairs={{0,6},{1,7},{2,4},{3,5},{4,2},{5,3},{6,0},{7,1},{8,14},{9,15},{10,... | collective-permute-start | bytes 221192 | tf_op jit(solution)/shard_map/ppermute | solution.py:376
  60.8 1.3 %collective-permute-start.9 = (bf16[288,128]{1,0:T(8,128)(2,1)S(1)}, bf16[288,128]{1,0:T(8,128)(2,1)S(1)}, u32[]{:S(2)}, u32[]{:S(2)}) collective-permute-start(bf16[288,128]{1,0:T(8,128)(2,1)S(1)} %add_convert_fusion), channel_id=1, source_target_pairs={{0,2},{1,3},{2,0},{3,1},{4,6},{5,7},{6,4},{7,5},{8,10},{9,11},{10,... | collective-permute-start | bytes 221192 | tf_op jit(solution)/shard_map/ppermute | solution.py:376
  62.1 0.9 %reshape.49 = bf16[64,2,1024]{2,1,0:T(2,128)(2,1)} reshape(bf16[64,2048]{1,0:T(8,128)(2,1)S(1)} %copy-done.3) | data formatting | bytes 524288 | tf_op jit(solution)/shard_map/reshape | solution.py:532
  63.1 1.1 %reshape.51 = bf16[64,32,64]{2,1,0:T(8,128)(2,1)} reshape(bf16[64,16,128]{2,1,0:T(8,128)(2,1)S(1)} %copy.12) | data formatting | bytes 524288 | tf_op jit(solution)/shard_map/reshape | solution.py:534
  64.3 0.8 %collective-permute-done.9 = bf16[288,128]{1,0:T(8,128)(2,1)S(1)} collective-permute-done((bf16[288,128]{1,0:T(8,128)(2,1)S(1)}, bf16[288,128]{1,0:T(8,128)(2,1)S(1)}, u32[]{:S(2)}, u32[]{:S(2)}) %collective-permute-start.9) | collective-permute-done | bytes 73760 | tf_op jit(solution)/shard_map/ppermute | solution.py:376
  65.3 1.6 %collective-permute-done.12.other_ref = bf16[1152,128]{1,0:T(8,128)(2,1)S(1)} collective-permute-done((bf16[1152,128]{1,0:T(8,128)(2,1)S(1)}, bf16[1152,128]{1,0:T(8,128)(2,1)S(1)}, u32[]{:S(2)}, u32[]{:S(2)}) %collective-permute-start.12) | collective-permute-done | bytes 294944 | tf_op jit(solution)/shard_map/ppermute | solution.py:376
  66.8 1.7 %finish.1 = (f32[54,32,128]{2,1,0:T(8,128)}, f32[16,32,128]{2,1,0:T(8,128)}) custom-call(s32[2]{0:T(128)S(1)} %pad_add_fusion.index_ref, bf16[1152,128]{1,0:T(8,128)(2,1)S(1)} %constant_dynamic-update-slice_fusion.mine_ref, bf16[1152,128]{1,0:T(8,128)(2,1)S(1)} %collective-permute-done.12.other_ref), custom_call_target="tpu_custom_call" | custom-call | flops 1955000064 | bytes 1000000 | tf_op jit(solution)/shard_map/finish/pallas_call | solution.py:394
  (35 shorter events, 2.7 us)
Async XLA Ops:
  0.6 10.6 %copy-start = (bf16[128,1,256]{2,0,1:T(8,128)(2,1)S(1)}, bf16[128,1,256]{2,0,1:T(8,128)(2,1)}, u32[]{:S(2)}) copy-start(bf16[128,1,256]{2,0,1:T(8,128)(2,1)} %param.5) | copy-start | bytes 196612
  0.6 11.9 %copy-start.2 = (bf16[8,64,128]{2,1,0:T(8,128)(2,1)S(1)}, bf16[8,64,128]{2,1,0:T(8,128)(2,1)}, u32[]{:S(2)}) copy-start(bf16[8,64,128]{2,1,0:T(8,128)(2,1)} %wup_ref.3) | copy-start | bytes 393220
  0.7 11.9 %copy-start.1 = (bf16[27,64,128]{2,1,0:T(8,128)(2,1)S(1)}, bf16[27,64,128]{2,1,0:T(8,128)(2,1)}, u32[]{:S(2)}) copy-start(bf16[27,64,128]{2,1,0:T(8,128)(2,1)} %wc_ref.1) | copy-start | bytes 1327108
  2.8 17.4 %all-to-all-start = ((bf16[16,64,128]{2,1,0:T(8,128)(2,1)}), bf16[16,64,128]{2,1,0:T(8,128)(2,1)S(1)}, u32[]{:S(2)}, u32[]{:S(2)}) async-start(bf16[16,64,128]{2,1,0:T(8,128)(2,1)} %bitcast.14), calls=%async_computation | async-start | bytes 524288 | tf_op jit(solution)/shard_map/all_to_all | solution.py:417
  11.3 9.6 %collective-permute-start.2 = (bf16[128,768]{1,0:T(8,128)(2,1)S(1)}, bf16[128,768]{1,0:T(8,128)(2,1)S(1)}, u32[]{:S(2)}, u32[]{:S(2)}) collective-permute-start(bf16[128,768]{1,0:T(8,128)(2,1)S(1)} %get-tuple-element.81), channel_id=1, source_target_pairs={{0,1},{1,0},{2,3},{3,2},{4,5},{5,4},{6,7},{7,6},{8,9},{9,8},{10,11... | collective-permute-start | bytes 589832 | tf_op jit(solution)/shard_map/ppermute | solution.py:429
  11.8 9.2 %collective-permute-start.3 = (bf16[128,768]{1,0:T(8,128)(2,1)S(1)}, bf16[128,768]{1,0:T(8,128)(2,1)S(1)}, u32[]{:S(2)}, u32[]{:S(2)}) collective-permute-start(bf16[128,768]{1,0:T(8,128)(2,1)S(1)} %get-tuple-element.80), channel_id=1, source_target_pairs={{1,2},{2,1},{3,4},{4,3},{5,6},{6,5},{7,8},{8,7},{9,10},{10,9},{11,... | collective-permute-start | bytes 589832 | tf_op jit(solution)/shard_map/ppermute | solution.py:430
  20.2 5.5 %collective-permute-start = (bf16[16,64,128]{2,1,0:T(8,128)(2,1)S(1)}, bf16[16,64,128]{2,1,0:T(8,128)(2,1)S(1)}, u32[]{:S(2)}, u32[]{:S(2)}) collective-permute-start(bf16[16,64,128]{2,1,0:T(8,128)(2,1)S(1)} %all-to-all-done), channel_id=1, source_target_pairs={{0,1},{1,0},{2,3},{3,2},{4,5},{5,4},{6,7},{7,6},{8,9},{9,8},{10,11... | collective-permute-start | bytes 786440 | tf_op jit(solution)/shard_map/ppermute | solution.py:450
  20.2 5.5 %collective-permute-start.1 = (bf16[16,64,128]{2,1,0:T(8,128)(2,1)S(1)}, bf16[16,64,128]{2,1,0:T(8,128)(2,1)S(1)}, u32[]{:S(2)}, u32[]{:S(2)}) collective-permute-start(bf16[16,64,128]{2,1,0:T(8,128)(2,1)S(1)} %all-to-all-done), channel_id=1, source_target_pairs={{1,2},{2,1},{3,4},{4,3},{5,6},{6,5},{7,8},{8,7},{9,10},{10,9},{11,... | collective-permute-start | bytes 786440 | tf_op jit(solution)/shard_map/ppermute | solution.py:451
  32.3 29.7 %copy-start.3 = (bf16[64,2048]{1,0:T(8,128)(2,1)S(1)}, bf16[64,2048]{1,0:T(8,128)(2,1)}, u32[]{:S(2)}) copy-start(bf16[64,2048]{1,0:T(8,128)(2,1)} %get-tuple-element.59) | copy-start | bytes 786436
  32.4 8.3 %collective-permute-start.4 = (bf16[1152,128]{1,0:T(8,128)(2,1)S(1)}, bf16[1152,128]{1,0:T(8,128)(2,1)S(1)}, u32[]{:S(2)}, u32[]{:S(2)}) collective-permute-start(bf16[1152,128]{1,0:T(8,128)(2,1)S(1)} %get-tuple-element.56), channel_id=1, source_target_pairs={{0,1},{1,0},{2,3},{3,2},{4,5},{5,4},{6,7},{7,6},{8,9},{9,8},{10,11... | collective-permute-start | bytes 884744 | tf_op jit(solution)/shard_map/ppermute | solution.py:376
  35.6 16.5 %all-to-all-start.1 = ((bf16[16,64,128]{2,1,0:T(8,128)(2,1)}), bf16[16,64,128]{2,1,0:T(8,128)(2,1)S(1)}, u32[]{:S(2)}, u32[]{:S(2)}) async-start(bf16[16,64,128]{2,1,0:T(8,128)(2,1)} %get-tuple-element.57), calls=%async_computation.1 | async-start | bytes 524288 | tf_op jit(solution)/shard_map/all_to_all | solution.py:528
  40.8 6.4 %collective-permute-start.5 = (bf16[288,128]{1,0:T(8,128)(2,1)S(1)}, bf16[288,128]{1,0:T(8,128)(2,1)S(1)}, u32[]{:S(2)}, u32[]{:S(2)}) collective-permute-start(bf16[288,128]{1,0:T(8,128)(2,1)S(1)} %get-tuple-element.73), channel_id=1, source_target_pairs={{0,2},{1,3},{2,0},{3,1},{4,6},{5,7},{6,4},{7,5},{8,10},{9,11},{10,... | collective-permute-start | bytes 221192 | tf_op jit(solution)/shard_map/ppermute | solution.py:376
  42.8 7.0 %collective-permute-start.6 = (bf16[288,128]{1,0:T(8,128)(2,1)S(1)}, bf16[288,128]{1,0:T(8,128)(2,1)S(1)}, u32[]{:S(2)}, u32[]{:S(2)}) collective-permute-start(bf16[288,128]{1,0:T(8,128)(2,1)S(1)} %get-tuple-element.75), channel_id=1, source_target_pairs={{0,4},{1,5},{2,6},{3,7},{4,0},{5,1},{6,2},{7,3},{8,12},{9,13},{10,... | collective-permute-start | bytes 221192 | tf_op jit(solution)/shard_map/ppermute | solution.py:376
  44.3 7.8 %collective-permute-start.7 = (bf16[288,128]{1,0:T(8,128)(2,1)S(1)}, bf16[288,128]{1,0:T(8,128)(2,1)S(1)}, u32[]{:S(2)}, u32[]{:S(2)}) collective-permute-start(bf16[288,128]{1,0:T(8,128)(2,1)S(1)} %get-tuple-element.74), channel_id=1, source_target_pairs={{0,6},{1,7},{2,4},{3,5},{4,2},{5,3},{6,0},{7,1},{8,14},{9,15},{10,... | collective-permute-start | bytes 221192 | tf_op jit(solution)/shard_map/ppermute | solution.py:376
  52.1 6.4 %collective-permute-start.8 = (bf16[288,128]{1,0:T(8,128)(2,1)S(1)}, bf16[288,128]{1,0:T(8,128)(2,1)S(1)}, u32[]{:S(2)}, u32[]{:S(2)}) collective-permute-start(bf16[288,128]{1,0:T(8,128)(2,1)S(1)} %fusion.1), channel_id=1, source_target_pairs={{0,8},{1,9},{2,10},{3,11},{4,12},{5,13},{6,14},{7,15},{8,0},{9,1},... | collective-permute-start | bytes 221192 | tf_op jit(solution)/shard_map/ppermute | solution.py:376
  58.5 5.7 %collective-permute-start.10 = (bf16[288,128]{1,0:T(8,128)(2,1)S(1)}, bf16[288,128]{1,0:T(8,128)(2,1)S(1)}, u32[]{:S(2)}, u32[]{:S(2)}) collective-permute-start(bf16[288,128]{1,0:T(8,128)(2,1)S(1)} %add_convert_fusion), channel_id=1, source_target_pairs={{0,4},{1,5},{2,6},{3,7},{4,0},{5,1},{6,2},{7,3},{8,12},{9,13},{10,... | collective-permute-start | bytes 221192 | tf_op jit(solution)/shard_map/ppermute | solution.py:376
  58.6 5.7 %collective-permute-start.11 = (bf16[288,128]{1,0:T(8,128)(2,1)S(1)}, bf16[288,128]{1,0:T(8,128)(2,1)S(1)}, u32[]{:S(2)}, u32[]{:S(2)}) collective-permute-start(bf16[288,128]{1,0:T(8,128)(2,1)S(1)} %add_convert_fusion), channel_id=1, source_target_pairs={{0,6},{1,7},{2,4},{3,5},{4,2},{5,3},{6,0},{7,1},{8,14},{9,15},{10,... | collective-permute-start | bytes 221192 | tf_op jit(solution)/shard_map/ppermute | solution.py:376
  60.8 4.4 %collective-permute-start.9 = (bf16[288,128]{1,0:T(8,128)(2,1)S(1)}, bf16[288,128]{1,0:T(8,128)(2,1)S(1)}, u32[]{:S(2)}, u32[]{:S(2)}) collective-permute-start(bf16[288,128]{1,0:T(8,128)(2,1)S(1)} %add_convert_fusion), channel_id=1, source_target_pairs={{0,2},{1,3},{2,0},{3,1},{4,6},{5,7},{6,4},{7,5},{8,10},{9,11},{10,... | collective-permute-start | bytes 221192 | tf_op jit(solution)/shard_map/ppermute | solution.py:376
  65.2 1.6 %collective-permute-start.12 = (bf16[1152,128]{1,0:T(8,128)(2,1)S(1)}, bf16[1152,128]{1,0:T(8,128)(2,1)S(1)}, u32[]{:S(2)}, u32[]{:S(2)}) collective-permute-start(bf16[1152,128]{1,0:T(8,128)(2,1)S(1)} %constant_dynamic-update-slice_fusion.mine_ref), channel_id=1, source_target_pairs={{0,1},{1,0},{2,3},{3,2},{4,5},{5,4},{6,7},{7,6},{8,9},{9,8},{10,11... | collective-permute-start | bytes 884744 | tf_op jit(solution)/shard_map/ppermute | solution.py:376

commit v5 on v4

--- a/solution.py
+++ b/solution.py
@@ -196,18 +196,24 @@
     wi_ref,
     wf_ref,
     wg_ref,
-    act_ref,
-    gi_ref,
-    skip_ref,
+    far_act_ref,
+    far_gi_ref,
+    far_skip_ref,
     keep_ref,
     send_ref,
     xs_ref,
     gs_ref,
     gw_ref,
-    sem,
+    act_ref,
+    gi_ref,
+    skip_ref,
+    sems,
 ):
-    copy = pltpu.make_async_copy(own_ref, xs_ref.at[384:768], sem)
+    copy = pltpu.make_async_copy(own_ref, xs_ref.at[384:768], sems.at[0])
     copy.start()
+    act_copy = pltpu.make_async_copy(act_ref, far_act_ref, sems.at[1])
+    skip_copy = pltpu.make_async_copy(skip_ref, far_skip_ref, sems.at[2])
+    gi_copy = pltpu.make_async_copy(gi_ref, far_gi_ref, sems.at[3])
     core = index_ref[0]
     quad = index_ref[1]
     before, after = in_order(core, near_ref, far_ref)
@@ -243,31 +249,7 @@
                     h * 64 : (h + 1) * 64, (tap >> 1) * W : (tap >> 1) * W + W
                 ]
 
-    copy.wait()
-    zero = jnp.zeros((64, W), BF16)
-    grads = []
-    for j in (1, 2):
-        grad = gs_ref[j * 192 + 64 : j * 192 + 128, :]
-        low = jnp.concatenate([grad[:, W:], zero], axis=1)
-        high = jnp.concatenate([zero, grad[:, :-W]], axis=1)
-        grads.append(jnp.concatenate([low, grad, high], axis=0))
-    for a in range(3):
-        total = None
-        for j in (1, 2):
-            pieces = []
-            for tap in range(3):
-                at = (j + a) * 192 + tap * 64
-                pieces += [xu_ref[at : at + 64, :], xs_ref[at : at + 64, :]]
-            term = lax.dot_general(
-                grads[j - 1], jnp.concatenate(pieces, axis=0), NT, preferred_element_type=F32
-            )
-            total = term if total is None else total + term
-        total = total * scale
-        for b in range(3):
-            for tap in range(3):
-                at = (9 * a + 3 * b + tap) * 64
-                gw_ref[at : at + 64, :] = total[b * 64 : (b + 1) * 64, tap * W : (tap + 1) * W]
-
+    act_copy.start()
     lower = lax.broadcasted_iota(jnp.int32, (64, W), 1) < 64
     ups = []
     skips = []
@@ -282,6 +264,7 @@
         skip_ref[2 * h] = jnp.where(lower, first, pltpu.roll(second, 64, 1)).astype(BF16)
         skip_ref[2 * h + 1] = jnp.where(lower, pltpu.roll(first, 64, 1), second).astype(BF16)
 
+    skip_copy.start()
     tiles = []
     for h in range(4):
         tiles.append(
@@ -312,6 +295,34 @@
         axis=0,
     )
     gi_ref[...] = mm(wg_ref[...], operand).astype(BF16)
+    gi_copy.start()
+
+    copy.wait()
+    zero = jnp.zeros((64, W), BF16)
+    grads = []
+    for j in (1, 2):
+        grad = gs_ref[j * 192 + 64 : j * 192 + 128, :]
+        low = jnp.concatenate([grad[:, W:], zero], axis=1)
+        high = jnp.concatenate([zero, grad[:, :-W]], axis=1)
+        grads.append(jnp.concatenate([low, grad, high], axis=0))
+    total = None
+    for j in (1, 2):
+        pieces = []
+        for e in range(j, j + 3):
+            for tap in range(3):
+                at = e * 192 + tap * 64
+                pieces += [xu_ref[at : at + 64, :], xs_ref[at : at + 64, :]]
+        term = lax.dot_general(
+            jnp.concatenate(pieces, axis=0), grads[j - 1], NT, preferred_element_type=F32
+        )
+        total = term if total is None else total + term
+    total = (total * scale).T
+    for a in range(3):
+        for b in range(3):
+            for tap in range(3):
+                at = (9 * a + 3 * b + tap) * 64
+                column = (3 * a + tap) * W
+                gw_ref[at : at + 64, :] = total[b * 64 : (b + 1) * 64, column : column + W]
 
     for k in range(4):
         row = jnp.bitwise_xor(quad, k) * 288
@@ -319,27 +330,38 @@
         other = pl.multiple_of((1 - core) * 1152 + row, 32)
         keep_ref[k * 288 : (k + 1) * 288, :] = gw_ref[pl.ds(mine, 288), :]
         send_ref[k * 288 : (k + 1) * 288, :] = gw_ref[pl.ds(other, 288), :].astype(BF16)
-
-
-def finish_kernel(index_ref, mine_ref, other_ref, conv_ref, up_ref):
-    core = index_ref[0]
-    quad = index_ref[1]
-    for side, ref in ((core, mine_ref), (1 - core, other_ref)):
+    for done in (act_copy, skip_copy, gi_copy):
+        done.wait()
+
+
+def finish_kernel(mine, index_ref, value_ref, *refs):
+    conv_ref, up_ref, stage_ref, sems = refs[-4:]
+    side = index_ref[0] if mine else 1 - index_ref[0]
+
+    def each(act):
         for k in range(4):
-            piece = 4 * side + jnp.bitwise_xor(quad, k)
-            rows = slice(k * 288, (k + 1) * 288)
+            piece = 4 * side + jnp.bitwise_xor(index_ref[1], k)
+            rows = slice(k * 9, k * 9 + 9)
 
             @pl.when(piece < 6)
             def _():
-                conv_ref[pl.ds(piece * 9, 9)] = ref[rows, :].astype(F32).reshape(9, 32, 128)
+                dst = conv_ref.at[pl.ds(piece * 9, 9)]
+                act(k, pltpu.make_async_copy(stage_ref.at[rows], dst, sems.at[k]))
 
             @pl.when(piece == 6)
             def _():
-                up_ref[0:9] = ref[rows, :].astype(F32).reshape(9, 32, 128)
+                act(k, pltpu.make_async_copy(stage_ref.at[rows], up_ref.at[0:9], sems.at[k]))
 
             @pl.when(piece == 7)
             def _():
-                up_ref[9:16] = ref[k * 288 : k * 288 + 224, :].astype(F32).reshape(7, 32, 128)
+                src = stage_ref.at[k * 9 : k * 9 + 7]
+                act(k, pltpu.make_async_copy(src, up_ref.at[9:16], sems.at[k]))
+
+    for k in range(4):
+        rows = slice(k * 288, (k + 1) * 288)
+        stage_ref[k * 9 : k * 9 + 9] = value_ref[rows, :].astype(F32).reshape(9, 32, 128)
+    each(lambda k, copy: copy.start())
+    each(lambda k, copy: copy.wait())
 
 
 def room(mebibytes):
@@ -391,15 +413,20 @@
     pieces, others = lax.optimization_barrier((pieces, finish_others(back)))
     mine = jnp.concatenate(pieces, axis=0)
     other = swap(mine, 1)
-    conv, up = pl.pallas_call(
-        finish_kernel,
-        out_shape=(like((54, 32, 128), F32), like((16, 32, 128), F32)),
-        in_specs=[SMEM, VMEM, VMEM],
-        out_specs=(VMEM, VMEM),
-        compiler_params=room(6),
-        cost_estimate=pl.CostEstimate(flops=1955000000, bytes_accessed=1000000, transcendentals=0),
-        name="finish",
-    )(index, mine, other)
+    sums = ()
+    for first, value in ((True, mine), (False, other)):
+        sums = pl.pallas_call(
+            functools.partial(finish_kernel, first),
+            out_shape=(outside((54, 32, 128), F32), outside((16, 32, 128), F32)),
+            in_specs=[SMEM, VMEM] + [FAR] * len(sums),
+            out_specs=(FAR, FAR),
+            scratch_shapes=[pltpu.VMEM((36, 32, 128), F32), pltpu.SemaphoreType.DMA((4,))],
+            input_output_aliases={} if first else {2: 0, 3: 1},
+            compiler_params=room(6),
+            cost_estimate=pl.CostEstimate(flops=1200000000, bytes_accessed=1000000, transcendentals=0),
+            name="finish",
+        )(index, value, *sums)
+    conv, up = sums
     return conv.reshape(27, 64, 128), up.reshape(8, 64, 128), others
 
 
@@ -490,12 +517,15 @@
             inside((1152, 128)),
         ),
         in_specs=[SMEM] + [VMEM] * 13,
-        out_specs=(VMEM,) * 5,
+        out_specs=(FAR,) * 3 + (VMEM,) * 2,
         scratch_shapes=[
             pltpu.VMEM((1152, 1024), BF16),
             pltpu.VMEM((768, 1024), BF16),
             pltpu.VMEM((2304, 128), F32),
-            pltpu.SemaphoreType.DMA,
+            pltpu.VMEM((64, 2048), BF16),
+            pltpu.VMEM((128, 256), BF16),
+            pltpu.VMEM((16, 64, 128), BF16),
+            pltpu.SemaphoreType.DMA((4,)),
         ],
         compiler_params=room(24),
         cost_estimate=pl.CostEstimate(flops=8280000000, bytes_accessed=1000000, transcendentals=0),

time: 69 us -> 67.9 us (0.984)
  waiting for transfers between devices: 19.9 us -> 18.5 us
    ppermute x9, waiting for transfers between devices: 14.1 us -> 12.7 us  [swap(): return lax.ppermute(value, AXIS, [(i, i ^ bit) for i in range(n)])]
    pallas_call x1 -> x2, Pallas kernels: 1.72 us -> 2.83 us  [reduce_weights(): pl.pallas_call(functools.partial(finish_kernel, first), out_shape=(outsid...]
    pallas_call x1, Pallas kernels: 6.61 us -> 5.85 us  [local(): pl.pallas_call(functools.partial(main_kernel, scale), out_shape=(outside(...]
  transfers between devices with their start and end apart: 15 -> 15, of which waited for: 8 -> 8; matrix products, arithmetic and copies ran while one was open for 5% -> 5% of each run, Pallas kernels for 10% -> 12%
where the time goes in v5:
time: 67.9 us; the launch traced here: 67.5 us
  starting transfers between devices  27.1 us (40%)
  waiting for transfers between devices  18.5 us (27%)
  Pallas kernels  15.4 us (23%)
  local copies, waits for them, and re-layouts  5.38 us (8%)
  between operations  0.88 us (1%)
    ppermute x9, starting transfers between devices, swap(): return lax.ppermute(value, AXIS, [(i, i ^ bit) for i in range(n)])  12.8 us
    ppermute x9, waiting for transfers between devices, swap(): return lax.ppermute(value, AXIS, [(i, i ^ bit) for i in range(n)])  12.7 us
    all_to_all x1, starting transfers between devices, local(): held = lax.all_to_all(sent, AXIS, split_axis=0, concat_axis=0, tiled=True)  7.36 us
    pallas_call x1, Pallas kernels, local(): pl.pallas_call(functools.partial(main_kernel, scale), out_shape=(outside(...  5.85 us
    all_to_all x1, waiting for transfers between devices, local(): held = lax.all_to_all(sent, AXIS, split_axis=0, concat_axis=0, tiled=True)  5.75 us
    all_to_all x1, starting transfers between devices, local(): lax.all_to_all(skip_part, AXIS, split_axis=0, concat_axis=0, tiled=True)  5.07 us
    pallas_call x1, Pallas kernels, local(): pl.pallas_call(edge_kernel, out_shape=(inside((1152, 1024)), inside((384,...  4.76 us
    pallas_call x2, Pallas kernels, reduce_weights(): pl.pallas_call(functools.partial(finish_kernel, first), out_shape=(outsid...  2.83 us
  transfers between devices with their start and end apart: 15, of which 8 were waited for; matrix products, arithmetic and copies ran while one was open for 5% of the time, Pallas kernels for 12%

profile of v5, /device:TPU:0, one launch (start us, length us, event | category | flops | bytes accessed | tf_op | source)
XLA Modules:
  0.0 67.5 jit_solution(13056992901507586889)
XLA Ops:
  0.7 1.4 %reshape.43 = bf16[64,16,128]{2,1,0:T(8,128)(2,1)S(1)} reshape(bf16[64,32,64]{2,1,0:T(8,128)(2,1)} %param.6) | data formatting | bytes 524288 | tf_op jit(solution)/shard_map/reshape | solution.py:443
  2.0 0.8 %copy.17 = bf16[64,16,128]{2,0,1:T(8,128)(2,1)} copy(bf16[64,16,128]{2,1,0:T(8,128)(2,1)S(1)} %reshape.43) | data formatting | bytes 524288 | tf_op jit(solution)/shard_map/reshape | solution.py:443
  2.8 7.4 %all-to-all-start = ((bf16[16,64,128]{2,1,0:T(8,128)(2,1)}), bf16[16,64,128]{2,1,0:T(8,128)(2,1)S(1)}, u32[]{:S(2)}, u32[]{:S(2)}) async-start(bf16[16,64,128]{2,1,0:T(8,128)(2,1)} %bitcast.14), calls=%async_computation | async-start | bytes 524288 | tf_op jit(solution)/shard_map/all_to_all | solution.py:444
  10.2 1.0 %copy.15 = bf16[8,8,2,1024]{3,1,2,0:T(8,128)(2,1)S(1)} copy(bf16[8,8,2,1024]{3,2,1,0:T(2,128)(2,1)} %bitcast.23) | data formatting | bytes 524288
  12.5 2.0 %prepare.1 = (bf16[384,1024]{1,0:T(8,128)(2,1)S(1)}, bf16[256,512]{1,0:T(8,128)(2,1)}, bf16[192,576]{1,0:T(8,128)(2,1)}, bf16[192,576]{1,0:T(8,128)(2,1)}, bf16[...) custom-call(bf16[128,256]{1,0:T(8,128)(2,1)S(1)} %bitcast.19, ...), custom_call_target="tpu_custom_call" | custom-call | flops 1840000000 | bytes 1000000 | tf_op jit(solution)/shard_map/prepare/pallas_call | solution.py:458
  14.5 5.7 %all-to-all-done = bf16[16,64,128]{2,1,0:T(8,128)(2,1)S(1)} async-done(((bf16[16,64,128]{2,1,0:T(8,128)(2,1)}), bf16[16,64,128]{2,1,0:T(8,128)(2,1)S(1)}, u32[]{:S(2)}, u32[]{:S(2)}) %all-to-all-start) | async-done | bytes 262176 | tf_op jit(solution)/shard_map/all_to_all | solution.py:444
  20.9 4.8 %edges.1 = (bf16[1152,1024]{1,0:T(8,128)(2,1)S(1)}, bf16[384,1024]{1,0:T(8,128)(2,1)S(1)}, f32[256,1024]{1,0:T(8,128)S(1)}, bf16[192,576]{1,0:T(8,128)(2,1)S(1)}...) custom-call(s32[2]{0:T(128)S(1)} %pad_add_fusion.index_ref, ...), custom_call_target="tpu_custom_call" | custom-call | flops 2990000128 | bytes 1000000 | tf_op jit(solution)/shard_map/edges/pallas_call | solution.py:480
  25.7 5.8 %section.1 = (bf16[64,2048]{1,0:T(8,128)(2,1)}, bf16[128,256]{1,0:T(8,128)(2,1)}, bf16[16,64,128]{2,1,0:T(8,128)(2,1)}, f32[1152,128]{1,0:T(8,128)S(1)}, bf16[1152,128]{1,0:T(8,128)(2,1)S(1)}) custom-call(s32[2]{0:T(128)S(1)} %pad_add_fusion.index_ref, bf16[8,2,64,128]{3,2,1,0:T(8,128)(2,1)S(1)} %bitcast.20, bf16[8,2,64,128]{3,2,1,0:T(8,128)(2,1)S(1)} %bitcast.21, ...), custom_call_target="tpu_custom_call" | custom-call | flops 8280000000 | bytes 1000000 | tf_op jit(solution)/shard_map/section/pallas_call | solution.py:510
  31.6 3.2 %collective-permute-start.4 = (bf16[1152,128]{1,0:T(8,128)(2,1)S(1)}, bf16[1152,128]{1,0:T(8,128)(2,1)S(1)}, u32[]{:S(2)}, u32[]{:S(2)}) collective-permute-start(bf16[1152,128]{1,0:T(8,128)(2,1)S(1)} %get-tuple-element.58), channel_id=1, source_target_pairs={{0,1},{1,0},{2,3},{3,2},{4,5},{5,4},{6,7},{7,6},{8,9},{9,8},{10,11... | collective-permute-start | bytes 884744 | tf_op jit(solution)/shard_map/ppermute | solution.py:398
  34.8 5.1 %all-to-all-start.1 = ((bf16[16,64,128]{2,1,0:T(8,128)(2,1)}), bf16[16,64,128]{2,1,0:T(8,128)(2,1)S(1)}, u32[]{:S(2)}, u32[]{:S(2)}) async-start(bf16[16,64,128]{2,1,0:T(8,128)(2,1)} %get-tuple-element.59), calls=%async_computation.1 | async-start | bytes 524288 | tf_op jit(solution)/shard_map/all_to_all | solution.py:558
  40.0 2.0 %collective-permute-start.5 = (bf16[288,128]{1,0:T(8,128)(2,1)S(1)}, bf16[288,128]{1,0:T(8,128)(2,1)S(1)}, u32[]{:S(2)}, u32[]{:S(2)}) collective-permute-start(bf16[288,128]{1,0:T(8,128)(2,1)S(1)} %get-tuple-element.77), channel_id=1, source_target_pairs={{0,2},{1,3},{2,0},{3,1},{4,6},{5,7},{6,4},{7,5},{8,10},{9,11},{10,... | collective-permute-start | bytes 221192 | tf_op jit(solution)/shard_map/ppermute | solution.py:398
  42.0 1.5 %collective-permute-start.6 = (bf16[288,128]{1,0:T(8,128)(2,1)S(1)}, bf16[288,128]{1,0:T(8,128)(2,1)S(1)}, u32[]{:S(2)}, u32[]{:S(2)}) collective-permute-start(bf16[288,128]{1,0:T(8,128)(2,1)S(1)} %get-tuple-element.79), channel_id=1, source_target_pairs={{0,4},{1,5},{2,6},{3,7},{4,0},{5,1},{6,2},{7,3},{8,12},{9,13},{10,... | collective-permute-start | bytes 221192 | tf_op jit(solution)/shard_map/ppermute | solution.py:398
  43.6 2.8 %collective-permute-done.5 = bf16[288,128]{1,0:T(8,128)(2,1)S(1)} collective-permute-done((bf16[288,128]{1,0:T(8,128)(2,1)S(1)}, bf16[288,128]{1,0:T(8,128)(2,1)S(1)}, u32[]{:S(2)}, u32[]{:S(2)}) %collective-permute-start.5) | collective-permute-done | bytes 73760 | tf_op jit(solution)/shard_map/ppermute | solution.py:398
  46.4 2.6 %collective-permute-done.6 = bf16[288,128]{1,0:T(8,128)(2,1)S(1)} collective-permute-done((bf16[288,128]{1,0:T(8,128)(2,1)S(1)}, bf16[288,128]{1,0:T(8,128)(2,1)S(1)}, u32[]{:S(2)}, u32[]{:S(2)}) %collective-permute-start.6) | collective-permute-done | bytes 73760 | tf_op jit(solution)/shard_map/ppermute | solution.py:398
  49.0 2.3 %collective-permute-done.7 = bf16[288,128]{1,0:T(8,128)(2,1)S(1)} collective-permute-done((bf16[288,128]{1,0:T(8,128)(2,1)S(1)}, bf16[288,128]{1,0:T(8,128)(2,1)S(1)}, u32[]{:S(2)}, u32[]{:S(2)}) %collective-permute-start.7) | collective-permute-done | bytes 73760 | tf_op jit(solution)/shard_map/ppermute | solution.py:398
  51.4 2.4 %collective-permute-start.8 = (bf16[288,128]{1,0:T(8,128)(2,1)S(1)}, bf16[288,128]{1,0:T(8,128)(2,1)S(1)}, u32[]{:S(2)}, u32[]{:S(2)}) collective-permute-start(bf16[288,128]{1,0:T(8,128)(2,1)S(1)} %fusion.1), channel_id=1, source_target_pairs={{0,8},{1,9},{2,10},{3,11},{4,12},{5,13},{6,14},{7,15},{8,0},{9,1},... | collective-permute-start | bytes 221192 | tf_op jit(solution)/shard_map/ppermute | solution.py:398
  53.8 3.9 %collective-permute-done.8 = bf16[288,128]{1,0:T(8,128)(2,1)S(1)} collective-permute-done((bf16[288,128]{1,0:T(8,128)(2,1)S(1)}, bf16[288,128]{1,0:T(8,128)(2,1)S(1)}, u32[]{:S(2)}, u32[]{:S(2)}) %collective-permute-start.8) | collective-permute-done | bytes 73760 | tf_op jit(solution)/shard_map/ppermute | solution.py:398
  57.8 2.2 %collective-permute-start.11 = (bf16[288,128]{1,0:T(8,128)(2,1)S(1)}, bf16[288,128]{1,0:T(8,128)(2,1)S(1)}, u32[]{:S(2)}, u32[]{:S(2)}) collective-permute-start(bf16[288,128]{1,0:T(8,128)(2,1)S(1)} %add_convert_fusion), channel_id=1, source_target_pairs={{0,6},{1,7},{2,4},{3,5},{4,2},{5,3},{6,0},{7,1},{8,14},{9,15},{10,... | collective-permute-start | bytes 221192 | tf_op jit(solution)/shard_map/ppermute | solution.py:398
  60.0 1.3 %collective-permute-start.9 = (bf16[288,128]{1,0:T(8,128)(2,1)S(1)}, bf16[288,128]{1,0:T(8,128)(2,1)S(1)}, u32[]{:S(2)}, u32[]{:S(2)}) collective-permute-start(bf16[288,128]{1,0:T(8,128)(2,1)S(1)} %add_convert_fusion), channel_id=1, source_target_pairs={{0,2},{1,3},{2,0},{3,1},{4,6},{5,7},{6,4},{7,5},{8,10},{9,11},{10,... | collective-permute-start | bytes 221192 | tf_op jit(solution)/shard_map/ppermute | solution.py:398
  61.3 0.9 %reshape.49 = bf16[64,2,1024]{2,1,0:T(2,128)(2,1)} reshape(bf16[64,2048]{1,0:T(8,128)(2,1)S(1)} %copy-done.3) | data formatting | bytes 524288 | tf_op jit(solution)/shard_map/reshape | solution.py:562
  62.4 1.1 %reshape.51 = bf16[64,32,64]{2,1,0:T(8,128)(2,1)} reshape(bf16[64,16,128]{2,1,0:T(8,128)(2,1)S(1)} %copy.14) | data formatting | bytes 524288 | tf_op jit(solution)/shard_map/reshape | solution.py:564
  63.5 0.8 %collective-permute-done.9 = bf16[288,128]{1,0:T(8,128)(2,1)S(1)} collective-permute-done((bf16[288,128]{1,0:T(8,128)(2,1)S(1)}, bf16[288,128]{1,0:T(8,128)(2,1)S(1)}, u32[]{:S(2)}, u32[]{:S(2)}) %collective-permute-start.9) | collective-permute-done | bytes 73760 | tf_op jit(solution)/shard_map/ppermute | solution.py:398
  64.5 1.4 %finish.2 = (f32[54,32,128]{2,1,0:T(8,128)}, f32[16,32,128]{2,1,0:T(8,128)}) custom-call(s32[2]{0:T(128)S(1)} %pad_add_fusion.index_ref, bf16[1152,128]{1,0:T(8,128)(2,1)S(1)} %constant_dynamic-update-slice_fusion.value_ref), custom_call_target="tpu_custom_call" | custom-call | flops 1200000000 | bytes 1000000 | tf_op jit(solution)/shard_map/finish/pallas_call | solution.py:418
  66.1 1.4 %finish.3 = (f32[54,32,128]{2,1,0:T(8,128)}, f32[16,32,128]{2,1,0:T(8,128)}) custom-call(s32[2]{0:T(128)S(1)} %pad_add_fusion.index_ref, bf16[1152,128]{1,0:T(8,128)(2,1)S(1)} %collective-permute-done.12.value_ref, f32[54,32,128]{2,1,0:T(8,128)} %get-tuple-element.71.refs_0_, ...), custom_call_target="tpu_custom_call", output_to_operand_aliasing={{0}: (2, {}), {1}: (3, {})} | custom-call | flops 1200000000 | bytes 1000000 | tf_op jit(solution)/shard_map/finish/pallas_call | solution.py:418
  (36 shorter events, 2.8 us)
Async XLA Ops:
  0.6 10.6 %copy-start = (bf16[128,1,256]{2,0,1:T(8,128)(2,1)S(1)}, bf16[128,1,256]{2,0,1:T(8,128)(2,1)}, u32[]{:S(2)}) copy-start(bf16[128,1,256]{2,0,1:T(8,128)(2,1)} %param.5) | copy-start | bytes 196612
  0.6 11.9 %copy-start.2 = (bf16[8,64,128]{2,1,0:T(8,128)(2,1)S(1)}, bf16[8,64,128]{2,1,0:T(8,128)(2,1)}, u32[]{:S(2)}) copy-start(bf16[8,64,128]{2,1,0:T(8,128)(2,1)} %wup_ref.3) | copy-start | bytes 393220
  0.7 11.9 %copy-start.1 = (bf16[27,64,128]{2,1,0:T(8,128)(2,1)S(1)}, bf16[27,64,128]{2,1,0:T(8,128)(2,1)}, u32[]{:S(2)}) copy-start(bf16[27,64,128]{2,1,0:T(8,128)(2,1)} %wc_ref.1) | copy-start | bytes 1327108
  2.8 17.4 %all-to-all-start = ((bf16[16,64,128]{2,1,0:T(8,128)(2,1)}), bf16[16,64,128]{2,1,0:T(8,128)(2,1)S(1)}, u32[]{:S(2)}, u32[]{:S(2)}) async-start(bf16[16,64,128]{2,1,0:T(8,128)(2,1)} %bitcast.14), calls=%async_computation | async-start | bytes 524288 | tf_op jit(solution)/shard_map/all_to_all | solution.py:444
  11.3 9.6 %collective-permute-start.2 = (bf16[128,768]{1,0:T(8,128)(2,1)S(1)}, bf16[128,768]{1,0:T(8,128)(2,1)S(1)}, u32[]{:S(2)}, u32[]{:S(2)}) collective-permute-start(bf16[128,768]{1,0:T(8,128)(2,1)S(1)} %get-tuple-element.85), channel_id=1, source_target_pairs={{0,1},{1,0},{2,3},{3,2},{4,5},{5,4},{6,7},{7,6},{8,9},{9,8},{10,11... | collective-permute-start | bytes 589832 | tf_op jit(solution)/shard_map/ppermute | solution.py:456
  11.8 9.2 %collective-permute-start.3 = (bf16[128,768]{1,0:T(8,128)(2,1)S(1)}, bf16[128,768]{1,0:T(8,128)(2,1)S(1)}, u32[]{:S(2)}, u32[]{:S(2)}) collective-permute-start(bf16[128,768]{1,0:T(8,128)(2,1)S(1)} %get-tuple-element.84), channel_id=1, source_target_pairs={{1,2},{2,1},{3,4},{4,3},{5,6},{6,5},{7,8},{8,7},{9,10},{10,9},{11,... | collective-permute-start | bytes 589832 | tf_op jit(solution)/shard_map/ppermute | solution.py:457
  20.2 5.5 %collective-permute-start = (bf16[16,64,128]{2,1,0:T(8,128)(2,1)S(1)}, bf16[16,64,128]{2,1,0:T(8,128)(2,1)S(1)}, u32[]{:S(2)}, u32[]{:S(2)}) collective-permute-start(bf16[16,64,128]{2,1,0:T(8,128)(2,1)S(1)} %all-to-all-done), channel_id=1, source_target_pairs={{0,1},{1,0},{2,3},{3,2},{4,5},{5,4},{6,7},{7,6},{8,9},{9,8},{10,11... | collective-permute-start | bytes 786440 | tf_op jit(solution)/shard_map/ppermute | solution.py:477
  20.2 5.5 %collective-permute-start.1 = (bf16[16,64,128]{2,1,0:T(8,128)(2,1)S(1)}, bf16[16,64,128]{2,1,0:T(8,128)(2,1)S(1)}, u32[]{:S(2)}, u32[]{:S(2)}) collective-permute-start(bf16[16,64,128]{2,1,0:T(8,128)(2,1)S(1)} %all-to-all-done), channel_id=1, source_target_pairs={{1,2},{2,1},{3,4},{4,3},{5,6},{6,5},{7,8},{8,7},{9,10},{10,9},{11,... | collective-permute-start | bytes 786440 | tf_op jit(solution)/shard_map/ppermute | solution.py:478
  31.6 29.7 %copy-start.3 = (bf16[64,2048]{1,0:T(8,128)(2,1)S(1)}, bf16[64,2048]{1,0:T(8,128)(2,1)}, u32[]{:S(2)}) copy-start(bf16[64,2048]{1,0:T(8,128)(2,1)} %get-tuple-element.61) | copy-start | bytes 786436
  31.6 8.3 %collective-permute-start.4 = (bf16[1152,128]{1,0:T(8,128)(2,1)S(1)}, bf16[1152,128]{1,0:T(8,128)(2,1)S(1)}, u32[]{:S(2)}, u32[]{:S(2)}) collective-permute-start(bf16[1152,128]{1,0:T(8,128)(2,1)S(1)} %get-tuple-element.58), channel_id=1, source_target_pairs={{0,1},{1,0},{2,3},{3,2},{4,5},{5,4},{6,7},{7,6},{8,9},{9,8},{10,11... | collective-permute-start | bytes 884744 | tf_op jit(solution)/shard_map/ppermute | solution.py:398
  34.8 16.5 %all-to-all-start.1 = ((bf16[16,64,128]{2,1,0:T(8,128)(2,1)}), bf16[16,64,128]{2,1,0:T(8,128)(2,1)S(1)}, u32[]{:S(2)}, u32[]{:S(2)}) async-start(bf16[16,64,128]{2,1,0:T(8,128)(2,1)} %get-tuple-element.59), calls=%async_computation.1 | async-start | bytes 524288 | tf_op jit(solution)/shard_map/all_to_all | solution.py:558
  40.0 6.4 %collective-permute-start.5 = (bf16[288,128]{1,0:T(8,128)(2,1)S(1)}, bf16[288,128]{1,0:T(8,128)(2,1)S(1)}, u32[]{:S(2)}, u32[]{:S(2)}) collective-permute-start(bf16[288,128]{1,0:T(8,128)(2,1)S(1)} %get-tuple-element.77), channel_id=1, source_target_pairs={{0,2},{1,3},{2,0},{3,1},{4,6},{5,7},{6,4},{7,5},{8,10},{9,11},{10,... | collective-permute-start | bytes 221192 | tf_op jit(solution)/shard_map/ppermute | solution.py:398
  42.0 7.0 %collective-permute-start.6 = (bf16[288,128]{1,0:T(8,128)(2,1)S(1)}, bf16[288,128]{1,0:T(8,128)(2,1)S(1)}, u32[]{:S(2)}, u32[]{:S(2)}) collective-permute-start(bf16[288,128]{1,0:T(8,128)(2,1)S(1)} %get-tuple-element.79), channel_id=1, source_target_pairs={{0,4},{1,5},{2,6},{3,7},{4,0},{5,1},{6,2},{7,3},{8,12},{9,13},{10,... | collective-permute-start | bytes 221192 | tf_op jit(solution)/shard_map/ppermute | solution.py:398
  43.5 7.8 %collective-permute-start.7 = (bf16[288,128]{1,0:T(8,128)(2,1)S(1)}, bf16[288,128]{1,0:T(8,128)(2,1)S(1)}, u32[]{:S(2)}, u32[]{:S(2)}) collective-permute-start(bf16[288,128]{1,0:T(8,128)(2,1)S(1)} %get-tuple-element.78), channel_id=1, source_target_pairs={{0,6},{1,7},{2,4},{3,5},{4,2},{5,3},{6,0},{7,1},{8,14},{9,15},{10,... | collective-permute-start | bytes 221192 | tf_op jit(solution)/shard_map/ppermute | solution.py:398
  51.4 6.4 %collective-permute-start.8 = (bf16[288,128]{1,0:T(8,128)(2,1)S(1)}, bf16[288,128]{1,0:T(8,128)(2,1)S(1)}, u32[]{:S(2)}, u32[]{:S(2)}) collective-permute-start(bf16[288,128]{1,0:T(8,128)(2,1)S(1)} %fusion.1), channel_id=1, source_target_pairs={{0,8},{1,9},{2,10},{3,11},{4,12},{5,13},{6,14},{7,15},{8,0},{9,1},... | collective-permute-start | bytes 221192 | tf_op jit(solution)/shard_map/ppermute | solution.py:398
  57.7 5.7 %collective-permute-start.10 = (bf16[288,128]{1,0:T(8,128)(2,1)S(1)}, bf16[288,128]{1,0:T(8,128)(2,1)S(1)}, u32[]{:S(2)}, u32[]{:S(2)}) collective-permute-start(bf16[288,128]{1,0:T(8,128)(2,1)S(1)} %add_convert_fusion), channel_id=1, source_target_pairs={{0,4},{1,5},{2,6},{3,7},{4,0},{5,1},{6,2},{7,3},{8,12},{9,13},{10,... | collective-permute-start | bytes 221192 | tf_op jit(solution)/shard_map/ppermute | solution.py:398
  57.8 5.7 %collective-permute-start.11 = (bf16[288,128]{1,0:T(8,128)(2,1)S(1)}, bf16[288,128]{1,0:T(8,128)(2,1)S(1)}, u32[]{:S(2)}, u32[]{:S(2)}) collective-permute-start(bf16[288,128]{1,0:T(8,128)(2,1)S(1)} %add_convert_fusion), channel_id=1, source_target_pairs={{0,6},{1,7},{2,4},{3,5},{4,2},{5,3},{6,0},{7,1},{8,14},{9,15},{10,... | collective-permute-start | bytes 221192 | tf_op jit(solution)/shard_map/ppermute | solution.py:398
  60.0 4.4 %collective-permute-start.9 = (bf16[288,128]{1,0:T(8,128)(2,1)S(1)}, bf16[288,128]{1,0:T(8,128)(2,1)S(1)}, u32[]{:S(2)}, u32[]{:S(2)}) collective-permute-start(bf16[288,128]{1,0:T(8,128)(2,1)S(1)} %add_convert_fusion), channel_id=1, source_target_pairs={{0,2},{1,3},{2,0},{3,1},{4,6},{5,7},{6,4},{7,5},{8,10},{9,11},{10,... | collective-permute-start | bytes 221192 | tf_op jit(solution)/shard_map/ppermute | solution.py:398
  64.4 1.6 %collective-permute-start.12 = (bf16[1152,128]{1,0:T(8,128)(2,1)S(1)}, bf16[1152,128]{1,0:T(8,128)(2,1)S(1)}, u32[]{:S(2)}, u32[]{:S(2)}) collective-permute-start(bf16[1152,128]{1,0:T(8,128)(2,1)S(1)} %constant_dynamic-update-slice_fusion.value_ref), channel_id=1, source_target_pairs={{0,1},{1,0},{2,3},{3,2},{4,5},{5,4},{6,7},{7,6},{8,9},{9,8},{10,11... | collective-permute-start | bytes 884744 | tf_op jit(solution)/shard_map/ppermute | solution.py:398

commit v6 on v5

--- a/solution.py
+++ b/solution.py
@@ -68,10 +68,53 @@
                 ]
 
 
-def in_order(core, core_ref, cross_ref):
-    near, far = (core_ref[...], cross_ref[...])
-    even = core == 0
-    return jnp.where(even, far, near), jnp.where(even, near, far)
+def shift_columns():
+    return one_hot((128, 256), lambda row, col: row == (col & 127) + 1 - 2 * (col >> 7))
+
+
+def gated(pre, cot):
+    gate = 1.0 / (1.0 + jnp.exp(-pre))
+    grad = (cot.astype(F32) * gate * (1.0 + pre * (1.0 - gate))).astype(BF16)
+    return (pre * gate).astype(BF16), grad
+
+
+def place_grad(grad, shift, gs_ref, base):
+    gs_ref[base + 64 : base + 128, :] = grad
+    tall = jnp.concatenate([grad[:, h * W : (h + 1) * W] for h in range(8)], axis=0)
+    moved = mm(tall, shift).astype(BF16)
+    for side in range(2):
+        at = base + side * 128
+        for h in range(8):
+            gs_ref[at : at + 64, h * W : (h + 1) * W] = moved[
+                h * 64 : (h + 1) * 64, side * W : side * W + W
+            ]
+
+
+def weight_term(grad, xu_ref, skip_rows, first):
+    zero = jnp.zeros((64, W), BF16)
+    low = jnp.concatenate([grad[:, W:], zero], axis=1)
+    high = jnp.concatenate([zero, grad[:, :-W]], axis=1)
+    pieces = []
+    for e in range(first, first + 3):
+        for tap in range(3):
+            at = e * 192 + tap * 64
+            pieces += [xu_ref[at : at + 64, :], skip_rows(e, tap)]
+    rows = jnp.concatenate([low, grad, high], axis=0)
+    return lax.dot_general(jnp.concatenate(pieces, axis=0), rows, NT, preferred_element_type=F32)
+
+
+def edge_cot(edge_ref):
+    return jnp.concatenate([edge_ref[:64, 256:], edge_ref[64:, 256:]], axis=1)
+
+
+def for_parity(core, body):
+    @pl.when(core == 0)
+    def _():
+        body(0)
+
+    @pl.when(core == 1)
+    def _():
+        body(1)
 
 
 def up_weights(wup_ref):
@@ -102,10 +145,9 @@
 
 
 def prepare_kernel(
-    own_ref, wup_ref, wc_ref, xu_ref, spread_ref, wfu_ref, wfs_ref, wi_ref, wg_ref, up_ref, skip_ref
+    own_ref, wup_ref, wc_ref, xu_ref, spread_ref, wfu_ref, wfs_ref, wi_ref, wg_ref, skip_ref
 ):
     select = spread_columns()
-    up_ref[...] = select
     skip_ref[...] = skip_columns()
     upsample(own_ref[...], up_weights(wup_ref), select, xu_ref, 0, spread_ref)
     rows = []
@@ -128,35 +170,51 @@
 
 
 def edge_kernel(
+    index_ref, core_ref, cross_ref, wup_ref, own_ref, far_wfu_ref, xu_ref, pre_ref, wfu_ref, sems
+):
+    pairs = ((far_wfu_ref, wfu_ref), (own_ref, xu_ref.at[384:768]))
+    copies = [pltpu.make_async_copy(src, dst, sems.at[i]) for i, (src, dst) in enumerate(pairs)]
+    for copy in copies:
+        copy.start()
+    weights = up_weights(wup_ref)
+    select = spread_columns()
+    even = index_ref[0] == 0
+    near, other = (core_ref[:, :256], cross_ref[:, :256])
+    upsample(jnp.where(even, other, near), weights, select, xu_ref, 0)
+    upsample(jnp.where(even, near, other), weights, select, xu_ref, 768)
+    for copy in copies:
+        copy.wait()
+    for j in range(4):
+        z = mm(wfu_ref[...], xu_ref[j * 192 : j * 192 + 576, :])
+        pre_ref[j * 64 : (j + 1) * 64, :] = row_taps(z, 64)
+
+
+def inner_kernel(
     index_ref,
-    core_ref,
-    cross_ref,
-    wup_ref,
-    own_ref,
+    edge_ref,
     held_ref,
+    held_core_ref,
+    cot_ref,
     skip_ref,
-    far_up_ref,
-    far_wfu_ref,
+    xu_ref,
+    pre_up_ref,
     far_wfs_ref,
     far_spread_ref,
     far_wi_ref,
     far_wg_ref,
-    xu_ref,
     xs_ref,
     pre_ref,
+    gs_ref,
+    act_ref,
+    term_ref,
     wfs_ref,
     spread_ref,
     wi_ref,
     wg_ref,
-    up_ref,
-    wfu_ref,
     sems,
 ):
     pairs = (
-        (far_up_ref, up_ref),
-        (far_wfu_ref, wfu_ref),
         (far_wfs_ref, wfs_ref),
-        (own_ref, xu_ref.at[384:768]),
         (far_spread_ref, spread_ref),
         (far_wi_ref, wi_ref),
         (far_wg_ref, wg_ref),
@@ -164,34 +222,52 @@
     copies = [pltpu.make_async_copy(src, dst, sems.at[i]) for i, (src, dst) in enumerate(pairs)]
     for copy in copies:
         copy.start()
-    place_skip(held_ref[...], skip_ref[...], xs_ref, 0)
-    weights = up_weights(wup_ref)
-    before, after = in_order(index_ref[0], core_ref, cross_ref)
-    copies[0].wait()
-    upsample(before[:, :256], weights, up_ref[...], xu_ref, 0)
-    upsample(after[:, :256], weights, up_ref[...], xu_ref, 768)
-    for copy in copies[1:]:
-        copy.wait()
-    for j in range(4):
-        z = mm(wfu_ref[...], xu_ref[j * 192 : j * 192 + 576, :])
-        low, high = (max(2 - j, 0), min(3 - j, 2))
-        rows = slice((low + j - 2) * 192, (high + j - 1) * 192)
-        z = z + mm(wfs_ref[:, low * 192 : (high + 1) * 192], xs_ref[rows, :])
-        pre_ref[j * 64 : (j + 1) * 64, :] = row_taps(z, 64)
+
+    def body(odd):
+        base = 0 if odd else 2
+        place_skip(held_ref[...], skip_ref[...], xs_ref, 384 * odd)
+        place_skip(held_core_ref[...], skip_ref[...], xs_ref, 384 * (1 - odd))
+        for copy in copies:
+            copy.wait()
+        shift = shift_columns()
+        for j in range(4):
+            planes = [e for e in range(j, j + 3) if base <= e < base + 4]
+            taps = slice((planes[0] - j) * 192, (planes[-1] - j + 1) * 192)
+            rows = slice((planes[0] - base) * 192, (planes[-1] - base + 1) * 192)
+            pre = pre_up_ref[j * 64 : (j + 1) * 64, :] + row_taps(mm(wfs_ref[:, taps], xs_ref[rows, :]), 64)
+            if (j >= 2) == bool(odd):
+                at = (j % 2) * 64
+                pre_ref[at : at + 64, :] = pre
+                continue
+            inner = j in (1, 2)
+            cot = cot_ref[:, (j - 1) * 1024 : j * 1024] if inner else edge_cot(edge_ref)
+            act, grad = gated(pre, cot)
+            place_grad(grad, shift, gs_ref, (j % 2) * 192)
+            if inner:
+                act_ref[...] = act
+
+                def skip_rows(e, tap):
+                    at = (e - base) * 192 + tap * 64
+                    return xs_ref[at : at + 64, :]
+
+                term_ref[...] = weight_term(grad, xu_ref, skip_rows, j)
+
+    for_parity(index_ref[0], body)
 
 
 def main_kernel(
     scale,
     index_ref,
-    near_ref,
-    far_ref,
+    cross_ref,
     cot_ref,
-    edge_core_ref,
-    edge_cross_ref,
-    own_ref,
+    edge_ref,
     select_ref,
+    xs_ref,
+    half_gs_ref,
+    half_act_ref,
     xu_ref,
     pre_ref,
+    term_ref,
     spread_ref,
     wi_ref,
     wf_ref,
@@ -201,7 +277,7 @@
     far_skip_ref,
     keep_ref,
     send_ref,
-    xs_ref,
+    xc_ref,
     gs_ref,
     gw_ref,
     act_ref,
@@ -209,47 +285,44 @@
     skip_ref,
     sems,
 ):
-    copy = pltpu.make_async_copy(own_ref, xs_ref.at[384:768], sems.at[0])
-    copy.start()
-    act_copy = pltpu.make_async_copy(act_ref, far_act_ref, sems.at[1])
-    skip_copy = pltpu.make_async_copy(skip_ref, far_skip_ref, sems.at[2])
-    gi_copy = pltpu.make_async_copy(gi_ref, far_gi_ref, sems.at[3])
     core = index_ref[0]
     quad = index_ref[1]
-    before, after = in_order(core, near_ref, far_ref)
-    place_skip(before, select_ref[...], xs_ref, 0)
-    place_skip(after, select_ref[...], xs_ref, 768)
-    edges = [
-        jnp.concatenate([edge[:64, 256:], edge[64:, 256:]], axis=1)
-        for edge in in_order(core, edge_core_ref, edge_cross_ref)
-    ]
-
-    shift = one_hot((128, 256), lambda row, col: row == (col & 127) + 1 - 2 * (col >> 7))
-    for j in range(4):
-        taps = slice(0, 384 - 192 * j) if j < 2 else slice(192 * (4 - j), 576)
-        planes = slice(192 * j, 384) if j < 2 else slice(768, 192 * (j + 3))
-        z = mm(wf_ref[:, taps], xs_ref[planes, :])
-        pre = pre_ref[j * 64 : (j + 1) * 64, :] + row_taps(z, 64)
-        gate = 1.0 / (1.0 + jnp.exp(-pre))
-        if j == 0:
-            cot = edges[0]
-        elif j == 3:
-            cot = edges[1]
-        else:
-            cot = cot_ref[:, (j - 1) * 1024 : j * 1024]
-            act_ref[:, (j - 1) * 1024 : j * 1024] = (pre * gate).astype(BF16)
-        grad = (cot.astype(F32) * gate * (1.0 + pre * (1.0 - gate))).astype(BF16)
-        gs_ref[j * 192 + 64 : j * 192 + 128, :] = grad
-        tall = jnp.concatenate([grad[:, h * W : (h + 1) * W] for h in range(8)], axis=0)
-        moved = mm(tall, shift).astype(BF16)
-        for tap in (0, 2):
-            at = j * 192 + tap * 64
-            for h in range(8):
-                gs_ref[at : at + 64, h * W : (h + 1) * W] = moved[
-                    h * 64 : (h + 1) * 64, (tap >> 1) * W : (tap >> 1) * W + W
-                ]
-
-    act_copy.start()
+    skip_copy = pltpu.make_async_copy(skip_ref, far_skip_ref, sems.at[3])
+    gi_copy = pltpu.make_async_copy(gi_ref, far_gi_ref, sems.at[4])
+
+    def copies_of(odd):
+        ready, late = (slice(0, 1024), slice(1024, 2048)) if odd else (slice(1024, 2048), slice(0, 1024))
+        return (
+            pltpu.make_async_copy(half_gs_ref, gs_ref.at[384 * (1 - odd) : 384 * (2 - odd)], sems.at[0]),
+            pltpu.make_async_copy(half_act_ref, far_act_ref.at[:, ready], sems.at[1]),
+            pltpu.make_async_copy(act_ref, far_act_ref.at[:, late], sems.at[2]),
+        )
+
+    def first(odd):
+        gs_copy, ready_copy, late_copy = copies_of(odd)
+        gs_copy.start()
+        ready_copy.start()
+        place_skip(cross_ref[...], select_ref[...], xc_ref, 0)
+        shift = shift_columns()
+        for j in (2, 3) if odd else (0, 1):
+            start = 4 * odd
+            planes = [e for e in range(j, j + 3) if start <= e < start + 2]
+            taps = slice((planes[0] - j) * 192, (planes[-1] - j + 1) * 192)
+            rows = slice((planes[0] - start) * 192, (planes[-1] - start + 1) * 192)
+            z = mm(wf_ref[:, taps], xc_ref[rows, :])
+            at = (j % 2) * 64
+            pre = pre_ref[at : at + 64, :] + row_taps(z, 64)
+            inner = j in (1, 2)
+            cot = cot_ref[:, (j - 1) * 1024 : j * 1024] if inner else edge_cot(edge_ref)
+            act, grad = gated(pre, cot)
+            place_grad(grad, shift, gs_ref, j * 192)
+            if inner:
+                act_ref[...] = act
+                late_copy.start()
+        gs_copy.wait()
+
+    for_parity(core, first)
+
     lower = lax.broadcasted_iota(jnp.int32, (64, W), 1) < 64
     ups = []
     skips = []
@@ -297,32 +370,30 @@
     gi_ref[...] = mm(wg_ref[...], operand).astype(BF16)
     gi_copy.start()
 
-    copy.wait()
-    zero = jnp.zeros((64, W), BF16)
-    grads = []
-    for j in (1, 2):
+    def second(odd):
+        j = 2 if odd else 1
+
+        def skip_rows(e, tap):
+            start = 4 * odd
+            if start <= e < start + 2:
+                ref, at = (xc_ref, (e - start) * 192 + tap * 64)
+            else:
+                ref, at = (xs_ref, (e - (0 if odd else 2)) * 192 + tap * 64)
+            return ref[at : at + 64, :]
+
         grad = gs_ref[j * 192 + 64 : j * 192 + 128, :]
-        low = jnp.concatenate([grad[:, W:], zero], axis=1)
-        high = jnp.concatenate([zero, grad[:, :-W]], axis=1)
-        grads.append(jnp.concatenate([low, grad, high], axis=0))
-    total = None
-    for j in (1, 2):
-        pieces = []
-        for e in range(j, j + 3):
-            for tap in range(3):
-                at = e * 192 + tap * 64
-                pieces += [xu_ref[at : at + 64, :], xs_ref[at : at + 64, :]]
-        term = lax.dot_general(
-            jnp.concatenate(pieces, axis=0), grads[j - 1], NT, preferred_element_type=F32
-        )
-        total = term if total is None else total + term
-    total = (total * scale).T
-    for a in range(3):
-        for b in range(3):
-            for tap in range(3):
-                at = (9 * a + 3 * b + tap) * 64
-                column = (3 * a + tap) * W
-                gw_ref[at : at + 64, :] = total[b * 64 : (b + 1) * 64, column : column + W]
+        total = weight_term(grad, xu_ref, skip_rows, j) + term_ref[...]
+        total = (total * scale).T
+        for a in range(3):
+            for b in range(3):
+                for tap in range(3):
+                    at = (9 * a + 3 * b + tap) * 64
+                    column = (3 * a + tap) * W
+                    gw_ref[at : at + 64, :] = total[b * 64 : (b + 1) * 64, column : column + W]
+        for done in copies_of(odd)[1:]:
+            done.wait()
+
+    for_parity(core, second)
 
     for k in range(4):
         row = jnp.bitwise_xor(quad, k) * 288
@@ -330,7 +401,7 @@
         other = pl.multiple_of((1 - core) * 1152 + row, 32)
         keep_ref[k * 288 : (k + 1) * 288, :] = gw_ref[pl.ds(mine, 288), :]
         send_ref[k * 288 : (k + 1) * 288, :] = gw_ref[pl.ds(other, 288), :].astype(BF16)
-    for done in (act_copy, skip_copy, gi_copy):
+    for done in (skip_copy, gi_copy):
         done.wait()
 
 
@@ -455,7 +526,7 @@
 
     edge_core = lax.ppermute(edge(1 - index[0]), AXIS, core_pairs)
     edge_cross = lax.ppermute(edge(index[0]), AXIS, cross_pairs)
-    xu, spread, wf_up, wf_skip, wi, wg, pick_up, pick_skip = pl.pallas_call(
+    xu, spread, wf_up, wf_skip, wi, wg, pick_skip = pl.pallas_call(
         prepare_kernel,
         out_shape=(
             inside((384, 1024)),
@@ -464,11 +535,10 @@
             outside((192, 576)),
             outside((384, 576)),
             outside((128, 512)),
-            outside((128, 1536)),
             inside((256, 768)),
         ),
         in_specs=[VMEM] * 3,
-        out_specs=(VMEM,) * 8,
+        out_specs=(VMEM,) * 7,
         compiler_params=room(8),
         cost_estimate=pl.CostEstimate(flops=1840000000, bytes_accessed=1000000, transcendentals=0),
         name="prepare",
@@ -477,33 +547,39 @@
     held_core = lax.ppermute(held, AXIS, core_pairs)
     held_cross = lax.ppermute(held, AXIS, cross_pairs)
     held, held_core, held_cross = [v.reshape(8, 2, 64, 128) for v in (held, held_core, held_cross)]
-    xu, xs, pre, wf_skip, spread, wi, wg = pl.pallas_call(
+    xu, pre_up = pl.pallas_call(
         edge_kernel,
+        out_shape=(inside((1152, 1024)), inside((256, 1024), F32)),
+        in_specs=[SMEM] + [VMEM] * 4 + [FAR],
+        out_specs=(VMEM,) * 2,
+        scratch_shapes=[pltpu.VMEM((192, 576), BF16), pltpu.SemaphoreType.DMA((2,))],
+        compiler_params=room(16),
+        cost_estimate=pl.CostEstimate(flops=3000000000, bytes_accessed=1000000, transcendentals=0),
+        name="edges",
+    )(index, near(edge_core), near(edge_cross), w_up, near(xu), far(wf_up))
+    xs, pre, half_gs, half_act, term, wf_skip, spread, wi, wg = pl.pallas_call(
+        inner_kernel,
         out_shape=(
-            inside((1152, 1024)),
+            inside((768, 1024)),
+            inside((128, 1024), F32),
             inside((384, 1024)),
-            inside((256, 1024), F32),
+            inside((64, 1024)),
+            inside((1152, 192), F32),
             inside((192, 576)),
             inside((256, 512)),
             inside((384, 576)),
             inside((128, 512)),
         ),
-        in_specs=[SMEM] + [VMEM] * 6 + [FAR] * 6,
-        out_specs=(VMEM,) * 7,
-        scratch_shapes=[
-            pltpu.VMEM((128, 1536), BF16),
-            pltpu.VMEM((192, 576), BF16),
-            pltpu.SemaphoreType.DMA((7,)),
-        ],
-        compiler_params=room(16),
-        cost_estimate=pl.CostEstimate(flops=2990000000, bytes_accessed=1000000, transcendentals=0),
-        name="edges",
+        in_specs=[SMEM] + [VMEM] * 7 + [FAR] * 4,
+        out_specs=(VMEM,) * 9,
+        scratch_shapes=[pltpu.SemaphoreType.DMA((4,))],
+        compiler_params=room(20),
+        cost_estimate=pl.CostEstimate(flops=4000000000, bytes_accessed=1000000, transcendentals=0),
+        name="inner",
     )(
         index,
-        *(near(v) for v in (edge_core, edge_cross)),
-        w_up,
-        *(near(v) for v in (xu, held, pick_skip)),
-        *(far(v) for v in (pick_up, wf_up, wf_skip, spread, wi, wg)),
+        *(near(v) for v in (edge_core, held, held_core, flat, pick_skip, xu, pre_up)),
+        *(far(v) for v in (wf_skip, spread, wi, wg)),
     )
 
     scale = 1.0 / math.sqrt(n * planes * cells)
@@ -516,16 +592,16 @@
             inside((1152, 128), F32),
             inside((1152, 128)),
         ),
-        in_specs=[SMEM] + [VMEM] * 13,
+        in_specs=[SMEM] + [VMEM] * 14,
         out_specs=(FAR,) * 3 + (VMEM,) * 2,
         scratch_shapes=[
-            pltpu.VMEM((1152, 1024), BF16),
+            pltpu.VMEM((384, 1024), BF16),
             pltpu.VMEM((768, 1024), BF16),
             pltpu.VMEM((2304, 128), F32),
-            pltpu.VMEM((64, 2048), BF16),
+            pltpu.VMEM((64, 1024), BF16),
             pltpu.VMEM((128, 256), BF16),
             pltpu.VMEM((16, 64, 128), BF16),
-            pltpu.SemaphoreType.DMA((4,)),
+            pltpu.SemaphoreType.DMA((5,)),
         ],
         compiler_params=room(24),
         cost_estimate=pl.CostEstimate(flops=8280000000, bytes_accessed=1000000, transcendentals=0),
@@ -535,15 +611,16 @@
         *(
             near(v)
             for v in (
-                held_core,
                 held_cross,
                 flat,
-                edge_core,
                 edge_cross,
+                pick_skip,
                 xs,
-                pick_skip,
+                half_gs,
+                half_act,
                 xu,
                 pre,
+                term,
                 spread,
                 wi,
                 wf_skip,

time: 67.9 us -> 66.9 us (0.985)
  waiting for transfers between devices: 18.5 us -> 16.5 us
  Pallas kernels: 15.4 us -> 16.7 us
  local copies, waits for them, and re-layouts: 5.38 us -> 4.42 us
    ppermute x1, starting transfers between devices: 0.46 us -> 3.33 us  [local(): edge_core = lax.ppermute(edge(1 - index[0]), AXIS, core_pairs)]
    pallas_call x1 -> x2, Pallas kernels: 4.76 us -> 7.1 us  [the longest x1 3.88 us: local(): pl.pallas_call(inner_kernel, out_shape=(inside((768, 1024)), inside((128,...]
    all_to_all x1, waiting for transfers between devices: 5.75 us -> 3.77 us  [local(): held = lax.all_to_all(sent, AXIS, split_axis=0, concat_axis=0, tiled=True)]
    ppermute x9, starting transfers between devices: 12.8 us -> 11.6 us  [swap(): return lax.ppermute(value, AXIS, [(i, i ^ bit) for i in range(n)])]
    all_to_all x1, starting transfers between devices: 5.07 us -> 3.86 us  [local(): lax.all_to_all(skip_part, AXIS, split_axis=0, concat_axis=0, tiled=True)]
    pallas_call x1, Pallas kernels: 5.85 us -> 4.74 us  [local(): pl.pallas_call(functools.partial(main_kernel, scale), out_shape=(outside(...]
    unnamed x12 -> x14, local copies, waits for them, and re-layouts: 1.06 us -> 0.11 us
  transfers between devices with their start and end apart: 15 -> 15, of which waited for: 8 -> 8; matrix products, arithmetic and copies ran while one was open for 5% -> 4% of each run, Pallas kernels for 12% -> 16%
where the time goes in v6:
time: 66.9 us; the launch traced here: 66.4 us
  starting transfers between devices  27.5 us (41%)
  Pallas kernels  16.7 us (25%)
  waiting for transfers between devices  16.5 us (25%)
  local copies, waits for them, and re-layouts  4.42 us (7%)
  between operations  1.06 us (2%)
    ppermute x9, waiting for transfers between devices, swap(): return lax.ppermute(value, AXIS, [(i, i ^ bit) for i in range(n)])  12.7 us
    ppermute x9, starting transfers between devices, swap(): return lax.ppermute(value, AXIS, [(i, i ^ bit) for i in range(n)])  11.6 us
    all_to_all x1, starting transfers between devices, local(): held = lax.all_to_all(sent, AXIS, split_axis=0, concat_axis=0, tiled=True)  7.36 us
    pallas_call x1, Pallas kernels, local(): pl.pallas_call(functools.partial(main_kernel, scale), out_shape=(outside(...  4.74 us
    pallas_call x1, Pallas kernels, local(): pl.pallas_call(inner_kernel, out_shape=(inside((768, 1024)), inside((128,...  3.88 us
    all_to_all x1, starting transfers between devices, local(): lax.all_to_all(skip_part, AXIS, split_axis=0, concat_axis=0, tiled=True)  3.86 us
    all_to_all x1, waiting for transfers between devices, local(): held = lax.all_to_all(sent, AXIS, split_axis=0, concat_axis=0, tiled=True)  3.77 us
    ppermute x1, starting transfers between devices, local(): edge_core = lax.ppermute(edge(1 - index[0]), AXIS, core_pairs)  3.33 us
  transfers between devices with their start and end apart: 15, of which 8 were waited for; matrix products, arithmetic and copies ran while one was open for 4% of the time, Pallas kernels for 16%

profile of v6, /device:TPU:0, one launch (start us, length us, event | category | flops | bytes accessed | tf_op | source)
XLA Modules:
  0.0 66.4 jit_solution(6070034017124058532)
XLA Ops:
  0.7 1.4 %reshape.43 = bf16[64,16,128]{2,1,0:T(8,128)(2,1)S(1)} reshape(bf16[64,32,64]{2,1,0:T(8,128)(2,1)} %param.6) | data formatting | bytes 524288 | tf_op jit(solution)/shard_map/reshape | solution.py:514
  2.8 7.4 %all-to-all-start = ((bf16[16,64,128]{2,1,0:T(8,128)(2,1)}), bf16[16,64,128]{2,1,0:T(8,128)(2,1)S(1)}, u32[]{:S(2)}, u32[]{:S(2)}) async-start(bf16[16,64,128]{2,1,0:T(8,128)(2,1)} %bitcast.14), calls=%async_computation | async-start | bytes 524288 | tf_op jit(solution)/shard_map/all_to_all | solution.py:515
  11.0 3.3 %collective-permute-start.2 = (bf16[128,768]{1,0:T(8,128)(2,1)S(1)}, bf16[128,768]{1,0:T(8,128)(2,1)S(1)}, u32[]{:S(2)}, u32[]{:S(2)}) collective-permute-start(bf16[128,768]{1,0:T(8,128)(2,1)S(1)} %get-tuple-element.90), channel_id=1, source_target_pairs={{0,1},{1,0},{2,3},{3,2},{4,5},{5,4},{6,7},{7,6},{8,9},{9,8},{10,11... | collective-permute-start | bytes 589832 | tf_op jit(solution)/shard_map/ppermute | solution.py:527
  14.4 2.0 %prepare.1 = (bf16[384,1024]{1,0:T(8,128)(2,1)S(1)}, bf16[256,512]{1,0:T(8,128)(2,1)}, bf16[192,576]{1,0:T(8,128)(2,1)}, bf16[192,576]{1,0:T(8,128)(2,1)}, bf16[...) custom-call(bf16[128,256]{1,0:T(8,128)(2,1)S(1)} %bitcast.20, ...), custom_call_target="tpu_custom_call" | custom-call | flops 1840000000 | bytes 1000000 | tf_op jit(solution)/shard_map/prepare/pallas_call | solution.py:529
  16.5 3.8 %all-to-all-done = bf16[16,64,128]{2,1,0:T(8,128)(2,1)S(1)} async-done(((bf16[16,64,128]{2,1,0:T(8,128)(2,1)}), bf16[16,64,128]{2,1,0:T(8,128)(2,1)S(1)}, u32[]{:S(2)}, u32[]{:S(2)}) %all-to-all-start) | async-done | bytes 262176 | tf_op jit(solution)/shard_map/all_to_all | solution.py:515
  20.9 3.2 %edges.1 = (bf16[1152,1024]{1,0:T(8,128)(2,1)S(1)}, f32[256,1024]{1,0:T(8,128)S(1)}) custom-call(s32[2]{0:T(128)S(1)} %pad_add_fusion.index_ref, bf16[128,768]{1,0:T(8,128)(2,1)S(1)} %collective-permute-done.2.core_ref.edge_ref, bf16[128,768]{1,0:T(8,128)(2,1)S(1)} %collective-permute-done.1.cross_ref.edge_ref, bf16[8,64,128]{2,1,0:T(8,128)(2,1)S(1)} %copy-done.2, ...), custom_call_target="tpu_custom_call" | custom-call | flops 3000000000 | bytes 1000000 | tf_op jit(solution)/shard_map/edges/pallas_call | solution.py:550
  24.2 3.9 %inner.1 = (bf16[768,1024]{1,0:T(8,128)(2,1)S(1)}, f32[128,1024]{1,0:T(8,128)S(1)}, bf16[384,1024]{1,0:T(8,128)(2,1)S(1)}, bf16[64,1024]{1,0:T(8,128)(2,1)S(1)},...) custom-call(s32[2]{0:T(128)S(1)} %pad_add_fusion.index_ref, ...), custom_call_target="tpu_custom_call" | custom-call | flops 4000000000 | bytes 1000000 | tf_op jit(solution)/shard_map/inner/pallas_call | solution.py:560
  28.1 4.7 %section.1 = (bf16[64,2048]{1,0:T(8,128)(2,1)}, bf16[128,256]{1,0:T(8,128)(2,1)}, bf16[16,64,128]{2,1,0:T(8,128)(2,1)}, f32[1152,128]{1,0:T(8,128)S(1)}, bf16[1152,128]{1,0:T(8,128)(2,1)S(1)}) custom-call(s32[2]{0:T(128)S(1)} %pad_add_fusion.index_ref, bf16[8,2,64,128]{3,2,1,0:T(8,128)(2,1)S(1)} %bitcast.21, bf16[64,2048]{1,0:T(8,128)(2,1)S(1)} %bitcast.17, ...), custom_call_target="tpu_custom_call" | custom-call | flops 8280000000 | bytes 1000000 | tf_op jit(solution)/shard_map/section/pallas_call | solution.py:586
  32.8 2.0 %collective-permute-start.4 = (bf16[1152,128]{1,0:T(8,128)(2,1)S(1)}, bf16[1152,128]{1,0:T(8,128)(2,1)S(1)}, u32[]{:S(2)}, u32[]{:S(2)}) collective-permute-start(bf16[1152,128]{1,0:T(8,128)(2,1)S(1)} %get-tuple-element.64), channel_id=1, source_target_pairs={{0,1},{1,0},{2,3},{3,2},{4,5},{5,4},{6,7},{7,6},{8,9},{9,8},{10,11... | collective-permute-start | bytes 884744 | tf_op jit(solution)/shard_map/ppermute | solution.py:469
  34.9 3.9 %all-to-all-start.1 = ((bf16[16,64,128]{2,1,0:T(8,128)(2,1)}), bf16[16,64,128]{2,1,0:T(8,128)(2,1)S(1)}, u32[]{:S(2)}, u32[]{:S(2)}) async-start(bf16[16,64,128]{2,1,0:T(8,128)(2,1)} %get-tuple-element.65), calls=%async_computation.1 | async-start | bytes 524288 | tf_op jit(solution)/shard_map/all_to_all | solution.py:635
  38.9 2.0 %collective-permute-start.5 = (bf16[288,128]{1,0:T(8,128)(2,1)S(1)}, bf16[288,128]{1,0:T(8,128)(2,1)S(1)}, u32[]{:S(2)}, u32[]{:S(2)}) collective-permute-start(bf16[288,128]{1,0:T(8,128)(2,1)S(1)} %get-tuple-element.83), channel_id=1, source_target_pairs={{0,2},{1,3},{2,0},{3,1},{4,6},{5,7},{6,4},{7,5},{8,10},{9,11},{10,... | collective-permute-start | bytes 221192 | tf_op jit(solution)/shard_map/ppermute | solution.py:469
  40.9 1.5 %collective-permute-start.6 = (bf16[288,128]{1,0:T(8,128)(2,1)S(1)}, bf16[288,128]{1,0:T(8,128)(2,1)S(1)}, u32[]{:S(2)}, u32[]{:S(2)}) collective-permute-start(bf16[288,128]{1,0:T(8,128)(2,1)S(1)} %get-tuple-element.85), channel_id=1, source_target_pairs={{0,4},{1,5},{2,6},{3,7},{4,0},{5,1},{6,2},{7,3},{8,12},{9,13},{10,... | collective-permute-start | bytes 221192 | tf_op jit(solution)/shard_map/ppermute | solution.py:469
  42.4 2.8 %collective-permute-done.5 = bf16[288,128]{1,0:T(8,128)(2,1)S(1)} collective-permute-done((bf16[288,128]{1,0:T(8,128)(2,1)S(1)}, bf16[288,128]{1,0:T(8,128)(2,1)S(1)}, u32[]{:S(2)}, u32[]{:S(2)}) %collective-permute-start.5) | collective-permute-done | bytes 73760 | tf_op jit(solution)/shard_map/ppermute | solution.py:469
  45.2 2.6 %collective-permute-done.6 = bf16[288,128]{1,0:T(8,128)(2,1)S(1)} collective-permute-done((bf16[288,128]{1,0:T(8,128)(2,1)S(1)}, bf16[288,128]{1,0:T(8,128)(2,1)S(1)}, u32[]{:S(2)}, u32[]{:S(2)}) %collective-permute-start.6) | collective-permute-done | bytes 73760 | tf_op jit(solution)/shard_map/ppermute | solution.py:469
  47.8 2.3 %collective-permute-done.7 = bf16[288,128]{1,0:T(8,128)(2,1)S(1)} collective-permute-done((bf16[288,128]{1,0:T(8,128)(2,1)S(1)}, bf16[288,128]{1,0:T(8,128)(2,1)S(1)}, u32[]{:S(2)}, u32[]{:S(2)}) %collective-permute-start.7) | collective-permute-done | bytes 73760 | tf_op jit(solution)/shard_map/ppermute | solution.py:469
  50.2 2.4 %collective-permute-start.8 = (bf16[288,128]{1,0:T(8,128)(2,1)S(1)}, bf16[288,128]{1,0:T(8,128)(2,1)S(1)}, u32[]{:S(2)}, u32[]{:S(2)}) collective-permute-start(bf16[288,128]{1,0:T(8,128)(2,1)S(1)} %fusion.1), channel_id=1, source_target_pairs={{0,8},{1,9},{2,10},{3,11},{4,12},{5,13},{6,14},{7,15},{8,0},{9,1},... | collective-permute-start | bytes 221192 | tf_op jit(solution)/shard_map/ppermute | solution.py:469
  52.6 3.9 %collective-permute-done.8 = bf16[288,128]{1,0:T(8,128)(2,1)S(1)} collective-permute-done((bf16[288,128]{1,0:T(8,128)(2,1)S(1)}, bf16[288,128]{1,0:T(8,128)(2,1)S(1)}, u32[]{:S(2)}, u32[]{:S(2)}) %collective-permute-start.8) | collective-permute-done | bytes 73760 | tf_op jit(solution)/shard_map/ppermute | solution.py:469
  56.6 2.2 %collective-permute-start.11 = (bf16[288,128]{1,0:T(8,128)(2,1)S(1)}, bf16[288,128]{1,0:T(8,128)(2,1)S(1)}, u32[]{:S(2)}, u32[]{:S(2)}) collective-permute-start(bf16[288,128]{1,0:T(8,128)(2,1)S(1)} %add_convert_fusion), channel_id=1, source_target_pairs={{0,6},{1,7},{2,4},{3,5},{4,2},{5,3},{6,0},{7,1},{8,14},{9,15},{10,... | collective-permute-start | bytes 221192 | tf_op jit(solution)/shard_map/ppermute | solution.py:469
  58.8 1.3 %collective-permute-start.9 = (bf16[288,128]{1,0:T(8,128)(2,1)S(1)}, bf16[288,128]{1,0:T(8,128)(2,1)S(1)}, u32[]{:S(2)}, u32[]{:S(2)}) collective-permute-start(bf16[288,128]{1,0:T(8,128)(2,1)S(1)} %add_convert_fusion), channel_id=1, source_target_pairs={{0,2},{1,3},{2,0},{3,1},{4,6},{5,7},{6,4},{7,5},{8,10},{9,11},{10,... | collective-permute-start | bytes 221192 | tf_op jit(solution)/shard_map/ppermute | solution.py:469
  60.1 0.9 %reshape.49 = bf16[64,2,1024]{2,1,0:T(2,128)(2,1)} reshape(bf16[64,2048]{1,0:T(8,128)(2,1)S(1)} %copy-done.4) | data formatting | bytes 524288 | tf_op jit(solution)/shard_map/reshape | solution.py:639
  61.2 1.1 %reshape.51 = bf16[64,32,64]{2,1,0:T(8,128)(2,1)} reshape(bf16[64,16,128]{2,1,0:T(8,128)(2,1)S(1)} %copy.14) | data formatting | bytes 524288 | tf_op jit(solution)/shard_map/reshape | solution.py:641
  62.3 0.8 %collective-permute-done.9 = bf16[288,128]{1,0:T(8,128)(2,1)S(1)} collective-permute-done((bf16[288,128]{1,0:T(8,128)(2,1)S(1)}, bf16[288,128]{1,0:T(8,128)(2,1)S(1)}, u32[]{:S(2)}, u32[]{:S(2)}) %collective-permute-start.9) | collective-permute-done | bytes 73760 | tf_op jit(solution)/shard_map/ppermute | solution.py:469
  63.3 1.4 %finish.2 = (f32[54,32,128]{2,1,0:T(8,128)}, f32[16,32,128]{2,1,0:T(8,128)}) custom-call(s32[2]{0:T(128)S(1)} %pad_add_fusion.index_ref, bf16[1152,128]{1,0:T(8,128)(2,1)S(1)} %constant_dynamic-update-slice_fusion.value_ref), custom_call_target="tpu_custom_call" | custom-call | flops 1200000000 | bytes 1000000 | tf_op jit(solution)/shard_map/finish/pallas_call | solution.py:489
  64.9 1.4 %finish.3 = (f32[54,32,128]{2,1,0:T(8,128)}, f32[16,32,128]{2,1,0:T(8,128)}) custom-call(s32[2]{0:T(128)S(1)} %pad_add_fusion.index_ref, bf16[1152,128]{1,0:T(8,128)(2,1)S(1)} %collective-permute-done.12.value_ref, f32[54,32,128]{2,1,0:T(8,128)} %get-tuple-element.77.refs_0_, ...), custom_call_target="tpu_custom_call", output_to_operand_aliasing={{0}: (2, {}), {1}: (3, {})} | custom-call | flops 1200000000 | bytes 1000000 | tf_op jit(solution)/shard_map/finish/pallas_call | solution.py:489
  (39 shorter events, 3.2 us)
Async XLA Ops:
  0.6 9.6 %copy-start.3 = (bf16[64,2,1024]{2,1,0:T(2,128)(2,1)S(1)}, bf16[64,2,1024]{2,1,0:T(2,128)(2,1)}, u32[]{:S(2)}) copy-start(bf16[64,2,1024]{2,1,0:T(2,128)(2,1)} %param.7) | copy-start | bytes 786436
  0.6 9.7 %copy-start = (bf16[128,1,256]{2,0,1:T(8,128)(2,1)S(1)}, bf16[128,1,256]{2,0,1:T(8,128)(2,1)}, u32[]{:S(2)}) copy-start(bf16[128,1,256]{2,0,1:T(8,128)(2,1)} %param.5) | copy-start | bytes 196612
  2.0 12.4 %copy-start.1 = (bf16[27,64,128]{2,1,0:T(8,128)(2,1)S(1)}, bf16[27,64,128]{2,1,0:T(8,128)(2,1)}, u32[]{:S(2)}) copy-start(bf16[27,64,128]{2,1,0:T(8,128)(2,1)} %wc_ref.1) | copy-start | bytes 1327108
  2.0 12.4 %copy-start.2 = (bf16[8,64,128]{2,1,0:T(8,128)(2,1)S(1)}, bf16[8,64,128]{2,1,0:T(8,128)(2,1)}, u32[]{:S(2)}) copy-start(bf16[8,64,128]{2,1,0:T(8,128)(2,1)} %wup_ref.3) | copy-start | bytes 393220
  2.8 17.4 %all-to-all-start = ((bf16[16,64,128]{2,1,0:T(8,128)(2,1)}), bf16[16,64,128]{2,1,0:T(8,128)(2,1)S(1)}, u32[]{:S(2)}, u32[]{:S(2)}) async-start(bf16[16,64,128]{2,1,0:T(8,128)(2,1)} %bitcast.14), calls=%async_computation | async-start | bytes 524288 | tf_op jit(solution)/shard_map/all_to_all | solution.py:515
  10.3 10.6 %collective-permute-start.1 = (bf16[128,768]{1,0:T(8,128)(2,1)S(1)}, bf16[128,768]{1,0:T(8,128)(2,1)S(1)}, u32[]{:S(2)}, u32[]{:S(2)}) collective-permute-start(bf16[128,768]{1,0:T(8,128)(2,1)S(1)} %get-tuple-element.91), channel_id=1, source_target_pairs={{1,2},{2,1},{3,4},{4,3},{5,6},{6,5},{7,8},{8,7},{9,10},{10,9},{11,... | collective-permute-start | bytes 589832 | tf_op jit(solution)/shard_map/ppermute | solution.py:528
  11.0 9.9 %collective-permute-start.2 = (bf16[128,768]{1,0:T(8,128)(2,1)S(1)}, bf16[128,768]{1,0:T(8,128)(2,1)S(1)}, u32[]{:S(2)}, u32[]{:S(2)}) collective-permute-start(bf16[128,768]{1,0:T(8,128)(2,1)S(1)} %get-tuple-element.90), channel_id=1, source_target_pairs={{0,1},{1,0},{2,3},{3,2},{4,5},{5,4},{6,7},{7,6},{8,9},{9,8},{10,11... | collective-permute-start | bytes 589832 | tf_op jit(solution)/shard_map/ppermute | solution.py:527
  20.2 3.9 %collective-permute-start.3 = (bf16[16,64,128]{2,1,0:T(8,128)(2,1)S(1)}, bf16[16,64,128]{2,1,0:T(8,128)(2,1)S(1)}, u32[]{:S(2)}, u32[]{:S(2)}) collective-permute-start(bf16[16,64,128]{2,1,0:T(8,128)(2,1)S(1)} %all-to-all-done), channel_id=1, source_target_pairs={{0,1},{1,0},{2,3},{3,2},{4,5},{5,4},{6,7},{7,6},{8,9},{9,8},{10,11... | collective-permute-start | bytes 786440 | tf_op jit(solution)/shard_map/ppermute | solution.py:547
  20.2 7.8 %collective-permute-start = (bf16[16,64,128]{2,1,0:T(8,128)(2,1)S(1)}, bf16[16,64,128]{2,1,0:T(8,128)(2,1)S(1)}, u32[]{:S(2)}, u32[]{:S(2)}) collective-permute-start(bf16[16,64,128]{2,1,0:T(8,128)(2,1)S(1)} %all-to-all-done), channel_id=1, source_target_pairs={{1,2},{2,1},{3,4},{4,3},{5,6},{6,5},{7,8},{8,7},{9,10},{10,9},{11,... | collective-permute-start | bytes 786440 | tf_op jit(solution)/shard_map/ppermute | solution.py:548
  32.8 5.9 %collective-permute-start.4 = (bf16[1152,128]{1,0:T(8,128)(2,1)S(1)}, bf16[1152,128]{1,0:T(8,128)(2,1)S(1)}, u32[]{:S(2)}, u32[]{:S(2)}) collective-permute-start(bf16[1152,128]{1,0:T(8,128)(2,1)S(1)} %get-tuple-element.64), channel_id=1, source_target_pairs={{0,1},{1,0},{2,3},{3,2},{4,5},{5,4},{6,7},{7,6},{8,9},{9,8},{10,11... | collective-permute-start | bytes 884744 | tf_op jit(solution)/shard_map/ppermute | solution.py:469
  34.9 15.3 %all-to-all-start.1 = ((bf16[16,64,128]{2,1,0:T(8,128)(2,1)}), bf16[16,64,128]{2,1,0:T(8,128)(2,1)S(1)}, u32[]{:S(2)}, u32[]{:S(2)}) async-start(bf16[16,64,128]{2,1,0:T(8,128)(2,1)} %get-tuple-element.65), calls=%async_computation.1 | async-start | bytes 524288 | tf_op jit(solution)/shard_map/all_to_all | solution.py:635
  38.7 21.4 %copy-start.4 = (bf16[64,2048]{1,0:T(8,128)(2,1)S(1)}, bf16[64,2048]{1,0:T(8,128)(2,1)}, u32[]{:S(2)}) copy-start(bf16[64,2048]{1,0:T(8,128)(2,1)} %get-tuple-element.67) | copy-start | bytes 786436
  38.9 6.4 %collective-permute-start.5 = (bf16[288,128]{1,0:T(8,128)(2,1)S(1)}, bf16[288,128]{1,0:T(8,128)(2,1)S(1)}, u32[]{:S(2)}, u32[]{:S(2)}) collective-permute-start(bf16[288,128]{1,0:T(8,128)(2,1)S(1)} %get-tuple-element.83), channel_id=1, source_target_pairs={{0,2},{1,3},{2,0},{3,1},{4,6},{5,7},{6,4},{7,5},{8,10},{9,11},{10,... | collective-permute-start | bytes 221192 | tf_op jit(solution)/shard_map/ppermute | solution.py:469
  40.9 6.9 %collective-permute-start.6 = (bf16[288,128]{1,0:T(8,128)(2,1)S(1)}, bf16[288,128]{1,0:T(8,128)(2,1)S(1)}, u32[]{:S(2)}, u32[]{:S(2)}) collective-permute-start(bf16[288,128]{1,0:T(8,128)(2,1)S(1)} %get-tuple-element.85), channel_id=1, source_target_pairs={{0,4},{1,5},{2,6},{3,7},{4,0},{5,1},{6,2},{7,3},{8,12},{9,13},{10,... | collective-permute-start | bytes 221192 | tf_op jit(solution)/shard_map/ppermute | solution.py:469
  42.3 7.8 %collective-permute-start.7 = (bf16[288,128]{1,0:T(8,128)(2,1)S(1)}, bf16[288,128]{1,0:T(8,128)(2,1)S(1)}, u32[]{:S(2)}, u32[]{:S(2)}) collective-permute-start(bf16[288,128]{1,0:T(8,128)(2,1)S(1)} %get-tuple-element.84), channel_id=1, source_target_pairs={{0,6},{1,7},{2,4},{3,5},{4,2},{5,3},{6,0},{7,1},{8,14},{9,15},{10,... | collective-permute-start | bytes 221192 | tf_op jit(solution)/shard_map/ppermute | solution.py:469
  50.2 6.4 %collective-permute-start.8 = (bf16[288,128]{1,0:T(8,128)(2,1)S(1)}, bf16[288,128]{1,0:T(8,128)(2,1)S(1)}, u32[]{:S(2)}, u32[]{:S(2)}) collective-permute-start(bf16[288,128]{1,0:T(8,128)(2,1)S(1)} %fusion.1), channel_id=1, source_target_pairs={{0,8},{1,9},{2,10},{3,11},{4,12},{5,13},{6,14},{7,15},{8,0},{9,1},... | collective-permute-start | bytes 221192 | tf_op jit(solution)/shard_map/ppermute | solution.py:469
  56.6 5.7 %collective-permute-start.10 = (bf16[288,128]{1,0:T(8,128)(2,1)S(1)}, bf16[288,128]{1,0:T(8,128)(2,1)S(1)}, u32[]{:S(2)}, u32[]{:S(2)}) collective-permute-start(bf16[288,128]{1,0:T(8,128)(2,1)S(1)} %add_convert_fusion), channel_id=1, source_target_pairs={{0,4},{1,5},{2,6},{3,7},{4,0},{5,1},{6,2},{7,3},{8,12},{9,13},{10,... | collective-permute-start | bytes 221192 | tf_op jit(solution)/shard_map/ppermute | solution.py:469
  56.6 5.7 %collective-permute-start.11 = (bf16[288,128]{1,0:T(8,128)(2,1)S(1)}, bf16[288,128]{1,0:T(8,128)(2,1)S(1)}, u32[]{:S(2)}, u32[]{:S(2)}) collective-permute-start(bf16[288,128]{1,0:T(8,128)(2,1)S(1)} %add_convert_fusion), channel_id=1, source_target_pairs={{0,6},{1,7},{2,4},{3,5},{4,2},{5,3},{6,0},{7,1},{8,14},{9,15},{10,... | collective-permute-start | bytes 221192 | tf_op jit(solution)/shard_map/ppermute | solution.py:469
  58.8 4.4 %collective-permute-start.9 = (bf16[288,128]{1,0:T(8,128)(2,1)S(1)}, bf16[288,128]{1,0:T(8,128)(2,1)S(1)}, u32[]{:S(2)}, u32[]{:S(2)}) collective-permute-start(bf16[288,128]{1,0:T(8,128)(2,1)S(1)} %add_convert_fusion), channel_id=1, source_target_pairs={{0,2},{1,3},{2,0},{3,1},{4,6},{5,7},{6,4},{7,5},{8,10},{9,11},{10,... | collective-permute-start | bytes 221192 | tf_op jit(solution)/shard_map/ppermute | solution.py:469
  63.2 1.6 %collective-permute-start.12 = (bf16[1152,128]{1,0:T(8,128)(2,1)S(1)}, bf16[1152,128]{1,0:T(8,128)(2,1)S(1)}, u32[]{:S(2)}, u32[]{:S(2)}) collective-permute-start(bf16[1152,128]{1,0:T(8,128)(2,1)S(1)} %constant_dynamic-update-slice_fusion.value_ref), channel_id=1, source_target_pairs={{0,1},{1,0},{2,3},{3,2},{4,5},{5,4},{6,7},{7,6},{8,9},{9,8},{10,11... | collective-permute-start | bytes 884744 | tf_op jit(solution)/shard_map/ppermute | solution.py:469

commit v7 on v6

--- a/solution.py
+++ b/solution.py
@@ -105,6 +105,11 @@
 
 def edge_cot(edge_ref):
     return jnp.concatenate([edge_ref[:64, 256:], edge_ref[64:, 256:]], axis=1)
+
+
+def position():
+    me = lax.axis_index(AXIS)
+    return me & 1, (me >> 1) & 3
 
 
 def for_parity(core, body):
@@ -170,7 +175,7 @@
 
 
 def edge_kernel(
-    index_ref, core_ref, cross_ref, wup_ref, own_ref, far_wfu_ref, xu_ref, pre_ref, wfu_ref, sems
+    core_ref, cross_ref, wup_ref, own_ref, far_wfu_ref, xu_ref, pre_ref, wfu_ref, sems
 ):
     pairs = ((far_wfu_ref, wfu_ref), (own_ref, xu_ref.at[384:768]))
     copies = [pltpu.make_async_copy(src, dst, sems.at[i]) for i, (src, dst) in enumerate(pairs)]
@@ -178,7 +183,7 @@
         copy.start()
     weights = up_weights(wup_ref)
     select = spread_columns()
-    even = index_ref[0] == 0
+    even = position()[0] == 0
     near, other = (core_ref[:, :256], cross_ref[:, :256])
     upsample(jnp.where(even, other, near), weights, select, xu_ref, 0)
     upsample(jnp.where(even, near, other), weights, select, xu_ref, 768)
@@ -190,7 +195,6 @@
 
 
 def inner_kernel(
-    index_ref,
     edge_ref,
     held_ref,
     held_core_ref,
@@ -252,12 +256,11 @@
 
                 term_ref[...] = weight_term(grad, xu_ref, skip_rows, j)
 
-    for_parity(index_ref[0], body)
+    for_parity(position()[0], body)
 
 
 def main_kernel(
     scale,
-    index_ref,
     cross_ref,
     cot_ref,
     edge_ref,
@@ -285,8 +288,7 @@
     skip_ref,
     sems,
 ):
-    core = index_ref[0]
-    quad = index_ref[1]
+    core, quad = position()
     skip_copy = pltpu.make_async_copy(skip_ref, far_skip_ref, sems.at[3])
     gi_copy = pltpu.make_async_copy(gi_ref, far_gi_ref, sems.at[4])
 
@@ -405,13 +407,14 @@
         done.wait()
 
 
-def finish_kernel(mine, index_ref, value_ref, *refs):
+def finish_kernel(mine, value_ref, *refs):
     conv_ref, up_ref, stage_ref, sems = refs[-4:]
-    side = index_ref[0] if mine else 1 - index_ref[0]
+    core, quad = position()
+    side = core if mine else 1 - core
 
     def each(act):
         for k in range(4):
-            piece = 4 * side + jnp.bitwise_xor(index_ref[1], k)
+            piece = 4 * side + jnp.bitwise_xor(quad, k)
             rows = slice(k * 9, k * 9 + 9)
 
             @pl.when(piece < 6)
@@ -440,7 +443,6 @@
 
 
 VMEM = pl.BlockSpec(memory_space=pltpu.VMEM)
-SMEM = pl.BlockSpec(memory_space=pltpu.SMEM)
 FAR = pl.BlockSpec(memory_space=pl.ANY)
 
 
@@ -464,7 +466,7 @@
     return pltpu.HBM(shape, dtype)
 
 
-def reduce_weights(index, keep, send, back, finish_others, n):
+def reduce_weights(keep, send, back, finish_others, n):
     def swap(value, bit):
         return lax.ppermute(value, AXIS, [(i, i ^ bit) for i in range(n)])
 
@@ -489,14 +491,14 @@
         sums = pl.pallas_call(
             functools.partial(finish_kernel, first),
             out_shape=(outside((54, 32, 128), F32), outside((16, 32, 128), F32)),
-            in_specs=[SMEM, VMEM] + [FAR] * len(sums),
+            in_specs=[VMEM] + [FAR] * len(sums),
             out_specs=(FAR, FAR),
             scratch_shapes=[pltpu.VMEM((36, 32, 128), F32), pltpu.SemaphoreType.DMA((4,))],
-            input_output_aliases={} if first else {2: 0, 3: 1},
+            input_output_aliases={} if first else {1: 0, 2: 1},
             compiler_params=room(6),
             cost_estimate=pl.CostEstimate(flops=1200000000, bytes_accessed=1000000, transcendentals=0),
             name="finish",
-        )(index, value, *sums)
+        )(near(value), *sums)
     conv, up = sums
     return conv.reshape(27, 64, 128), up.reshape(8, 64, 128), others
 
@@ -509,7 +511,7 @@
     core_pairs = [(i, i ^ 1) for i in range(n)]
     cross_pairs = [(i, i + 1 if i % 2 else i - 1) for i in range(1, n - 1)]
     me = lax.axis_index(AXIS)
-    index = jnp.stack([me & 1, (me >> 1) & 3]).astype(jnp.int32)
+    core = me & 1
 
     sent = skip.reshape(64, n, 2 * positions).transpose(1, 0, 2)
     held = lax.all_to_all(sent, AXIS, split_axis=0, concat_axis=0, tiled=True)
@@ -524,8 +526,8 @@
         halves = [lax.dynamic_slice_in_dim(flat, 1024 * plane + 512 * i, 512, 1) for i in range(2)]
         return jnp.concatenate([coarse, jnp.concatenate(halves, axis=0)], axis=1)
 
-    edge_core = lax.ppermute(edge(1 - index[0]), AXIS, core_pairs)
-    edge_cross = lax.ppermute(edge(index[0]), AXIS, cross_pairs)
+    edge_core = lax.ppermute(edge(1 - core), AXIS, core_pairs)
+    edge_cross = lax.ppermute(edge(core), AXIS, cross_pairs)
     xu, spread, wf_up, wf_skip, wi, wg, pick_skip = pl.pallas_call(
         prepare_kernel,
         out_shape=(
@@ -550,13 +552,13 @@
     xu, pre_up = pl.pallas_call(
         edge_kernel,
         out_shape=(inside((1152, 1024)), inside((256, 1024), F32)),
-        in_specs=[SMEM] + [VMEM] * 4 + [FAR],
+        in_specs=[VMEM] * 4 + [FAR],
         out_specs=(VMEM,) * 2,
         scratch_shapes=[pltpu.VMEM((192, 576), BF16), pltpu.SemaphoreType.DMA((2,))],
         compiler_params=room(16),
         cost_estimate=pl.CostEstimate(flops=3000000000, bytes_accessed=1000000, transcendentals=0),
         name="edges",
-    )(index, near(edge_core), near(edge_cross), w_up, near(xu), far(wf_up))
+    )(near(edge_core), near(edge_cross), w_up, near(xu), far(wf_up))
     xs, pre, half_gs, half_act, term, wf_skip, spread, wi, wg = pl.pallas_call(
         inner_kernel,
         out_shape=(
@@ -570,14 +572,13 @@
             inside((384, 576)),
             inside((128, 512)),
         ),
-        in_specs=[SMEM] + [VMEM] * 7 + [FAR] * 4,
+        in_specs=[VMEM] * 7 + [FAR] * 4,
         out_specs=(VMEM,) * 9,
         scratch_shapes=[pltpu.SemaphoreType.DMA((4,))],
         compiler_params=room(20),
         cost_estimate=pl.CostEstimate(flops=4000000000, bytes_accessed=1000000, transcendentals=0),
         name="inner",
     )(
-        index,
         *(near(v) for v in (edge_core, held, held_core, flat, pick_skip, xu, pre_up)),
         *(far(v) for v in (wf_skip, spread, wi, wg)),
     )
@@ -592,7 +593,7 @@
             inside((1152, 128), F32),
             inside((1152, 128)),
         ),
-        in_specs=[SMEM] + [VMEM] * 14,
+        in_specs=[VMEM] * 14,
         out_specs=(FAR,) * 3 + (VMEM,) * 2,
         scratch_shapes=[
             pltpu.VMEM((384, 1024), BF16),
@@ -607,7 +608,6 @@
         cost_estimate=pl.CostEstimate(flops=8280000000, bytes_accessed=1000000, transcendentals=0),
         name="section",
     )(
-        index,
         *(
             near(v)
             for v in (
@@ -641,7 +641,7 @@
             back.transpose(1, 0, 2).reshape(64, 2 * n, positions),
         )
 
-    grad_w_conv, grad_w_up, rest = reduce_weights(index, keep, send, back, others, n)
+    grad_w_conv, grad_w_up, rest = reduce_weights(keep, send, back, others, n)
     return (*rest, grad_w_up, grad_w_conv)
 
 

time: 66.9 us -> 65.7 us (0.982)
  Pallas kernels: 16.7 us -> 13.9 us
  starting transfers between devices: 27.5 us -> 28.6 us
    all_to_all x1, starting transfers between devices: 3.86 us -> 4.99 us  [local(): lax.all_to_all(skip_part, AXIS, split_axis=0, concat_axis=0, tiled=True)]
    pallas_call x2, Pallas kernels: 2.83 us -> 1.75 us  [reduce_weights(): pl.pallas_call(functools.partial(finish_kernel, first), out_shape=(outsid...]
  transfers between devices with their start and end apart: 15 -> 15, of which waited for: 8 -> 8; matrix products, arithmetic and copies ran while one was open for 4% -> 4% of each run, Pallas kernels for 16% -> 14%
where the time goes in v7:
time: 65.7 us; the launch traced here: 65.3 us
  starting transfers between devices  28.6 us (44%)
  waiting for transfers between devices  17.1 us (26%)
  Pallas kernels  13.9 us (21%)
  local copies, waits for them, and re-layouts  4.42 us (7%)
  between operations  1.06 us (2%)
    ppermute x9, waiting for transfers between devices, swap(): return lax.ppermute(value, AXIS, [(i, i ^ bit) for i in range(n)])  13.2 us
    ppermute x9, starting transfers between devices, swap(): return lax.ppermute(value, AXIS, [(i, i ^ bit) for i in range(n)])  11.6 us
    all_to_all x1, starting transfers between devices, local(): held = lax.all_to_all(sent, AXIS, split_axis=0, concat_axis=0, tiled=True)  7.36 us
    all_to_all x1, starting transfers between devices, local(): lax.all_to_all(skip_part, AXIS, split_axis=0, concat_axis=0, tiled=True)  4.99 us
    pallas_call x1, Pallas kernels, local(): pl.pallas_call(functools.partial(main_kernel, scale), out_shape=(outside(...  4.16 us
    all_to_all x1, waiting for transfers between devices, local(): held = lax.all_to_all(sent, AXIS, split_axis=0, concat_axis=0, tiled=True)  3.84 us
    ppermute x1, starting transfers between devices, local(): edge_core = lax.ppermute(edge(1 - core), AXIS, core_pairs)  3.33 us
    pallas_call x1, Pallas kernels, local(): pl.pallas_call(inner_kernel, out_shape=(inside((768, 1024)), inside((128,...  3.31 us
  transfers between devices with their start and end apart: 15, of which 8 were waited for; matrix products, arithmetic and copies ran while one was open for 4% of the time, Pallas kernels for 14%

profile of v7, /device:TPU:0, one launch (start us, length us, event | category | flops | bytes accessed | tf_op | source)
XLA Modules:
  0.0 65.3 jit_solution(14021378494102293561)
XLA Ops:
  0.7 1.4 %reshape.43 = bf16[64,16,128]{2,1,0:T(8,128)(2,1)S(1)} reshape(bf16[64,32,64]{2,1,0:T(8,128)(2,1)} %param.6) | data formatting | bytes 524288 | tf_op jit(solution)/shard_map/reshape | solution.py:516
  2.8 7.4 %all-to-all-start = ((bf16[16,64,128]{2,1,0:T(8,128)(2,1)}), bf16[16,64,128]{2,1,0:T(8,128)(2,1)S(1)}, u32[]{:S(2)}, u32[]{:S(2)}) async-start(bf16[16,64,128]{2,1,0:T(8,128)(2,1)} %bitcast.12), calls=%async_computation | async-start | bytes 524288 | tf_op jit(solution)/shard_map/all_to_all | solution.py:517
  11.0 3.3 %collective-permute-start.2 = (bf16[128,768]{1,0:T(8,128)(2,1)S(1)}, bf16[128,768]{1,0:T(8,128)(2,1)S(1)}, u32[]{:S(2)}, u32[]{:S(2)}) collective-permute-start(bf16[128,768]{1,0:T(8,128)(2,1)S(1)} %get-tuple-element.90), channel_id=1, source_target_pairs={{0,1},{1,0},{2,3},{3,2},{4,5},{5,4},{6,7},{7,6},{8,9},{9,8},{10,11... | collective-permute-start | bytes 589832 | tf_op jit(solution)/shard_map/ppermute | solution.py:529
  14.4 2.0 %prepare.1 = (bf16[384,1024]{1,0:T(8,128)(2,1)S(1)}, bf16[256,512]{1,0:T(8,128)(2,1)}, bf16[192,576]{1,0:T(8,128)(2,1)}, bf16[192,576]{1,0:T(8,128)(2,1)}, bf16[...) custom-call(bf16[128,256]{1,0:T(8,128)(2,1)S(1)} %bitcast.18, ...), custom_call_target="tpu_custom_call" | custom-call | flops 1840000000 | bytes 1000000 | tf_op jit(solution)/shard_map/prepare/pallas_call | solution.py:531
  16.4 3.8 %all-to-all-done = bf16[16,64,128]{2,1,0:T(8,128)(2,1)S(1)} async-done(((bf16[16,64,128]{2,1,0:T(8,128)(2,1)}), bf16[16,64,128]{2,1,0:T(8,128)(2,1)S(1)}, u32[]{:S(2)}, u32[]{:S(2)}) %all-to-all-start) | async-done | bytes 262176 | tf_op jit(solution)/shard_map/all_to_all | solution.py:517
  20.9 2.7 %edges.1 = (bf16[1152,1024]{1,0:T(8,128)(2,1)S(1)}, f32[256,1024]{1,0:T(8,128)S(1)}) custom-call(bf16[128,768]{1,0:T(8,128)(2,1)S(1)} %collective-permute-done.2.core_ref.edge_ref, bf16[128,768]{1,0:T(8,128)(2,1)S(1)} %collective-permute-done.1.cross_ref.edge_ref, bf16[8,64,128]{2,1,0:T(8,128)(2,1)S(1)} %copy-done.2, ...), custom_call_target="tpu_custom_call" | custom-call | flops 3000000000 | bytes 1000000 | tf_op jit(solution)/shard_map/edges/pallas_call | solution.py:552
  23.6 3.3 %inner.1 = (bf16[768,1024]{1,0:T(8,128)(2,1)S(1)}, f32[128,1024]{1,0:T(8,128)S(1)}, bf16[384,1024]{1,0:T(8,128)(2,1)S(1)}, bf16[64,1024]{1,0:T(8,128)(2,1)S(1)},...) custom-call(bf16[128,768]{1,0:T(8,128)(2,1)S(1)} %collective-permute, ...), custom_call_target="tpu_custom_call" | custom-call | flops 4000000000 | bytes 1000000 | tf_op jit(solution)/shard_map/inner/pallas_call | solution.py:562
  26.9 4.2 %section.1 = (bf16[64,2048]{1,0:T(8,128)(2,1)}, bf16[128,256]{1,0:T(8,128)(2,1)}, bf16[16,64,128]{2,1,0:T(8,128)(2,1)}, f32[1152,128]{1,0:T(8,128)S(1)}, bf16[1152,128]{1,0:T(8,128)(2,1)S(1)}) custom-call(bf16[8,2,64,128]{3,2,1,0:T(8,128)(2,1)S(1)} %bitcast.19, bf16[64,2048]{1,0:T(8,128)(2,1)S(1)} %bitcast.15, ...), custom_call_target="tpu_custom_call" | custom-call | flops 8280000000 | bytes 1000000 | tf_op jit(solution)/shard_map/section/pallas_call | solution.py:587
  31.1 2.0 %collective-permute-start.4 = (bf16[1152,128]{1,0:T(8,128)(2,1)S(1)}, bf16[1152,128]{1,0:T(8,128)(2,1)S(1)}, u32[]{:S(2)}, u32[]{:S(2)}) collective-permute-start(bf16[1152,128]{1,0:T(8,128)(2,1)S(1)} %get-tuple-element.64), channel_id=1, source_target_pairs={{0,1},{1,0},{2,3},{3,2},{4,5},{5,4},{6,7},{7,6},{8,9},{9,8},{10,11... | collective-permute-start | bytes 884744 | tf_op jit(solution)/shard_map/ppermute | solution.py:471
  33.1 5.0 %all-to-all-start.1 = ((bf16[16,64,128]{2,1,0:T(8,128)(2,1)}), bf16[16,64,128]{2,1,0:T(8,128)(2,1)S(1)}, u32[]{:S(2)}, u32[]{:S(2)}) async-start(bf16[16,64,128]{2,1,0:T(8,128)(2,1)} %get-tuple-element.65), calls=%async_computation.1 | async-start | bytes 524288 | tf_op jit(solution)/shard_map/all_to_all | solution.py:635
  38.3 2.0 %collective-permute-start.5 = (bf16[288,128]{1,0:T(8,128)(2,1)S(1)}, bf16[288,128]{1,0:T(8,128)(2,1)S(1)}, u32[]{:S(2)}, u32[]{:S(2)}) collective-permute-start(bf16[288,128]{1,0:T(8,128)(2,1)S(1)} %get-tuple-element.83), channel_id=1, source_target_pairs={{0,2},{1,3},{2,0},{3,1},{4,6},{5,7},{6,4},{7,5},{8,10},{9,11},{10,... | collective-permute-start | bytes 221192 | tf_op jit(solution)/shard_map/ppermute | solution.py:471
  40.2 1.5 %collective-permute-start.6 = (bf16[288,128]{1,0:T(8,128)(2,1)S(1)}, bf16[288,128]{1,0:T(8,128)(2,1)S(1)}, u32[]{:S(2)}, u32[]{:S(2)}) collective-permute-start(bf16[288,128]{1,0:T(8,128)(2,1)S(1)} %get-tuple-element.85), channel_id=1, source_target_pairs={{0,4},{1,5},{2,6},{3,7},{4,0},{5,1},{6,2},{7,3},{8,12},{9,13},{10,... | collective-permute-start | bytes 221192 | tf_op jit(solution)/shard_map/ppermute | solution.py:471
  41.8 2.8 %collective-permute-done.5 = bf16[288,128]{1,0:T(8,128)(2,1)S(1)} collective-permute-done((bf16[288,128]{1,0:T(8,128)(2,1)S(1)}, bf16[288,128]{1,0:T(8,128)(2,1)S(1)}, u32[]{:S(2)}, u32[]{:S(2)}) %collective-permute-start.5) | collective-permute-done | bytes 73760 | tf_op jit(solution)/shard_map/ppermute | solution.py:471
  44.6 2.6 %collective-permute-done.6 = bf16[288,128]{1,0:T(8,128)(2,1)S(1)} collective-permute-done((bf16[288,128]{1,0:T(8,128)(2,1)S(1)}, bf16[288,128]{1,0:T(8,128)(2,1)S(1)}, u32[]{:S(2)}, u32[]{:S(2)}) %collective-permute-start.6) | collective-permute-done | bytes 73760 | tf_op jit(solution)/shard_map/ppermute | solution.py:471
  47.2 2.3 %collective-permute-done.7 = bf16[288,128]{1,0:T(8,128)(2,1)S(1)} collective-permute-done((bf16[288,128]{1,0:T(8,128)(2,1)S(1)}, bf16[288,128]{1,0:T(8,128)(2,1)S(1)}, u32[]{:S(2)}, u32[]{:S(2)}) %collective-permute-start.7) | collective-permute-done | bytes 73760 | tf_op jit(solution)/shard_map/ppermute | solution.py:471
  49.6 2.4 %collective-permute-start.8 = (bf16[288,128]{1,0:T(8,128)(2,1)S(1)}, bf16[288,128]{1,0:T(8,128)(2,1)S(1)}, u32[]{:S(2)}, u32[]{:S(2)}) collective-permute-start(bf16[288,128]{1,0:T(8,128)(2,1)S(1)} %fusion.1), channel_id=1, source_target_pairs={{0,8},{1,9},{2,10},{3,11},{4,12},{5,13},{6,14},{7,15},{8,0},{9,1},... | collective-permute-start | bytes 221192 | tf_op jit(solution)/shard_map/ppermute | solution.py:471
  52.0 3.9 %collective-permute-done.8 = bf16[288,128]{1,0:T(8,128)(2,1)S(1)} collective-permute-done((bf16[288,128]{1,0:T(8,128)(2,1)S(1)}, bf16[288,128]{1,0:T(8,128)(2,1)S(1)}, u32[]{:S(2)}, u32[]{:S(2)}) %collective-permute-start.8) | collective-permute-done | bytes 73760 | tf_op jit(solution)/shard_map/ppermute | solution.py:471
  56.0 2.2 %collective-permute-start.11 = (bf16[288,128]{1,0:T(8,128)(2,1)S(1)}, bf16[288,128]{1,0:T(8,128)(2,1)S(1)}, u32[]{:S(2)}, u32[]{:S(2)}) collective-permute-start(bf16[288,128]{1,0:T(8,128)(2,1)S(1)} %add_convert_fusion), channel_id=1, source_target_pairs={{0,6},{1,7},{2,4},{3,5},{4,2},{5,3},{6,0},{7,1},{8,14},{9,15},{10,... | collective-permute-start | bytes 221192 | tf_op jit(solution)/shard_map/ppermute | solution.py:471
  58.2 1.3 %collective-permute-start.9 = (bf16[288,128]{1,0:T(8,128)(2,1)S(1)}, bf16[288,128]{1,0:T(8,128)(2,1)S(1)}, u32[]{:S(2)}, u32[]{:S(2)}) collective-permute-start(bf16[288,128]{1,0:T(8,128)(2,1)S(1)} %add_convert_fusion), channel_id=1, source_target_pairs={{0,2},{1,3},{2,0},{3,1},{4,6},{5,7},{6,4},{7,5},{8,10},{9,11},{10,... | collective-permute-start | bytes 221192 | tf_op jit(solution)/shard_map/ppermute | solution.py:471
  59.5 0.9 %reshape.49 = bf16[64,2,1024]{2,1,0:T(2,128)(2,1)} reshape(bf16[64,2048]{1,0:T(8,128)(2,1)S(1)} %copy-done.4) | data formatting | bytes 524288 | tf_op jit(solution)/shard_map/reshape | solution.py:639
  60.6 1.1 %reshape.51 = bf16[64,32,64]{2,1,0:T(8,128)(2,1)} reshape(bf16[64,16,128]{2,1,0:T(8,128)(2,1)S(1)} %copy.14) | data formatting | bytes 524288 | tf_op jit(solution)/shard_map/reshape | solution.py:641
  61.7 0.8 %collective-permute-done.9 = bf16[288,128]{1,0:T(8,128)(2,1)S(1)} collective-permute-done((bf16[288,128]{1,0:T(8,128)(2,1)S(1)}, bf16[288,128]{1,0:T(8,128)(2,1)S(1)}, u32[]{:S(2)}, u32[]{:S(2)}) %collective-permute-start.9) | collective-permute-done | bytes 73760 | tf_op jit(solution)/shard_map/ppermute | solution.py:471
  62.7 0.9 %finish.2 = (f32[54,32,128]{2,1,0:T(8,128)}, f32[16,32,128]{2,1,0:T(8,128)}) custom-call(bf16[1152,128]{1,0:T(8,128)(2,1)S(1)} %constant_dynamic-update-slice_fusion.value_ref), custom_call_target="tpu_custom_call" | custom-call | flops 1200000000 | bytes 1000000 | tf_op jit(solution)/shard_map/finish/pallas_call | solution.py:491
  64.3 0.9 %finish.3 = (f32[54,32,128]{2,1,0:T(8,128)}, f32[16,32,128]{2,1,0:T(8,128)}) custom-call(bf16[1152,128]{1,0:T(8,128)(2,1)S(1)} %collective-permute-done.12.value_ref, f32[54,32,128]{2,1,0:T(8,128)} %get-tuple-element.77.refs_0_, f32[16,32,128]{2,1,0:T(8,128)} %get-tuple-element.78.refs_1_), custom_call_target="tpu_custom_call", output_to_operand_aliasing={{0}: (1, {}), {1}: (2, {})} | custom-call | flops 1200000000 | bytes 1000000 | tf_op jit(solution)/shard_map/finish/pallas_call | solution.py:491
  (38 shorter events, 3.7 us)
Async XLA Ops:
  0.6 9.6 %copy-start.3 = (bf16[64,2,1024]{2,1,0:T(2,128)(2,1)S(1)}, bf16[64,2,1024]{2,1,0:T(2,128)(2,1)}, u32[]{:S(2)}) copy-start(bf16[64,2,1024]{2,1,0:T(2,128)(2,1)} %param.7) | copy-start | bytes 786436
  0.6 9.7 %copy-start = (bf16[128,1,256]{2,0,1:T(8,128)(2,1)S(1)}, bf16[128,1,256]{2,0,1:T(8,128)(2,1)}, u32[]{:S(2)}) copy-start(bf16[128,1,256]{2,0,1:T(8,128)(2,1)} %param.5) | copy-start | bytes 196612
  2.0 12.3 %copy-start.1 = (bf16[27,64,128]{2,1,0:T(8,128)(2,1)S(1)}, bf16[27,64,128]{2,1,0:T(8,128)(2,1)}, u32[]{:S(2)}) copy-start(bf16[27,64,128]{2,1,0:T(8,128)(2,1)} %wc_ref.1) | copy-start | bytes 1327108
  2.0 12.3 %copy-start.2 = (bf16[8,64,128]{2,1,0:T(8,128)(2,1)S(1)}, bf16[8,64,128]{2,1,0:T(8,128)(2,1)}, u32[]{:S(2)}) copy-start(bf16[8,64,128]{2,1,0:T(8,128)(2,1)} %wup_ref.3) | copy-start | bytes 393220
  2.8 17.4 %all-to-all-start = ((bf16[16,64,128]{2,1,0:T(8,128)(2,1)}), bf16[16,64,128]{2,1,0:T(8,128)(2,1)S(1)}, u32[]{:S(2)}, u32[]{:S(2)}) async-start(bf16[16,64,128]{2,1,0:T(8,128)(2,1)} %bitcast.12), calls=%async_computation | async-start | bytes 524288 | tf_op jit(solution)/shard_map/all_to_all | solution.py:517
  10.3 10.6 %collective-permute-start.1 = (bf16[128,768]{1,0:T(8,128)(2,1)S(1)}, bf16[128,768]{1,0:T(8,128)(2,1)S(1)}, u32[]{:S(2)}, u32[]{:S(2)}) collective-permute-start(bf16[128,768]{1,0:T(8,128)(2,1)S(1)} %get-tuple-element.91), channel_id=1, source_target_pairs={{1,2},{2,1},{3,4},{4,3},{5,6},{6,5},{7,8},{8,7},{9,10},{10,9},{11,... | collective-permute-start | bytes 589832 | tf_op jit(solution)/shard_map/ppermute | solution.py:530
  11.0 9.9 %collective-permute-start.2 = (bf16[128,768]{1,0:T(8,128)(2,1)S(1)}, bf16[128,768]{1,0:T(8,128)(2,1)S(1)}, u32[]{:S(2)}, u32[]{:S(2)}) collective-permute-start(bf16[128,768]{1,0:T(8,128)(2,1)S(1)} %get-tuple-element.90), channel_id=1, source_target_pairs={{0,1},{1,0},{2,3},{3,2},{4,5},{5,4},{6,7},{7,6},{8,9},{9,8},{10,11... | collective-permute-start | bytes 589832 | tf_op jit(solution)/shard_map/ppermute | solution.py:529
  20.2 3.4 %collective-permute-start.3 = (bf16[16,64,128]{2,1,0:T(8,128)(2,1)S(1)}, bf16[16,64,128]{2,1,0:T(8,128)(2,1)S(1)}, u32[]{:S(2)}, u32[]{:S(2)}) collective-permute-start(bf16[16,64,128]{2,1,0:T(8,128)(2,1)S(1)} %all-to-all-done), channel_id=1, source_target_pairs={{0,1},{1,0},{2,3},{3,2},{4,5},{5,4},{6,7},{7,6},{8,9},{9,8},{10,11... | collective-permute-start | bytes 786440 | tf_op jit(solution)/shard_map/ppermute | solution.py:549
  20.2 6.7 %collective-permute-start = (bf16[16,64,128]{2,1,0:T(8,128)(2,1)S(1)}, bf16[16,64,128]{2,1,0:T(8,128)(2,1)S(1)}, u32[]{:S(2)}, u32[]{:S(2)}) collective-permute-start(bf16[16,64,128]{2,1,0:T(8,128)(2,1)S(1)} %all-to-all-done), channel_id=1, source_target_pairs={{1,2},{2,1},{3,4},{4,3},{5,6},{6,5},{7,8},{8,7},{9,10},{10,9},{11,... | collective-permute-start | bytes 786440 | tf_op jit(solution)/shard_map/ppermute | solution.py:550
  31.1 7.0 %collective-permute-start.4 = (bf16[1152,128]{1,0:T(8,128)(2,1)S(1)}, bf16[1152,128]{1,0:T(8,128)(2,1)S(1)}, u32[]{:S(2)}, u32[]{:S(2)}) collective-permute-start(bf16[1152,128]{1,0:T(8,128)(2,1)S(1)} %get-tuple-element.64), channel_id=1, source_target_pairs={{0,1},{1,0},{2,3},{3,2},{4,5},{5,4},{6,7},{7,6},{8,9},{9,8},{10,11... | collective-permute-start | bytes 884744 | tf_op jit(solution)/shard_map/ppermute | solution.py:471
  33.1 16.4 %all-to-all-start.1 = ((bf16[16,64,128]{2,1,0:T(8,128)(2,1)}), bf16[16,64,128]{2,1,0:T(8,128)(2,1)S(1)}, u32[]{:S(2)}, u32[]{:S(2)}) async-start(bf16[16,64,128]{2,1,0:T(8,128)(2,1)} %get-tuple-element.65), calls=%async_computation.1 | async-start | bytes 524288 | tf_op jit(solution)/shard_map/all_to_all | solution.py:635
  38.1 21.4 %copy-start.4 = (bf16[64,2048]{1,0:T(8,128)(2,1)S(1)}, bf16[64,2048]{1,0:T(8,128)(2,1)}, u32[]{:S(2)}) copy-start(bf16[64,2048]{1,0:T(8,128)(2,1)} %get-tuple-element.67) | copy-start | bytes 786436
  38.3 6.4 %collective-permute-start.5 = (bf16[288,128]{1,0:T(8,128)(2,1)S(1)}, bf16[288,128]{1,0:T(8,128)(2,1)S(1)}, u32[]{:S(2)}, u32[]{:S(2)}) collective-permute-start(bf16[288,128]{1,0:T(8,128)(2,1)S(1)} %get-tuple-element.83), channel_id=1, source_target_pairs={{0,2},{1,3},{2,0},{3,1},{4,6},{5,7},{6,4},{7,5},{8,10},{9,11},{10,... | collective-permute-start | bytes 221192 | tf_op jit(solution)/shard_map/ppermute | solution.py:471
  40.2 6.9 %collective-permute-start.6 = (bf16[288,128]{1,0:T(8,128)(2,1)S(1)}, bf16[288,128]{1,0:T(8,128)(2,1)S(1)}, u32[]{:S(2)}, u32[]{:S(2)}) collective-permute-start(bf16[288,128]{1,0:T(8,128)(2,1)S(1)} %get-tuple-element.85), channel_id=1, source_target_pairs={{0,4},{1,5},{2,6},{3,7},{4,0},{5,1},{6,2},{7,3},{8,12},{9,13},{10,... | collective-permute-start | bytes 221192 | tf_op jit(solution)/shard_map/ppermute | solution.py:471
  41.7 7.8 %collective-permute-start.7 = (bf16[288,128]{1,0:T(8,128)(2,1)S(1)}, bf16[288,128]{1,0:T(8,128)(2,1)S(1)}, u32[]{:S(2)}, u32[]{:S(2)}) collective-permute-start(bf16[288,128]{1,0:T(8,128)(2,1)S(1)} %get-tuple-element.84), channel_id=1, source_target_pairs={{0,6},{1,7},{2,4},{3,5},{4,2},{5,3},{6,0},{7,1},{8,14},{9,15},{10,... | collective-permute-start | bytes 221192 | tf_op jit(solution)/shard_map/ppermute | solution.py:471
  49.6 6.4 %collective-permute-start.8 = (bf16[288,128]{1,0:T(8,128)(2,1)S(1)}, bf16[288,128]{1,0:T(8,128)(2,1)S(1)}, u32[]{:S(2)}, u32[]{:S(2)}) collective-permute-start(bf16[288,128]{1,0:T(8,128)(2,1)S(1)} %fusion.1), channel_id=1, source_target_pairs={{0,8},{1,9},{2,10},{3,11},{4,12},{5,13},{6,14},{7,15},{8,0},{9,1},... | collective-permute-start | bytes 221192 | tf_op jit(solution)/shard_map/ppermute | solution.py:471
  56.0 5.7 %collective-permute-start.10 = (bf16[288,128]{1,0:T(8,128)(2,1)S(1)}, bf16[288,128]{1,0:T(8,128)(2,1)S(1)}, u32[]{:S(2)}, u32[]{:S(2)}) collective-permute-start(bf16[288,128]{1,0:T(8,128)(2,1)S(1)} %add_convert_fusion), channel_id=1, source_target_pairs={{0,4},{1,5},{2,6},{3,7},{4,0},{5,1},{6,2},{7,3},{8,12},{9,13},{10,... | collective-permute-start | bytes 221192 | tf_op jit(solution)/shard_map/ppermute | solution.py:471
  56.0 5.7 %collective-permute-start.11 = (bf16[288,128]{1,0:T(8,128)(2,1)S(1)}, bf16[288,128]{1,0:T(8,128)(2,1)S(1)}, u32[]{:S(2)}, u32[]{:S(2)}) collective-permute-start(bf16[288,128]{1,0:T(8,128)(2,1)S(1)} %add_convert_fusion), channel_id=1, source_target_pairs={{0,6},{1,7},{2,4},{3,5},{4,2},{5,3},{6,0},{7,1},{8,14},{9,15},{10,... | collective-permute-start | bytes 221192 | tf_op jit(solution)/shard_map/ppermute | solution.py:471
  58.2 4.4 %collective-permute-start.9 = (bf16[288,128]{1,0:T(8,128)(2,1)S(1)}, bf16[288,128]{1,0:T(8,128)(2,1)S(1)}, u32[]{:S(2)}, u32[]{:S(2)}) collective-permute-start(bf16[288,128]{1,0:T(8,128)(2,1)S(1)} %add_convert_fusion), channel_id=1, source_target_pairs={{0,2},{1,3},{2,0},{3,1},{4,6},{5,7},{6,4},{7,5},{8,10},{9,11},{10,... | collective-permute-start | bytes 221192 | tf_op jit(solution)/shard_map/ppermute | solution.py:471
  62.6 1.6 %collective-permute-start.12 = (bf16[1152,128]{1,0:T(8,128)(2,1)S(1)}, bf16[1152,128]{1,0:T(8,128)(2,1)S(1)}, u32[]{:S(2)}, u32[]{:S(2)}) collective-permute-start(bf16[1152,128]{1,0:T(8,128)(2,1)S(1)} %constant_dynamic-update-slice_fusion.value_ref), channel_id=1, source_target_pairs={{0,1},{1,0},{2,3},{3,2},{4,5},{5,4},{6,7},{7,6},{8,9},{9,8},{10,11... | collective-permute-start | bytes 884744 | tf_op jit(solution)/shard_map/ppermute | solution.py:471

commit v8 on v7

--- a/solution.py
+++ b/solution.py
@@ -101,6 +101,13 @@
             pieces += [xu_ref[at : at + 64, :], skip_rows(e, tap)]
     rows = jnp.concatenate([low, grad, high], axis=0)
     return lax.dot_general(jnp.concatenate(pieces, axis=0), rows, NT, preferred_element_type=F32)
+
+
+def input_grad(held, gs_ref, wi_ref, plane):
+    ours = [j for j in range(plane, plane + 3) if j in held]
+    taps = slice((ours[0] - plane) * 192, (ours[-1] - plane + 1) * 192)
+    rows = slice((ours[0] - held[0]) * 192, (ours[-1] - held[0] + 1) * 192)
+    return row_taps_back(mm(wi_ref[:, taps], gs_ref[rows, :]), 128)
 
 
 def edge_cot(edge_ref):
@@ -208,13 +215,14 @@
     far_wg_ref,
     xs_ref,
     pre_ref,
-    gs_ref,
+    part_ref,
     act_ref,
     term_ref,
     wfs_ref,
     spread_ref,
     wi_ref,
     wg_ref,
+    gs_ref,
     sems,
 ):
     pairs = (
@@ -256,6 +264,10 @@
 
                 term_ref[...] = weight_term(grad, xu_ref, skip_rows, j)
 
+        for plane in range(2):
+            part = input_grad((0, 1) if odd else (2, 3), gs_ref, wi_ref, plane)
+            part_ref[plane * 128 : (plane + 1) * 128, :] = part
+
     for_parity(position()[0], body)
 
 
@@ -266,7 +278,7 @@
     edge_ref,
     select_ref,
     xs_ref,
-    half_gs_ref,
+    part_ref,
     half_act_ref,
     xu_ref,
     pre_ref,
@@ -283,26 +295,25 @@
     xc_ref,
     gs_ref,
     gw_ref,
+    gj_ref,
     act_ref,
     gi_ref,
     skip_ref,
     sems,
 ):
     core, quad = position()
-    skip_copy = pltpu.make_async_copy(skip_ref, far_skip_ref, sems.at[3])
-    gi_copy = pltpu.make_async_copy(gi_ref, far_gi_ref, sems.at[4])
+    skip_copy = pltpu.make_async_copy(skip_ref, far_skip_ref, sems.at[2])
+    gi_copy = pltpu.make_async_copy(gi_ref, far_gi_ref, sems.at[3])
 
     def copies_of(odd):
         ready, late = (slice(0, 1024), slice(1024, 2048)) if odd else (slice(1024, 2048), slice(0, 1024))
         return (
-            pltpu.make_async_copy(half_gs_ref, gs_ref.at[384 * (1 - odd) : 384 * (2 - odd)], sems.at[0]),
-            pltpu.make_async_copy(half_act_ref, far_act_ref.at[:, ready], sems.at[1]),
-            pltpu.make_async_copy(act_ref, far_act_ref.at[:, late], sems.at[2]),
+            pltpu.make_async_copy(half_act_ref, far_act_ref.at[:, ready], sems.at[0]),
+            pltpu.make_async_copy(act_ref, far_act_ref.at[:, late], sems.at[1]),
         )
 
     def first(odd):
-        gs_copy, ready_copy, late_copy = copies_of(odd)
-        gs_copy.start()
+        ready_copy, late_copy = copies_of(odd)
         ready_copy.start()
         place_skip(cross_ref[...], select_ref[...], xc_ref, 0)
         shift = shift_columns()
@@ -317,11 +328,13 @@
             inner = j in (1, 2)
             cot = cot_ref[:, (j - 1) * 1024 : j * 1024] if inner else edge_cot(edge_ref)
             act, grad = gated(pre, cot)
-            place_grad(grad, shift, gs_ref, j * 192)
+            place_grad(grad, shift, gs_ref, (j % 2) * 192)
             if inner:
                 act_ref[...] = act
                 late_copy.start()
-        gs_copy.wait()
+        for plane in range(2):
+            at = slice(plane * 128, (plane + 1) * 128)
+            gj_ref[at, :] = part_ref[at, :] + input_grad((2, 3) if odd else (0, 1), gs_ref, wi_ref, plane)
 
     for_parity(core, first)
 
@@ -329,8 +342,7 @@
     ups = []
     skips = []
     for j in range(2):
-        z = mm(wi_ref[...], gs_ref[j * 192 : j * 192 + 576, :])
-        grad = row_taps_back(z, 128)
+        grad = gj_ref[j * 128 : (j + 1) * 128, :]
         ups.append(grad[:64].astype(BF16))
         skips.append(grad[64:])
     for h in range(8):
@@ -383,7 +395,8 @@
                 ref, at = (xs_ref, (e - (0 if odd else 2)) * 192 + tap * 64)
             return ref[at : at + 64, :]
 
-        grad = gs_ref[j * 192 + 64 : j * 192 + 128, :]
+        at = (j % 2) * 192 + 64
+        grad = gs_ref[at : at + 64, :]
         total = weight_term(grad, xu_ref, skip_rows, j) + term_ref[...]
         total = (total * scale).T
         for a in range(3):
@@ -392,7 +405,7 @@
                     at = (9 * a + 3 * b + tap) * 64
                     column = (3 * a + tap) * W
                     gw_ref[at : at + 64, :] = total[b * 64 : (b + 1) * 64, column : column + W]
-        for done in copies_of(odd)[1:]:
+        for done in copies_of(odd):
             done.wait()
 
     for_parity(core, second)
@@ -559,12 +572,12 @@
         cost_estimate=pl.CostEstimate(flops=3000000000, bytes_accessed=1000000, transcendentals=0),
         name="edges",
     )(near(edge_core), near(edge_cross), w_up, near(xu), far(wf_up))
-    xs, pre, half_gs, half_act, term, wf_skip, spread, wi, wg = pl.pallas_call(
+    xs, pre, part, half_act, term, wf_skip, spread, wi, wg = pl.pallas_call(
         inner_kernel,
         out_shape=(
             inside((768, 1024)),
             inside((128, 1024), F32),
-            inside((384, 1024)),
+            inside((256, 1024), F32),
             inside((64, 1024)),
             inside((1152, 192), F32),
             inside((192, 576)),
@@ -574,7 +587,7 @@
         ),
         in_specs=[VMEM] * 7 + [FAR] * 4,
         out_specs=(VMEM,) * 9,
-        scratch_shapes=[pltpu.SemaphoreType.DMA((4,))],
+        scratch_shapes=[pltpu.VMEM((384, 1024), BF16), pltpu.SemaphoreType.DMA((4,))],
         compiler_params=room(20),
         cost_estimate=pl.CostEstimate(flops=4000000000, bytes_accessed=1000000, transcendentals=0),
         name="inner",
@@ -597,12 +610,13 @@
         out_specs=(FAR,) * 3 + (VMEM,) * 2,
         scratch_shapes=[
             pltpu.VMEM((384, 1024), BF16),
-            pltpu.VMEM((768, 1024), BF16),
+            pltpu.VMEM((384, 1024), BF16),
             pltpu.VMEM((2304, 128), F32),
+            pltpu.VMEM((256, 1024), F32),
             pltpu.VMEM((64, 1024), BF16),
             pltpu.VMEM((128, 256), BF16),
             pltpu.VMEM((16, 64, 128), BF16),
-            pltpu.SemaphoreType.DMA((5,)),
+            pltpu.SemaphoreType.DMA((4,)),
         ],
         compiler_params=room(24),
         cost_estimate=pl.CostEstimate(flops=8280000000, bytes_accessed=1000000, transcendentals=0),
@@ -616,7 +630,7 @@
                 edge_cross,
                 pick_skip,
                 xs,
-                half_gs,
+                part,
                 half_act,
                 xu,
                 pre,

time: 65.7 us -> 64.9 us (0.988)
  starting transfers between devices: 28.6 us -> 27.7 us
    all_to_all x1, starting transfers between devices: 4.99 us -> 4.19 us  [local(): lax.all_to_all(skip_part, AXIS, split_axis=0, concat_axis=0, tiled=True)]
    pallas_call x1, Pallas kernels: 3.31 us -> 3.98 us  [local(): pl.pallas_call(inner_kernel, out_shape=(inside((768, 1024)), inside((128,...]
  transfers between devices with their start and end apart: 15 -> 15, of which waited for: 8 -> 8; matrix products, arithmetic and copies ran while one was open for 4% -> 4% of each run, Pallas kernels for 14% -> 15%
where the time goes in v8:
time: 64.9 us; the launch traced here: 64.5 us
  starting transfers between devices  27.7 us (43%)
  waiting for transfers between devices  17.1 us (26%)
  Pallas kernels  14.1 us (22%)
  local copies, waits for them, and re-layouts  4.42 us (7%)
  between operations  1.06 us (2%)
    ppermute x9, waiting for transfers between devices, swap(): return lax.ppermute(value, AXIS, [(i, i ^ bit) for i in range(n)])  13.2 us
    ppermute x9, starting transfers between devices, swap(): return lax.ppermute(value, AXIS, [(i, i ^ bit) for i in range(n)])  11.5 us
    all_to_all x1, starting transfers between devices, local(): held = lax.all_to_all(sent, AXIS, split_axis=0, concat_axis=0, tiled=True)  7.36 us
    all_to_all x1, starting transfers between devices, local(): lax.all_to_all(skip_part, AXIS, split_axis=0, concat_axis=0, tiled=True)  4.19 us
    pallas_call x1, Pallas kernels, local(): pl.pallas_call(inner_kernel, out_shape=(inside((768, 1024)), inside((128,...  3.98 us
    all_to_all x1, waiting for transfers between devices, local(): held = lax.all_to_all(sent, AXIS, split_axis=0, concat_axis=0, tiled=True)  3.84 us
    pallas_call x1, Pallas kernels, local(): pl.pallas_call(functools.partial(main_kernel, scale), out_shape=(outside(...  3.65 us
    ppermute x1, starting transfers between devices, local(): edge_core = lax.ppermute(edge(1 - core), AXIS, core_pairs)  3.33 us
  transfers between devices with their start and end apart: 15, of which 8 were waited for; matrix products, arithmetic and copies ran while one was open for 4% of the time, Pallas kernels for 15%

profile of v8, /device:TPU:0, one launch (start us, length us, event | category | flops | bytes accessed | tf_op | source)
XLA Modules:
  0.0 64.5 jit_solution(15472964334163027565)
XLA Ops:
  0.7 1.4 %reshape.43 = bf16[64,16,128]{2,1,0:T(8,128)(2,1)S(1)} reshape(bf16[64,32,64]{2,1,0:T(8,128)(2,1)} %param.6) | data formatting | bytes 524288 | tf_op jit(solution)/shard_map/reshape | solution.py:529
  2.8 7.4 %all-to-all-start = ((bf16[16,64,128]{2,1,0:T(8,128)(2,1)}), bf16[16,64,128]{2,1,0:T(8,128)(2,1)S(1)}, u32[]{:S(2)}, u32[]{:S(2)}) async-start(bf16[16,64,128]{2,1,0:T(8,128)(2,1)} %bitcast.12), calls=%async_computation | async-start | bytes 524288 | tf_op jit(solution)/shard_map/all_to_all | solution.py:530
  11.0 3.3 %collective-permute-start.2 = (bf16[128,768]{1,0:T(8,128)(2,1)S(1)}, bf16[128,768]{1,0:T(8,128)(2,1)S(1)}, u32[]{:S(2)}, u32[]{:S(2)}) collective-permute-start(bf16[128,768]{1,0:T(8,128)(2,1)S(1)} %get-tuple-element.90), channel_id=1, source_target_pairs={{0,1},{1,0},{2,3},{3,2},{4,5},{5,4},{6,7},{7,6},{8,9},{9,8},{10,11... | collective-permute-start | bytes 589832 | tf_op jit(solution)/shard_map/ppermute | solution.py:542
  14.4 2.0 %prepare.1 = (bf16[384,1024]{1,0:T(8,128)(2,1)S(1)}, bf16[256,512]{1,0:T(8,128)(2,1)}, bf16[192,576]{1,0:T(8,128)(2,1)}, bf16[192,576]{1,0:T(8,128)(2,1)}, bf16[...) custom-call(bf16[128,256]{1,0:T(8,128)(2,1)S(1)} %bitcast.18, ...), custom_call_target="tpu_custom_call" | custom-call | flops 1840000000 | bytes 1000000 | tf_op jit(solution)/shard_map/prepare/pallas_call | solution.py:544
  16.4 3.8 %all-to-all-done = bf16[16,64,128]{2,1,0:T(8,128)(2,1)S(1)} async-done(((bf16[16,64,128]{2,1,0:T(8,128)(2,1)}), bf16[16,64,128]{2,1,0:T(8,128)(2,1)S(1)}, u32[]{:S(2)}, u32[]{:S(2)}) %all-to-all-start) | async-done | bytes 262176 | tf_op jit(solution)/shard_map/all_to_all | solution.py:530
  20.9 2.7 %edges.1 = (bf16[1152,1024]{1,0:T(8,128)(2,1)S(1)}, f32[256,1024]{1,0:T(8,128)S(1)}) custom-call(bf16[128,768]{1,0:T(8,128)(2,1)S(1)} %collective-permute-done.2.core_ref.edge_ref, bf16[128,768]{1,0:T(8,128)(2,1)S(1)} %collective-permute-done.1.cross_ref.edge_ref, bf16[8,64,128]{2,1,0:T(8,128)(2,1)S(1)} %copy-done.2, ...), custom_call_target="tpu_custom_call" | custom-call | flops 3000000000 | bytes 1000000 | tf_op jit(solution)/shard_map/edges/pallas_call | solution.py:565
  23.6 4.0 %inner.1 = (bf16[768,1024]{1,0:T(8,128)(2,1)S(1)}, f32[128,1024]{1,0:T(8,128)S(1)}, f32[256,1024]{1,0:T(8,128)S(1)}, bf16[64,1024]{1,0:T(8,128)(2,1)S(1)}, f32[1...) custom-call(bf16[128,768]{1,0:T(8,128)(2,1)S(1)} %collective-permute, ...), custom_call_target="tpu_custom_call" | custom-call | flops 4000000000 | bytes 1000000 | tf_op jit(solution)/shard_map/inner/pallas_call | solution.py:575
  27.6 3.7 %section.1 = (bf16[64,2048]{1,0:T(8,128)(2,1)}, bf16[128,256]{1,0:T(8,128)(2,1)}, bf16[16,64,128]{2,1,0:T(8,128)(2,1)}, f32[1152,128]{1,0:T(8,128)S(1)}, bf16[1152,128]{1,0:T(8,128)(2,1)S(1)}) custom-call(bf16[8,2,64,128]{3,2,1,0:T(8,128)(2,1)S(1)} %bitcast.19, bf16[64,2048]{1,0:T(8,128)(2,1)S(1)} %bitcast.15, ...), custom_call_target="tpu_custom_call" | custom-call | flops 8280000000 | bytes 1000000 | tf_op jit(solution)/shard_map/section/pallas_call | solution.py:600
  31.3 1.9 %collective-permute-start.4 = (bf16[1152,128]{1,0:T(8,128)(2,1)S(1)}, bf16[1152,128]{1,0:T(8,128)(2,1)S(1)}, u32[]{:S(2)}, u32[]{:S(2)}) collective-permute-start(bf16[1152,128]{1,0:T(8,128)(2,1)S(1)} %get-tuple-element.64), channel_id=1, source_target_pairs={{0,1},{1,0},{2,3},{3,2},{4,5},{5,4},{6,7},{7,6},{8,9},{9,8},{10,11... | collective-permute-start | bytes 884744 | tf_op jit(solution)/shard_map/ppermute | solution.py:484
  33.1 4.2 %all-to-all-start.1 = ((bf16[16,64,128]{2,1,0:T(8,128)(2,1)}), bf16[16,64,128]{2,1,0:T(8,128)(2,1)S(1)}, u32[]{:S(2)}, u32[]{:S(2)}) async-start(bf16[16,64,128]{2,1,0:T(8,128)(2,1)} %get-tuple-element.65), calls=%async_computation.1 | async-start | bytes 524288 | tf_op jit(solution)/shard_map/all_to_all | solution.py:649
  37.5 2.0 %collective-permute-start.5 = (bf16[288,128]{1,0:T(8,128)(2,1)S(1)}, bf16[288,128]{1,0:T(8,128)(2,1)S(1)}, u32[]{:S(2)}, u32[]{:S(2)}) collective-permute-start(bf16[288,128]{1,0:T(8,128)(2,1)S(1)} %get-tuple-element.83), channel_id=1, source_target_pairs={{0,2},{1,3},{2,0},{3,1},{4,6},{5,7},{6,4},{7,5},{8,10},{9,11},{10,... | collective-permute-start | bytes 221192 | tf_op jit(solution)/shard_map/ppermute | solution.py:484
  39.5 1.5 %collective-permute-start.6 = (bf16[288,128]{1,0:T(8,128)(2,1)S(1)}, bf16[288,128]{1,0:T(8,128)(2,1)S(1)}, u32[]{:S(2)}, u32[]{:S(2)}) collective-permute-start(bf16[288,128]{1,0:T(8,128)(2,1)S(1)} %get-tuple-element.85), channel_id=1, source_target_pairs={{0,4},{1,5},{2,6},{3,7},{4,0},{5,1},{6,2},{7,3},{8,12},{9,13},{10,... | collective-permute-start | bytes 221192 | tf_op jit(solution)/shard_map/ppermute | solution.py:484
  41.0 2.8 %collective-permute-done.5 = bf16[288,128]{1,0:T(8,128)(2,1)S(1)} collective-permute-done((bf16[288,128]{1,0:T(8,128)(2,1)S(1)}, bf16[288,128]{1,0:T(8,128)(2,1)S(1)}, u32[]{:S(2)}, u32[]{:S(2)}) %collective-permute-start.5) | collective-permute-done | bytes 73760 | tf_op jit(solution)/shard_map/ppermute | solution.py:484
  43.8 2.6 %collective-permute-done.6 = bf16[288,128]{1,0:T(8,128)(2,1)S(1)} collective-permute-done((bf16[288,128]{1,0:T(8,128)(2,1)S(1)}, bf16[288,128]{1,0:T(8,128)(2,1)S(1)}, u32[]{:S(2)}, u32[]{:S(2)}) %collective-permute-start.6) | collective-permute-done | bytes 73760 | tf_op jit(solution)/shard_map/ppermute | solution.py:484
  46.4 2.3 %collective-permute-done.7 = bf16[288,128]{1,0:T(8,128)(2,1)S(1)} collective-permute-done((bf16[288,128]{1,0:T(8,128)(2,1)S(1)}, bf16[288,128]{1,0:T(8,128)(2,1)S(1)}, u32[]{:S(2)}, u32[]{:S(2)}) %collective-permute-start.7) | collective-permute-done | bytes 73760 | tf_op jit(solution)/shard_map/ppermute | solution.py:484
  48.8 2.4 %collective-permute-start.8 = (bf16[288,128]{1,0:T(8,128)(2,1)S(1)}, bf16[288,128]{1,0:T(8,128)(2,1)S(1)}, u32[]{:S(2)}, u32[]{:S(2)}) collective-permute-start(bf16[288,128]{1,0:T(8,128)(2,1)S(1)} %fusion.1), channel_id=1, source_target_pairs={{0,8},{1,9},{2,10},{3,11},{4,12},{5,13},{6,14},{7,15},{8,0},{9,1},... | collective-permute-start | bytes 221192 | tf_op jit(solution)/shard_map/ppermute | solution.py:484
  51.2 3.9 %collective-permute-done.8 = bf16[288,128]{1,0:T(8,128)(2,1)S(1)} collective-permute-done((bf16[288,128]{1,0:T(8,128)(2,1)S(1)}, bf16[288,128]{1,0:T(8,128)(2,1)S(1)}, u32[]{:S(2)}, u32[]{:S(2)}) %collective-permute-start.8) | collective-permute-done | bytes 73760 | tf_op jit(solution)/shard_map/ppermute | solution.py:484
  55.2 2.2 %collective-permute-start.11 = (bf16[288,128]{1,0:T(8,128)(2,1)S(1)}, bf16[288,128]{1,0:T(8,128)(2,1)S(1)}, u32[]{:S(2)}, u32[]{:S(2)}) collective-permute-start(bf16[288,128]{1,0:T(8,128)(2,1)S(1)} %add_convert_fusion), channel_id=1, source_target_pairs={{0,6},{1,7},{2,4},{3,5},{4,2},{5,3},{6,0},{7,1},{8,14},{9,15},{10,... | collective-permute-start | bytes 221192 | tf_op jit(solution)/shard_map/ppermute | solution.py:484
  57.4 1.3 %collective-permute-start.9 = (bf16[288,128]{1,0:T(8,128)(2,1)S(1)}, bf16[288,128]{1,0:T(8,128)(2,1)S(1)}, u32[]{:S(2)}, u32[]{:S(2)}) collective-permute-start(bf16[288,128]{1,0:T(8,128)(2,1)S(1)} %add_convert_fusion), channel_id=1, source_target_pairs={{0,2},{1,3},{2,0},{3,1},{4,6},{5,7},{6,4},{7,5},{8,10},{9,11},{10,... | collective-permute-start | bytes 221192 | tf_op jit(solution)/shard_map/ppermute | solution.py:484
  58.7 0.9 %reshape.49 = bf16[64,2,1024]{2,1,0:T(2,128)(2,1)} reshape(bf16[64,2048]{1,0:T(8,128)(2,1)S(1)} %copy-done.4) | data formatting | bytes 524288 | tf_op jit(solution)/shard_map/reshape | solution.py:653
  59.8 1.1 %reshape.51 = bf16[64,32,64]{2,1,0:T(8,128)(2,1)} reshape(bf16[64,16,128]{2,1,0:T(8,128)(2,1)S(1)} %copy.14) | data formatting | bytes 524288 | tf_op jit(solution)/shard_map/reshape | solution.py:655
  60.9 0.8 %collective-permute-done.9 = bf16[288,128]{1,0:T(8,128)(2,1)S(1)} collective-permute-done((bf16[288,128]{1,0:T(8,128)(2,1)S(1)}, bf16[288,128]{1,0:T(8,128)(2,1)S(1)}, u32[]{:S(2)}, u32[]{:S(2)}) %collective-permute-start.9) | collective-permute-done | bytes 73760 | tf_op jit(solution)/shard_map/ppermute | solution.py:484
  61.9 0.9 %finish.2 = (f32[54,32,128]{2,1,0:T(8,128)}, f32[16,32,128]{2,1,0:T(8,128)}) custom-call(bf16[1152,128]{1,0:T(8,128)(2,1)S(1)} %constant_dynamic-update-slice_fusion.value_ref), custom_call_target="tpu_custom_call" | custom-call | flops 1200000000 | bytes 1000000 | tf_op jit(solution)/shard_map/finish/pallas_call | solution.py:504
  63.5 0.9 %finish.3 = (f32[54,32,128]{2,1,0:T(8,128)}, f32[16,32,128]{2,1,0:T(8,128)}) custom-call(bf16[1152,128]{1,0:T(8,128)(2,1)S(1)} %collective-permute-done.12.value_ref, f32[54,32,128]{2,1,0:T(8,128)} %get-tuple-element.77.refs_0_, f32[16,32,128]{2,1,0:T(8,128)} %get-tuple-element.78.refs_1_), custom_call_target="tpu_custom_call", output_to_operand_aliasing={{0}: (1, {}), {1}: (2, {})} | custom-call | flops 1200000000 | bytes 1000000 | tf_op jit(solution)/shard_map/finish/pallas_call | solution.py:504
  (38 shorter events, 3.7 us)
Async XLA Ops:
  0.6 9.6 %copy-start.3 = (bf16[64,2,1024]{2,1,0:T(2,128)(2,1)S(1)}, bf16[64,2,1024]{2,1,0:T(2,128)(2,1)}, u32[]{:S(2)}) copy-start(bf16[64,2,1024]{2,1,0:T(2,128)(2,1)} %param.7) | copy-start | bytes 786436
  0.6 9.7 %copy-start = (bf16[128,1,256]{2,0,1:T(8,128)(2,1)S(1)}, bf16[128,1,256]{2,0,1:T(8,128)(2,1)}, u32[]{:S(2)}) copy-start(bf16[128,1,256]{2,0,1:T(8,128)(2,1)} %param.5) | copy-start | bytes 196612
  2.0 12.3 %copy-start.1 = (bf16[27,64,128]{2,1,0:T(8,128)(2,1)S(1)}, bf16[27,64,128]{2,1,0:T(8,128)(2,1)}, u32[]{:S(2)}) copy-start(bf16[27,64,128]{2,1,0:T(8,128)(2,1)} %wc_ref.1) | copy-start | bytes 1327108
  2.0 12.3 %copy-start.2 = (bf16[8,64,128]{2,1,0:T(8,128)(2,1)S(1)}, bf16[8,64,128]{2,1,0:T(8,128)(2,1)}, u32[]{:S(2)}) copy-start(bf16[8,64,128]{2,1,0:T(8,128)(2,1)} %wup_ref.3) | copy-start | bytes 393220
  2.8 17.4 %all-to-all-start = ((bf16[16,64,128]{2,1,0:T(8,128)(2,1)}), bf16[16,64,128]{2,1,0:T(8,128)(2,1)S(1)}, u32[]{:S(2)}, u32[]{:S(2)}) async-start(bf16[16,64,128]{2,1,0:T(8,128)(2,1)} %bitcast.12), calls=%async_computation | async-start | bytes 524288 | tf_op jit(solution)/shard_map/all_to_all | solution.py:530
  10.3 10.6 %collective-permute-start.1 = (bf16[128,768]{1,0:T(8,128)(2,1)S(1)}, bf16[128,768]{1,0:T(8,128)(2,1)S(1)}, u32[]{:S(2)}, u32[]{:S(2)}) collective-permute-start(bf16[128,768]{1,0:T(8,128)(2,1)S(1)} %get-tuple-element.91), channel_id=1, source_target_pairs={{1,2},{2,1},{3,4},{4,3},{5,6},{6,5},{7,8},{8,7},{9,10},{10,9},{11,... | collective-permute-start | bytes 589832 | tf_op jit(solution)/shard_map/ppermute | solution.py:543
  11.0 9.9 %collective-permute-start.2 = (bf16[128,768]{1,0:T(8,128)(2,1)S(1)}, bf16[128,768]{1,0:T(8,128)(2,1)S(1)}, u32[]{:S(2)}, u32[]{:S(2)}) collective-permute-start(bf16[128,768]{1,0:T(8,128)(2,1)S(1)} %get-tuple-element.90), channel_id=1, source_target_pairs={{0,1},{1,0},{2,3},{3,2},{4,5},{5,4},{6,7},{7,6},{8,9},{9,8},{10,11... | collective-permute-start | bytes 589832 | tf_op jit(solution)/shard_map/ppermute | solution.py:542
  20.2 3.4 %collective-permute-start.3 = (bf16[16,64,128]{2,1,0:T(8,128)(2,1)S(1)}, bf16[16,64,128]{2,1,0:T(8,128)(2,1)S(1)}, u32[]{:S(2)}, u32[]{:S(2)}) collective-permute-start(bf16[16,64,128]{2,1,0:T(8,128)(2,1)S(1)} %all-to-all-done), channel_id=1, source_target_pairs={{0,1},{1,0},{2,3},{3,2},{4,5},{5,4},{6,7},{7,6},{8,9},{9,8},{10,11... | collective-permute-start | bytes 786440 | tf_op jit(solution)/shard_map/ppermute | solution.py:562
  20.2 7.4 %collective-permute-start = (bf16[16,64,128]{2,1,0:T(8,128)(2,1)S(1)}, bf16[16,64,128]{2,1,0:T(8,128)(2,1)S(1)}, u32[]{:S(2)}, u32[]{:S(2)}) collective-permute-start(bf16[16,64,128]{2,1,0:T(8,128)(2,1)S(1)} %all-to-all-done), channel_id=1, source_target_pairs={{1,2},{2,1},{3,4},{4,3},{5,6},{6,5},{7,8},{8,7},{9,10},{10,9},{11,... | collective-permute-start | bytes 786440 | tf_op jit(solution)/shard_map/ppermute | solution.py:563
  31.3 6.1 %collective-permute-start.4 = (bf16[1152,128]{1,0:T(8,128)(2,1)S(1)}, bf16[1152,128]{1,0:T(8,128)(2,1)S(1)}, u32[]{:S(2)}, u32[]{:S(2)}) collective-permute-start(bf16[1152,128]{1,0:T(8,128)(2,1)S(1)} %get-tuple-element.64), channel_id=1, source_target_pairs={{0,1},{1,0},{2,3},{3,2},{4,5},{5,4},{6,7},{7,6},{8,9},{9,8},{10,11... | collective-permute-start | bytes 884744 | tf_op jit(solution)/shard_map/ppermute | solution.py:484
  33.1 15.6 %all-to-all-start.1 = ((bf16[16,64,128]{2,1,0:T(8,128)(2,1)}), bf16[16,64,128]{2,1,0:T(8,128)(2,1)S(1)}, u32[]{:S(2)}, u32[]{:S(2)}) async-start(bf16[16,64,128]{2,1,0:T(8,128)(2,1)} %get-tuple-element.65), calls=%async_computation.1 | async-start | bytes 524288 | tf_op jit(solution)/shard_map/all_to_all | solution.py:649
  37.3 21.4 %copy-start.4 = (bf16[64,2048]{1,0:T(8,128)(2,1)S(1)}, bf16[64,2048]{1,0:T(8,128)(2,1)}, u32[]{:S(2)}) copy-start(bf16[64,2048]{1,0:T(8,128)(2,1)} %get-tuple-element.67) | copy-start | bytes 786436
  37.5 6.4 %collective-permute-start.5 = (bf16[288,128]{1,0:T(8,128)(2,1)S(1)}, bf16[288,128]{1,0:T(8,128)(2,1)S(1)}, u32[]{:S(2)}, u32[]{:S(2)}) collective-permute-start(bf16[288,128]{1,0:T(8,128)(2,1)S(1)} %get-tuple-element.83), channel_id=1, source_target_pairs={{0,2},{1,3},{2,0},{3,1},{4,6},{5,7},{6,4},{7,5},{8,10},{9,11},{10,... | collective-permute-start | bytes 221192 | tf_op jit(solution)/shard_map/ppermute | solution.py:484
  39.5 6.9 %collective-permute-start.6 = (bf16[288,128]{1,0:T(8,128)(2,1)S(1)}, bf16[288,128]{1,0:T(8,128)(2,1)S(1)}, u32[]{:S(2)}, u32[]{:S(2)}) collective-permute-start(bf16[288,128]{1,0:T(8,128)(2,1)S(1)} %get-tuple-element.85), channel_id=1, source_target_pairs={{0,4},{1,5},{2,6},{3,7},{4,0},{5,1},{6,2},{7,3},{8,12},{9,13},{10,... | collective-permute-start | bytes 221192 | tf_op jit(solution)/shard_map/ppermute | solution.py:484
  40.9 7.8 %collective-permute-start.7 = (bf16[288,128]{1,0:T(8,128)(2,1)S(1)}, bf16[288,128]{1,0:T(8,128)(2,1)S(1)}, u32[]{:S(2)}, u32[]{:S(2)}) collective-permute-start(bf16[288,128]{1,0:T(8,128)(2,1)S(1)} %get-tuple-element.84), channel_id=1, source_target_pairs={{0,6},{1,7},{2,4},{3,5},{4,2},{5,3},{6,0},{7,1},{8,14},{9,15},{10,... | collective-permute-start | bytes 221192 | tf_op jit(solution)/shard_map/ppermute | solution.py:484
  48.8 6.4 %collective-permute-start.8 = (bf16[288,128]{1,0:T(8,128)(2,1)S(1)}, bf16[288,128]{1,0:T(8,128)(2,1)S(1)}, u32[]{:S(2)}, u32[]{:S(2)}) collective-permute-start(bf16[288,128]{1,0:T(8,128)(2,1)S(1)} %fusion.1), channel_id=1, source_target_pairs={{0,8},{1,9},{2,10},{3,11},{4,12},{5,13},{6,14},{7,15},{8,0},{9,1},... | collective-permute-start | bytes 221192 | tf_op jit(solution)/shard_map/ppermute | solution.py:484
  55.2 5.7 %collective-permute-start.10 = (bf16[288,128]{1,0:T(8,128)(2,1)S(1)}, bf16[288,128]{1,0:T(8,128)(2,1)S(1)}, u32[]{:S(2)}, u32[]{:S(2)}) collective-permute-start(bf16[288,128]{1,0:T(8,128)(2,1)S(1)} %add_convert_fusion), channel_id=1, source_target_pairs={{0,4},{1,5},{2,6},{3,7},{4,0},{5,1},{6,2},{7,3},{8,12},{9,13},{10,... | collective-permute-start | bytes 221192 | tf_op jit(solution)/shard_map/ppermute | solution.py:484
  55.2 5.7 %collective-permute-start.11 = (bf16[288,128]{1,0:T(8,128)(2,1)S(1)}, bf16[288,128]{1,0:T(8,128)(2,1)S(1)}, u32[]{:S(2)}, u32[]{:S(2)}) collective-permute-start(bf16[288,128]{1,0:T(8,128)(2,1)S(1)} %add_convert_fusion), channel_id=1, source_target_pairs={{0,6},{1,7},{2,4},{3,5},{4,2},{5,3},{6,0},{7,1},{8,14},{9,15},{10,... | collective-permute-start | bytes 221192 | tf_op jit(solution)/shard_map/ppermute | solution.py:484
  57.4 4.4 %collective-permute-start.9 = (bf16[288,128]{1,0:T(8,128)(2,1)S(1)}, bf16[288,128]{1,0:T(8,128)(2,1)S(1)}, u32[]{:S(2)}, u32[]{:S(2)}) collective-permute-start(bf16[288,128]{1,0:T(8,128)(2,1)S(1)} %add_convert_fusion), channel_id=1, source_target_pairs={{0,2},{1,3},{2,0},{3,1},{4,6},{5,7},{6,4},{7,5},{8,10},{9,11},{10,... | collective-permute-start | bytes 221192 | tf_op jit(solution)/shard_map/ppermute | solution.py:484
  61.8 1.6 %collective-permute-start.12 = (bf16[1152,128]{1,0:T(8,128)(2,1)S(1)}, bf16[1152,128]{1,0:T(8,128)(2,1)S(1)}, u32[]{:S(2)}, u32[]{:S(2)}) collective-permute-start(bf16[1152,128]{1,0:T(8,128)(2,1)S(1)} %constant_dynamic-update-slice_fusion.value_ref), channel_id=1, source_target_pairs={{0,1},{1,0},{2,3},{3,2},{4,5},{5,4},{6,7},{7,6},{8,9},{9,8},{10,11... | collective-permute-start | bytes 884744 | tf_op jit(solution)/shard_map/ppermute | solution.py:484

commit v9 on v8

--- a/solution.py
+++ b/solution.py
@@ -486,7 +486,7 @@
     summed = keep + swap(send, 1).astype(F32)
     rounded = summed.astype(BF16)
     total = summed[:288]
-    for k in (1, 2, 3):
+    for k in (1, 3, 2):
         total = total + swap(rounded[k * 288 : (k + 1) * 288], 2 * k).astype(F32)
     total, back = lax.optimization_barrier((total, back))
     bit = 8
@@ -495,9 +495,11 @@
         total = own.astype(F32) + swap(own, bit).astype(F32)
         bit *= 2
     own = total.astype(BF16)
-    pieces = [own] + [swap(own, 2 * k) for k in (1, 2, 3)]
-    pieces, others = lax.optimization_barrier((pieces, finish_others(back)))
-    mine = jnp.concatenate(pieces, axis=0)
+    gathered = {k: swap(own, 2 * k) for k in (1, 3, 2)}
+    arrived = [gathered[k] for k in (1, 2, 3)]
+    arrived, own, others = lax.optimization_barrier((arrived, own, finish_others(back)))
+    gathered = dict(zip((1, 2, 3), arrived))
+    mine = jnp.concatenate([own] + [gathered[k] for k in (1, 2, 3)], axis=0)
     other = swap(mine, 1)
     sums = ()
     for first, value in ((True, mine), (False, other)):
@@ -559,8 +561,9 @@
         name="prepare",
     )(coarse, w_up, w_conv)
     held, wf_up = lax.optimization_barrier((held, wf_up))
-    held_core = lax.ppermute(held, AXIS, core_pairs)
     held_cross = lax.ppermute(held, AXIS, cross_pairs)
+    later, edge_core, edge_cross = lax.optimization_barrier((held, edge_core, edge_cross))
+    held_core = lax.ppermute(later, AXIS, core_pairs)
     held, held_core, held_cross = [v.reshape(8, 2, 64, 128) for v in (held, held_core, held_cross)]
     xu, pre_up = pl.pallas_call(
         edge_kernel,

time: 64.9 us -> 64.5 us (level)
  starting transfers between devices: 27.7 us -> 24.5 us
  waiting for transfers between devices: 17.1 us -> 19.8 us
    ppermute x1, starting transfers between devices: 3.33 us -> 0.46 us  [local(): edge_core = lax.ppermute(edge(1 - core), AXIS, core_pairs)]
    all_to_all x1, waiting for transfers between devices: 3.84 us -> 6.7 us  [local(): held = lax.all_to_all(sent, AXIS, split_axis=0, concat_axis=0, tiled=True)]
    ppermute x9, starting transfers between devices: 11.5 us -> 9.68 us  [swap(): return lax.ppermute(value, AXIS, [(i, i ^ bit) for i in range(n)])]
    ppermute x1, starting transfers between devices: 0.01 us -> 1.17 us  [local(): held_core = lax.ppermute(later, AXIS, core_pairs)]
where the time goes in v9:
time: 64.5 us; the launch traced here: 64.1 us
  starting transfers between devices  24.5 us (38%)
  waiting for transfers between devices  19.8 us (31%)
  Pallas kernels  14.1 us (22%)
  local copies, waits for them, and re-layouts  4.42 us (7%)
  between operations  1.08 us (2%)
    ppermute x9, waiting for transfers between devices, swap(): return lax.ppermute(value, AXIS, [(i, i ^ bit) for i in range(n)])  13.1 us
    ppermute x9, starting transfers between devices, swap(): return lax.ppermute(value, AXIS, [(i, i ^ bit) for i in range(n)])  9.68 us
    all_to_all x1, starting transfers between devices, local(): held = lax.all_to_all(sent, AXIS, split_axis=0, concat_axis=0, tiled=True)  7.36 us
    all_to_all x1, waiting for transfers between devices, local(): held = lax.all_to_all(sent, AXIS, split_axis=0, concat_axis=0, tiled=True)  6.7 us
    all_to_all x1, starting transfers between devices, local(): lax.all_to_all(skip_part, AXIS, split_axis=0, concat_axis=0, tiled=True)  4.56 us
    pallas_call x1, Pallas kernels, local(): pl.pallas_call(inner_kernel, out_shape=(inside((768, 1024)), inside((128,...  3.98 us
    pallas_call x1, Pallas kernels, local(): pl.pallas_call(functools.partial(main_kernel, scale), out_shape=(outside(...  3.65 us
    pallas_call x1, Pallas kernels, local(): pl.pallas_call(edge_kernel, out_shape=(inside((1152, 1024)), inside((256,...  2.66 us
  transfers between devices with their start and end apart: 15, of which 8 were waited for; matrix products, arithmetic and copies ran while one was open for 4% of the time, Pallas kernels for 15%

profile of v9, /device:TPU:0, one launch (start us, length us, event | category | flops | bytes accessed | tf_op | source)
XLA Modules:
  0.0 64.1 jit_solution(10107198727196774344)
XLA Ops:
  0.7 1.4 %reshape.43 = bf16[64,16,128]{2,1,0:T(8,128)(2,1)S(1)} reshape(bf16[64,32,64]{2,1,0:T(8,128)(2,1)} %param.6) | data formatting | bytes 524288 | tf_op jit(solution)/shard_map/reshape | solution.py:531
  2.0 0.8 %copy.17 = bf16[64,16,128]{2,0,1:T(8,128)(2,1)} copy(bf16[64,16,128]{2,1,0:T(8,128)(2,1)S(1)} %reshape.43) | data formatting | bytes 524288 | tf_op jit(solution)/shard_map/reshape | solution.py:531
  2.8 7.4 %all-to-all-start = ((bf16[16,64,128]{2,1,0:T(8,128)(2,1)}), bf16[16,64,128]{2,1,0:T(8,128)(2,1)S(1)}, u32[]{:S(2)}, u32[]{:S(2)}) async-start(bf16[16,64,128]{2,1,0:T(8,128)(2,1)} %bitcast.12), calls=%async_computation | async-start | bytes 524288 | tf_op jit(solution)/shard_map/all_to_all | solution.py:532
  11.5 2.0 %prepare.1 = (bf16[384,1024]{1,0:T(8,128)(2,1)S(1)}, bf16[256,512]{1,0:T(8,128)(2,1)}, bf16[192,576]{1,0:T(8,128)(2,1)}, bf16[192,576]{1,0:T(8,128)(2,1)}, bf16[...) custom-call(bf16[128,256]{1,0:T(8,128)(2,1)S(1)} %bitcast.18, ...), custom_call_target="tpu_custom_call" | custom-call | flops 1840000000 | bytes 1000000 | tf_op jit(solution)/shard_map/prepare/pallas_call | solution.py:546
  13.5 6.7 %all-to-all-done = bf16[16,64,128]{2,1,0:T(8,128)(2,1)S(1)} async-done(((bf16[16,64,128]{2,1,0:T(8,128)(2,1)}), bf16[16,64,128]{2,1,0:T(8,128)(2,1)S(1)}, u32[]{:S(2)}, u32[]{:S(2)}) %all-to-all-start) | async-done | bytes 262176 | tf_op jit(solution)/shard_map/all_to_all | solution.py:532
  20.9 1.2 %collective-permute-start.3 = (bf16[16,64,128]{2,1,0:T(8,128)(2,1)S(1)}, bf16[16,64,128]{2,1,0:T(8,128)(2,1)S(1)}, u32[]{:S(2)}, u32[]{:S(2)}) collective-permute-start(bf16[16,64,128]{2,1,0:T(8,128)(2,1)S(1)} %all-to-all-done), channel_id=1, source_target_pairs={{0,1},{1,0},{2,3},{3,2},{4,5},{5,4},{6,7},{7,6},{8,9},{9,8},{10,11... | collective-permute-start | bytes 786440 | tf_op jit(solution)/shard_map/ppermute | solution.py:566
  22.1 2.7 %edges.1 = (bf16[1152,1024]{1,0:T(8,128)(2,1)S(1)}, f32[256,1024]{1,0:T(8,128)S(1)}) custom-call(bf16[128,768]{1,0:T(8,128)(2,1)S(1)} %collective-permute-done.1.core_ref.edge_ref, bf16[128,768]{1,0:T(8,128)(2,1)S(1)} %collective-permute-done.2.cross_ref.edge_ref, bf16[8,64,128]{2,1,0:T(8,128)(2,1)S(1)} %copy-done.2, ...), custom_call_target="tpu_custom_call" | custom-call | flops 3000000000 | bytes 1000000 | tf_op jit(solution)/shard_map/edges/pallas_call | solution.py:568
  24.8 4.0 %inner.1 = (bf16[768,1024]{1,0:T(8,128)(2,1)S(1)}, f32[128,1024]{1,0:T(8,128)S(1)}, f32[256,1024]{1,0:T(8,128)S(1)}, bf16[64,1024]{1,0:T(8,128)(2,1)S(1)}, f32[1...) custom-call(bf16[128,768]{1,0:T(8,128)(2,1)S(1)} %collective-permute, ...), custom_call_target="tpu_custom_call" | custom-call | flops 4000000000 | bytes 1000000 | tf_op jit(solution)/shard_map/inner/pallas_call | solution.py:578
  28.8 3.6 %section.1 = (bf16[64,2048]{1,0:T(8,128)(2,1)}, bf16[128,256]{1,0:T(8,128)(2,1)}, bf16[16,64,128]{2,1,0:T(8,128)(2,1)}, f32[1152,128]{1,0:T(8,128)S(1)}, bf16[1152,128]{1,0:T(8,128)(2,1)S(1)}) custom-call(bf16[8,2,64,128]{3,2,1,0:T(8,128)(2,1)S(1)} %bitcast.19, bf16[64,2048]{1,0:T(8,128)(2,1)S(1)} %bitcast.15, ...), custom_call_target="tpu_custom_call" | custom-call | flops 8280000000 | bytes 1000000 | tf_op jit(solution)/shard_map/section/pallas_call | solution.py:603
  32.5 4.6 %all-to-all-start.1 = ((bf16[16,64,128]{2,1,0:T(8,128)(2,1)}), bf16[16,64,128]{2,1,0:T(8,128)(2,1)S(1)}, u32[]{:S(2)}, u32[]{:S(2)}) async-start(bf16[16,64,128]{2,1,0:T(8,128)(2,1)} %get-tuple-element.71), calls=%async_computation.1 | async-start | bytes 524288 | tf_op jit(solution)/shard_map/all_to_all | solution.py:652
  37.2 2.0 %collective-permute-start.5 = (bf16[288,128]{1,0:T(8,128)(2,1)S(1)}, bf16[288,128]{1,0:T(8,128)(2,1)S(1)}, u32[]{:S(2)}, u32[]{:S(2)}) collective-permute-start(bf16[288,128]{1,0:T(8,128)(2,1)S(1)} %get-tuple-element.89), channel_id=1, source_target_pairs={{0,2},{1,3},{2,0},{3,1},{4,6},{5,7},{6,4},{7,5},{8,10},{9,11},{10,... | collective-permute-start | bytes 221192 | tf_op jit(solution)/shard_map/ppermute | solution.py:484
  39.2 1.5 %collective-permute-start.6 = (bf16[288,128]{1,0:T(8,128)(2,1)S(1)}, bf16[288,128]{1,0:T(8,128)(2,1)S(1)}, u32[]{:S(2)}, u32[]{:S(2)}) collective-permute-start(bf16[288,128]{1,0:T(8,128)(2,1)S(1)} %get-tuple-element.91), channel_id=1, source_target_pairs={{0,6},{1,7},{2,4},{3,5},{4,2},{5,3},{6,0},{7,1},{8,14},{9,15},{10,... | collective-permute-start | bytes 221192 | tf_op jit(solution)/shard_map/ppermute | solution.py:484
  40.8 3.2 %collective-permute-done.5 = bf16[288,128]{1,0:T(8,128)(2,1)S(1)} collective-permute-done((bf16[288,128]{1,0:T(8,128)(2,1)S(1)}, bf16[288,128]{1,0:T(8,128)(2,1)S(1)}, u32[]{:S(2)}, u32[]{:S(2)}) %collective-permute-start.5) | collective-permute-done | bytes 73760 | tf_op jit(solution)/shard_map/ppermute | solution.py:484
  44.0 2.9 %collective-permute-done.6 = bf16[288,128]{1,0:T(8,128)(2,1)S(1)} collective-permute-done((bf16[288,128]{1,0:T(8,128)(2,1)S(1)}, bf16[288,128]{1,0:T(8,128)(2,1)S(1)}, u32[]{:S(2)}, u32[]{:S(2)}) %collective-permute-start.6) | collective-permute-done | bytes 73760 | tf_op jit(solution)/shard_map/ppermute | solution.py:484
  46.9 0.7 %collective-permute-done.7 = bf16[288,128]{1,0:T(8,128)(2,1)S(1)} collective-permute-done((bf16[288,128]{1,0:T(8,128)(2,1)S(1)}, bf16[288,128]{1,0:T(8,128)(2,1)S(1)}, u32[]{:S(2)}, u32[]{:S(2)}) %collective-permute-start.7) | collective-permute-done | bytes 73760 | tf_op jit(solution)/shard_map/ppermute | solution.py:484
  47.6 2.4 %collective-permute-start.8 = (bf16[288,128]{1,0:T(8,128)(2,1)S(1)}, bf16[288,128]{1,0:T(8,128)(2,1)S(1)}, u32[]{:S(2)}, u32[]{:S(2)}) collective-permute-start(bf16[288,128]{1,0:T(8,128)(2,1)S(1)} %fusion.1), channel_id=1, source_target_pairs={{0,8},{1,9},{2,10},{3,11},{4,12},{5,13},{6,14},{7,15},{8,0},{9,1},... | collective-permute-start | bytes 221192 | tf_op jit(solution)/shard_map/ppermute | solution.py:484
  50.1 4.0 %collective-permute-done.8 = bf16[288,128]{1,0:T(8,128)(2,1)S(1)} collective-permute-done((bf16[288,128]{1,0:T(8,128)(2,1)S(1)}, bf16[288,128]{1,0:T(8,128)(2,1)S(1)}, u32[]{:S(2)}, u32[]{:S(2)}) %collective-permute-start.8) | collective-permute-done | bytes 73760 | tf_op jit(solution)/shard_map/ppermute | solution.py:484
  54.2 2.8 %collective-permute-start.11 = (bf16[288,128]{1,0:T(8,128)(2,1)S(1)}, bf16[288,128]{1,0:T(8,128)(2,1)S(1)}, u32[]{:S(2)}, u32[]{:S(2)}) collective-permute-start(bf16[288,128]{1,0:T(8,128)(2,1)S(1)} %add_convert_fusion), channel_id=1, source_target_pairs={{0,6},{1,7},{2,4},{3,5},{4,2},{5,3},{6,0},{7,1},{8,14},{9,15},{10,... | collective-permute-start | bytes 221192 | tf_op jit(solution)/shard_map/ppermute | solution.py:484
  57.6 0.9 %reshape.49 = bf16[64,2,1024]{2,1,0:T(2,128)(2,1)} reshape(bf16[64,2048]{1,0:T(8,128)(2,1)S(1)} %copy-done.4) | data formatting | bytes 524288 | tf_op jit(solution)/shard_map/reshape | solution.py:656
  58.7 1.1 %reshape.51 = bf16[64,32,64]{2,1,0:T(8,128)(2,1)} reshape(bf16[64,16,128]{2,1,0:T(8,128)(2,1)S(1)} %copy.14) | data formatting | bytes 524288 | tf_op jit(solution)/shard_map/reshape | solution.py:658
  60.3 1.1 %collective-permute-done.9 = bf16[288,128]{1,0:T(8,128)(2,1)S(1)} collective-permute-done((bf16[288,128]{1,0:T(8,128)(2,1)S(1)}, bf16[288,128]{1,0:T(8,128)(2,1)S(1)}, u32[]{:S(2)}, u32[]{:S(2)}) %collective-permute-start.9) | collective-permute-done | bytes 73760 | tf_op jit(solution)/shard_map/ppermute | solution.py:484
  61.5 0.9 %finish.2 = (f32[54,32,128]{2,1,0:T(8,128)}, f32[16,32,128]{2,1,0:T(8,128)}) custom-call(bf16[1152,128]{1,0:T(8,128)(2,1)S(1)} %constant_dynamic-update-slice_fusion.value_ref), custom_call_target="tpu_custom_call" | custom-call | flops 1200000000 | bytes 1000000 | tf_op jit(solution)/shard_map/finish/pallas_call | solution.py:506
  62.4 0.7 %collective-permute-done.12.value_ref = bf16[1152,128]{1,0:T(8,128)(2,1)S(1)} collective-permute-done((bf16[1152,128]{1,0:T(8,128)(2,1)S(1)}, bf16[1152,128]{1,0:T(8,128)(2,1)S(1)}, u32[]{:S(2)}, u32[]{:S(2)}) %collective-permute-start.12) | collective-permute-done | bytes 294944 | tf_op jit(solution)/shard_map/ppermute | solution.py:484
  63.1 0.9 %finish.3 = (f32[54,32,128]{2,1,0:T(8,128)}, f32[16,32,128]{2,1,0:T(8,128)}) custom-call(bf16[1152,128]{1,0:T(8,128)(2,1)S(1)} %collective-permute-done.12.value_ref, f32[54,32,128]{2,1,0:T(8,128)} %get-tuple-element.83.refs_0_, f32[16,32,128]{2,1,0:T(8,128)} %get-tuple-element.84.refs_1_), custom_call_target="tpu_custom_call", output_to_operand_aliasing={{0}: (1, {}), {1}: (2, {})} | custom-call | flops 1200000000 | bytes 1000000 | tf_op jit(solution)/shard_map/finish/pallas_call | solution.py:506
  (38 shorter events, 3.8 us)
Async XLA Ops:
  0.6 9.6 %copy-start.3 = (bf16[64,2,1024]{2,1,0:T(2,128)(2,1)S(1)}, bf16[64,2,1024]{2,1,0:T(2,128)(2,1)}, u32[]{:S(2)}) copy-start(bf16[64,2,1024]{2,1,0:T(2,128)(2,1)} %param.7) | copy-start | bytes 786436
  0.6 9.7 %copy-start = (bf16[128,1,256]{2,0,1:T(8,128)(2,1)S(1)}, bf16[128,1,256]{2,0,1:T(8,128)(2,1)}, u32[]{:S(2)}) copy-start(bf16[128,1,256]{2,0,1:T(8,128)(2,1)} %param.5) | copy-start | bytes 196612
  2.0 9.5 %copy-start.1 = (bf16[27,64,128]{2,1,0:T(8,128)(2,1)S(1)}, bf16[27,64,128]{2,1,0:T(8,128)(2,1)}, u32[]{:S(2)}) copy-start(bf16[27,64,128]{2,1,0:T(8,128)(2,1)} %wc_ref.1) | copy-start | bytes 1327108
  2.0 9.5 %copy-start.2 = (bf16[8,64,128]{2,1,0:T(8,128)(2,1)S(1)}, bf16[8,64,128]{2,1,0:T(8,128)(2,1)}, u32[]{:S(2)}) copy-start(bf16[8,64,128]{2,1,0:T(8,128)(2,1)} %wup_ref.3) | copy-start | bytes 393220
  2.8 17.4 %all-to-all-start = ((bf16[16,64,128]{2,1,0:T(8,128)(2,1)}), bf16[16,64,128]{2,1,0:T(8,128)(2,1)S(1)}, u32[]{:S(2)}, u32[]{:S(2)}) async-start(bf16[16,64,128]{2,1,0:T(8,128)(2,1)} %bitcast.12), calls=%async_computation | async-start | bytes 524288 | tf_op jit(solution)/shard_map/all_to_all | solution.py:532
  10.3 10.6 %collective-permute-start.1 = (bf16[128,768]{1,0:T(8,128)(2,1)S(1)}, bf16[128,768]{1,0:T(8,128)(2,1)S(1)}, u32[]{:S(2)}, u32[]{:S(2)}) collective-permute-start(bf16[128,768]{1,0:T(8,128)(2,1)S(1)} %get-tuple-element.97), channel_id=1, source_target_pairs={{0,1},{1,0},{2,3},{3,2},{4,5},{5,4},{6,7},{7,6},{8,9},{9,8},{10,11... | collective-permute-start | bytes 589832 | tf_op jit(solution)/shard_map/ppermute | solution.py:544
  10.8 10.1 %collective-permute-start.2 = (bf16[128,768]{1,0:T(8,128)(2,1)S(1)}, bf16[128,768]{1,0:T(8,128)(2,1)S(1)}, u32[]{:S(2)}, u32[]{:S(2)}) collective-permute-start(bf16[128,768]{1,0:T(8,128)(2,1)S(1)} %get-tuple-element.96), channel_id=1, source_target_pairs={{1,2},{2,1},{3,4},{4,3},{5,6},{6,5},{7,8},{8,7},{9,10},{10,9},{11,... | collective-permute-start | bytes 589832 | tf_op jit(solution)/shard_map/ppermute | solution.py:545
  20.2 8.5 %collective-permute-start = (bf16[16,64,128]{2,1,0:T(8,128)(2,1)S(1)}, bf16[16,64,128]{2,1,0:T(8,128)(2,1)S(1)}, u32[]{:S(2)}, u32[]{:S(2)}) collective-permute-start(bf16[16,64,128]{2,1,0:T(8,128)(2,1)S(1)} %all-to-all-done), channel_id=1, source_target_pairs={{1,2},{2,1},{3,4},{4,3},{5,6},{6,5},{7,8},{8,7},{9,10},{10,9},{11,... | collective-permute-start | bytes 786440 | tf_op jit(solution)/shard_map/ppermute | solution.py:564
  20.9 3.8 %collective-permute-start.3 = (bf16[16,64,128]{2,1,0:T(8,128)(2,1)S(1)}, bf16[16,64,128]{2,1,0:T(8,128)(2,1)S(1)}, u32[]{:S(2)}, u32[]{:S(2)}) collective-permute-start(bf16[16,64,128]{2,1,0:T(8,128)(2,1)S(1)} %all-to-all-done), channel_id=1, source_target_pairs={{0,1},{1,0},{2,3},{3,2},{4,5},{5,4},{6,7},{7,6},{8,9},{9,8},{10,11... | collective-permute-start | bytes 786440 | tf_op jit(solution)/shard_map/ppermute | solution.py:566
  32.4 4.7 %collective-permute-start.4 = (bf16[1152,128]{1,0:T(8,128)(2,1)S(1)}, bf16[1152,128]{1,0:T(8,128)(2,1)S(1)}, u32[]{:S(2)}, u32[]{:S(2)}) collective-permute-start(bf16[1152,128]{1,0:T(8,128)(2,1)S(1)} %get-tuple-element.70), channel_id=1, source_target_pairs={{0,1},{1,0},{2,3},{3,2},{4,5},{5,4},{6,7},{7,6},{8,9},{9,8},{10,11... | collective-permute-start | bytes 884744 | tf_op jit(solution)/shard_map/ppermute | solution.py:484
  32.5 15.1 %all-to-all-start.1 = ((bf16[16,64,128]{2,1,0:T(8,128)(2,1)}), bf16[16,64,128]{2,1,0:T(8,128)(2,1)S(1)}, u32[]{:S(2)}, u32[]{:S(2)}) async-start(bf16[16,64,128]{2,1,0:T(8,128)(2,1)} %get-tuple-element.71), calls=%async_computation.1 | async-start | bytes 524288 | tf_op jit(solution)/shard_map/all_to_all | solution.py:652
  37.1 20.6 %copy-start.4 = (bf16[64,2048]{1,0:T(8,128)(2,1)S(1)}, bf16[64,2048]{1,0:T(8,128)(2,1)}, u32[]{:S(2)}) copy-start(bf16[64,2048]{1,0:T(8,128)(2,1)} %get-tuple-element.73) | copy-start | bytes 786436
  37.2 6.8 %collective-permute-start.5 = (bf16[288,128]{1,0:T(8,128)(2,1)S(1)}, bf16[288,128]{1,0:T(8,128)(2,1)S(1)}, u32[]{:S(2)}, u32[]{:S(2)}) collective-permute-start(bf16[288,128]{1,0:T(8,128)(2,1)S(1)} %get-tuple-element.89), channel_id=1, source_target_pairs={{0,2},{1,3},{2,0},{3,1},{4,6},{5,7},{6,4},{7,5},{8,10},{9,11},{10,... | collective-permute-start | bytes 221192 | tf_op jit(solution)/shard_map/ppermute | solution.py:484
  39.2 7.7 %collective-permute-start.6 = (bf16[288,128]{1,0:T(8,128)(2,1)S(1)}, bf16[288,128]{1,0:T(8,128)(2,1)S(1)}, u32[]{:S(2)}, u32[]{:S(2)}) collective-permute-start(bf16[288,128]{1,0:T(8,128)(2,1)S(1)} %get-tuple-element.91), channel_id=1, source_target_pairs={{0,6},{1,7},{2,4},{3,5},{4,2},{5,3},{6,0},{7,1},{8,14},{9,15},{10,... | collective-permute-start | bytes 221192 | tf_op jit(solution)/shard_map/ppermute | solution.py:484
  40.7 6.9 %collective-permute-start.7 = (bf16[288,128]{1,0:T(8,128)(2,1)S(1)}, bf16[288,128]{1,0:T(8,128)(2,1)S(1)}, u32[]{:S(2)}, u32[]{:S(2)}) collective-permute-start(bf16[288,128]{1,0:T(8,128)(2,1)S(1)} %get-tuple-element.90), channel_id=1, source_target_pairs={{0,4},{1,5},{2,6},{3,7},{4,0},{5,1},{6,2},{7,3},{8,12},{9,13},{10,... | collective-permute-start | bytes 221192 | tf_op jit(solution)/shard_map/ppermute | solution.py:484
  47.6 6.4 %collective-permute-start.8 = (bf16[288,128]{1,0:T(8,128)(2,1)S(1)}, bf16[288,128]{1,0:T(8,128)(2,1)S(1)}, u32[]{:S(2)}, u32[]{:S(2)}) collective-permute-start(bf16[288,128]{1,0:T(8,128)(2,1)S(1)} %fusion.1), channel_id=1, source_target_pairs={{0,8},{1,9},{2,10},{3,11},{4,12},{5,13},{6,14},{7,15},{8,0},{9,1},... | collective-permute-start | bytes 221192 | tf_op jit(solution)/shard_map/ppermute | solution.py:484
  54.1 5.7 %collective-permute-start.10 = (bf16[288,128]{1,0:T(8,128)(2,1)S(1)}, bf16[288,128]{1,0:T(8,128)(2,1)S(1)}, u32[]{:S(2)}, u32[]{:S(2)}) collective-permute-start(bf16[288,128]{1,0:T(8,128)(2,1)S(1)} %add_convert_fusion), channel_id=1, source_target_pairs={{0,4},{1,5},{2,6},{3,7},{4,0},{5,1},{6,2},{7,3},{8,12},{9,13},{10,... | collective-permute-start | bytes 221192 | tf_op jit(solution)/shard_map/ppermute | solution.py:484
  54.2 6.1 %collective-permute-start.11 = (bf16[288,128]{1,0:T(8,128)(2,1)S(1)}, bf16[288,128]{1,0:T(8,128)(2,1)S(1)}, u32[]{:S(2)}, u32[]{:S(2)}) collective-permute-start(bf16[288,128]{1,0:T(8,128)(2,1)S(1)} %add_convert_fusion), channel_id=1, source_target_pairs={{0,6},{1,7},{2,4},{3,5},{4,2},{5,3},{6,0},{7,1},{8,14},{9,15},{10,... | collective-permute-start | bytes 221192 | tf_op jit(solution)/shard_map/ppermute | solution.py:484
  57.0 4.4 %collective-permute-start.9 = (bf16[288,128]{1,0:T(8,128)(2,1)S(1)}, bf16[288,128]{1,0:T(8,128)(2,1)S(1)}, u32[]{:S(2)}, u32[]{:S(2)}) collective-permute-start(bf16[288,128]{1,0:T(8,128)(2,1)S(1)} %add_convert_fusion), channel_id=1, source_target_pairs={{0,2},{1,3},{2,0},{3,1},{4,6},{5,7},{6,4},{7,5},{8,10},{9,11},{10,... | collective-permute-start | bytes 221192 | tf_op jit(solution)/shard_map/ppermute | solution.py:484
  61.4 1.6 %collective-permute-start.12 = (bf16[1152,128]{1,0:T(8,128)(2,1)S(1)}, bf16[1152,128]{1,0:T(8,128)(2,1)S(1)}, u32[]{:S(2)}, u32[]{:S(2)}) collective-permute-start(bf16[1152,128]{1,0:T(8,128)(2,1)S(1)} %constant_dynamic-update-slice_fusion.value_ref), channel_id=1, source_target_pairs={{0,1},{1,0},{2,3},{3,2},{4,5},{5,4},{6,7},{7,6},{8,9},{9,8},{10,11... | collective-permute-start | bytes 884744 | tf_op jit(solution)/shard_map/ppermute | solution.py:484

commit v10 on v9

--- a/solution.py
+++ b/solution.py
@@ -239,8 +239,7 @@
         base = 0 if odd else 2
         place_skip(held_ref[...], skip_ref[...], xs_ref, 384 * odd)
         place_skip(held_core_ref[...], skip_ref[...], xs_ref, 384 * (1 - odd))
-        for copy in copies:
-            copy.wait()
+        copies[0].wait()
         shift = shift_columns()
         for j in range(4):
             planes = [e for e in range(j, j + 3) if base <= e < base + 4]
@@ -264,6 +263,8 @@
 
                 term_ref[...] = weight_term(grad, xu_ref, skip_rows, j)
 
+        for copy in copies[1:]:
+            copy.wait()
         for plane in range(2):
             part = input_grad((0, 1) if odd else (2, 3), gs_ref, wi_ref, plane)
             part_ref[plane * 128 : (plane + 1) * 128, :] = part
@@ -486,7 +487,7 @@
     summed = keep + swap(send, 1).astype(F32)
     rounded = summed.astype(BF16)
     total = summed[:288]
-    for k in (1, 3, 2):
+    for k in (3, 2, 1):
         total = total + swap(rounded[k * 288 : (k + 1) * 288], 2 * k).astype(F32)
     total, back = lax.optimization_barrier((total, back))
     bit = 8
@@ -496,9 +497,9 @@
         bit *= 2
     own = total.astype(BF16)
     gathered = {k: swap(own, 2 * k) for k in (1, 3, 2)}
-    arrived = [gathered[k] for k in (1, 2, 3)]
+    arrived = [gathered[k] for k in (1, 3, 2)]
     arrived, own, others = lax.optimization_barrier((arrived, own, finish_others(back)))
-    gathered = dict(zip((1, 2, 3), arrived))
+    gathered = dict(zip((1, 3, 2), arrived))
     mine = jnp.concatenate([own] + [gathered[k] for k in (1, 2, 3)], axis=0)
     other = swap(mine, 1)
     sums = ()

time: 64.5 us -> 64.6 us (level)
  transfers between devices with their start and end apart: 15 -> 15, of which waited for: 8 -> 7; matrix products, arithmetic and copies ran while one was open for 4% -> 4% of each run, Pallas kernels for 15% -> 15%
where the time goes in v10:
time: 64.6 us; the launch traced here: 64.2 us
  starting transfers between devices  24.6 us (38%)
  waiting for transfers between devices  19.8 us (31%)
  Pallas kernels  14.1 us (22%)
  local copies, waits for them, and re-layouts  4.42 us (7%)
  between operations  1.07 us (2%)
    ppermute x9, waiting for transfers between devices, swap(): return lax.ppermute(value, AXIS, [(i, i ^ bit) for i in range(n)])  13.1 us
    ppermute x9, starting transfers between devices, swap(): return lax.ppermute(value, AXIS, [(i, i ^ bit) for i in range(n)])  9.79 us
    all_to_all x1, starting transfers between devices, local(): held = lax.all_to_all(sent, AXIS, split_axis=0, concat_axis=0, tiled=True)  7.36 us
    all_to_all x1, waiting for transfers between devices, local(): held = lax.all_to_all(sent, AXIS, split_axis=0, concat_axis=0, tiled=True)  6.7 us
    all_to_all x1, starting transfers between devices, local(): lax.all_to_all(skip_part, AXIS, split_axis=0, concat_axis=0, tiled=True)  4.49 us
    pallas_call x1, Pallas kernels, local(): pl.pallas_call(inner_kernel, out_shape=(inside((768, 1024)), inside((128,...  4.06 us
    pallas_call x1, Pallas kernels, local(): pl.pallas_call(functools.partial(main_kernel, scale), out_shape=(outside(...  3.65 us
    pallas_call x1, Pallas kernels, local(): pl.pallas_call(edge_kernel, out_shape=(inside((1152, 1024)), inside((256,...  2.66 us
  transfers between devices with their start and end apart: 15, of which 7 were waited for; matrix products, arithmetic and copies ran while one was open for 4% of the time, Pallas kernels for 15%

profile of v10, /device:TPU:0, one launch (start us, length us, event | category | flops | bytes accessed | tf_op | source)
XLA Modules:
  0.0 64.2 jit_solution(14421861212211556762)
XLA Ops:
  0.7 1.4 %reshape.43 = bf16[64,16,128]{2,1,0:T(8,128)(2,1)S(1)} reshape(bf16[64,32,64]{2,1,0:T(8,128)(2,1)} %param.6) | data formatting | bytes 524288 | tf_op jit(solution)/shard_map/reshape | solution.py:532
  2.0 0.8 %copy.17 = bf16[64,16,128]{2,0,1:T(8,128)(2,1)} copy(bf16[64,16,128]{2,1,0:T(8,128)(2,1)S(1)} %reshape.43) | data formatting | bytes 524288 | tf_op jit(solution)/shard_map/reshape | solution.py:532
  2.8 7.4 %all-to-all-start = ((bf16[16,64,128]{2,1,0:T(8,128)(2,1)}), bf16[16,64,128]{2,1,0:T(8,128)(2,1)S(1)}, u32[]{:S(2)}, u32[]{:S(2)}) async-start(bf16[16,64,128]{2,1,0:T(8,128)(2,1)} %bitcast.12), calls=%async_computation | async-start | bytes 524288 | tf_op jit(solution)/shard_map/all_to_all | solution.py:533
  10.8 0.7 %collective-permute-start.2 = (bf16[128,768]{1,0:T(8,128)(2,1)S(1)}, bf16[128,768]{1,0:T(8,128)(2,1)S(1)}, u32[]{:S(2)}, u32[]{:S(2)}) collective-permute-start(bf16[128,768]{1,0:T(8,128)(2,1)S(1)} %get-tuple-element.96), channel_id=1, source_target_pairs={{1,2},{2,1},{3,4},{4,3},{5,6},{6,5},{7,8},{8,7},{9,10},{10,9},{11,... | collective-permute-start | bytes 589832 | tf_op jit(solution)/shard_map/ppermute | solution.py:546
  11.5 2.0 %prepare.1 = (bf16[384,1024]{1,0:T(8,128)(2,1)S(1)}, bf16[256,512]{1,0:T(8,128)(2,1)}, bf16[192,576]{1,0:T(8,128)(2,1)}, bf16[192,576]{1,0:T(8,128)(2,1)}, bf16[...) custom-call(bf16[128,256]{1,0:T(8,128)(2,1)S(1)} %bitcast.18, ...), custom_call_target="tpu_custom_call" | custom-call | flops 1840000000 | bytes 1000000 | tf_op jit(solution)/shard_map/prepare/pallas_call | solution.py:547
  13.5 6.7 %all-to-all-done = bf16[16,64,128]{2,1,0:T(8,128)(2,1)S(1)} async-done(((bf16[16,64,128]{2,1,0:T(8,128)(2,1)}), bf16[16,64,128]{2,1,0:T(8,128)(2,1)S(1)}, u32[]{:S(2)}, u32[]{:S(2)}) %all-to-all-start) | async-done | bytes 262176 | tf_op jit(solution)/shard_map/all_to_all | solution.py:533
  20.2 0.7 %collective-permute-start = (bf16[16,64,128]{2,1,0:T(8,128)(2,1)S(1)}, bf16[16,64,128]{2,1,0:T(8,128)(2,1)S(1)}, u32[]{:S(2)}, u32[]{:S(2)}) collective-permute-start(bf16[16,64,128]{2,1,0:T(8,128)(2,1)S(1)} %all-to-all-done), channel_id=1, source_target_pairs={{1,2},{2,1},{3,4},{4,3},{5,6},{6,5},{7,8},{8,7},{9,10},{10,9},{11,... | collective-permute-start | bytes 786440 | tf_op jit(solution)/shard_map/ppermute | solution.py:565
  20.9 1.2 %collective-permute-start.3 = (bf16[16,64,128]{2,1,0:T(8,128)(2,1)S(1)}, bf16[16,64,128]{2,1,0:T(8,128)(2,1)S(1)}, u32[]{:S(2)}, u32[]{:S(2)}) collective-permute-start(bf16[16,64,128]{2,1,0:T(8,128)(2,1)S(1)} %all-to-all-done), channel_id=1, source_target_pairs={{0,1},{1,0},{2,3},{3,2},{4,5},{5,4},{6,7},{7,6},{8,9},{9,8},{10,11... | collective-permute-start | bytes 786440 | tf_op jit(solution)/shard_map/ppermute | solution.py:567
  22.1 2.7 %edges.1 = (bf16[1152,1024]{1,0:T(8,128)(2,1)S(1)}, f32[256,1024]{1,0:T(8,128)S(1)}) custom-call(bf16[128,768]{1,0:T(8,128)(2,1)S(1)} %collective-permute-done.1.core_ref.edge_ref, bf16[128,768]{1,0:T(8,128)(2,1)S(1)} %collective-permute-done.2.cross_ref.edge_ref, bf16[8,64,128]{2,1,0:T(8,128)(2,1)S(1)} %copy-done.2, ...), custom_call_target="tpu_custom_call" | custom-call | flops 3000000000 | bytes 1000000 | tf_op jit(solution)/shard_map/edges/pallas_call | solution.py:569
  24.8 4.1 %inner.1 = (bf16[768,1024]{1,0:T(8,128)(2,1)S(1)}, f32[128,1024]{1,0:T(8,128)S(1)}, f32[256,1024]{1,0:T(8,128)S(1)}, bf16[64,1024]{1,0:T(8,128)(2,1)S(1)}, f32[1...) custom-call(bf16[128,768]{1,0:T(8,128)(2,1)S(1)} %collective-permute, ...), custom_call_target="tpu_custom_call" | custom-call | flops 4000000000 | bytes 1000000 | tf_op jit(solution)/shard_map/inner/pallas_call | solution.py:579
  28.8 3.7 %section.1 = (bf16[64,2048]{1,0:T(8,128)(2,1)}, bf16[128,256]{1,0:T(8,128)(2,1)}, bf16[16,64,128]{2,1,0:T(8,128)(2,1)}, f32[1152,128]{1,0:T(8,128)S(1)}, bf16[1152,128]{1,0:T(8,128)(2,1)S(1)}) custom-call(bf16[8,2,64,128]{3,2,1,0:T(8,128)(2,1)S(1)} %bitcast.19, bf16[64,2048]{1,0:T(8,128)(2,1)S(1)} %bitcast.15, ...), custom_call_target="tpu_custom_call" | custom-call | flops 8280000000 | bytes 1000000 | tf_op jit(solution)/shard_map/section/pallas_call | solution.py:604
  32.7 4.5 %all-to-all-start.1 = ((bf16[16,64,128]{2,1,0:T(8,128)(2,1)}), bf16[16,64,128]{2,1,0:T(8,128)(2,1)S(1)}, u32[]{:S(2)}, u32[]{:S(2)}) async-start(bf16[16,64,128]{2,1,0:T(8,128)(2,1)} %get-tuple-element.71), calls=%async_computation.1 | async-start | bytes 524288 | tf_op jit(solution)/shard_map/all_to_all | solution.py:653
  37.3 2.9 %collective-permute-start.5 = (bf16[288,128]{1,0:T(8,128)(2,1)S(1)}, bf16[288,128]{1,0:T(8,128)(2,1)S(1)}, u32[]{:S(2)}, u32[]{:S(2)}) collective-permute-start(bf16[288,128]{1,0:T(8,128)(2,1)S(1)} %get-tuple-element.89), channel_id=1, source_target_pairs={{0,6},{1,7},{2,4},{3,5},{4,2},{5,3},{6,0},{7,1},{8,14},{9,15},{10,... | collective-permute-start | bytes 221192 | tf_op jit(solution)/shard_map/ppermute | solution.py:485
  40.9 6.4 %collective-permute-done.5 = bf16[288,128]{1,0:T(8,128)(2,1)S(1)} collective-permute-done((bf16[288,128]{1,0:T(8,128)(2,1)S(1)}, bf16[288,128]{1,0:T(8,128)(2,1)S(1)}, u32[]{:S(2)}, u32[]{:S(2)}) %collective-permute-start.5) | collective-permute-done | bytes 73760 | tf_op jit(solution)/shard_map/ppermute | solution.py:485
  47.7 2.4 %collective-permute-start.8 = (bf16[288,128]{1,0:T(8,128)(2,1)S(1)}, bf16[288,128]{1,0:T(8,128)(2,1)S(1)}, u32[]{:S(2)}, u32[]{:S(2)}) collective-permute-start(bf16[288,128]{1,0:T(8,128)(2,1)S(1)} %fusion.1), channel_id=1, source_target_pairs={{0,8},{1,9},{2,10},{3,11},{4,12},{5,13},{6,14},{7,15},{8,0},{9,1},... | collective-permute-start | bytes 221192 | tf_op jit(solution)/shard_map/ppermute | solution.py:485
  50.2 4.0 %collective-permute-done.8 = bf16[288,128]{1,0:T(8,128)(2,1)S(1)} collective-permute-done((bf16[288,128]{1,0:T(8,128)(2,1)S(1)}, bf16[288,128]{1,0:T(8,128)(2,1)S(1)}, u32[]{:S(2)}, u32[]{:S(2)}) %collective-permute-start.8) | collective-permute-done | bytes 73760 | tf_op jit(solution)/shard_map/ppermute | solution.py:485
  54.7 2.4 %collective-permute-start.11 = (bf16[288,128]{1,0:T(8,128)(2,1)S(1)}, bf16[288,128]{1,0:T(8,128)(2,1)S(1)}, u32[]{:S(2)}, u32[]{:S(2)}) collective-permute-start(bf16[288,128]{1,0:T(8,128)(2,1)S(1)} %add_convert_fusion), channel_id=1, source_target_pairs={{0,4},{1,5},{2,6},{3,7},{4,0},{5,1},{6,2},{7,3},{8,12},{9,13},{10,... | collective-permute-start | bytes 221192 | tf_op jit(solution)/shard_map/ppermute | solution.py:485
  57.1 0.6 collective-permute-start.9
  57.8 0.9 %reshape.49 = bf16[64,2,1024]{2,1,0:T(2,128)(2,1)} reshape(bf16[64,2048]{1,0:T(8,128)(2,1)S(1)} %copy-done.4) | data formatting | bytes 524288 | tf_op jit(solution)/shard_map/reshape | solution.py:657
  58.8 1.1 %reshape.51 = bf16[64,32,64]{2,1,0:T(8,128)(2,1)} reshape(bf16[64,16,128]{2,1,0:T(8,128)(2,1)S(1)} %copy.14) | data formatting | bytes 524288 | tf_op jit(solution)/shard_map/reshape | solution.py:659
  60.4 1.1 %collective-permute-done.9 = bf16[288,128]{1,0:T(8,128)(2,1)S(1)} collective-permute-done((bf16[288,128]{1,0:T(8,128)(2,1)S(1)}, bf16[288,128]{1,0:T(8,128)(2,1)S(1)}, u32[]{:S(2)}, u32[]{:S(2)}) %collective-permute-start.9) | collective-permute-done | bytes 73760 | tf_op jit(solution)/shard_map/ppermute | solution.py:485
  61.6 0.9 %finish.2 = (f32[54,32,128]{2,1,0:T(8,128)}, f32[16,32,128]{2,1,0:T(8,128)}) custom-call(bf16[1152,128]{1,0:T(8,128)(2,1)S(1)} %constant_dynamic-update-slice_fusion.value_ref), custom_call_target="tpu_custom_call" | custom-call | flops 1200000000 | bytes 1000000 | tf_op jit(solution)/shard_map/finish/pallas_call | solution.py:507
  62.5 0.7 %collective-permute-done.12.value_ref = bf16[1152,128]{1,0:T(8,128)(2,1)S(1)} collective-permute-done((bf16[1152,128]{1,0:T(8,128)(2,1)S(1)}, bf16[1152,128]{1,0:T(8,128)(2,1)S(1)}, u32[]{:S(2)}, u32[]{:S(2)}) %collective-permute-start.12) | collective-permute-done | bytes 294944 | tf_op jit(solution)/shard_map/ppermute | solution.py:485
  63.2 0.9 %finish.3 = (f32[54,32,128]{2,1,0:T(8,128)}, f32[16,32,128]{2,1,0:T(8,128)}) custom-call(bf16[1152,128]{1,0:T(8,128)(2,1)S(1)} %collective-permute-done.12.value_ref, f32[54,32,128]{2,1,0:T(8,128)} %get-tuple-element.83.refs_0_, f32[16,32,128]{2,1,0:T(8,128)} %get-tuple-element.84.refs_1_), custom_call_target="tpu_custom_call", output_to_operand_aliasing={{0}: (1, {}), {1}: (2, {})} | custom-call | flops 1200000000 | bytes 1000000 | tf_op jit(solution)/shard_map/finish/pallas_call | solution.py:507
  (38 shorter events, 3.3 us)
Async XLA Ops:
  0.6 9.6 %copy-start.3 = (bf16[64,2,1024]{2,1,0:T(2,128)(2,1)S(1)}, bf16[64,2,1024]{2,1,0:T(2,128)(2,1)}, u32[]{:S(2)}) copy-start(bf16[64,2,1024]{2,1,0:T(2,128)(2,1)} %param.7) | copy-start | bytes 786436
  0.6 9.7 %copy-start = (bf16[128,1,256]{2,0,1:T(8,128)(2,1)S(1)}, bf16[128,1,256]{2,0,1:T(8,128)(2,1)}, u32[]{:S(2)}) copy-start(bf16[128,1,256]{2,0,1:T(8,128)(2,1)} %param.5) | copy-start | bytes 196612
  2.0 9.5 %copy-start.1 = (bf16[27,64,128]{2,1,0:T(8,128)(2,1)S(1)}, bf16[27,64,128]{2,1,0:T(8,128)(2,1)}, u32[]{:S(2)}) copy-start(bf16[27,64,128]{2,1,0:T(8,128)(2,1)} %wc_ref.1) | copy-start | bytes 1327108
  2.0 9.5 %copy-start.2 = (bf16[8,64,128]{2,1,0:T(8,128)(2,1)S(1)}, bf16[8,64,128]{2,1,0:T(8,128)(2,1)}, u32[]{:S(2)}) copy-start(bf16[8,64,128]{2,1,0:T(8,128)(2,1)} %wup_ref.3) | copy-start | bytes 393220
  2.8 17.4 %all-to-all-start = ((bf16[16,64,128]{2,1,0:T(8,128)(2,1)}), bf16[16,64,128]{2,1,0:T(8,128)(2,1)S(1)}, u32[]{:S(2)}, u32[]{:S(2)}) async-start(bf16[16,64,128]{2,1,0:T(8,128)(2,1)} %bitcast.12), calls=%async_computation | async-start | bytes 524288 | tf_op jit(solution)/shard_map/all_to_all | solution.py:533
  10.3 10.6 %collective-permute-start.1 = (bf16[128,768]{1,0:T(8,128)(2,1)S(1)}, bf16[128,768]{1,0:T(8,128)(2,1)S(1)}, u32[]{:S(2)}, u32[]{:S(2)}) collective-permute-start(bf16[128,768]{1,0:T(8,128)(2,1)S(1)} %get-tuple-element.97), channel_id=1, source_target_pairs={{0,1},{1,0},{2,3},{3,2},{4,5},{5,4},{6,7},{7,6},{8,9},{9,8},{10,11... | collective-permute-start | bytes 589832 | tf_op jit(solution)/shard_map/ppermute | solution.py:545
  10.8 10.1 %collective-permute-start.2 = (bf16[128,768]{1,0:T(8,128)(2,1)S(1)}, bf16[128,768]{1,0:T(8,128)(2,1)S(1)}, u32[]{:S(2)}, u32[]{:S(2)}) collective-permute-start(bf16[128,768]{1,0:T(8,128)(2,1)S(1)} %get-tuple-element.96), channel_id=1, source_target_pairs={{1,2},{2,1},{3,4},{4,3},{5,6},{6,5},{7,8},{8,7},{9,10},{10,9},{11,... | collective-permute-start | bytes 589832 | tf_op jit(solution)/shard_map/ppermute | solution.py:546
  20.2 8.6 %collective-permute-start = (bf16[16,64,128]{2,1,0:T(8,128)(2,1)S(1)}, bf16[16,64,128]{2,1,0:T(8,128)(2,1)S(1)}, u32[]{:S(2)}, u32[]{:S(2)}) collective-permute-start(bf16[16,64,128]{2,1,0:T(8,128)(2,1)S(1)} %all-to-all-done), channel_id=1, source_target_pairs={{1,2},{2,1},{3,4},{4,3},{5,6},{6,5},{7,8},{8,7},{9,10},{10,9},{11,... | collective-permute-start | bytes 786440 | tf_op jit(solution)/shard_map/ppermute | solution.py:565
  20.9 3.8 %collective-permute-start.3 = (bf16[16,64,128]{2,1,0:T(8,128)(2,1)S(1)}, bf16[16,64,128]{2,1,0:T(8,128)(2,1)S(1)}, u32[]{:S(2)}, u32[]{:S(2)}) collective-permute-start(bf16[16,64,128]{2,1,0:T(8,128)(2,1)S(1)} %all-to-all-done), channel_id=1, source_target_pairs={{0,1},{1,0},{2,3},{3,2},{4,5},{5,4},{6,7},{7,6},{8,9},{9,8},{10,11... | collective-permute-start | bytes 786440 | tf_op jit(solution)/shard_map/ppermute | solution.py:567
  32.5 4.7 %collective-permute-start.4 = (bf16[1152,128]{1,0:T(8,128)(2,1)S(1)}, bf16[1152,128]{1,0:T(8,128)(2,1)S(1)}, u32[]{:S(2)}, u32[]{:S(2)}) collective-permute-start(bf16[1152,128]{1,0:T(8,128)(2,1)S(1)} %get-tuple-element.70), channel_id=1, source_target_pairs={{0,1},{1,0},{2,3},{3,2},{4,5},{5,4},{6,7},{7,6},{8,9},{9,8},{10,11... | collective-permute-start | bytes 884744 | tf_op jit(solution)/shard_map/ppermute | solution.py:485
  32.7 15.1 %all-to-all-start.1 = ((bf16[16,64,128]{2,1,0:T(8,128)(2,1)}), bf16[16,64,128]{2,1,0:T(8,128)(2,1)S(1)}, u32[]{:S(2)}, u32[]{:S(2)}) async-start(bf16[16,64,128]{2,1,0:T(8,128)(2,1)} %get-tuple-element.71), calls=%async_computation.1 | async-start | bytes 524288 | tf_op jit(solution)/shard_map/all_to_all | solution.py:653
  37.2 20.6 %copy-start.4 = (bf16[64,2048]{1,0:T(8,128)(2,1)S(1)}, bf16[64,2048]{1,0:T(8,128)(2,1)}, u32[]{:S(2)}) copy-start(bf16[64,2048]{1,0:T(8,128)(2,1)} %get-tuple-element.73) | copy-start | bytes 786436
  37.3 10.0 %collective-permute-start.5 = (bf16[288,128]{1,0:T(8,128)(2,1)S(1)}, bf16[288,128]{1,0:T(8,128)(2,1)S(1)}, u32[]{:S(2)}, u32[]{:S(2)}) collective-permute-start(bf16[288,128]{1,0:T(8,128)(2,1)S(1)} %get-tuple-element.89), channel_id=1, source_target_pairs={{0,6},{1,7},{2,4},{3,5},{4,2},{5,3},{6,0},{7,1},{8,14},{9,15},{10,... | collective-permute-start | bytes 221192 | tf_op jit(solution)/shard_map/ppermute | solution.py:485
  40.2 7.5 %collective-permute-start.6 = (bf16[288,128]{1,0:T(8,128)(2,1)S(1)}, bf16[288,128]{1,0:T(8,128)(2,1)S(1)}, u32[]{:S(2)}, u32[]{:S(2)}) collective-permute-start(bf16[288,128]{1,0:T(8,128)(2,1)S(1)} %get-tuple-element.91), channel_id=1, source_target_pairs={{0,4},{1,5},{2,6},{3,7},{4,0},{5,1},{6,2},{7,3},{8,12},{9,13},{10,... | collective-permute-start | bytes 221192 | tf_op jit(solution)/shard_map/ppermute | solution.py:485
  40.8 6.9 %collective-permute-start.7 = (bf16[288,128]{1,0:T(8,128)(2,1)S(1)}, bf16[288,128]{1,0:T(8,128)(2,1)S(1)}, u32[]{:S(2)}, u32[]{:S(2)}) collective-permute-start(bf16[288,128]{1,0:T(8,128)(2,1)S(1)} %get-tuple-element.90), channel_id=1, source_target_pairs={{0,2},{1,3},{2,0},{3,1},{4,6},{5,7},{6,4},{7,5},{8,10},{9,11},{10,... | collective-permute-start | bytes 221192 | tf_op jit(solution)/shard_map/ppermute | solution.py:485
  47.7 6.4 %collective-permute-start.8 = (bf16[288,128]{1,0:T(8,128)(2,1)S(1)}, bf16[288,128]{1,0:T(8,128)(2,1)S(1)}, u32[]{:S(2)}, u32[]{:S(2)}) collective-permute-start(bf16[288,128]{1,0:T(8,128)(2,1)S(1)} %fusion.1), channel_id=1, source_target_pairs={{0,8},{1,9},{2,10},{3,11},{4,12},{5,13},{6,14},{7,15},{8,0},{9,1},... | collective-permute-start | bytes 221192 | tf_op jit(solution)/shard_map/ppermute | solution.py:485
  54.2 5.7 %collective-permute-start.10 = (bf16[288,128]{1,0:T(8,128)(2,1)S(1)}, bf16[288,128]{1,0:T(8,128)(2,1)S(1)}, u32[]{:S(2)}, u32[]{:S(2)}) collective-permute-start(bf16[288,128]{1,0:T(8,128)(2,1)S(1)} %add_convert_fusion), channel_id=1, source_target_pairs={{0,6},{1,7},{2,4},{3,5},{4,2},{5,3},{6,0},{7,1},{8,14},{9,15},{10,... | collective-permute-start | bytes 221192 | tf_op jit(solution)/shard_map/ppermute | solution.py:485
  54.7 5.7 %collective-permute-start.11 = (bf16[288,128]{1,0:T(8,128)(2,1)S(1)}, bf16[288,128]{1,0:T(8,128)(2,1)S(1)}, u32[]{:S(2)}, u32[]{:S(2)}) collective-permute-start(bf16[288,128]{1,0:T(8,128)(2,1)S(1)} %add_convert_fusion), channel_id=1, source_target_pairs={{0,4},{1,5},{2,6},{3,7},{4,0},{5,1},{6,2},{7,3},{8,12},{9,13},{10,... | collective-permute-start | bytes 221192 | tf_op jit(solution)/shard_map/ppermute | solution.py:485
  57.1 4.4 %collective-permute-start.9 = (bf16[288,128]{1,0:T(8,128)(2,1)S(1)}, bf16[288,128]{1,0:T(8,128)(2,1)S(1)}, u32[]{:S(2)}, u32[]{:S(2)}) collective-permute-start(bf16[288,128]{1,0:T(8,128)(2,1)S(1)} %add_convert_fusion), channel_id=1, source_target_pairs={{0,2},{1,3},{2,0},{3,1},{4,6},{5,7},{6,4},{7,5},{8,10},{9,11},{10,... | collective-permute-start | bytes 221192 | tf_op jit(solution)/shard_map/ppermute | solution.py:485
  61.5 1.6 %collective-permute-start.12 = (bf16[1152,128]{1,0:T(8,128)(2,1)S(1)}, bf16[1152,128]{1,0:T(8,128)(2,1)S(1)}, u32[]{:S(2)}, u32[]{:S(2)}) collective-permute-start(bf16[1152,128]{1,0:T(8,128)(2,1)S(1)} %constant_dynamic-update-slice_fusion.value_ref), channel_id=1, source_target_pairs={{0,1},{1,0},{2,3},{3,2},{4,5},{5,4},{6,7},{7,6},{8,9},{9,8},{10,11... | collective-permute-start | bytes 884744 | tf_op jit(solution)/shard_map/ppermute | solution.py:485
